TPU v7x, 32 devices: a whole 2x2x4 slice. The times are simulated.
32 devices in a mesh: dp: 16 (over z, y, x), rep: 2 (over core).
Axes of the slice: x: 2, y: 2, z: 4, core: 2. Of those that a mesh axis runs over, the one named last changes fastest.
Arguments:
- hidden_old: bfloat16 [8192, 6144], P(('dp', 'rep')), may hold values from -400 to 400
- cotangent: bfloat16 [8192, 128], P(('dp', 'rep')), may hold values from -0.15625 to 0.15625
- gain_old: float32 [6144], replicated, may hold values from 0.1 to 1.9
- old_bounds: int32 [17], replicated, may hold values from 0 to 6144, as said below
- new_bounds: int32 [17], replicated, may hold values from 0 to 8192, as said below
- source_map: int32 [8192], replicated, may hold values from 0 to 6143, as said below
- weight_old: bfloat16 [8192, 128], P('dp'), may hold values from -0.078125 to 0.078125
- moment_first: float32 [8192, 128], P('dp'), may hold values from -6 to 6
- moment_second: float32 [8192, 128], P('dp'), may hold values from 0.25 to 4
Outputs:
- projected: bfloat16 [8192, 128], P(('dp', 'rep'))
- gain_grad: float32 [8192], replicated
- first_next: float32 [10240, 128], P('dp')
- second_next: float32 [10240, 128], P('dp')
- adam_step: float32 [10240, 128], P('dp')
Inputs may be any that keep to these rules, and one draw needn't show every extreme that they name: old_bounds[0] = 0, old_bounds[16] = 6144; device p holds old units old_bounds[p] to old_bounds[p+1] - 1, between 256 and 512 of them, exactly 512 on some device. new_bounds[0] = 0, new_bounds[16] = 8192; device q holds new units new_bounds[q] to new_bounds[q+1] - 1, between 384 and 640 of them, exactly 640 on some device. `source_map`: the s-th new unit of a device (counted from its first) copies an old unit held by old device (s + c) mod 16, with an offset c of that new device; so at most 40 new units of one device copy units of one old device, and some pair of devices reaches 40.
All inputs are finite; a program needn't handle non-finite values.
Results may differ from a plain program's by a relative error of at most 0.0049.
Values may be sent and summed in bfloat16 or wider, within the bound.
No kernel may reach another device: no remote copies, remote signals or barrier semaphores. Data moves between devices by JAX's collectives and lax.ppermute only.
A program may use at most 64 MiB of HBM per device.

v0:
```python
import jax
import jax.numpy as jnp
from jax import lax
from jax.sharding import PartitionSpec as P

D_OLD = 6144
D_NEW = 8192


def owners(bounds, unit_ids):
    return jnp.sum((bounds[None, 1:] <= unit_ids[:, None]).astype(jnp.int32), axis=1)


def routing(
    owner_of,
    local_of,
    table_rows,
    slot_cap,
    dev_index,
    dest_owner,
    new_bounds,
    positions,
    wanted,
    own_slots,
    dp_count,
):
    from_me = (owner_of == dev_index).astype(jnp.int32)
    before = jnp.cumsum(from_me) - from_me
    send_slot = before - before[new_bounds[dest_owner]]
    target = jnp.where(from_me > 0, dest_owner * slot_cap + send_slot, dp_count * slot_cap)
    chosen = jnp.zeros((dp_count * slot_cap,), jnp.int32).at[target].set(positions, mode="drop")
    filled = jnp.zeros((dp_count * slot_cap,), jnp.bool_).at[target].set(True, mode="drop")
    local_row = jnp.clip(local_of[chosen], 0, table_rows - 1)
    anchor = owner_of[wanted]
    earlier = (own_slots[None, :] < own_slots[:, None]) & (anchor[None, :] == anchor[:, None])
    arrival_rank = jnp.sum(earlier.astype(jnp.int32), axis=1)
    incoming = jnp.minimum(anchor * slot_cap + arrival_rank, dp_count * slot_cap - 1)
    return (local_row, filled, incoming)


def outgoing(source_table, route_info):
    return jnp.where(
        route_info[1][:, None], source_table[route_info[0]], jnp.zeros((), source_table.dtype)
    )


def arrived(source_table, route_info, live_new):
    return jnp.where(live_new[:, None], source_table[route_info[2]], 0.0)


def on_device(
    hidden_old,
    cotangent,
    gain_old,
    old_bounds,
    new_bounds,
    source_map,
    weight_old,
    moment_first,
    moment_second,
):
    dp_count = lax.axis_size("dp")
    dev_index = lax.axis_index("dp")
    old_cap = weight_old.shape[0]
    new_mean = D_NEW // dp_count
    new_cap = new_mean + new_mean // 4
    pair_cap = (new_cap + dp_count - 1) // dp_count
    positions = jnp.arange(D_NEW, dtype=jnp.int32)
    first_use = jnp.full((D_OLD,), D_NEW, jnp.int32).at[source_map].min(positions)
    unit_used = first_use < D_NEW
    keep_mask = first_use[source_map] == positions
    copies = jnp.zeros((D_OLD,), jnp.float32).at[source_map].add(1.0)
    padded = jnp.arange(dp_count * old_cap, dtype=jnp.int32)
    slot_owner = padded // old_cap
    within = padded - slot_owner * old_cap
    live_old = within < old_bounds[slot_owner + 1] - old_bounds[slot_owner]
    slot_unit = jnp.minimum(old_bounds[slot_owner] + within, D_OLD - 1)
    weight_live = live_old & unit_used[slot_unit]
    source_owner = owners(old_bounds, source_map)
    source_slot = source_owner * old_cap + source_map - old_bounds[source_owner]
    dest_owner = owners(new_bounds, positions)
    own_slots = jnp.arange(new_cap, dtype=jnp.int32)
    live_new = own_slots < new_bounds[dev_index + 1] - new_bounds[dev_index]
    wanted = jnp.minimum(new_bounds[dev_index] + own_slots, D_NEW - 1)
    grad_route = routing(
        source_owner,
        source_map - old_bounds[dev_index],
        old_cap,
        pair_cap,
        dev_index,
        dest_owner,
        new_bounds,
        positions,
        wanted,
        own_slots,
        dp_count,
    )
    moment_route = routing(
        source_owner,
        source_map - old_bounds[dev_index],
        old_cap,
        pair_cap,
        dev_index,
        dest_owner,
        new_bounds,
        positions,
        wanted,
        own_slots,
        dp_count,
    )
    stream = hidden_old.astype(jnp.float32)
    squares = jnp.sum(stream * stream * copies, axis=1)
    inv_rms = lax.rsqrt(squares / D_NEW + 1e-05)
    normed = (stream * inv_rms[:, None] * gain_old).astype(jnp.bfloat16)
    normed_slots = jnp.take(normed, slot_unit, axis=1)
    hidden_slots = jnp.take(hidden_old, slot_unit, axis=1)
    weight_block = lax.all_gather(weight_old, "dp", axis=0, tiled=True)
    masked_block = jnp.where(weight_live[:, None], weight_block, jnp.zeros((), weight_block.dtype))
    columns = normed_slots
    key_sums = jnp.dot(columns, masked_block, preferred_element_type=jnp.float32)
    slopes = lax.dot_general(
        cotangent, masked_block, (((1,), (1,)), ((), ())), preferred_element_type=jnp.float32
    )
    scaled = hidden_slots.astype(jnp.float32) * inv_rms[:, None]
    column_terms = jnp.sum(slopes * scaled, axis=0)
    key_sums, column_terms = (key_sums, column_terms)
    projected = key_sums.astype(jnp.bfloat16)
    columns = normed_slots
    grad_own = lax.psum_scatter(
        lax.dot_general(
            columns, cotangent, (((0,), (0,)), ((), ())), preferred_element_type=jnp.float32
        ),
        "dp",
        scatter_dimension=0,
        tiled=True,
    )
    grad_own = lax.psum(grad_own.astype(jnp.bfloat16), "rep").astype(jnp.float32)
    column_total = lax.psum(column_terms, ("dp", "rep"))
    gain_grad = jnp.where(keep_mask, column_total[source_slot], 0.0)
    moved_grad, moved_first, moved_second = (
        lax.all_to_all(
            outgoing(grad_own, grad_route), "dp", split_axis=0, concat_axis=0, tiled=True
        ),
        lax.all_to_all(
            outgoing(moment_first, moment_route), "dp", split_axis=0, concat_axis=0, tiled=True
        ),
        lax.all_to_all(
            outgoing(moment_second, moment_route), "dp", split_axis=0, concat_axis=0, tiled=True
        ),
    )
    grad_new = arrived(moved_grad, grad_route, live_new)
    first_next = jnp.where(
        live_new[:, None], 0.9 * arrived(moved_first, moment_route, live_new) + 0.1 * grad_new, 0.0
    )
    second_next = jnp.where(
        live_new[:, None],
        0.95 * arrived(moved_second, moment_route, live_new) + 0.05 * grad_new * grad_new,
        0.0,
    )
    adam_step = first_next / (jnp.sqrt(second_next) + 1e-08)
    return (projected, gain_grad, first_next, second_next, adam_step)


def solution(mesh):
    placed = (
        P(("dp", "rep"), None),
        P(("dp", "rep"), None),
        P(),
        P(),
        P(),
        P(),
        P("dp", None),
        P("dp", None),
        P("dp", None),
    )
    return jax.shard_map(
        on_device,
        mesh=mesh,
        in_specs=placed,
        out_specs=(P(("dp", "rep"), None), P(), P("dp", None), P("dp", None), P("dp", None)),
        check_vma=False,
    )
```

profile of v0, /device:TPU:0, one launch (start us, length us, event | category | flops | bytes accessed | tf_op | source)
XLA Modules:
  0.0 749.5 jit_solution(12491640202311818620)
XLA Ops:
  9.9 4.5 compare_select_fusion.25
  14.4 6.3 compare_and_fusion
  20.7 3.2 copy.20
  25.8 44.6 %scatter_custom_fusion = f32[6144]{0:T(1024)} fusion(s32[8192]{0:T(1024)} %get-tuple-element.42, f32[8192]{0:T(1024)} %broadcast.609, f32[]{:T(128)} %constant.37.clone.1), kind=kCustom, calls=%fused_computation.165 | custom fusion | flops 8192 | bytes 25088 | tf_op jit(solution)/shard_map/scatter-add | solution.py:72
  72.1 2.9 fusion.4
  75.0 33.2 %gather_fusion.12 = bf16[8192,256]{1,0:T(8,128)(2,1)} fusion(bf16[256,6144]{0,1:T(8,128)(2,1)} %fusion.4, s32[8192]{0:T(1024)S(1)} %broadcast_clamp_fusion.3), kind=kCustom, calls=%fused_computation.clone | custom fusion | bytes 8421376 | tf_op jit(solution)/shard_map/jit(_take)/gather | solution.py:115
  108.2 7.2 fusion.5
  115.5 97.9 %reduce-scatter.2.cloned.1.call-done = f32[512,128]{1,0:T(8,128)} async-done(((f32[8192,128]{1,0:T(8,128)}), f32[512,128]{1,0:T(8,128)}) %reduce-scatter.2.cloned.1.call-update) | async-done | bytes 262160 | tf_op jit(solution)/shard_map/reduce_scatter | solution.py:129
  218.0 4.5 compare_select_fusion.7
  223.5 6.2 select_select_fusion
  237.4 80.7 %gather_fusion.3 = s32[8192]{0:T(1024)} fusion(s32[8192]{0:T(1024)S(1)} %get-tuple-element.31, s32[8192]{0:T(1024)} %broadcast_clamp_fusion), kind=kCustom, calls=%fused_computation.5 | custom fusion | bytes 98304 | tf_op jit(solution)/shard_map/gather | solution.py:29
  318.1 6.1 compare_select_fusion.13
  324.2 30.8 %scatter_custom_fusion.3 = s32[640]{0:T(1024)S(1)} fusion(s32[8192]{0:T(1024)} %bitcast.97, s32[8192]{0:T(1024)S(1)} %iota.49, s32[]{:T(128)} %constant.38.clone.1), kind=kCustom, calls=%fused_computation.178 | custom fusion | bytes 3072 | tf_op jit(solution)/shard_map/scatter | solution.py:31
  355.0 3.9 gather_fusion.4
  361.2 3.2 gather_fusion.10
  364.4 34.7 %scatter_custom_fusion.2 = pred[640]{0:T(1024)(128)(4,1)S(1)} fusion(s32[8192]{0:T(1024)} %bitcast.98, pred[8192]{0:T(1024)(128)(4,1)S(1)} %broadcast.610, pred[]{:T(512)} %constant.95.clone.1), kind=kCustom, calls=%fused_computation.180 | custom fusion | bytes 1152 | tf_op jit(solution)/shard_map/scatter | solution.py:32
  400.5 3.9 gather_fusion.6
  406.3 44.3 %scatter_custom_fusion.1 = s32[6144]{0:T(1024)S(1)} fusion(s32[8192]{0:T(1024)} %get-tuple-element.42, s32[8192]{0:T(1024)} %iota.45, s32[]{:T(128)} %constant.34.clone.1), kind=kCustom, calls=%fused_computation.163 | custom fusion | flops 8192 | bytes 25088 | tf_op jit(solution)/shard_map/scatter-min | solution.py:69
  459.7 3.2 gather_fusion.8
  465.2 5.2 all-to-all-start.2
  471.1 32.9 %gather_fusion.13 = bf16[8192,256]{1,0:T(8,128)(2,1)} fusion(bf16[256,6144]{0,1:T(8,128)(2,1)S(1)} %copy.20, s32[8192]{0:T(1024)S(1)} %copy-done.6), kind=kCustom, calls=%fused_computation.1.clone | custom fusion | bytes 8421376 | tf_op jit(solution)/shard_map/jit(_take)/gather | solution.py:116
  504.0 6.4 copy.22
  510.4 45.5 %gather_fusion.1 = s32[8192]{0:T(1024)S(1)} fusion(s32[6144]{0:T(1024)S(1)} %scatter_custom_fusion.1, s32[8192]{0:T(1024)S(1)} %copy-done.13), kind=kCustom, calls=%fused_computation.3 | custom fusion | bytes 98304 | tf_op jit(solution)/shard_map/gather | solution.py:71
  556.1 50.7 %gather_fusion = pred[8192]{0:T(1024)(128)(4,1)S(1)} fusion(pred[6144]{0:T(1024)(128)(4,1)S(1)} %broadcast_compare_fusion.1, s32[8192]{0:T(1024)S(1)} %copy-done.9), kind=kCustom, calls=%fused_computation.2 | custom fusion | bytes 49152 | tf_op jit(solution)/shard_map/gather | solution.py:78
  608.0 6.3 fusion.25
  614.3 6.3 fusion.22
  620.7 6.9 all-to-all-start
  627.6 7.3 fusion.9
  635.0 40.8 %psum.14 = f32[8192]{0:T(1024)S(1)} all-reduce(f32[8192]{0:T(1024)S(1)} %fusion.9), channel_id=1, replica_groups=mesh['dp'=16,'rep'=2] {'dp','rep'}, use_global_device_ids=true, to_apply=%region_4.6 | all-reduce | flops 8192 | bytes 65536 | tf_op jit(solution)/shard_map/psum | solution.py:138
  675.8 45.5 %gather_fusion.2 = f32[8192]{0:T(1024)S(1)} fusion(f32[8192]{0:T(1024)S(1)} %psum.14, s32[8192]{0:T(1024)S(1)} %fusion.22), kind=kCustom, calls=%fused_computation.4 | custom fusion | bytes 98304 | tf_op jit(solution)/shard_map/gather | solution.py:139
  721.3 5.4 all-to-all-start.1
  727.4 8.4 %fusion.11 = bf16[256,128]{1,0:T(8,128)(2,1)} fusion(bf16[8192,256]{1,0:T(8,128)(2,1)} %gather_fusion.12, pred[8192]{0:T(1024)(128)(4,1)S(1)} %get-tuple-element.37, bf16[8192,128]{1,0:T(8,128)(2,1)S(1)} %copy-done.28, pred[8192]{0:T(1024)(128)(4,1)S(1)} %fusion.25), kind=kOutput, calls=%fused_computation.36 | convolution fusion | flops 540049408 | bytes 6373376 | tf_op jit(solution)/shard_map/dot_general | solution.py:120
  (139 shorter events, 44.6 us)
Async XLA Ops:
  7.2 351.8 %copy-start = (f32[512,128]{1,0:T(8,128)S(1)}, f32[512,128]{1,0:T(8,128)}, u32[]{:S(2)}) copy-start(f32[512,128]{1,0:T(8,128)} %param.18) | copy-start | bytes 786436
  7.2 16.8 %copy-start.2 = (s32[8192]{0:T(1024)S(1)}, s32[8192]{0:T(1024)}, u32[]{:S(2)}) copy-start(s32[8192]{0:T(1024)} %param.16) | copy-start | bytes 98308
  7.2 206.2 %reduce-scatter.2.cloned.1.call-start = ((), (), s32[]{:S(2)}) async-start(), calls=%async_computation.5 | async-start | bytes 4456448 | tf_op jit(solution)/shard_map/reduce_scatter | solution.py:129
  20.7 54.3 %copy-start.5 = (s32[8192]{0:T(1024)}, s32[8192]{0:T(1024)S(1)}, u32[]{:S(2)}) copy-start(s32[8192]{0:T(1024)S(1)} %broadcast_clamp_fusion.3) | copy-start | bytes 98308
  72.1 36.1 %copy-start.25 = (f32[256]{0:T(256)}, f32[256]{0:T(256)S(1)}, u32[]{:S(2)}) copy-start(f32[256]{0:T(256)S(1)} %add_rsqrt_fusion) | copy-start | bytes 3076
  115.4 100.4 %copy-start.8 = (s32[17]{0:T(128)S(1)}, s32[17]{0:T(128)}, u32[]{:S(2)}) copy-start(s32[17]{0:T(128)} %param.15) | copy-start | bytes 208
  115.4 101.1 %copy-start.7 = (s32[17]{0:T(128)S(1)}, s32[17]{0:T(128)}, u32[]{:S(2)}) copy-start(s32[17]{0:T(128)} %param.14) | copy-start | bytes 208
  115.4 342.7 %all-reduce.2.cloned.1.call-start = ((), (), s32[]{:S(2)}) async-start(), calls=%async_computation.6 | async-start | bytes 262144 | tf_op jit(solution)/shard_map/psum | solution.py:137
  215.0 412.5 %all-gather.2.cloned.1.call-start = ((), (), s32[]{:S(2)}) async-start(), calls=%async_computation.4 | async-start | bytes 2228224 | tf_op jit(solution)/shard_map/all_gather | solution.py:117
  218.0 11.8 %copy-start.4 = (s32[8192]{0:T(1024)}, s32[8192]{0:T(1024)S(1)}, u32[]{:S(2)}) copy-start(s32[8192]{0:T(1024)S(1)} %convert_reduce_fusion.1) | copy-start | bytes 98308
  404.4 66.7 %copy-start.6 = (s32[8192]{0:T(1024)S(1)}, s32[8192]{0:T(1024)}, u32[]{:S(2)}) copy-start(s32[8192]{0:T(1024)} %copy-done.5) | copy-start | bytes 98308
  465.2 155.5 %all-to-all-start.2 = ((f32[16,40,128]{2,1,0:T(8,128)}), f32[16,40,128]{2,1,0:T(8,128)}, u32[]{:S(2)}, u32[]{:S(2)}) async-start(f32[16,40,128]{2,1,0:T(8,128)} %get-tuple-element.45), calls=%async_computation.3 | async-start | bytes 655360 | tf_op jit(solution)/shard_map/all_to_all | solution.py:147
  510.4 45.5 %copy-start.9 = (s32[8192]{0:T(1024)S(1)}, s32[8192]{0:T(1024)}, u32[]{:S(2)}) copy-start(s32[8192]{0:T(1024)} %broadcast_clamp_fusion.2) | copy-start | bytes 98308
  556.0 50.9 %copy-start.10 = (s32[8192,1]{0,1:T(1,128)S(1)}, s32[8192,1]{0,1:T(1,128)}, u32[]{:S(2)}) copy-start(s32[8192,1]{0,1:T(1,128)} %get-tuple-element.36) | copy-start | bytes 98308
  556.0 51.9 %copy-start.12 = (s32[8192,1]{0,1:T(1,128)S(1)}, s32[8192,1]{0,1:T(1,128)}, u32[]{:S(2)}) copy-start(s32[8192,1]{0,1:T(1,128)} %get-tuple-element.82) | copy-start | bytes 98308
  556.0 51.9 %copy-start.15 = (pred[8192]{0:T(1024)(128)(4,1)S(1)}, pred[8192]{0:T(1024)(128)(4,1)}, u32[]{:S(2)}) copy-start(pred[8192]{0:T(1024)(128)(4,1)} %compare_reduce_fusion.20) | copy-start | bytes 24580
  556.0 51.9 %copy-start.16 = (pred[8192]{0:T(1024)(128)(4,1)S(1)}, pred[8192]{0:T(1024)(128)(4,1)}, u32[]{:S(2)}) copy-start(pred[8192]{0:T(1024)(128)(4,1)} %compare_reduce_fusion.21) | copy-start | bytes 24580
  556.0 51.9 %copy-start.17 = (pred[8192]{0:T(1024)(128)(4,1)S(1)}, pred[8192]{0:T(1024)(128)(4,1)}, u32[]{:S(2)}) copy-start(pred[8192]{0:T(1024)(128)(4,1)} %compare_reduce_fusion.22) | copy-start | bytes 24580
  556.0 51.9 %copy-start.18 = (pred[8192]{0:T(1024)(128)(4,1)S(1)}, pred[8192]{0:T(1024)(128)(4,1)}, u32[]{:S(2)}) copy-start(pred[8192]{0:T(1024)(128)(4,1)} %compare_reduce_fusion.23) | copy-start | bytes 24580
  556.0 51.9 %copy-start.19 = (pred[8192]{0:T(1024)(128)(4,1)S(1)}, pred[8192]{0:T(1024)(128)(4,1)}, u32[]{:S(2)}) copy-start(pred[8192]{0:T(1024)(128)(4,1)} %compare_reduce_fusion.24) | copy-start | bytes 24580
  556.0 51.9 %copy-start.20 = (pred[8192]{0:T(1024)(128)(4,1)S(1)}, pred[8192]{0:T(1024)(128)(4,1)}, u32[]{:S(2)}) copy-start(pred[8192]{0:T(1024)(128)(4,1)} %compare_reduce_fusion.25) | copy-start | bytes 24580
  556.1 51.9 %copy-start.21 = (pred[8192]{0:T(1024)(128)(4,1)S(1)}, pred[8192]{0:T(1024)(128)(4,1)}, u32[]{:S(2)}) copy-start(pred[8192]{0:T(1024)(128)(4,1)} %compare_reduce_fusion.26) | copy-start | bytes 24580
  556.1 51.9 %copy-start.22 = (pred[8192]{0:T(1024)(128)(4,1)S(1)}, pred[8192]{0:T(1024)(128)(4,1)}, u32[]{:S(2)}) copy-start(pred[8192]{0:T(1024)(128)(4,1)} %compare_reduce_fusion.27) | copy-start | bytes 24580
  556.1 51.9 %copy-start.23 = (pred[8192]{0:T(1024)(128)(4,1)S(1)}, pred[8192]{0:T(1024)(128)(4,1)}, u32[]{:S(2)}) copy-start(pred[8192]{0:T(1024)(128)(4,1)} %compare_reduce_fusion.28) | copy-start | bytes 24580
  556.1 51.9 %copy-start.24 = (pred[8192]{0:T(1024)(128)(4,1)S(1)}, pred[8192]{0:T(1024)(128)(4,1)}, u32[]{:S(2)}) copy-start(pred[8192]{0:T(1024)(128)(4,1)} %compare_reduce_fusion.29) | copy-start | bytes 24580
  556.1 58.2 %copy-start.3 = (s32[8192]{0:T(1024)S(1)}, s32[8192]{0:T(1024)}, u32[]{:S(2)}) copy-start(s32[8192]{0:T(1024)} %param.16) | copy-start | bytes 98308
  556.1 58.2 %copy-start.11 = (s32[8192,1]{0,1:T(1,128)S(1)}, s32[8192,1]{0,1:T(1,128)}, u32[]{:S(2)}) copy-start(s32[8192,1]{0,1:T(1,128)} %get-tuple-element.35) | copy-start | bytes 98308
  556.1 71.5 %copy-start.14 = (bf16[256,128]{1,0:T(8,128)(2,1)S(1)}, bf16[256,128]{1,0:T(8,128)(2,1)}, u32[]{:S(2)}) copy-start(bf16[256,128]{1,0:T(8,128)(2,1)} %param.12) | copy-start | bytes 196612
  556.1 71.5 %copy-start.26 = (f32[256]{0:T(256)S(1)}, f32[256]{0:T(256)}, u32[]{:S(2)}) copy-start(f32[256]{0:T(256)} %copy-done.25) | copy-start | bytes 3076
  620.7 100.7 %all-to-all-start = ((f32[16,40,128]{2,1,0:T(8,128)}), f32[16,40,128]{2,1,0:T(8,128)S(1)}, u32[]{:S(2)}, u32[]{:S(2)}) async-start(f32[16,40,128]{2,1,0:T(8,128)} %get-tuple-element.43), calls=%async_computation | async-start | bytes 655360 | tf_op jit(solution)/shard_map/all_to_all | solution.py:144
  675.8 51.6 %copy-start.28 = (bf16[8192,128]{1,0:T(8,128)(2,1)S(1)}, bf16[8192,128]{1,0:T(8,128)(2,1)}, u32[]{:S(2)}) copy-start(bf16[8192,128]{1,0:T(8,128)(2,1)} %all-gather.2.cloned.1.call-done) | copy-start | bytes 6291460
  721.3 18.7 %all-to-all-start.1 = ((f32[16,40,128]{2,1,0:T(8,128)}), f32[16,40,128]{2,1,0:T(8,128)S(1)}, u32[]{:S(2)}, u32[]{:S(2)}) async-start(f32[16,40,128]{2,1,0:T(8,128)} %get-tuple-element.44), calls=%async_computation.2 | async-start | bytes 655360 | tf_op jit(solution)/shard_map/all_to_all | solution.py:141
  (3 other events, 15.4 us)
Sparse Core Ops, SparseCore 0:
  115.5 97.8 reduce-scatter.1
  216.3 17.4 all-reduce.1
  236.6 61.8 all-gather.1
where the time goes:
time: 752 us; the launch traced here: 750 us
  local copies, waits for them, and re-layouts  394 us (52%)
  other arithmetic  160 us (21%)
  waiting for transfers between devices  98.7 us (13%)
  blocking collectives  40.8 us (5%)
  matrix products  22.9 us (3%)
  starting transfers between devices  17.7 us (2%)
  between operations  15.8 us (2%)
    reduce_scatter x1, waiting for transfers between devices, on_device(): lax.psum_scatter(lax.dot_general(columns, cotangent, (((0,), (0,)), ((),...  97.9 us
    gather x2, local copies, waits for them, and re-layouts, routing(): send_slot = before - before[new_bounds[dest_owner]]  81.3 us
    gather x1, local copies, waits for them, and re-layouts, on_device(): weight_live = live_old & unit_used[slot_unit]  50.7 us
    gather x1, local copies, waits for them, and re-layouts, on_device(): gain_grad = jnp.where(keep_mask, column_total[source_slot], 0.0)  45.5 us
    gather x1, local copies, waits for them, and re-layouts, on_device(): keep_mask = first_use[source_map] == positions  45.5 us
    scatter-add x1, other arithmetic, on_device(): copies = jnp.zeros((D_OLD,), jnp.float32).at[source_map].add(1.0)  44.6 us
    another operation x1, other arithmetic, on_device(): jnp.full((D_OLD,), D_NEW, jnp.int32).at[source_map].min(positions)  44.3 us
    psum x1, blocking collectives, on_device(): column_total = lax.psum(column_terms, ('dp', 'rep'))  40.8 us
  transfers between devices with their start and end apart: 6, of which 1 were waited for; matrix products, arithmetic and copies ran while one was open for 62% of the time, Pallas kernels for 0%

commit v1 on v0

v1 whole, which is shorter than its diff:
```python
import jax
import jax.numpy as jnp
from jax import lax
from jax.experimental import pallas as pl
from jax.experimental.pallas import tpu as pltpu
from jax.sharding import PartitionSpec as P

D_OLD = 6144
D_NEW = 8192
LANES = 128
VMEM_LIMIT = 56 * 1024 * 1024
F32 = jnp.float32
BF16 = jnp.bfloat16

SMEM_SPEC = pl.BlockSpec(memory_space=pltpu.SMEM)
VMEM_SPEC = pl.BlockSpec(memory_space=pltpu.VMEM)


def dot(left, right, contract):
    return lax.dot_general(left, right, ((contract[:1], contract[1:]), ((), ())), preferred_element_type=F32)


def one_hot(rows, values):
    lanes = values.shape[1]
    match = lax.broadcasted_iota(jnp.int32, (rows, lanes), 0) == values
    return jnp.where(match, 1.0, 0.0).astype(BF16)


def split(value):
    high = value.astype(BF16)
    return high, (value - high.astype(F32)).astype(BF16)


def token_kernel(dp_count, rep_count, cap, ob, src, gain, hidden, cot, x_out, own, other, hist, grads):
    rep = lax.axis_index("rep")
    part = cap // rep_count
    tiles = D_OLD // LANES
    step = 1024
    total = jnp.zeros((tiles, LANES), F32)
    for at in range(0, D_NEW, step):
        units = src[:, at : at + step]
        total = total + dot(one_hot(tiles, units >> 7), one_hot(LANES, units & 127), (1, 1))
    hist[...] = total
    tokens = hidden.shape[0]
    squares = jnp.zeros((tokens, LANES), F32)
    for tile in range(tiles):
        stream = hidden[:, tile * LANES : (tile + 1) * LANES].astype(F32)
        squares = squares + stream * stream * hist[tile : tile + 1, :]
    inv_rms = lax.rsqrt(jnp.sum(squares, axis=1, keepdims=True) / D_NEW + 1e-05)
    for tile in range(tiles):
        at = tile * LANES
        stream = hidden[:, at : at + LANES].astype(F32)
        normed = (stream * inv_rms) * gain[tile : tile + 1, :]
        normed = jnp.where(hist[tile : tile + 1, :] > 0.5, normed, 0.0).astype(BF16)
        x_out[:, at : at + LANES] = normed
        grads[at : at + LANES, :] = dot(normed, cot[...], (0, 0))
    grads[D_OLD:, :] = jnp.zeros((cap, LANES), F32)
    for p in range(dp_count):
        first = ob[p]
        own[p] = grads[pl.ds(first + rep * part, part), :].astype(BF16)
        for away in range(1, rep_count):
            mate = (rep + away) % rep_count
            other[away - 1, p] = grads[pl.ds(first + mate * part, part), :].astype(BF16)


def project_kernel(dp_count, cap, ob, x, weights, out, dense):
    for p in range(dp_count):
        dense[pl.ds(ob[p], cap), :] = weights[p * cap : (p + 1) * cap, :].astype(F32)
    out[...] = dot(x[...], dense[0:D_OLD, :].astype(BF16), (1, 0)).astype(BF16)


def offset_of(src, ob, nb, q, dp_count):
    first = src[nb[q]]
    holder = jnp.int32(0)
    for p in range(1, dp_count):
        holder = holder + (ob[p] <= first).astype(jnp.int32)
    return holder


def pack_kernel(dp_count, cap, slots, table_rows, ob, nb, src, gain, grad, weight, first, second, out, rows, gains):
    me = lax.axis_index("dp")
    mine = ob[me]
    pairs = dp_count * slots
    groups = cap // LANES
    rows[...] = jnp.full(rows.shape, -1, jnp.int32)
    for q in range(dp_count):
        start = nb[q] + ((me - offset_of(src, ob, nb, q, dp_count)) & (dp_count - 1))
        end = nb[q + 1]
        for k in range(slots):
            unit = start + dp_count * k
            row = jnp.where(unit < end, src[jnp.minimum(unit, D_NEW - 1)] - mine, -1)
            rows[q * slots + k : q * slots + k + 1, :] = jnp.full((1, LANES), row, jnp.int32)
    lanes = lax.broadcasted_iota(jnp.int32, rows.shape, 1)
    chosen = jnp.concatenate(
        [jnp.where(rows[...] == lanes + g * LANES, 1.0, 0.0).astype(BF16) for g in range(groups)], axis=1
    )
    gains[0 : gain.shape[0], :] = gain[...]
    gains[gain.shape[0] :, :] = jnp.ones((gains.shape[0] - gain.shape[0], LANES), F32)
    gain_rows = gains[pl.ds(mine >> 7, groups + 1), :]
    shift = mine & 127
    rolled = pltpu.roll(gain_rows, (LANES - shift) & 127, 1)
    lane_row = lax.broadcasted_iota(jnp.int32, (groups, LANES), 1)
    own_gain = jnp.where(lane_row < LANES - shift, rolled[:groups], rolled[1:])
    own_row = jnp.concatenate([own_gain[g : g + 1] for g in range(groups)], axis=1)
    high, low = split(weight[...].astype(F32) * grad[...].astype(F32))
    ones = jnp.ones((8, LANES), BF16)
    column = (dot(ones, high, (1, 1)) + dot(ones, low, (1, 1))) / own_row
    high, low = split(column)
    same = dot(chosen, chosen, (1, 1))
    earlier = lax.broadcasted_iota(jnp.int32, same.shape, 0) < lax.broadcasted_iota(jnp.int32, same.shape, 1)
    repeated = jnp.max(jnp.where(earlier, same, 0.0), axis=0, keepdims=True)
    keep = repeated < 0.5
    high = jnp.where(keep, dot(high, chosen, (1, 1))[0:1], 0.0)
    low = jnp.where(keep, dot(low, chosen, (1, 1))[0:1], 0.0)
    table = [part[:, r * LANES : (r + 1) * LANES] for part in (high, low) for r in range(table_rows)]
    spare = out.shape[1] - 3 * slots - 2 * table_rows
    table = jnp.concatenate(table + [jnp.zeros((spare, LANES), F32)], axis=0).astype(BF16)
    picked = chosen[0:pairs]
    for at, value in enumerate((grad[...], first[...].astype(BF16), second[...].astype(BF16))):
        moved = dot(picked, value, (1, 0)).astype(BF16).reshape(dp_count, slots, LANES)
        out[:, at * slots : (at + 1) * slots, :] = moved
    for q in range(dp_count):
        out[q, 3 * slots :, :] = table


def finish_kernel(
    dp_count, slots, table_rows, ob, nb, src, units, moved, gain_grad, first, second, adam, grads, ones, twos, table
):
    me = lax.axis_index("dp")
    offset = offset_of(src, ob, nb, me, dp_count)
    for i in range(dp_count):
        p = (i + offset) & (dp_count - 1)
        strided = pl.ds(i, slots, stride=dp_count)
        grads[strided, :] = moved[p, 0:slots, :].astype(F32)
        ones[strided, :] = moved[p, slots : 2 * slots, :].astype(F32)
        twos[strided, :] = moved[p, 2 * slots : 3 * slots, :].astype(F32)
    cap = first.shape[0]
    live = lax.broadcasted_iota(jnp.int32, (cap, LANES), 0) < nb[me + 1] - nb[me]
    grad = grads[0:cap, :]
    first_next = jnp.where(live, 0.9 * ones[0:cap, :] + 0.1 * grad, 0.0)
    second_next = jnp.where(live, 0.95 * twos[0:cap, :] + 0.05 * grad * grad, 0.0)
    first[...] = first_next
    second[...] = second_next
    adam[...] = first_next / (jnp.sqrt(second_next) + 1e-08)
    at = 3 * slots
    for p in range(dp_count):
        here = p * table_rows
        table[here : here + table_rows, 0:LANES] = moved[p, at : at + table_rows, :].astype(F32)
        table[here : here + table_rows, LANES:] = moved[p, at + table_rows : at + 2 * table_rows, :].astype(F32)
    values = table[...].astype(BF16)
    step = 1024
    for start in range(0, D_NEW, step):
        source = units[:, start : start + step]
        position = start + lax.broadcasted_iota(jnp.int32, (1, step), 1)
        holder = jnp.zeros((1, step), jnp.int32)
        dest = jnp.zeros((1, step), jnp.int32)
        begin = jnp.zeros((1, step), jnp.int32)
        for p in range(1, dp_count):
            holder = holder + jnp.where(source >= ob[p], 1, 0)
            past = position >= nb[p]
            dest = jnp.where(past, p, dest)
            begin = jnp.where(past, nb[p], begin)
        rank = (position - begin) // dp_count
        slot = holder * (table_rows * LANES) + dest * slots + rank
        spread = dot(values, one_hot(values.shape[0], slot >> 7), (0, 0))
        mask = lax.broadcasted_iota(jnp.int32, (LANES, step), 0) == (slot & 127)
        value = jnp.where(mask, spread[:LANES] + spread[LANES:], 0.0)
        gain_grad[:, start : start + step] = jnp.sum(value, axis=0, keepdims=True)


def call(kernel, out_shape, specs, scratch, *args):
    return pl.pallas_call(
        kernel,
        out_shape=out_shape,
        in_specs=specs,
        out_specs=jax.tree.map(lambda _: VMEM_SPEC, out_shape),
        scratch_shapes=scratch,
        compiler_params=pltpu.CompilerParams(vmem_limit_bytes=VMEM_LIMIT),
    )(*args)


def on_device(
    hidden_old,
    cotangent,
    gain_old,
    old_bounds,
    new_bounds,
    source_map,
    weight_old,
    moment_first,
    moment_second,
):
    dp_count = lax.axis_size("dp")
    rep_count = lax.axis_size("rep")
    cap = weight_old.shape[0]
    mean = D_NEW // dp_count
    new_cap = mean + mean // 4
    slots = (new_cap + dp_count - 1) // dp_count
    table_rows = (dp_count * slots + LANES - 1) // LANES
    tokens = hidden_old.shape[0]
    part = cap // rep_count
    shape = jax.ShapeDtypeStruct

    units = source_map.reshape(1, D_NEW)
    gain = gain_old.reshape(D_OLD // LANES, LANES)
    weights = lax.all_gather(weight_old, "dp", axis=0, tiled=True)

    normed, own, other = call(
        lambda *refs: token_kernel(dp_count, rep_count, cap, *refs),
        (
            shape((tokens, D_OLD), BF16),
            shape((dp_count, part, LANES), BF16),
            shape((rep_count - 1, dp_count, part, LANES), BF16),
        ),
        [SMEM_SPEC] + [VMEM_SPEC] * 4,
        [pltpu.VMEM((D_OLD // LANES, LANES), F32), pltpu.VMEM((D_OLD + cap, LANES), F32)],
        old_bounds,
        units,
        gain,
        hidden_old,
        cotangent,
    )
    chip = own.astype(F32)
    for away in range(1, rep_count):
        ring = [(r, (r + away) % rep_count) for r in range(rep_count)]
        chip = chip + lax.ppermute(other[away - 1], "rep", ring).astype(F32)
    parts = lax.all_to_all(chip.astype(BF16), "dp", split_axis=0, concat_axis=0)
    grad_part = jnp.sum(parts.astype(F32), axis=0).astype(BF16)
    grad_own = lax.all_gather(grad_part, "rep", axis=0, tiled=True)

    message = 3 * slots + 2 * table_rows
    message = (message + 7) // 8 * 8
    packed = call(
        lambda *refs: pack_kernel(dp_count, cap, slots, table_rows, *refs),
        shape((dp_count, message, LANES), BF16),
        [SMEM_SPEC] * 3 + [VMEM_SPEC] * 5,
        [pltpu.VMEM((table_rows * LANES, LANES), jnp.int32), pltpu.VMEM((D_OLD // LANES + 8, LANES), F32)],
        old_bounds,
        new_bounds,
        source_map,
        gain,
        grad_own,
        weight_old,
        moment_first,
        moment_second,
    )
    moved = lax.all_to_all(packed, "dp", split_axis=0, concat_axis=0)
    rows = shape((new_cap, LANES), F32)
    gain_grad, first_next, second_next, adam_step = call(
        lambda *refs: finish_kernel(dp_count, slots, table_rows, *refs),
        (shape((1, D_NEW), F32), rows, rows, rows),
        [SMEM_SPEC] * 3 + [VMEM_SPEC] * 2,
        [pltpu.VMEM((dp_count * slots, LANES), F32)] * 3
        + [pltpu.VMEM((dp_count * table_rows, 2 * LANES), F32)],
        old_bounds,
        new_bounds,
        source_map,
        units,
        moved,
    )
    projected = call(
        lambda *refs: project_kernel(dp_count, cap, *refs),
        shape((tokens, LANES), BF16),
        [SMEM_SPEC] + [VMEM_SPEC] * 2,
        [pltpu.VMEM((D_OLD + cap, LANES), F32)],
        old_bounds,
        normed,
        weights,
    )
    return (projected, gain_grad.reshape(D_NEW), first_next, second_next, adam_step)


def solution(mesh):
    placed = (
        P(("dp", "rep"), None),
        P(("dp", "rep"), None),
        P(),
        P(),
        P(),
        P(),
        P("dp", None),
        P("dp", None),
        P("dp", None),
    )
    return jax.shard_map(
        on_device,
        mesh=mesh,
        in_specs=placed,
        out_specs=(P(("dp", "rep"), None), P(), P("dp", None), P("dp", None), P("dp", None)),
        check_vma=False,
    )
```

time: 752 us -> 108 us (0.14)
  local copies, waits for them, and re-layouts: 394 us -> 0.82 us
  other arithmetic: 160 us -> 1.64 us
  waiting for transfers between devices: 98.7 us -> 19.4 us
  matrix products: 22.9 us -> 0 us
  Pallas kernels: 0 us -> 22.8 us
  starting transfers between devices: 17.7 us -> 4.64 us
    gather x16 -> x0, local copies, waits for them, and re-layouts: 318 us -> none  [the longest x2 81.3 us: routing(): send_slot = before - before[new_bounds[dest_owner]]]
    reduce_scatter x1 -> x0, waiting for transfers between devices: 97.9 us -> none  [on_device(): lax.psum_scatter(lax.dot_general(columns, cotangent, (((0,), (0,)), ((),...]
    scatter x2 -> x0, local copies, waits for them, and re-layouts: 65.5 us -> none  [the longest x1 34.7 us: routing(): jnp.zeros((dp_count * slot_cap,), jnp.bool_).at[target]]
    another operation x3 -> x0, other arithmetic: 46.8 us -> none  [the longest x1 44.3 us: on_device(): jnp.full((D_OLD,), D_NEW, jnp.int32).at[source_map].min(positions)]
    scatter-add x1 -> x0, other arithmetic: 44.6 us -> none  [on_device(): copies = jnp.zeros((D_OLD,), jnp.float32).at[source_map].add(1.0)]
    all_to_all x0 -> x1, blocking collectives: none -> 42.3 us  [on_device(): parts = lax.all_to_all(chip.astype(BF16), 'dp', split_axis=0, concat_axis=0)]
    psum x1 -> x0, blocking collectives: 40.8 us -> none  [on_device(): column_total = lax.psum(column_terms, ('dp', 'rep'))]
    gather x34 -> x0, other arithmetic: 37.9 us -> none  [the longest x4 12.4 us: routing(): send_slot = before - before[new_bounds[dest_owner]]]
  transfers between devices with their start and end apart: 6 -> 3, of which waited for: 1 -> 2; matrix products, arithmetic and copies ran while one was open for 62% -> 2% of each run, Pallas kernels for 0% -> 9%
where the time goes in v1:
time: 108 us
  blocking collectives  44.3 us (41%)
  Pallas kernels  22.8 us (21%)
  waiting for transfers between devices  19.4 us (18%)
  between operations  14 us (13%)
  starting transfers between devices  4.64 us (4%)
  other arithmetic  1.64 us (2%)
    all_to_all x1, blocking collectives, on_device(): parts = lax.all_to_all(chip.astype(BF16), 'dp', split_axis=0, concat_axis=0)  42.3 us
    pallas_call x4, Pallas kernels, call(): pl.pallas_call(kernel, out_shape=out_shape, in_specs=specs, out_specs=jax...  22.8 us
    all_gather x1, waiting for transfers between devices, on_device(): weights = lax.all_gather(weight_old, 'dp', axis=0, tiled=True)  16.9 us
    all_to_all x1, starting transfers between devices, on_device(): moved = lax.all_to_all(packed, 'dp', split_axis=0, concat_axis=0)  4.15 us
    ppermute x1, waiting for transfers between devices, on_device(): chip = chip + lax.ppermute(other[away - 1], 'rep', ring).astype(F32)  2.47 us
  transfers between devices with their start and end apart: 3, of which 2 were waited for; matrix products, arithmetic and copies ran while one was open for 2% of the time, Pallas kernels for 9%

profile of v1, /device:TPU:0, one launch (start us, length us, event | category | flops | bytes accessed | tf_op | source)
XLA Modules:
  0.0 107.6 jit_solution(13203288261460078563)
XLA Ops:
  7.2 0.0 all-gather.2.cloned.1.call-start
  7.2 8.4 %shard_map.128 = (bf16[256,6144]{1,0:T(8,128)(2,1)}, bf16[16,256,128]{2,1,0:T(8,128)(2,1)}, bf16[1,16,256,128]{3,2,1,0:T(8,128)(2,1)}) custom-call(s32[17]{0:T(128)} %refs_0_.7, s32[1,8192]{1,0:T(1,128)} %bitcast.4, f32[48,128]{1,0:T(8,128)} %bitcast.6, bf16[256,6144]{1,0:T(8,128)(2,1)} %refs_3_.1, bf16[256,128]{1,0:T(8,128)(2,1)} %refs_4_.1), custom_call_target="tpu_custom_call" | custom-call | tf_op jit(solution)/shard_map/pallas_call | solution.py:172
  15.6 0.5 collective-permute-start
  16.1 0.0 all-gather.2.cloned.1.call-update
  16.1 2.5 %collective-permute-done = bf16[16,256,128]{2,1,0:T(8,128)(2,1)S(1)} collective-permute-done((bf16[16,256,128]{2,1,0:T(8,128)(2,1)}, bf16[16,256,128]{2,1,0:T(8,128)(2,1)S(1)}, u32[]{:S(2)}, u32[]{:S(2)}) %collective-permute-start) | collective-permute-done | bytes 1048608 | tf_op jit(solution)/shard_map/ppermute | solution.py:226
  18.6 1.5 %add_convert_fusion = bf16[16,256,128]{2,1,0:T(8,128)(2,1)S(1)} fusion(bf16[16,256,128]{2,1,0:T(8,128)(2,1)S(1)} %collective-permute-done, bf16[16,256,128]{2,1,0:T(8,128)(2,1)} %get-tuple-element.13), kind=kLoop, calls=%fused_computation | loop fusion | flops 2097152 | bytes 3145728 | tf_op jit(solution)/shard_map/convert_element_type | solution.py:227
  20.1 42.3 %all_to_all.10 = bf16[16,256,128]{2,1,0:T(8,128)(2,1)S(1)} all-to-all(bf16[16,256,128]{2,1,0:T(8,128)(2,1)S(1)} %add_convert_fusion), channel_id=1, replica_groups=mesh['dp'=16,'rep'=2] {'dp'}, dimensions={0} | all-to-all | bytes 2097152 | tf_op jit(solution)/shard_map/all_to_all | solution.py:227
  62.4 0.1 reduce_sum.12
  62.5 2.0 %all_gather.7.refs_4_ = bf16[512,128]{1,0:T(8,128)(2,1)} all-gather(bf16[256,128]{1,0:T(8,128)(2,1)S(1)} %reduce_sum.12), channel_id=1, replica_groups=mesh['dp'=16,'rep'=2] {'rep'}, dimensions={0}, use_global_device_ids=true | all-gather | bytes 196608 | tf_op jit(solution)/shard_map/all_gather | solution.py:229
  64.5 5.3 %shard_map.130 = bf16[16,136,128]{2,1,0:T(8,128)(2,1)} custom-call(s32[17]{0:T(128)} %refs_0_.7, s32[17]{0:T(128)} %refs_1_.3, s32[8192]{0:T(1024)} %refs_2_.3, f32[48,128]{1,0:T(8,128)} %bitcast.7, bf16[512,128]{1,0:T(8,128)(2,1)} %all_gather.7.refs_4_, bf16[512,128]{1,0:T(8,128)(2,1)} %refs_5_.1, f32[512,128]{1,0:T(8,128)} %refs_6_.1, f32[512,128]{1,0:T(8,128)} %refs_7_.1), custom_call_target="tpu_custom_call" | custom-call | tf_op jit(solution)/shard_map/pallas_call | solution.py:172
  69.9 4.2 %all-to-all-start.1 = ((bf16[16,136,128]{2,1,0:T(8,128)(2,1)}), bf16[16,136,128]{2,1,0:T(8,128)(2,1)S(1)}, u32[]{:S(2)}, u32[]{:S(2)}) async-start(bf16[16,136,128]{2,1,0:T(8,128)(2,1)} %shard_map.130), calls=%async_computation.1 | async-start | bytes 1114112 | tf_op jit(solution)/shard_map/all_to_all | solution.py:247
  74.0 16.9 %all-gather.2.cloned.1.call-done.refs_2_ = bf16[8192,128]{1,0:T(8,128)(2,1)} async-done(((bf16[512,128]{1,0:T(8,128)(2,1)}), bf16[8192,128]{1,0:T(8,128)(2,1)}) %all-gather.2.cloned.1.call-update) | async-done | bytes 2097168 | tf_op jit(solution)/shard_map/all_gather | solution.py:206
  90.9 4.4 %shard_map.129 = bf16[256,128]{1,0:T(8,128)(2,1)} custom-call(s32[17]{0:T(128)} %refs_0_.7, bf16[256,6144]{1,0:T(8,128)(2,1)} %get-tuple-element.12.refs_1_, bf16[8192,128]{1,0:T(8,128)(2,1)} %all-gather.2.cloned.1.call-done.refs_2_), custom_call_target="tpu_custom_call" | custom-call | tf_op jit(solution)/shard_map/pallas_call | solution.py:172
  95.3 0.0 all-to-all-done.1.refs_4_
  95.3 0.0 copy-start
  95.3 0.8 copy-done
  96.2 4.6 %shard_map.131 = (f32[1,8192]{1,0:T(1,128)}, f32[640,128]{1,0:T(8,128)}, f32[640,128]{1,0:T(8,128)}, f32[640,128]{1,0:T(8,128)}) custom-call(s32[17]{0:T(128)} %refs_0_.7, s32[17]{0:T(128)} %refs_1_.3, s32[8192]{0:T(1024)} %refs_2_.3, s32[1,8192]{1,0:T(1,128)} %bitcast.5, bf16[16,136,128]{2,1,0:T(8,128)(2,1)} %copy-done), custom_call_target="tpu_custom_call" | custom-call | tf_op jit(solution)/shard_map/pallas_call | solution.py:172
Async XLA Ops:
  7.2 83.8 %all-gather.2.cloned.1.call-start = ((), (), s32[]{:S(2)}) async-start(), calls=%async_computation.2 | async-start | bytes 2228224 | tf_op jit(solution)/shard_map/all_gather | solution.py:206
  15.6 3.0 %collective-permute-start = (bf16[16,256,128]{2,1,0:T(8,128)(2,1)}, bf16[16,256,128]{2,1,0:T(8,128)(2,1)S(1)}, u32[]{:S(2)}, u32[]{:S(2)}) collective-permute-start(bf16[16,256,128]{2,1,0:T(8,128)(2,1)} %bitcast.8), channel_id=1, source_target_pairs={{0,1},{1,0},{2,3},{3,2},{4,5},{5,4},{6,7},{7,6},{8,9},{9,8},{10,11... | collective-permute-start | bytes 3145736 | tf_op jit(solution)/shard_map/ppermute | solution.py:226
  69.9 25.5 %all-to-all-start.1 = ((bf16[16,136,128]{2,1,0:T(8,128)(2,1)}), bf16[16,136,128]{2,1,0:T(8,128)(2,1)S(1)}, u32[]{:S(2)}, u32[]{:S(2)}) async-start(bf16[16,136,128]{2,1,0:T(8,128)(2,1)} %shard_map.130), calls=%async_computation.1 | async-start | bytes 1114112 | tf_op jit(solution)/shard_map/all_to_all | solution.py:247
  95.3 0.8 copy-start
Sparse Core Ops, SparseCore 0:
  16.2 74.6 all-gather.1

commit v2 on v1

--- a/solution.py
+++ b/solution.py
@@ -31,7 +31,9 @@
     return high, (value - high.astype(F32)).astype(BF16)
 
 
-def token_kernel(dp_count, rep_count, cap, ob, src, gain, hidden, cot, x_out, own, other, hist, grads):
+def token_kernel(rels, rep_count, cap, ob, src, gain, hidden, cot, x_out, *rest):
+    *owns, other, hist, grads = rest
+    me = lax.axis_index("dp")
     rep = lax.axis_index("rep")
     part = cap // rep_count
     tiles = D_OLD // LANES
@@ -55,15 +57,46 @@
         x_out[:, at : at + LANES] = normed
         grads[at : at + LANES, :] = dot(normed, cot[...], (0, 0))
     grads[D_OLD:, :] = jnp.zeros((cap, LANES), F32)
-    for p in range(dp_count):
-        first = ob[p]
-        own[p] = grads[pl.ds(first + rep * part, part), :].astype(BF16)
+    dp_count = len(rels[0])
+    half = dp_count // len(owns)
+    for at in range(dp_count):
+        first = ob[holder_at(rels, rep, me, at)]
+        owns[at // half][at % half] = grads[pl.ds(first + rep * part, part), :]
         for away in range(1, rep_count):
             mate = (rep + away) % rep_count
-            other[away - 1, p] = grads[pl.ds(first + mate * part, part), :].astype(BF16)
-
-
-def project_kernel(dp_count, cap, ob, x, weights, out, dense):
+            first = ob[holder_at(rels, mate, me, at)] if len(rels) > 1 else first
+            other[away - 1, at] = grads[pl.ds(first + mate * part, part), :].astype(BF16)
+
+
+def holder_at(rels, rep, me, at):
+    if len(rels) == 1:
+        return rels[0][at]
+    return me ^ jnp.where(rep == 0, rels[0][at], rels[1][at])
+
+
+def project_kernel(dp_count, orders, cap, ob, x, mine, mate, out, dense):
+    me = lax.axis_index("dp")
+    rep = lax.axis_index("rep")
+    part = cap // 2
+    for p in range(dp_count):
+        away = me ^ p
+        at = [sum(((away >> bit) & 1) << s for s, bit in enumerate(order)) for order in orders]
+        first = ob[p]
+
+        @pl.when(rep == 0)
+        def _():
+            dense[pl.ds(first, part), :] = mine[at[0]].astype(F32)
+            dense[pl.ds(first + part, part), :] = mate[at[1]].astype(F32)
+
+        @pl.when(rep != 0)
+        def _():
+            dense[pl.ds(first, part), :] = mate[at[0]].astype(F32)
+            dense[pl.ds(first + part, part), :] = mine[at[1]].astype(F32)
+
+    out[...] = dot(x[...], dense[0:D_OLD, :].astype(BF16), (1, 0)).astype(BF16)
+
+
+def project_gathered_kernel(dp_count, cap, ob, x, weights, out, dense):
     for p in range(dp_count):
         dense[pl.ds(ob[p], cap), :] = weights[p * cap : (p + 1) * cap, :].astype(F32)
     out[...] = dot(x[...], dense[0:D_OLD, :].astype(BF16), (1, 0)).astype(BF16)
@@ -77,10 +110,9 @@
     return holder
 
 
-def pack_kernel(dp_count, cap, slots, table_rows, ob, nb, src, gain, grad, weight, first, second, out, rows, gains):
+def index_kernel(dp_count, cap, slots, table_rows, ob, nb, src, gain, units, chosen, keep, own_gain, places, rows, gains):
     me = lax.axis_index("dp")
     mine = ob[me]
-    pairs = dp_count * slots
     groups = cap // LANES
     rows[...] = jnp.full(rows.shape, -1, jnp.int32)
     for q in range(dp_count):
@@ -91,40 +123,59 @@
             row = jnp.where(unit < end, src[jnp.minimum(unit, D_NEW - 1)] - mine, -1)
             rows[q * slots + k : q * slots + k + 1, :] = jnp.full((1, LANES), row, jnp.int32)
     lanes = lax.broadcasted_iota(jnp.int32, rows.shape, 1)
-    chosen = jnp.concatenate(
-        [jnp.where(rows[...] == lanes + g * LANES, 1.0, 0.0).astype(BF16) for g in range(groups)], axis=1
-    )
+    for g in range(groups):
+        chosen[:, g * LANES : (g + 1) * LANES] = jnp.where(rows[...] == lanes + g * LANES, 1.0, 0.0).astype(BF16)
     gains[0 : gain.shape[0], :] = gain[...]
     gains[gain.shape[0] :, :] = jnp.ones((gains.shape[0] - gain.shape[0], LANES), F32)
     gain_rows = gains[pl.ds(mine >> 7, groups + 1), :]
     shift = mine & 127
     rolled = pltpu.roll(gain_rows, (LANES - shift) & 127, 1)
     lane_row = lax.broadcasted_iota(jnp.int32, (groups, LANES), 1)
-    own_gain = jnp.where(lane_row < LANES - shift, rolled[:groups], rolled[1:])
-    own_row = jnp.concatenate([own_gain[g : g + 1] for g in range(groups)], axis=1)
-    high, low = split(weight[...].astype(F32) * grad[...].astype(F32))
-    ones = jnp.ones((8, LANES), BF16)
-    column = (dot(ones, high, (1, 1)) + dot(ones, low, (1, 1))) / own_row
-    high, low = split(column)
-    same = dot(chosen, chosen, (1, 1))
+    inverse = 1.0 / jnp.where(lane_row < LANES - shift, rolled[:groups], rolled[1:])
+    for g in range(groups):
+        own_gain[:, g * LANES : (g + 1) * LANES] = inverse[g : g + 1]
+    same = dot(chosen[...], chosen[...], (1, 1))
     earlier = lax.broadcasted_iota(jnp.int32, same.shape, 0) < lax.broadcasted_iota(jnp.int32, same.shape, 1)
     repeated = jnp.max(jnp.where(earlier, same, 0.0), axis=0, keepdims=True)
-    keep = repeated < 0.5
-    high = jnp.where(keep, dot(high, chosen, (1, 1))[0:1], 0.0)
-    low = jnp.where(keep, dot(low, chosen, (1, 1))[0:1], 0.0)
-    table = [part[:, r * LANES : (r + 1) * LANES] for part in (high, low) for r in range(table_rows)]
+    keep[...] = jnp.where(repeated < 0.5, 1.0, 0.0)
+    step = 1024
+    for first in range(0, D_NEW, step):
+        source = units[:, first : first + step]
+        position = first + lax.broadcasted_iota(jnp.int32, (1, step), 1)
+        holder = jnp.zeros((1, step), jnp.int32)
+        dest = jnp.zeros((1, step), jnp.int32)
+        begin = jnp.zeros((1, step), jnp.int32)
+        for p in range(1, dp_count):
+            holder = holder + jnp.where(source >= ob[p], 1, 0)
+            past = position >= nb[p]
+            dest = jnp.where(past, p, dest)
+            begin = jnp.where(past, nb[p], begin)
+        rank = (position - begin) >> (dp_count.bit_length() - 1)
+        places[:, first : first + step] = holder * (table_rows * LANES) + dest * slots + rank
+
+
+def pack_kernel(dp_count, slots, table_rows, chosen, keep, own_gain, grad, weight, first, second, out):
+    pairs = dp_count * slots
+    high, low = split(weight[...].astype(F32) * grad[...])
+    ones = jnp.ones((8, LANES), BF16)
+    column = (dot(ones, high, (1, 1)) + dot(ones, low, (1, 1))) * own_gain[...]
+    high, low = split(column)
+    table = []
+    for part in (high, low):
+        part = dot(part, chosen[...], (1, 1))[0:1] * keep[...]
+        table += [part[:, r * LANES : (r + 1) * LANES] for r in range(table_rows)]
     spare = out.shape[1] - 3 * slots - 2 * table_rows
     table = jnp.concatenate(table + [jnp.zeros((spare, LANES), F32)], axis=0).astype(BF16)
     picked = chosen[0:pairs]
-    for at, value in enumerate((grad[...], first[...].astype(BF16), second[...].astype(BF16))):
-        moved = dot(picked, value, (1, 0)).astype(BF16).reshape(dp_count, slots, LANES)
+    for at, value in enumerate((grad, first, second)):
+        moved = dot(picked, value[...].astype(BF16), (1, 0)).astype(BF16).reshape(dp_count, slots, LANES)
         out[:, at * slots : (at + 1) * slots, :] = moved
     for q in range(dp_count):
         out[q, 3 * slots :, :] = table
 
 
 def finish_kernel(
-    dp_count, slots, table_rows, ob, nb, src, units, moved, gain_grad, first, second, adam, grads, ones, twos, table
+    dp_count, slots, table_rows, ob, nb, src, places, moved, gain_grad, first, second, adam, grads, ones, twos, table
 ):
     me = lax.axis_index("dp")
     offset = offset_of(src, ob, nb, me, dp_count)
@@ -150,18 +201,7 @@
     values = table[...].astype(BF16)
     step = 1024
     for start in range(0, D_NEW, step):
-        source = units[:, start : start + step]
-        position = start + lax.broadcasted_iota(jnp.int32, (1, step), 1)
-        holder = jnp.zeros((1, step), jnp.int32)
-        dest = jnp.zeros((1, step), jnp.int32)
-        begin = jnp.zeros((1, step), jnp.int32)
-        for p in range(1, dp_count):
-            holder = holder + jnp.where(source >= ob[p], 1, 0)
-            past = position >= nb[p]
-            dest = jnp.where(past, p, dest)
-            begin = jnp.where(past, nb[p], begin)
-        rank = (position - begin) // dp_count
-        slot = holder * (table_rows * LANES) + dest * slots + rank
+        slot = places[:, start : start + step]
         spread = dot(values, one_hot(values.shape[0], slot >> 7), (0, 0))
         mask = lax.broadcasted_iota(jnp.int32, (LANES, step), 0) == (slot & 127)
         value = jnp.where(mask, spread[:LANES] + spread[LANES:], 0.0)
@@ -203,13 +243,41 @@
 
     units = source_map.reshape(1, D_NEW)
     gain = gain_old.reshape(D_OLD // LANES, LANES)
-    weights = lax.all_gather(weight_old, "dp", axis=0, tiled=True)
-
-    normed, own, other = call(
-        lambda *refs: token_kernel(dp_count, rep_count, cap, *refs),
+    staged = rep_count == 2 and dp_count >= 4
+    bits = dp_count.bit_length() - 1
+    line = list(range(bits - 1))
+    halving = [line + [bits - 1], line[::-1] + [bits - 1]]
+    doubling = [[bits - 1] + line, [bits - 1] + line[::-1]]
+    if staged:
+        rels = [
+            [sum(((at >> (bits - 1 - s)) & 1) << bit for s, bit in enumerate(order)) for at in range(dp_count)]
+            for order in halving
+        ]
+        parts = 2
+    else:
+        rels = [list(range(dp_count))]
+        parts = 1
+
+    def across(value, orders, stage):
+        pairs = [
+            (dp * rep_count + rep, (dp ^ (1 << orders[rep][stage])) * rep_count + rep)
+            for dp in range(dp_count)
+            for rep in range(rep_count)
+        ]
+        return lax.ppermute(value, ("dp", "rep"), pairs)
+
+    swap = [(0, 1), (1, 0)]
+    if staged:
+        gathered = lax.dynamic_slice_in_dim(weight_old, lax.axis_index("rep") * part, part)[None]
+        gathered = jnp.concatenate([gathered, across(gathered, doubling, 0)])
+    else:
+        weights = lax.all_gather(weight_old, "dp", axis=0, tiled=True)
+
+    normed, *owns, other = call(
+        lambda *refs: token_kernel(rels, rep_count, cap, *refs),
         (
             shape((tokens, D_OLD), BF16),
-            shape((dp_count, part, LANES), BF16),
+            *[shape((dp_count // parts, part, LANES), F32)] * parts,
             shape((rep_count - 1, dp_count, part, LANES), BF16),
         ),
         [SMEM_SPEC] + [VMEM_SPEC] * 4,
@@ -220,25 +288,77 @@
         hidden_old,
         cotangent,
     )
-    chip = own.astype(F32)
-    for away in range(1, rep_count):
-        ring = [(r, (r + away) % rep_count) for r in range(rep_count)]
-        chip = chip + lax.ppermute(other[away - 1], "rep", ring).astype(F32)
-    parts = lax.all_to_all(chip.astype(BF16), "dp", split_axis=0, concat_axis=0)
-    grad_part = jnp.sum(parts.astype(F32), axis=0).astype(BF16)
-    grad_own = lax.all_gather(grad_part, "rep", axis=0, tiled=True)
-
-    message = 3 * slots + 2 * table_rows
-    message = (message + 7) // 8 * 8
-    packed = call(
-        lambda *refs: pack_kernel(dp_count, cap, slots, table_rows, *refs),
-        shape((dp_count, message, LANES), BF16),
-        [SMEM_SPEC] * 3 + [VMEM_SPEC] * 5,
+    chosen, keep, own_gain, places = call(
+        lambda *refs: index_kernel(dp_count, cap, slots, table_rows, *refs),
+        (
+            shape((table_rows * LANES, cap), BF16),
+            shape((1, table_rows * LANES), F32),
+            shape((1, cap), F32),
+            shape((1, D_NEW), jnp.int32),
+        ),
+        [SMEM_SPEC] * 3 + [VMEM_SPEC] * 2,
         [pltpu.VMEM((table_rows * LANES, LANES), jnp.int32), pltpu.VMEM((D_OLD // LANES + 8, LANES), F32)],
         old_bounds,
         new_bounds,
         source_map,
         gain,
+        units,
+    )
+    project_shape = shape((tokens, LANES), BF16)
+    dense = [pltpu.VMEM((D_OLD + cap, LANES), F32)]
+    if staged:
+        from_mate = lax.ppermute(other[0], "rep", swap).astype(F32)
+        half = dp_count // 2
+        low, high = owns[0] + from_mate[:half], owns[1] + from_mate[half:]
+        for stage in range(bits):
+            kind = BF16 if stage < 2 else F32
+            came = across(high.astype(kind), halving, stage).astype(F32)
+            if stage < bits - 1:
+                sent = across(gathered, doubling, stage + 1)
+                gathered = jnp.concatenate([gathered, sent])
+                half = half // 2
+                low, high = low[:half] + came[:half], low[half:] + came[half:]
+            else:
+                grad_part = (low + came)[0]
+        from_mate = lax.ppermute(gathered, "rep", swap)
+        projected = call(
+            lambda *refs: project_kernel(dp_count, doubling, cap, *refs),
+            project_shape,
+            [SMEM_SPEC] + [VMEM_SPEC] * 3,
+            dense,
+            old_bounds,
+            normed,
+            gathered,
+            from_mate,
+        )
+    else:
+        chip = owns[0]
+        for away in range(1, rep_count):
+            ring = [(r, (r + away) % rep_count) for r in range(rep_count)]
+            chip = chip + lax.ppermute(other[away - 1], "rep", ring).astype(F32)
+        blocks = lax.all_to_all(chip.astype(BF16), "dp", split_axis=0, concat_axis=0)
+        grad_part = jnp.sum(blocks.astype(F32), axis=0)
+        projected = call(
+            lambda *refs: project_gathered_kernel(dp_count, cap, *refs),
+            project_shape,
+            [SMEM_SPEC] + [VMEM_SPEC] * 2,
+            dense,
+            old_bounds,
+            normed,
+            weights,
+        )
+    grad_own = lax.all_gather(grad_part, "rep", axis=0, tiled=True)
+
+    message = 3 * slots + 2 * table_rows
+    message = (message + 7) // 8 * 8
+    packed = call(
+        lambda *refs: pack_kernel(dp_count, slots, table_rows, *refs),
+        shape((dp_count, message, LANES), BF16),
+        [VMEM_SPEC] * 7,
+        [],
+        chosen,
+        keep,
+        own_gain,
         grad_own,
         weight_old,
         moment_first,
@@ -255,17 +375,8 @@
         old_bounds,
         new_bounds,
         source_map,
-        units,
+        places,
         moved,
-    )
-    projected = call(
-        lambda *refs: project_kernel(dp_count, cap, *refs),
-        shape((tokens, LANES), BF16),
-        [SMEM_SPEC] + [VMEM_SPEC] * 2,
-        [pltpu.VMEM((D_OLD + cap, LANES), F32)],
-        old_bounds,
-        normed,
-        weights,
     )
     return (projected, gain_grad.reshape(D_NEW), first_next, second_next, adam_step)
 

time: 108 us -> 84.3 us (0.78)
  blocking collectives: 44.3 us -> 2.93 us
  starting transfers between devices: 4.64 us -> 23.7 us
  between operations: 14 us -> 0.8 us
  waiting for transfers between devices: 19.4 us -> 28.9 us
  Pallas kernels: 22.8 us -> 24.8 us
  local copies, waits for them, and re-layouts: 0.82 us -> 1.97 us
    all_to_all x1 -> x0, blocking collectives: 42.3 us -> none  [on_device(): parts = lax.all_to_all(chip.astype(BF16), 'dp', split_axis=0, concat_axis=0)]
    all_gather x1 -> x0, waiting for transfers between devices: 16.9 us -> none  [on_device(): weights = lax.all_gather(weight_old, 'dp', axis=0, tiled=True)]
    ppermute x1 -> x10, waiting for transfers between devices: 2.47 us -> 18.7 us  [the longest x8 16.2 us: across(): return lax.ppermute(value, ('dp', 'rep'), pairs)]
    ppermute x1 -> x10, starting transfers between devices: 0.45 us -> 16.4 us  [the longest x8 15.9 us: across(): return lax.ppermute(value, ('dp', 'rep'), pairs)]
    all_to_all x1, waiting for transfers between devices: 0.01 us -> 10.2 us  [on_device(): moved = lax.all_to_all(packed, 'dp', split_axis=0, concat_axis=0)]
    all_to_all x1, starting transfers between devices: 4.15 us -> 7.34 us  [on_device(): moved = lax.all_to_all(packed, 'dp', split_axis=0, concat_axis=0)]
    pallas_call x4 -> x5, Pallas kernels: 22.8 us -> 24.8 us  [call(): pl.pallas_call(kernel, out_shape=out_shape, in_specs=specs, out_specs=jax...]
    convert_element_type x1 -> x3, other arithmetic: 1.5 us -> 0.31 us  [the longest x1 0.2 us: on_device(): from_mate = lax.ppermute(other[0], 'rep', swap).astype(F32)]
  transfers between devices with their start and end apart: 3 -> 11, of which waited for: 2 -> 7; matrix products, arithmetic and copies ran while one was open for 2% -> 1% of each run, Pallas kernels for 9% -> 15%
where the time goes in v2:
time: 84.3 us; the launch traced here: 83.9 us
  waiting for transfers between devices  28.9 us (34%)
  Pallas kernels  24.8 us (29%)
  starting transfers between devices  23.7 us (28%)
  blocking collectives  2.93 us (3%)
  local copies, waits for them, and re-layouts  1.97 us (2%)
  other arithmetic  0.88 us (1%)
    pallas_call x5, Pallas kernels, call(): pl.pallas_call(kernel, out_shape=out_shape, in_specs=specs, out_specs=jax...  24.8 us
    ppermute x8, waiting for transfers between devices, across(): return lax.ppermute(value, ('dp', 'rep'), pairs)  16.2 us
    ppermute x8, starting transfers between devices, across(): return lax.ppermute(value, ('dp', 'rep'), pairs)  15.9 us
    all_to_all x1, waiting for transfers between devices, on_device(): moved = lax.all_to_all(packed, 'dp', split_axis=0, concat_axis=0)  10.2 us
    all_to_all x1, starting transfers between devices, on_device(): moved = lax.all_to_all(packed, 'dp', split_axis=0, concat_axis=0)  7.34 us
    all_gather x1, blocking collectives, on_device(): grad_own = lax.all_gather(grad_part, 'rep', axis=0, tiled=True)  2.93 us
    ppermute x1, waiting for transfers between devices, on_device(): from_mate = lax.ppermute(other[0], 'rep', swap).astype(F32)  2.5 us
    unnamed x16, local copies, waits for them, and re-layouts  1.9 us
  transfers between devices with their start and end apart: 11, of which 7 were waited for; matrix products, arithmetic and copies ran while one was open for 1% of the time, Pallas kernels for 15%

profile of v2, /device:TPU:0, one launch (start us, length us, event | category | flops | bytes accessed | tf_op | source)
XLA Modules:
  0.0 83.9 jit_solution(14188456235014864375)
XLA Ops:
  0.6 8.0 %shard_map.128 = (bf16[256,6144]{1,0:T(8,128)(2,1)}, f32[8,256,128]{2,1,0:T(8,128)}, f32[8,256,128]{2,1,0:T(8,128)}, bf16[1,16,256,128]{3,2,1,0:T(8,128)(2,1)}) custom-call(s32[17]{0:T(128)} %refs_0_.7, s32[1,8192]{1,0:T(1,128)} %bitcast.9, f32[48,128]{1,0:T(8,128)} %bitcast.11, bf16[256,6144]{1,0:T(8,128)(2,1)} %refs_3_.1, bf16[256,128]{1,0:T(8,128)(2,1)} %refs_4_.2), custom_call_target="tpu_custom_call" | custom-call | tf_op jit(solution)/shard_map/pallas_call | solution.py:212
  8.6 0.5 collective-permute-start.5
  9.1 2.5 %collective-permute-done.5 = bf16[16,256,128]{2,1,0:T(8,128)(2,1)S(1)} collective-permute-done((bf16[16,256,128]{2,1,0:T(8,128)(2,1)}, bf16[16,256,128]{2,1,0:T(8,128)(2,1)S(1)}, u32[]{:S(2)}, u32[]{:S(2)}) %collective-permute-start.5) | collective-permute-done | bytes 1048608 | tf_op jit(solution)/shard_map/ppermute | solution.py:310
  11.6 0.2 convert_element_type.15
  11.8 0.2 slice_add_fusion.1
  12.1 2.9 %collective-permute-start.6 = (bf16[8,256,128]{2,1,0:T(8,128)(2,1)S(1)}, bf16[8,256,128]{2,1,0:T(8,128)(2,1)S(1)}, u32[]{:S(2)}, u32[]{:S(2)}) collective-permute-start(bf16[8,256,128]{2,1,0:T(8,128)(2,1)S(1)} %get-tuple-element.34), channel_id=1, source_target_pairs={{0,2},{1,9},{2,0},{3,11},{4,6},{5,13},{6,4},{7,15},{8,10},{9,1},{1... | collective-permute-start | bytes 1572872 | tf_op jit(solution)/shard_map/ppermute | solution.py:267
  15.0 2.7 %collective-permute-start = (bf16[1,256,128]{2,1,0:T(8,128)(2,1)S(1)}, bf16[1,256,128]{2,1,0:T(8,128)(2,1)S(1)}, u32[]{:S(2)}, u32[]{:S(2)}) collective-permute-start(bf16[1,256,128]{2,1,0:T(8,128)(2,1)S(1)} %get-tuple-element.30), channel_id=1, source_target_pairs={{0,16},{1,17},{2,18},{3,19},{4,20},{5,21},{6,22},{7,23},{8,24},{9,... | collective-permute-start | bytes 196616 | tf_op jit(solution)/shard_map/ppermute | solution.py:267
  17.7 4.5 %collective-permute-done.6 = bf16[8,256,128]{2,1,0:T(8,128)(2,1)S(1)} collective-permute-done((bf16[8,256,128]{2,1,0:T(8,128)(2,1)S(1)}, bf16[8,256,128]{2,1,0:T(8,128)(2,1)S(1)}, u32[]{:S(2)}, u32[]{:S(2)}) %collective-permute-start.6) | collective-permute-done | bytes 524320 | tf_op jit(solution)/shard_map/ppermute | solution.py:267
  22.2 0.1 convert_element_type.17
  22.2 0.1 slice_add_fusion.3
  22.4 2.1 %collective-permute-start.7 = (bf16[4,256,128]{2,1,0:T(8,128)(2,1)S(1)}, bf16[4,256,128]{2,1,0:T(8,128)(2,1)S(1)}, u32[]{:S(2)}, u32[]{:S(2)}) collective-permute-start(bf16[4,256,128]{2,1,0:T(8,128)(2,1)S(1)} %get-tuple-element.32), channel_id=1, source_target_pairs={{0,4},{1,5},{2,6},{3,7},{4,0},{5,1},{6,2},{7,3},{8,12},{9,13},{10,... | collective-permute-start | bytes 786440 | tf_op jit(solution)/shard_map/ppermute | solution.py:267
  24.5 1.6 %collective-permute-start.1 = (bf16[2,256,128]{2,1,0:T(8,128)(2,1)S(1)}, bf16[2,256,128]{2,1,0:T(8,128)(2,1)S(1)}, u32[]{:S(2)}, u32[]{:S(2)}) collective-permute-start(bf16[2,256,128]{2,1,0:T(8,128)(2,1)S(1)} %pad_maximum_fusion.2), channel_id=1, source_target_pairs={{0,2},{1,9},{2,0},{3,11},{4,6},{5,13},{6,4},{7,15},{8,10},{9,1},{1... | collective-permute-start | bytes 393224 | tf_op jit(solution)/shard_map/ppermute | solution.py:267
  26.1 3.5 %collective-permute-done.1 = bf16[2,256,128]{2,1,0:T(8,128)(2,1)S(1)} collective-permute-done((bf16[2,256,128]{2,1,0:T(8,128)(2,1)S(1)}, bf16[2,256,128]{2,1,0:T(8,128)(2,1)S(1)}, u32[]{:S(2)}, u32[]{:S(2)}) %collective-permute-start.1) | collective-permute-done | bytes 131104 | tf_op jit(solution)/shard_map/ppermute | solution.py:267
  29.6 0.1 collective-permute-start.2
  29.7 4.6 %shard_map.130 = (bf16[640,512]{1,0:T(8,128)(2,1)}, f32[1,640]{1,0:T(1,128)}, f32[1,512]{1,0:T(1,128)}, s32[1,8192]{1,0:T(1,128)}) custom-call(s32[17]{0:T(128)} %refs_0_.7, s32[17]{0:T(128)} %refs_1_.3, s32[8192]{0:T(1024)} %refs_2_.3, f32[48,128]{1,0:T(8,128)} %bitcast.12, s32[1,8192]{1,0:T(1,128)} %bitcast.10), custom_call_target="tpu_custom_call" | custom-call | tf_op jit(solution)/shard_map/pallas_call | solution.py:212
  34.3 0.1 slice_add_fusion.5
  34.4 2.1 %collective-permute-start.8 = (f32[2,256,128]{2,1,0:T(8,128)S(1)}, f32[2,256,128]{2,1,0:T(8,128)S(1)}, u32[]{:S(2)}, u32[]{:S(2)}) collective-permute-start(f32[2,256,128]{2,1,0:T(8,128)S(1)} %get-tuple-element.36), channel_id=1, source_target_pairs={{0,8},{1,3},{2,10},{3,1},{4,12},{5,7},{6,14},{7,5},{8,0},{9,11},{1... | collective-permute-start | bytes 786440 | tf_op jit(solution)/shard_map/ppermute | solution.py:267
  36.5 0.6 collective-permute-done.2
  37.1 1.3 %collective-permute-start.3 = (bf16[8,256,128]{2,1,0:T(8,128)(2,1)S(1)}, bf16[8,256,128]{2,1,0:T(8,128)(2,1)S(1)}, u32[]{:S(2)}, u32[]{:S(2)}) collective-permute-start(bf16[8,256,128]{2,1,0:T(8,128)(2,1)S(1)} %pad_maximum_fusion), channel_id=1, source_target_pairs={{0,8},{1,3},{2,10},{3,1},{4,12},{5,7},{6,14},{7,5},{8,0},{9,11},{1... | collective-permute-start | bytes 1572872 | tf_op jit(solution)/shard_map/ppermute | solution.py:267
  38.5 2.3 %collective-permute-done.8 = f32[2,256,128]{2,1,0:T(8,128)S(1)} collective-permute-done((f32[2,256,128]{2,1,0:T(8,128)S(1)}, f32[2,256,128]{2,1,0:T(8,128)S(1)}, u32[]{:S(2)}, u32[]{:S(2)}) %collective-permute-start.8) | collective-permute-done | bytes 262176 | tf_op jit(solution)/shard_map/ppermute | solution.py:267
  40.8 3.1 %collective-permute-start.9 = (f32[1,256,128]{2,1,0:T(8,128)S(1)}, f32[1,256,128]{2,1,0:T(8,128)S(1)}, u32[]{:S(2)}, u32[]{:S(2)}) collective-permute-start(f32[1,256,128]{2,1,0:T(8,128)S(1)} %slice_add_fusion.6), channel_id=1, source_target_pairs={{0,16},{1,17},{2,18},{3,19},{4,20},{5,21},{6,22},{7,23},{8,24},{9,... | collective-permute-start | bytes 393224 | tf_op jit(solution)/shard_map/ppermute | solution.py:267
  44.0 5.3 %collective-permute-done.3 = bf16[8,256,128]{2,1,0:T(8,128)(2,1)S(1)} collective-permute-done((bf16[8,256,128]{2,1,0:T(8,128)(2,1)S(1)}, bf16[8,256,128]{2,1,0:T(8,128)(2,1)S(1)}, u32[]{:S(2)}, u32[]{:S(2)}) %collective-permute-start.3) | collective-permute-done | bytes 524320 | tf_op jit(solution)/shard_map/ppermute | solution.py:267
  49.3 0.1 constant_dynamic-update-slice_fusion.refs_2_
  49.3 0.1 collective-permute-start.4
  49.5 2.9 %all-gather = f32[1,512,128]{2,1,0:T(8,128)} all-gather(f32[1,256,128]{2,1,0:T(8,128)S(1)} %fusion.2), channel_id=2, replica_groups=mesh['dp'=16,'rep'=2] {'rep'}, dimensions={1}, use_global_device_ids=true | all-gather | bytes 393216 | tf_op jit(solution)/shard_map/all_gather | solution.py:350
  52.4 3.3 %shard_map.131 = bf16[16,136,128]{2,1,0:T(8,128)(2,1)} custom-call(bf16[640,512]{1,0:T(8,128)(2,1)} %get-tuple-element.19.refs_0_, f32[1,640]{1,0:T(1,128)} %get-tuple-element.20.refs_1_, f32[1,512]{1,0:T(1,128)} %get-tuple-element.21.refs_2_, f32[512,128]{1,0:T(8,128)} %bitcast.8, bf16[512,128]{1,0:T(8,128)(2,1)} %refs_4_.3, f32[512,128]{1,0:T(8,128)} %refs_5_.1, ...), custom_call_target="tpu_custom_call" | custom-call | tf_op jit(solution)/shard_map/pallas_call | solution.py:212
  55.7 7.3 %all-to-all-start = ((bf16[16,136,128]{2,1,0:T(8,128)(2,1)}), bf16[16,136,128]{2,1,0:T(8,128)(2,1)S(1)}, u32[]{:S(2)}, u32[]{:S(2)}) async-start(bf16[16,136,128]{2,1,0:T(8,128)(2,1)} %shard_map.131), calls=%async_computation | async-start | bytes 1114112 | tf_op jit(solution)/shard_map/all_to_all | solution.py:367
  63.1 1.0 %copy-done.2 = bf16[16,256,128]{2,1,0:T(8,128)(2,1)} copy-done((bf16[16,256,128]{2,1,0:T(8,128)(2,1)}, bf16[16,256,128]{2,1,0:T(8,128)(2,1)S(1)}, u32[]{:S(2)}) %copy-start.2) | copy-done | bytes 1048600
  64.1 4.7 %shard_map.129 = bf16[256,128]{1,0:T(8,128)(2,1)} custom-call(s32[17]{0:T(128)} %refs_0_.7, bf16[256,6144]{1,0:T(8,128)(2,1)} %get-tuple-element.17.refs_1_, bf16[16,256,128]{2,1,0:T(8,128)(2,1)} %copy-done.1, bf16[16,256,128]{2,1,0:T(8,128)(2,1)} %copy-done.2), custom_call_target="tpu_custom_call" | custom-call | tf_op jit(solution)/shard_map/pallas_call | solution.py:212
  68.8 10.2 %all-to-all-done.refs_4_ = bf16[16,136,128]{2,1,0:T(8,128)(2,1)S(1)} async-done(((bf16[16,136,128]{2,1,0:T(8,128)(2,1)}), bf16[16,136,128]{2,1,0:T(8,128)(2,1)S(1)}, u32[]{:S(2)}, u32[]{:S(2)}) %all-to-all-start) | async-done | bytes 557088 | tf_op jit(solution)/shard_map/all_to_all | solution.py:367
  79.0 0.8 copy-done
  79.8 4.1 %shard_map.132 = (f32[1,8192]{1,0:T(1,128)}, f32[640,128]{1,0:T(8,128)}, f32[640,128]{1,0:T(8,128)}, f32[640,128]{1,0:T(8,128)}) custom-call(s32[17]{0:T(128)} %refs_0_.7, s32[17]{0:T(128)} %refs_1_.3, s32[8192]{0:T(1024)} %refs_2_.3, s32[1,8192]{1,0:T(1,128)} %get-tuple-element.18.refs_3_, bf16[16,136,128]{2,1,0:T(8,128)(2,1)} %copy-done), custom_call_target="tpu_custom_call" | custom-call | tf_op jit(solution)/shard_map/pallas_call | solution.py:212
  (24 shorter events, 0.3 us)
Async XLA Ops:
  8.6 3.2 %copy-start.3 = (f32[8,256,128]{2,1,0:T(8,128)S(1)}, f32[8,256,128]{2,1,0:T(8,128)}, u32[]{:S(2)}) copy-start(f32[8,256,128]{2,1,0:T(8,128)} %get-tuple-element.22) | copy-start | bytes 3145732
  8.6 3.2 %copy-start.4 = (f32[8,256,128]{2,1,0:T(8,128)S(1)}, f32[8,256,128]{2,1,0:T(8,128)}, u32[]{:S(2)}) copy-start(f32[8,256,128]{2,1,0:T(8,128)} %get-tuple-element.24) | copy-start | bytes 3145732
  8.6 3.0 %collective-permute-start.5 = (bf16[16,256,128]{2,1,0:T(8,128)(2,1)}, bf16[16,256,128]{2,1,0:T(8,128)(2,1)S(1)}, u32[]{:S(2)}, u32[]{:S(2)}) collective-permute-start(bf16[16,256,128]{2,1,0:T(8,128)(2,1)} %bitcast.13), channel_id=1, source_target_pairs={{0,1},{1,0},{2,3},{3,2},{4,5},{5,4},{6,7},{7,6},{8,9},{9,8},{10,11... | collective-permute-start | bytes 3145736 | tf_op jit(solution)/shard_map/ppermute | solution.py:310
  11.8 3.2 %copy-start.5 = (bf16[512,128]{1,0:T(8,128)(2,1)S(1)}, bf16[512,128]{1,0:T(8,128)(2,1)}, u32[]{:S(2)}) copy-start(bf16[512,128]{1,0:T(8,128)(2,1)} %refs_4_.3) | copy-start | bytes 393220
  12.1 10.1 %collective-permute-start.6 = (bf16[8,256,128]{2,1,0:T(8,128)(2,1)S(1)}, bf16[8,256,128]{2,1,0:T(8,128)(2,1)S(1)}, u32[]{:S(2)}, u32[]{:S(2)}) collective-permute-start(bf16[8,256,128]{2,1,0:T(8,128)(2,1)S(1)} %get-tuple-element.34), channel_id=1, source_target_pairs={{0,2},{1,9},{2,0},{3,11},{4,6},{5,13},{6,4},{7,15},{8,10},{9,1},{1... | collective-permute-start | bytes 1572872 | tf_op jit(solution)/shard_map/ppermute | solution.py:267
  15.0 9.5 %collective-permute-start = (bf16[1,256,128]{2,1,0:T(8,128)(2,1)S(1)}, bf16[1,256,128]{2,1,0:T(8,128)(2,1)S(1)}, u32[]{:S(2)}, u32[]{:S(2)}) collective-permute-start(bf16[1,256,128]{2,1,0:T(8,128)(2,1)S(1)} %get-tuple-element.30), channel_id=1, source_target_pairs={{0,16},{1,17},{2,18},{3,19},{4,20},{5,21},{6,22},{7,23},{8,24},{9,... | collective-permute-start | bytes 196616 | tf_op jit(solution)/shard_map/ppermute | solution.py:267
  22.4 11.9 %collective-permute-start.7 = (bf16[4,256,128]{2,1,0:T(8,128)(2,1)S(1)}, bf16[4,256,128]{2,1,0:T(8,128)(2,1)S(1)}, u32[]{:S(2)}, u32[]{:S(2)}) collective-permute-start(bf16[4,256,128]{2,1,0:T(8,128)(2,1)S(1)} %get-tuple-element.32), channel_id=1, source_target_pairs={{0,4},{1,5},{2,6},{3,7},{4,0},{5,1},{6,2},{7,3},{8,12},{9,13},{10,... | collective-permute-start | bytes 786440 | tf_op jit(solution)/shard_map/ppermute | solution.py:267
  24.5 5.0 %collective-permute-start.1 = (bf16[2,256,128]{2,1,0:T(8,128)(2,1)S(1)}, bf16[2,256,128]{2,1,0:T(8,128)(2,1)S(1)}, u32[]{:S(2)}, u32[]{:S(2)}) collective-permute-start(bf16[2,256,128]{2,1,0:T(8,128)(2,1)S(1)} %pad_maximum_fusion.2), channel_id=1, source_target_pairs={{0,2},{1,9},{2,0},{3,11},{4,6},{5,13},{6,4},{7,15},{8,10},{9,1},{1... | collective-permute-start | bytes 393224 | tf_op jit(solution)/shard_map/ppermute | solution.py:267
  29.6 7.5 %collective-permute-start.2 = (bf16[4,256,128]{2,1,0:T(8,128)(2,1)S(1)}, bf16[4,256,128]{2,1,0:T(8,128)(2,1)S(1)}, u32[]{:S(2)}, u32[]{:S(2)}) collective-permute-start(bf16[4,256,128]{2,1,0:T(8,128)(2,1)S(1)} %pad_maximum_fusion.1), channel_id=1, source_target_pairs={{0,4},{1,5},{2,6},{3,7},{4,0},{5,1},{6,2},{7,3},{8,12},{9,13},{10,... | collective-permute-start | bytes 786440 | tf_op jit(solution)/shard_map/ppermute | solution.py:267
  34.4 6.4 %collective-permute-start.8 = (f32[2,256,128]{2,1,0:T(8,128)S(1)}, f32[2,256,128]{2,1,0:T(8,128)S(1)}, u32[]{:S(2)}, u32[]{:S(2)}) collective-permute-start(f32[2,256,128]{2,1,0:T(8,128)S(1)} %get-tuple-element.36), channel_id=1, source_target_pairs={{0,8},{1,3},{2,10},{3,1},{4,12},{5,7},{6,14},{7,5},{8,0},{9,11},{1... | collective-permute-start | bytes 786440 | tf_op jit(solution)/shard_map/ppermute | solution.py:267
  37.1 12.1 %collective-permute-start.3 = (bf16[8,256,128]{2,1,0:T(8,128)(2,1)S(1)}, bf16[8,256,128]{2,1,0:T(8,128)(2,1)S(1)}, u32[]{:S(2)}, u32[]{:S(2)}) collective-permute-start(bf16[8,256,128]{2,1,0:T(8,128)(2,1)S(1)} %pad_maximum_fusion), channel_id=1, source_target_pairs={{0,8},{1,3},{2,10},{3,1},{4,12},{5,7},{6,14},{7,5},{8,0},{9,11},{1... | collective-permute-start | bytes 1572872 | tf_op jit(solution)/shard_map/ppermute | solution.py:267
  40.8 8.6 %collective-permute-start.9 = (f32[1,256,128]{2,1,0:T(8,128)S(1)}, f32[1,256,128]{2,1,0:T(8,128)S(1)}, u32[]{:S(2)}, u32[]{:S(2)}) collective-permute-start(f32[1,256,128]{2,1,0:T(8,128)S(1)} %slice_add_fusion.6), channel_id=1, source_target_pairs={{0,16},{1,17},{2,18},{3,19},{4,20},{5,21},{6,22},{7,23},{8,24},{9,... | collective-permute-start | bytes 393224 | tf_op jit(solution)/shard_map/ppermute | solution.py:267
  49.3 13.8 %copy-start.1 = (bf16[16,256,128]{2,1,0:T(8,128)(2,1)}, bf16[16,256,128]{2,1,0:T(8,128)(2,1)S(1)}, u32[]{:S(2)}) copy-start(bf16[16,256,128]{2,1,0:T(8,128)(2,1)S(1)} %constant_dynamic-update-slice_fusion.refs_2_) | copy-start | bytes 3145732
  49.3 13.7 %collective-permute-start.4 = (bf16[16,256,128]{2,1,0:T(8,128)(2,1)S(1)}, bf16[16,256,128]{2,1,0:T(8,128)(2,1)S(1)}, u32[]{:S(2)}, u32[]{:S(2)}) collective-permute-start(bf16[16,256,128]{2,1,0:T(8,128)(2,1)S(1)} %constant_dynamic-update-slice_fusion.refs_2_), channel_id=1, source_target_pairs={{0,1},{1,0},{2,3},{3,2},{4,5},{5,4},{6,7},{7,6},{8,9},{9,8},{10,11... | collective-permute-start | bytes 3145736 | tf_op jit(solution)/shard_map/ppermute | solution.py:323
  55.7 23.3 %all-to-all-start = ((bf16[16,136,128]{2,1,0:T(8,128)(2,1)}), bf16[16,136,128]{2,1,0:T(8,128)(2,1)S(1)}, u32[]{:S(2)}, u32[]{:S(2)}) async-start(bf16[16,136,128]{2,1,0:T(8,128)(2,1)} %shard_map.131), calls=%async_computation | async-start | bytes 1114112 | tf_op jit(solution)/shard_map/all_to_all | solution.py:367
  63.1 1.0 %copy-start.2 = (bf16[16,256,128]{2,1,0:T(8,128)(2,1)}, bf16[16,256,128]{2,1,0:T(8,128)(2,1)S(1)}, u32[]{:S(2)}) copy-start(bf16[16,256,128]{2,1,0:T(8,128)(2,1)S(1)} %collective-permute-done.4.refs_3_) | copy-start | bytes 3145732
  79.0 0.8 copy-start

commit v3 on v2

--- a/solution.py
+++ b/solution.py
@@ -8,6 +8,7 @@
 D_OLD = 6144
 D_NEW = 8192
 LANES = 128
+BYTES_PER_US = 3_000_000
 VMEM_LIMIT = 56 * 1024 * 1024
 F32 = jnp.float32
 BF16 = jnp.bfloat16
@@ -31,11 +32,7 @@
     return high, (value - high.astype(F32)).astype(BF16)
 
 
-def token_kernel(rels, rep_count, cap, ob, src, gain, hidden, cot, x_out, *rest):
-    *owns, other, hist, grads = rest
-    me = lax.axis_index("dp")
-    rep = lax.axis_index("rep")
-    part = cap // rep_count
+def statistics_kernel(src, hidden, hist, inv_rms):
     tiles = D_OLD // LANES
     step = 1024
     total = jnp.zeros((tiles, LANES), F32)
@@ -48,11 +45,20 @@
     for tile in range(tiles):
         stream = hidden[:, tile * LANES : (tile + 1) * LANES].astype(F32)
         squares = squares + stream * stream * hist[tile : tile + 1, :]
-    inv_rms = lax.rsqrt(jnp.sum(squares, axis=1, keepdims=True) / D_NEW + 1e-05)
-    for tile in range(tiles):
+    mean = jnp.sum(squares, axis=1, keepdims=True) / D_NEW
+    inv_rms[...] = jnp.broadcast_to(lax.rsqrt(mean + 1e-05), (tokens, LANES))
+
+
+def token_kernel(rels, rep_count, cap, ob, hist, inv_rms, gain, hidden, cot, x_out, *rest):
+    *blocks, grads = rest
+    owns, others = blocks[: len(blocks) // 2], blocks[len(blocks) // 2 :]
+    me = lax.axis_index("dp")
+    rep = lax.axis_index("rep")
+    part = cap // rep_count
+    for tile in range(D_OLD // LANES):
         at = tile * LANES
         stream = hidden[:, at : at + LANES].astype(F32)
-        normed = (stream * inv_rms) * gain[tile : tile + 1, :]
+        normed = (stream * inv_rms[...]) * gain[tile : tile + 1, :]
         normed = jnp.where(hist[tile : tile + 1, :] > 0.5, normed, 0.0).astype(BF16)
         x_out[:, at : at + LANES] = normed
         grads[at : at + LANES, :] = dot(normed, cot[...], (0, 0))
@@ -65,7 +71,7 @@
         for away in range(1, rep_count):
             mate = (rep + away) % rep_count
             first = ob[holder_at(rels, mate, me, at)] if len(rels) > 1 else first
-            other[away - 1, at] = grads[pl.ds(first + mate * part, part), :].astype(BF16)
+            others[at // half][away - 1, at % half] = grads[pl.ds(first + mate * part, part), :].astype(BF16)
 
 
 def holder_at(rels, rep, me, at):
@@ -74,25 +80,26 @@
     return me ^ jnp.where(rep == 0, rels[0][at], rels[1][at])
 
 
-def project_kernel(dp_count, orders, cap, ob, x, mine, mate, out, dense):
+def project_kernel(dp_count, orders, cap, ob, x, *rest):
+    *pieces, out, dense, blocks, sems = rest
     me = lax.axis_index("dp")
     rep = lax.axis_index("rep")
     part = cap // 2
+    half = dp_count // 2
+    copies = []
+    for at, piece in enumerate(pieces):
+        side = rep if at < 2 else 1 - rep
+        place = blocks.at[side, pl.ds((at % 2) * half, half)]
+        copies.append(pltpu.make_async_copy(piece, place, sems.at[at]))
+    for copy in copies:
+        copy.start()
+    for copy in copies:
+        copy.wait()
     for p in range(dp_count):
         away = me ^ p
-        at = [sum(((away >> bit) & 1) << s for s, bit in enumerate(order)) for order in orders]
-        first = ob[p]
-
-        @pl.when(rep == 0)
-        def _():
-            dense[pl.ds(first, part), :] = mine[at[0]].astype(F32)
-            dense[pl.ds(first + part, part), :] = mate[at[1]].astype(F32)
-
-        @pl.when(rep != 0)
-        def _():
-            dense[pl.ds(first, part), :] = mate[at[0]].astype(F32)
-            dense[pl.ds(first + part, part), :] = mine[at[1]].astype(F32)
-
+        for side, order in enumerate(orders):
+            at = sum(((away >> bit) & 1) << s for s, bit in enumerate(order))
+            dense[pl.ds(ob[p] + side * part, part), :] = blocks[side, at].astype(F32)
     out[...] = dot(x[...], dense[0:D_OLD, :].astype(BF16), (1, 0)).astype(BF16)
 
 
@@ -154,9 +161,15 @@
         places[:, first : first + step] = holder * (table_rows * LANES) + dest * slots + rank
 
 
-def pack_kernel(dp_count, slots, table_rows, chosen, keep, own_gain, grad, weight, first, second, out):
+def pack_kernel(dp_count, slots, table_rows, chosen, keep, own_gain, mine, *rest):
+    *mate, weight, first, second, out = rest
     pairs = dp_count * slots
-    high, low = split(weight[...].astype(F32) * grad[...])
+    grad = mine[...]
+    if mate:
+        grad, other = mine[0], mate[0][0]
+        own_first = lax.axis_index("rep") == 0
+        grad = jnp.concatenate([jnp.where(own_first, grad, other), jnp.where(own_first, other, grad)], axis=0)
+    high, low = split(weight[...].astype(F32) * grad)
     ones = jnp.ones((8, LANES), BF16)
     column = (dot(ones, high, (1, 1)) + dot(ones, low, (1, 1))) * own_gain[...]
     high, low = split(column)
@@ -164,36 +177,35 @@
     for part in (high, low):
         part = dot(part, chosen[...], (1, 1))[0:1] * keep[...]
         table += [part[:, r * LANES : (r + 1) * LANES] for r in range(table_rows)]
-    spare = out.shape[1] - 3 * slots - 2 * table_rows
+    spare = out.shape[1] - 2 * slots - 2 * table_rows
     table = jnp.concatenate(table + [jnp.zeros((spare, LANES), F32)], axis=0).astype(BF16)
     picked = chosen[0:pairs]
-    for at, value in enumerate((grad, first, second)):
-        moved = dot(picked, value[...].astype(BF16), (1, 0)).astype(BF16).reshape(dp_count, slots, LANES)
+    updated = (0.9 * first[...] + 0.1 * grad, 0.95 * second[...] + 0.05 * grad * grad)
+    for at, value in enumerate(updated):
+        moved = dot(picked, value.astype(BF16), (1, 0)).astype(BF16).reshape(dp_count, slots, LANES)
         out[:, at * slots : (at + 1) * slots, :] = moved
     for q in range(dp_count):
-        out[q, 3 * slots :, :] = table
+        out[q, 2 * slots :, :] = table
 
 
 def finish_kernel(
-    dp_count, slots, table_rows, ob, nb, src, places, moved, gain_grad, first, second, adam, grads, ones, twos, table
+    dp_count, slots, table_rows, ob, nb, src, places, moved, gain_grad, first, second, adam, ones, twos, table
 ):
     me = lax.axis_index("dp")
     offset = offset_of(src, ob, nb, me, dp_count)
     for i in range(dp_count):
         p = (i + offset) & (dp_count - 1)
         strided = pl.ds(i, slots, stride=dp_count)
-        grads[strided, :] = moved[p, 0:slots, :].astype(F32)
-        ones[strided, :] = moved[p, slots : 2 * slots, :].astype(F32)
-        twos[strided, :] = moved[p, 2 * slots : 3 * slots, :].astype(F32)
+        ones[strided, :] = moved[p, 0:slots, :].astype(F32)
+        twos[strided, :] = moved[p, slots : 2 * slots, :].astype(F32)
     cap = first.shape[0]
     live = lax.broadcasted_iota(jnp.int32, (cap, LANES), 0) < nb[me + 1] - nb[me]
-    grad = grads[0:cap, :]
-    first_next = jnp.where(live, 0.9 * ones[0:cap, :] + 0.1 * grad, 0.0)
-    second_next = jnp.where(live, 0.95 * twos[0:cap, :] + 0.05 * grad * grad, 0.0)
+    first_next = jnp.where(live, ones[0:cap, :], 0.0)
+    second_next = jnp.where(live, twos[0:cap, :], 0.0)
     first[...] = first_next
     second[...] = second_next
     adam[...] = first_next / (jnp.sqrt(second_next) + 1e-08)
-    at = 3 * slots
+    at = 2 * slots
     for p in range(dp_count):
         here = p * table_rows
         table[here : here + table_rows, 0:LANES] = moved[p, at : at + table_rows, :].astype(F32)
@@ -208,13 +220,14 @@
         gain_grad[:, start : start + step] = jnp.sum(value, axis=0, keepdims=True)
 
 
-def call(kernel, out_shape, specs, scratch, *args):
+def call(kernel, micros, out_shape, specs, scratch, *args):
     return pl.pallas_call(
         kernel,
         out_shape=out_shape,
         in_specs=specs,
         out_specs=jax.tree.map(lambda _: VMEM_SPEC, out_shape),
         scratch_shapes=scratch,
+        cost_estimate=pl.CostEstimate(flops=0, transcendentals=0, bytes_accessed=micros * BYTES_PER_US),
         compiler_params=pltpu.CompilerParams(vmem_limit_bytes=VMEM_LIMIT),
     )(*args)
 
@@ -269,27 +282,44 @@
     swap = [(0, 1), (1, 0)]
     if staged:
         gathered = lax.dynamic_slice_in_dim(weight_old, lax.axis_index("rep") * part, part)[None]
-        gathered = jnp.concatenate([gathered, across(gathered, doubling, 0)])
     else:
         weights = lax.all_gather(weight_old, "dp", axis=0, tiled=True)
 
-    normed, *owns, other = call(
+    tiles = D_OLD // LANES
+    hist, inv_rms = call(
+        statistics_kernel,
+        4,
+        (shape((tiles, LANES), F32), shape((tokens, LANES), F32)),
+        [VMEM_SPEC] * 2,
+        [],
+        units,
+        hidden_old,
+    )
+    if staged:
+        hist, sent = lax.optimization_barrier((hist, across(gathered, doubling, 0)))
+        gathered = jnp.concatenate([gathered, sent])
+        sent = across(gathered, doubling, 1)
+    normed, *blocks = call(
         lambda *refs: token_kernel(rels, rep_count, cap, *refs),
+        5,
         (
             shape((tokens, D_OLD), BF16),
             *[shape((dp_count // parts, part, LANES), F32)] * parts,
-            shape((rep_count - 1, dp_count, part, LANES), BF16),
+            *[shape((rep_count - 1, dp_count // parts, part, LANES), BF16)] * parts,
         ),
-        [SMEM_SPEC] + [VMEM_SPEC] * 4,
-        [pltpu.VMEM((D_OLD // LANES, LANES), F32), pltpu.VMEM((D_OLD + cap, LANES), F32)],
+        [SMEM_SPEC] + [VMEM_SPEC] * 5,
+        [pltpu.VMEM((D_OLD + cap, LANES), F32)],
         old_bounds,
-        units,
+        hist,
+        inv_rms,
         gain,
         hidden_old,
         cotangent,
     )
+    owns, others = blocks[:parts], blocks[parts:]
     chosen, keep, own_gain, places = call(
         lambda *refs: index_kernel(dp_count, cap, slots, table_rows, *refs),
+        5,
         (
             shape((table_rows * LANES, cap), BF16),
             shape((1, table_rows * LANES), F32),
@@ -307,39 +337,46 @@
     project_shape = shape((tokens, LANES), BF16)
     dense = [pltpu.VMEM((D_OLD + cap, LANES), F32)]
     if staged:
-        from_mate = lax.ppermute(other[0], "rep", swap).astype(F32)
         half = dp_count // 2
-        low, high = owns[0] + from_mate[:half], owns[1] + from_mate[half:]
-        for stage in range(bits):
-            kind = BF16 if stage < 2 else F32
-            came = across(high.astype(kind), halving, stage).astype(F32)
-            if stage < bits - 1:
-                sent = across(gathered, doubling, stage + 1)
+        high = owns[1] + lax.ppermute(others[1][0], "rep", swap).astype(F32)
+        low = owns[0] + lax.ppermute(others[0][0], "rep", swap).astype(F32)
+        high, sent = lax.optimization_barrier((high.astype(BF16), sent))
+        for stage in range(bits - 1):
+            came = across(high, halving, stage)
+            if stage < bits - 2:
                 gathered = jnp.concatenate([gathered, sent])
-                half = half // 2
-                low, high = low[:half] + came[:half], low[half:] + came[half:]
-            else:
-                grad_part = (low + came)[0]
-        from_mate = lax.ppermute(gathered, "rep", swap)
+                sent = across(gathered, doubling, stage + 2)
+                came, sent, chosen = lax.optimization_barrier((came, sent, chosen))
+            came = came.astype(F32)
+            half = half // 2
+            low, high = low[:half] + came[:half], low[half:] + came[half:]
+            if stage < 1:
+                high = high.astype(BF16)
+        grad_part = low + across(high, halving, bits - 1).astype(F32)
+        grads = [grad_part, lax.ppermute(grad_part, "rep", swap)]
+        pieces = [gathered, sent]
+        pieces += [lax.ppermute(piece, "rep", swap) for piece in pieces]
         projected = call(
             lambda *refs: project_kernel(dp_count, doubling, cap, *refs),
+            5,
             project_shape,
-            [SMEM_SPEC] + [VMEM_SPEC] * 3,
-            dense,
+            [SMEM_SPEC, VMEM_SPEC] + [pl.BlockSpec(memory_space=pl.ANY)] * 4,
+            dense + [pltpu.VMEM((2, dp_count, part, LANES), BF16), pltpu.SemaphoreType.DMA((4,))],
             old_bounds,
             normed,
-            gathered,
-            from_mate,
+            *pieces,
         )
     else:
         chip = owns[0]
         for away in range(1, rep_count):
             ring = [(r, (r + away) % rep_count) for r in range(rep_count)]
-            chip = chip + lax.ppermute(other[away - 1], "rep", ring).astype(F32)
+            chip = chip + lax.ppermute(others[0][away - 1], "rep", ring).astype(F32)
         blocks = lax.all_to_all(chip.astype(BF16), "dp", split_axis=0, concat_axis=0)
         grad_part = jnp.sum(blocks.astype(F32), axis=0)
+        grads = [lax.all_gather(grad_part, "rep", axis=0, tiled=True)]
         projected = call(
             lambda *refs: project_gathered_kernel(dp_count, cap, *refs),
+            5,
             project_shape,
             [SMEM_SPEC] + [VMEM_SPEC] * 2,
             dense,
@@ -347,19 +384,18 @@
             normed,
             weights,
         )
-    grad_own = lax.all_gather(grad_part, "rep", axis=0, tiled=True)
-
-    message = 3 * slots + 2 * table_rows
+    message = 2 * slots + 2 * table_rows
     message = (message + 7) // 8 * 8
     packed = call(
         lambda *refs: pack_kernel(dp_count, slots, table_rows, *refs),
+        3,
         shape((dp_count, message, LANES), BF16),
-        [VMEM_SPEC] * 7,
+        [VMEM_SPEC] * (6 + len(grads)),
         [],
         chosen,
         keep,
         own_gain,
-        grad_own,
+        *grads,
         weight_old,
         moment_first,
         moment_second,
@@ -368,9 +404,10 @@
     rows = shape((new_cap, LANES), F32)
     gain_grad, first_next, second_next, adam_step = call(
         lambda *refs: finish_kernel(dp_count, slots, table_rows, *refs),
+        4,
         (shape((1, D_NEW), F32), rows, rows, rows),
         [SMEM_SPEC] * 3 + [VMEM_SPEC] * 2,
-        [pltpu.VMEM((dp_count * slots, LANES), F32)] * 3
+        [pltpu.VMEM((dp_count * slots, LANES), F32)] * 2
         + [pltpu.VMEM((dp_count * table_rows, 2 * LANES), F32)],
         old_bounds,
         new_bounds,

time: 84.3 us -> 88.1 us (1.045)
  blocking collectives: 2.93 us -> 0 us
  waiting for transfers between devices: 28.9 us -> 31.8 us
  Pallas kernels: 24.8 us -> 27.7 us
  starting transfers between devices: 23.7 us -> 22.3 us
  local copies, waits for them, and re-layouts: 1.97 us -> 3.07 us
  other arithmetic: 0.88 us -> 1.87 us
    ppermute x8, waiting for transfers between devices: 16.2 us -> 24.2 us  [across(): return lax.ppermute(value, ('dp', 'rep'), pairs)]
    all_to_all x1, waiting for transfers between devices: 10.2 us -> 4.03 us  [on_device(): moved = lax.all_to_all(packed, 'dp', split_axis=0, concat_axis=0)]
    pallas_call x5 -> x6, Pallas kernels: 24.8 us -> 27.7 us  [call(): pl.pallas_call(kernel, out_shape=out_shape, in_specs=specs, out_specs=jax...]
    all_gather x1 -> x0, blocking collectives: 2.93 us -> none  [on_device(): grad_own = lax.all_gather(grad_part, 'rep', axis=0, tiled=True)]
    all_to_all x1, starting transfers between devices: 7.34 us -> 5.75 us  [on_device(): moved = lax.all_to_all(packed, 'dp', split_axis=0, concat_axis=0)]
    convert_element_type x3, other arithmetic: 0.31 us -> 1.44 us  [the longest x1 1.33 us: on_device(): high, sent = lax.optimization_barrier((high.astype(BF16), sent))]
    ppermute x2 -> x5, waiting for transfers between devices: 2.5 us -> 3.52 us  [the longest x2 2.15 us: on_device(): pieces += [lax.ppermute(piece, 'rep', swap) for piece in pieces]]
  transfers between devices with their start and end apart: 11 -> 14, of which waited for: 7 -> 10; matrix products, arithmetic and copies ran while one was open for 1% -> 2% of each run, Pallas kernels for 15% -> 16%
where the time goes in v3:
time: 88.1 us; the launch traced here: 87.5 us
  waiting for transfers between devices  31.8 us (36%)
  Pallas kernels  27.7 us (31%)
  starting transfers between devices  22.3 us (25%)
  local copies, waits for them, and re-layouts  3.07 us (3%)
  other arithmetic  1.87 us (2%)
    pallas_call x6, Pallas kernels, call(): pl.pallas_call(kernel, out_shape=out_shape, in_specs=specs, out_specs=jax...  27.7 us
    ppermute x8, waiting for transfers between devices, across(): return lax.ppermute(value, ('dp', 'rep'), pairs)  24.2 us
    ppermute x8, starting transfers between devices, across(): return lax.ppermute(value, ('dp', 'rep'), pairs)  15.4 us
    all_to_all x1, starting transfers between devices, on_device(): moved = lax.all_to_all(packed, 'dp', split_axis=0, concat_axis=0)  5.75 us
    all_to_all x1, waiting for transfers between devices, on_device(): moved = lax.all_to_all(packed, 'dp', split_axis=0, concat_axis=0)  4.03 us
    unnamed x16, local copies, waits for them, and re-layouts  2.22 us
    ppermute x2, waiting for transfers between devices, on_device(): pieces += [lax.ppermute(piece, 'rep', swap) for piece in pieces]  2.15 us
  transfers between devices with their start and end apart: 14, of which 10 were waited for; matrix products, arithmetic and copies ran while one was open for 2% of the time, Pallas kernels for 16%

profile of v3, /device:TPU:0, one launch (start us, length us, event | category | flops | bytes accessed | tf_op | source)
XLA Modules:
  0.0 87.5 jit_solution(5777764464323176256)
XLA Ops:
  0.6 0.8 dynamic-slice_bitcast_fusion
  1.5 4.0 %collective-permute-start = (bf16[1,256,128]{2,1,0:T(8,128)(2,1)S(1)}, bf16[1,256,128]{2,1,0:T(8,128)(2,1)S(1)}, u32[]{:S(2)}, u32[]{:S(2)}) collective-permute-start(bf16[1,256,128]{2,1,0:T(8,128)(2,1)S(1)} %dynamic-slice_bitcast_fusion), channel_id=1, source_target_pairs={{0,16},{1,17},{2,18},{3,19},{4,20},{5,21},{6,22},{7,23},{8,24},{9,... | collective-permute-start | bytes 196616 | tf_op jit(solution)/shard_map/ppermute | solution.py:280
  5.5 4.3 %shard_map.128 = (f32[48,128]{1,0:T(8,128)}, f32[256,128]{1,0:T(8,128)}) custom-call(s32[1,8192]{1,0:T(1,128)} %bitcast.7, bf16[256,6144]{1,0:T(8,128)(2,1)} %refs_4_.1), custom_call_target="tpu_custom_call" | custom-call | bytes 12000000 | tf_op jit(solution)/shard_map/pallas_call | solution.py:224
  9.8 6.5 %shard_map.129 = (bf16[256,6144]{1,0:T(8,128)(2,1)}, f32[8,256,128]{2,1,0:T(8,128)}, f32[8,256,128]{2,1,0:T(8,128)}, bf16[1,8,256,128]{3,2,1,0:T(8,128)(2,1)}, bf16[1,8,256,128]{3,2,1,0:T(8,128)(2,1)}) custom-call(s32[17]{0:T(128)} %refs_0_.7, f32[48,128]{1,0:T(8,128)} %get-tuple-element.31.refs_1_, f32[256,128]{1,0:T(8,128)} %get-tuple-element.32.refs_2_, ...), custom_call_target="tpu_custom_call" | custom-call | bytes 15000000 | tf_op jit(solution)/shard_map/pallas_call | solution.py:224
  16.3 0.5 collective-permute-start.5
  16.9 1.6 %collective-permute-start.2 = (bf16[2,256,128]{2,1,0:T(8,128)(2,1)S(1)}, bf16[2,256,128]{2,1,0:T(8,128)(2,1)S(1)}, u32[]{:S(2)}, u32[]{:S(2)}) collective-permute-start(bf16[2,256,128]{2,1,0:T(8,128)(2,1)S(1)} %pad_maximum_fusion.2), channel_id=1, source_target_pairs={{0,2},{1,9},{2,0},{3,11},{4,6},{5,13},{6,4},{7,15},{8,10},{9,1},{1... | collective-permute-start | bytes 393224 | tf_op jit(solution)/shard_map/ppermute | solution.py:280
  18.5 1.3 %add_convert_fusion = bf16[8,256,128]{2,1,0:T(8,128)(2,1)S(1)} fusion(f32[8,256,128]{2,1,0:T(8,128)} %get-tuple-element.35, bf16[8,256,128]{2,1,0:T(8,128)(2,1)S(1)} %collective-permute-done.1), kind=kLoop, calls=%fused_computation.1 | loop fusion | flops 786432 | bytes 2097152 | tf_op jit(solution)/shard_map/convert_element_type | solution.py:343
  19.8 2.1 %collective-permute-done.2 = bf16[2,256,128]{2,1,0:T(8,128)(2,1)S(1)} collective-permute-done((bf16[2,256,128]{2,1,0:T(8,128)(2,1)S(1)}, bf16[2,256,128]{2,1,0:T(8,128)(2,1)S(1)}, u32[]{:S(2)}, u32[]{:S(2)}) %collective-permute-start.2) | collective-permute-done | bytes 131104 | tf_op jit(solution)/shard_map/ppermute | solution.py:280
  21.9 1.5 %collective-permute-start.3 = (bf16[8,256,128]{2,1,0:T(8,128)(2,1)S(1)}, bf16[8,256,128]{2,1,0:T(8,128)(2,1)S(1)}, u32[]{:S(2)}, u32[]{:S(2)}) collective-permute-start(bf16[8,256,128]{2,1,0:T(8,128)(2,1)S(1)} %add_convert_fusion), channel_id=1, source_target_pairs={{0,2},{1,9},{2,0},{3,11},{4,6},{5,13},{6,4},{7,15},{8,10},{9,1},{1... | collective-permute-start | bytes 1572872 | tf_op jit(solution)/shard_map/ppermute | solution.py:280
  23.4 4.6 %shard_map.130 = (bf16[640,512]{1,0:T(8,128)(2,1)}, f32[1,640]{1,0:T(1,128)}, f32[1,512]{1,0:T(1,128)}, s32[1,8192]{1,0:T(1,128)}) custom-call(s32[17]{0:T(128)} %refs_0_.7, s32[17]{0:T(128)} %refs_1_.3, s32[8192]{0:T(1024)} %refs_2_.3, f32[48,128]{1,0:T(8,128)} %bitcast.10, s32[1,8192]{1,0:T(1,128)} %bitcast.8), custom_call_target="tpu_custom_call" | custom-call | bytes 15000000 | tf_op jit(solution)/shard_map/pallas_call | solution.py:224
  28.0 1.6 %collective-permute-start.4 = (bf16[4,256,128]{2,1,0:T(8,128)(2,1)S(1)}, bf16[4,256,128]{2,1,0:T(8,128)(2,1)S(1)}, u32[]{:S(2)}, u32[]{:S(2)}) collective-permute-start(bf16[4,256,128]{2,1,0:T(8,128)(2,1)S(1)} %pad_maximum_fusion.1), channel_id=1, source_target_pairs={{0,4},{1,5},{2,6},{3,7},{4,0},{5,1},{6,2},{7,3},{8,12},{9,13},{10,... | collective-permute-start | bytes 786440 | tf_op jit(solution)/shard_map/ppermute | solution.py:280
  29.7 5.6 %collective-permute-done.4 = bf16[4,256,128]{2,1,0:T(8,128)(2,1)S(1)} collective-permute-done((bf16[4,256,128]{2,1,0:T(8,128)(2,1)S(1)}, bf16[4,256,128]{2,1,0:T(8,128)(2,1)S(1)}, u32[]{:S(2)}, u32[]{:S(2)}) %collective-permute-start.4) | collective-permute-done | bytes 262176 | tf_op jit(solution)/shard_map/ppermute | solution.py:280
  35.5 0.8 collective-permute-start.7
  36.3 1.6 %collective-permute-start.6 = (bf16[4,256,128]{2,1,0:T(8,128)(2,1)S(1)}, bf16[4,256,128]{2,1,0:T(8,128)(2,1)S(1)}, u32[]{:S(2)}, u32[]{:S(2)}) collective-permute-start(bf16[4,256,128]{2,1,0:T(8,128)(2,1)S(1)} %get-tuple-element.56), channel_id=1, source_target_pairs={{0,4},{1,5},{2,6},{3,7},{4,0},{5,1},{6,2},{7,3},{8,12},{9,13},{10,... | collective-permute-start | bytes 786440 | tf_op jit(solution)/shard_map/ppermute | solution.py:280
  37.9 6.3 %collective-permute-done.6 = bf16[4,256,128]{2,1,0:T(8,128)(2,1)S(1)} collective-permute-done((bf16[4,256,128]{2,1,0:T(8,128)(2,1)S(1)}, bf16[4,256,128]{2,1,0:T(8,128)(2,1)S(1)}, u32[]{:S(2)}, u32[]{:S(2)}) %collective-permute-start.6) | collective-permute-done | bytes 262176 | tf_op jit(solution)/shard_map/ppermute | solution.py:280
  44.2 0.5 collective-permute-done.7.refs_3_
  44.8 0.8 collective-permute-start.10
  45.6 5.7 %collective-permute-done.10 = f32[2,256,128]{2,1,0:T(8,128)S(1)} collective-permute-done((f32[2,256,128]{2,1,0:T(8,128)S(1)}, f32[2,256,128]{2,1,0:T(8,128)S(1)}, u32[]{:S(2)}, u32[]{:S(2)}) %collective-permute-start.10) | collective-permute-done | bytes 262176 | tf_op jit(solution)/shard_map/ppermute | solution.py:280
  51.3 3.6 %collective-permute-start.11 = (f32[1,256,128]{2,1,0:T(8,128)S(1)}, f32[1,256,128]{2,1,0:T(8,128)S(1)}, u32[]{:S(2)}, u32[]{:S(2)}) collective-permute-start(f32[1,256,128]{2,1,0:T(8,128)S(1)} %slice_add_fusion.4), channel_id=1, source_target_pairs={{0,16},{1,17},{2,18},{3,19},{4,20},{5,21},{6,22},{7,23},{8,24},{9,... | collective-permute-start | bytes 393224 | tf_op jit(solution)/shard_map/ppermute | solution.py:280
  54.9 4.1 %collective-permute-done.11 = f32[1,256,128]{2,1,0:T(8,128)S(1)} collective-permute-done((f32[1,256,128]{2,1,0:T(8,128)S(1)}, f32[1,256,128]{2,1,0:T(8,128)S(1)}, u32[]{:S(2)}, u32[]{:S(2)}) %collective-permute-start.11) | collective-permute-done | bytes 131104 | tf_op jit(solution)/shard_map/ppermute | solution.py:280
  59.1 1.3 %collective-permute-done.12.refs_4_ = f32[1,256,128]{2,1,0:T(8,128)S(1)} collective-permute-done((f32[1,256,128]{2,1,0:T(8,128)S(1)}, f32[1,256,128]{2,1,0:T(8,128)S(1)}, u32[]{:S(2)}, u32[]{:S(2)}) %collective-permute-start.12) | collective-permute-done | bytes 131104 | tf_op jit(solution)/shard_map/ppermute | solution.py:356
  60.5 0.7 copy-done.7
  61.1 3.2 %shard_map.132 = bf16[16,96,128]{2,1,0:T(8,128)(2,1)} custom-call(bf16[640,512]{1,0:T(8,128)(2,1)} %get-tuple-element.47.refs_0_, f32[1,640]{1,0:T(1,128)} %get-tuple-element.48.refs_1_, f32[1,512]{1,0:T(1,128)} %get-tuple-element.49.refs_2_, f32[1,256,128]{2,1,0:T(8,128)} %copy-done.3, f32[1,256,128]{2,1,0:T(8,128)} %copy-done.7, bf16[512,128]{1,0:T(8,128)(2,1)} %refs_5_.3, ...), custom_call_target="tpu_custom_call" | custom-call | bytes 9000000 | tf_op jit(solution)/shard_map/pallas_call | solution.py:224
  64.3 5.7 %all-to-all-start = ((bf16[16,96,128]{2,1,0:T(8,128)(2,1)}), bf16[16,96,128]{2,1,0:T(8,128)(2,1)S(1)}, u32[]{:S(2)}, u32[]{:S(2)}) async-start(bf16[16,96,128]{2,1,0:T(8,128)(2,1)} %shard_map.132), calls=%async_computation | async-start | bytes 786432 | tf_op jit(solution)/shard_map/all_to_all | solution.py:403
  70.1 0.5 collective-permute-start.9
  70.6 1.4 %collective-permute-done.8.refs_4_ = bf16[8,256,128]{2,1,0:T(8,128)(2,1)S(1)} collective-permute-done((bf16[8,256,128]{2,1,0:T(8,128)(2,1)S(1)}, bf16[8,256,128]{2,1,0:T(8,128)(2,1)S(1)}, u32[]{:S(2)}, u32[]{:S(2)}) %collective-permute-start.8) | collective-permute-done | bytes 524320 | tf_op jit(solution)/shard_map/ppermute | solution.py:358
  72.0 0.7 collective-permute-done.9.refs_5_
  72.8 0.7 copy-done.6
  73.6 5.3 %shard_map.131 = bf16[256,128]{1,0:T(8,128)(2,1)} custom-call(s32[17]{0:T(128)} %refs_0_.7, bf16[256,6144]{1,0:T(8,128)(2,1)} %get-tuple-element.33.refs_1_, bf16[8,256,128]{2,1,0:T(8,128)(2,1)} %copy-done, bf16[8,256,128]{2,1,0:T(8,128)(2,1)} %copy-done.4, bf16[8,256,128]{2,1,0:T(8,128)(2,1)} %copy-done.5, bf16[8,256,128]{2,1,0:T(8,128)(2,1)} %copy-done.6), custom_call_target="tpu_custom_call" | custom-call | bytes 15000000 | tf_op jit(solution)/shard_map/pallas_call | solution.py:224
  78.9 4.0 %all-to-all-done.refs_4_ = bf16[16,96,128]{2,1,0:T(8,128)(2,1)S(1)} async-done(((bf16[16,96,128]{2,1,0:T(8,128)(2,1)}), bf16[16,96,128]{2,1,0:T(8,128)(2,1)S(1)}, u32[]{:S(2)}, u32[]{:S(2)}) %all-to-all-start) | async-done | bytes 393248 | tf_op jit(solution)/shard_map/all_to_all | solution.py:403
  82.9 0.8 copy-done.1
  83.7 3.8 %shard_map.133 = (f32[1,8192]{1,0:T(1,128)}, f32[640,128]{1,0:T(8,128)}, f32[640,128]{1,0:T(8,128)}, f32[640,128]{1,0:T(8,128)}) custom-call(s32[17]{0:T(128)} %refs_0_.7, s32[17]{0:T(128)} %refs_1_.3, s32[8192]{0:T(1024)} %refs_2_.3, s32[1,8192]{1,0:T(1,128)} %get-tuple-element.46.refs_3_, bf16[16,96,128]{2,1,0:T(8,128)(2,1)} %copy-done.1), custom_call_target="tpu_custom_call" | custom-call | bytes 12000000 | tf_op jit(solution)/shard_map/pallas_call | solution.py:224
  (30 shorter events, 0.8 us)
Async XLA Ops:
  1.5 8.3 %collective-permute-start = (bf16[1,256,128]{2,1,0:T(8,128)(2,1)S(1)}, bf16[1,256,128]{2,1,0:T(8,128)(2,1)S(1)}, u32[]{:S(2)}, u32[]{:S(2)}) collective-permute-start(bf16[1,256,128]{2,1,0:T(8,128)(2,1)S(1)} %dynamic-slice_bitcast_fusion), channel_id=1, source_target_pairs={{0,16},{1,17},{2,18},{3,19},{4,20},{5,21},{6,22},{7,23},{8,24},{9,... | collective-permute-start | bytes 196616 | tf_op jit(solution)/shard_map/ppermute | solution.py:280
  16.3 13.3 %copy-start.2 = (f32[8,256,128]{2,1,0:T(8,128)S(1)}, f32[8,256,128]{2,1,0:T(8,128)}, u32[]{:S(2)}) copy-start(f32[8,256,128]{2,1,0:T(8,128)} %get-tuple-element.41) | copy-start | bytes 3145732
  16.3 2.1 %collective-permute-start.1 = (bf16[8,256,128]{2,1,0:T(8,128)(2,1)}, bf16[8,256,128]{2,1,0:T(8,128)(2,1)S(1)}, u32[]{:S(2)}, u32[]{:S(2)}) collective-permute-start(bf16[8,256,128]{2,1,0:T(8,128)(2,1)} %bitcast.12), channel_id=1, source_target_pairs={{0,1},{1,0},{2,3},{3,2},{4,5},{5,4},{6,7},{7,6},{8,9},{9,8},{10,11... | collective-permute-start | bytes 1572872 | tf_op jit(solution)/shard_map/ppermute | solution.py:341
  16.3 13.3 %collective-permute-start.5 = (bf16[8,256,128]{2,1,0:T(8,128)(2,1)}, bf16[8,256,128]{2,1,0:T(8,128)(2,1)S(1)}, u32[]{:S(2)}, u32[]{:S(2)}) collective-permute-start(bf16[8,256,128]{2,1,0:T(8,128)(2,1)} %bitcast.11), channel_id=1, source_target_pairs={{0,1},{1,0},{2,3},{3,2},{4,5},{5,4},{6,7},{7,6},{8,9},{9,8},{10,11... | collective-permute-start | bytes 1572872 | tf_op jit(solution)/shard_map/ppermute | solution.py:342
  16.9 5.0 %collective-permute-start.2 = (bf16[2,256,128]{2,1,0:T(8,128)(2,1)S(1)}, bf16[2,256,128]{2,1,0:T(8,128)(2,1)S(1)}, u32[]{:S(2)}, u32[]{:S(2)}) collective-permute-start(bf16[2,256,128]{2,1,0:T(8,128)(2,1)S(1)} %pad_maximum_fusion.2), channel_id=1, source_target_pairs={{0,2},{1,9},{2,0},{3,11},{4,6},{5,13},{6,4},{7,15},{8,10},{9,1},{1... | collective-permute-start | bytes 393224 | tf_op jit(solution)/shard_map/ppermute | solution.py:280
  21.9 13.4 %collective-permute-start.3 = (bf16[8,256,128]{2,1,0:T(8,128)(2,1)S(1)}, bf16[8,256,128]{2,1,0:T(8,128)(2,1)S(1)}, u32[]{:S(2)}, u32[]{:S(2)}) collective-permute-start(bf16[8,256,128]{2,1,0:T(8,128)(2,1)S(1)} %add_convert_fusion), channel_id=1, source_target_pairs={{0,2},{1,9},{2,0},{3,11},{4,6},{5,13},{6,4},{7,15},{8,10},{9,1},{1... | collective-permute-start | bytes 1572872 | tf_op jit(solution)/shard_map/ppermute | solution.py:280
  28.0 7.3 %collective-permute-start.4 = (bf16[4,256,128]{2,1,0:T(8,128)(2,1)S(1)}, bf16[4,256,128]{2,1,0:T(8,128)(2,1)S(1)}, u32[]{:S(2)}, u32[]{:S(2)}) collective-permute-start(bf16[4,256,128]{2,1,0:T(8,128)(2,1)S(1)} %pad_maximum_fusion.1), channel_id=1, source_target_pairs={{0,4},{1,5},{2,6},{3,7},{4,0},{5,1},{6,2},{7,3},{8,12},{9,13},{10,... | collective-permute-start | bytes 786440 | tf_op jit(solution)/shard_map/ppermute | solution.py:280
  35.4 34.7 %copy-start = (bf16[8,256,128]{2,1,0:T(8,128)(2,1)}, bf16[8,256,128]{2,1,0:T(8,128)(2,1)S(1)}, u32[]{:S(2)}) copy-start(bf16[8,256,128]{2,1,0:T(8,128)(2,1)S(1)} %pad_maximum_fusion.refs_2_) | copy-start | bytes 1572868
  35.5 9.2 %collective-permute-start.7 = (bf16[8,256,128]{2,1,0:T(8,128)(2,1)S(1)}, bf16[8,256,128]{2,1,0:T(8,128)(2,1)S(1)}, u32[]{:S(2)}, u32[]{:S(2)}) collective-permute-start(bf16[8,256,128]{2,1,0:T(8,128)(2,1)S(1)} %pad_maximum_fusion.refs_2_), channel_id=1, source_target_pairs={{0,8},{1,3},{2,10},{3,1},{4,12},{5,7},{6,14},{7,5},{8,0},{9,11},{1... | collective-permute-start | bytes 1572872 | tf_op jit(solution)/shard_map/ppermute | solution.py:280
  36.3 7.9 %collective-permute-start.6 = (bf16[4,256,128]{2,1,0:T(8,128)(2,1)S(1)}, bf16[4,256,128]{2,1,0:T(8,128)(2,1)S(1)}, u32[]{:S(2)}, u32[]{:S(2)}) collective-permute-start(bf16[4,256,128]{2,1,0:T(8,128)(2,1)S(1)} %get-tuple-element.56), channel_id=1, source_target_pairs={{0,4},{1,5},{2,6},{3,7},{4,0},{5,1},{6,2},{7,3},{8,12},{9,13},{10,... | collective-permute-start | bytes 786440 | tf_op jit(solution)/shard_map/ppermute | solution.py:280
  44.7 28.1 %copy-start.4 = (bf16[8,256,128]{2,1,0:T(8,128)(2,1)}, bf16[8,256,128]{2,1,0:T(8,128)(2,1)S(1)}, u32[]{:S(2)}) copy-start(bf16[8,256,128]{2,1,0:T(8,128)(2,1)S(1)} %collective-permute-done.7.refs_3_) | copy-start | bytes 1572868
  44.8 6.4 %collective-permute-start.10 = (f32[2,256,128]{2,1,0:T(8,128)S(1)}, f32[2,256,128]{2,1,0:T(8,128)S(1)}, u32[]{:S(2)}, u32[]{:S(2)}) collective-permute-start(f32[2,256,128]{2,1,0:T(8,128)S(1)} %get-tuple-element.58), channel_id=1, source_target_pairs={{0,8},{1,3},{2,10},{3,1},{4,12},{5,7},{6,14},{7,5},{8,0},{9,11},{1... | collective-permute-start | bytes 786440 | tf_op jit(solution)/shard_map/ppermute | solution.py:280
  51.3 7.7 %collective-permute-start.11 = (f32[1,256,128]{2,1,0:T(8,128)S(1)}, f32[1,256,128]{2,1,0:T(8,128)S(1)}, u32[]{:S(2)}, u32[]{:S(2)}) collective-permute-start(f32[1,256,128]{2,1,0:T(8,128)S(1)} %slice_add_fusion.4), channel_id=1, source_target_pairs={{0,16},{1,17},{2,18},{3,19},{4,20},{5,21},{6,22},{7,23},{8,24},{9,... | collective-permute-start | bytes 393224 | tf_op jit(solution)/shard_map/ppermute | solution.py:280
  59.0 1.4 %copy-start.3 = (f32[1,256,128]{2,1,0:T(8,128)}, f32[1,256,128]{2,1,0:T(8,128)S(1)}, u32[]{:S(2)}) copy-start(f32[1,256,128]{2,1,0:T(8,128)S(1)} %fusion.1.refs_3_) | copy-start | bytes 393220
  59.0 1.4 %collective-permute-start.12 = (f32[1,256,128]{2,1,0:T(8,128)S(1)}, f32[1,256,128]{2,1,0:T(8,128)S(1)}, u32[]{:S(2)}, u32[]{:S(2)}) collective-permute-start(f32[1,256,128]{2,1,0:T(8,128)S(1)} %fusion.1.refs_3_), channel_id=1, source_target_pairs={{0,1},{1,0},{2,3},{3,2},{4,5},{5,4},{6,7},{7,6},{8,9},{9,8},{10,11... | collective-permute-start | bytes 393224 | tf_op jit(solution)/shard_map/ppermute | solution.py:356
  60.5 0.7 copy-start.7
  64.3 18.7 %all-to-all-start = ((bf16[16,96,128]{2,1,0:T(8,128)(2,1)}), bf16[16,96,128]{2,1,0:T(8,128)(2,1)S(1)}, u32[]{:S(2)}, u32[]{:S(2)}) async-start(bf16[16,96,128]{2,1,0:T(8,128)(2,1)} %shard_map.132), calls=%async_computation | async-start | bytes 786432 | tf_op jit(solution)/shard_map/all_to_all | solution.py:403
  70.0 2.0 %collective-permute-start.8 = (bf16[8,256,128]{2,1,0:T(8,128)(2,1)S(1)}, bf16[8,256,128]{2,1,0:T(8,128)(2,1)S(1)}, u32[]{:S(2)}, u32[]{:S(2)}) collective-permute-start(bf16[8,256,128]{2,1,0:T(8,128)(2,1)S(1)} %pad_maximum_fusion.refs_2_), channel_id=1, source_target_pairs={{0,1},{1,0},{2,3},{3,2},{4,5},{5,4},{6,7},{7,6},{8,9},{9,8},{10,11... | collective-permute-start | bytes 1572872 | tf_op jit(solution)/shard_map/ppermute | solution.py:358
  70.1 2.6 %collective-permute-start.9 = (bf16[8,256,128]{2,1,0:T(8,128)(2,1)S(1)}, bf16[8,256,128]{2,1,0:T(8,128)(2,1)S(1)}, u32[]{:S(2)}, u32[]{:S(2)}) collective-permute-start(bf16[8,256,128]{2,1,0:T(8,128)(2,1)S(1)} %collective-permute-done.7.refs_3_), channel_id=1, source_target_pairs={{0,1},{1,0},{2,3},{3,2},{4,5},{5,4},{6,7},{7,6},{8,9},{9,8},{10,11... | collective-permute-start | bytes 1572872 | tf_op jit(solution)/shard_map/ppermute | solution.py:358
  72.0 0.8 copy-start.5
  72.8 0.8 copy-start.6
  82.9 0.8 copy-start.1

commit v4 on v3

--- a/solution.py
+++ b/solution.py
@@ -32,56 +32,87 @@
     return high, (value - high.astype(F32)).astype(BF16)
 
 
-def statistics_kernel(src, hidden, hist, inv_rms):
+def normed_tile(tile, hidden, inv_rms, gain, hist):
+    stream = hidden[:, tile * LANES : (tile + 1) * LANES].astype(F32)
+    normed = (stream * inv_rms) * gain[tile : tile + 1, :]
+    return jnp.where(hist[tile : tile + 1, :] > 0.5, normed, 0.0).astype(BF16)
+
+
+def lower_half(rows):
+    return lax.broadcasted_iota(jnp.int32, (rows, LANES), 1) < LANES // 2
+
+
+def token_kernel(rels, rep_count, cap, ob, src, gain, hidden_hbm, cot, hist, inv_out, *rest):
+    *blocks, hidden, own_grads, other_grads, sem = rest
+    owns, others = blocks[: len(blocks) // 2], blocks[len(blocks) // 2 :]
+    copy = pltpu.make_async_copy(hidden_hbm, hidden, sem)
+    copy.start()
+    me = lax.axis_index("dp")
+    rep = lax.axis_index("rep")
     tiles = D_OLD // LANES
+    tokens = hidden.shape[0]
     step = 1024
     total = jnp.zeros((tiles, LANES), F32)
     for at in range(0, D_NEW, step):
         units = src[:, at : at + step]
         total = total + dot(one_hot(tiles, units >> 7), one_hot(LANES, units & 127), (1, 1))
     hist[...] = total
-    tokens = hidden.shape[0]
+    copy.wait()
     squares = jnp.zeros((tokens, LANES), F32)
     for tile in range(tiles):
         stream = hidden[:, tile * LANES : (tile + 1) * LANES].astype(F32)
         squares = squares + stream * stream * hist[tile : tile + 1, :]
-    mean = jnp.sum(squares, axis=1, keepdims=True) / D_NEW
-    inv_rms[...] = jnp.broadcast_to(lax.rsqrt(mean + 1e-05), (tokens, LANES))
-
-
-def token_kernel(rels, rep_count, cap, ob, hist, inv_rms, gain, hidden, cot, x_out, *rest):
-    *blocks, grads = rest
-    owns, others = blocks[: len(blocks) // 2], blocks[len(blocks) // 2 :]
-    me = lax.axis_index("dp")
-    rep = lax.axis_index("rep")
-    part = cap // rep_count
-    for tile in range(D_OLD // LANES):
+    inv_rms = lax.rsqrt(jnp.sum(squares, axis=1, keepdims=True) / D_NEW + 1e-05)
+    inv_out[...] = jnp.broadcast_to(inv_rms, (tokens, LANES))
+    staged = len(rels) > 1
+    columns = cot[...]
+    if staged:
+        lower = lower_half(tokens)
+        columns = columns.astype(F32)
+        turned = pltpu.roll(columns, LANES // 2, 1)
+        left, right = jnp.where(lower, columns, turned), jnp.where(lower, turned, columns)
+        sides = [jnp.where(rep == 0, left, right), jnp.where(rep == 0, right, left)]
+        columns = jnp.concatenate(sides, axis=1).astype(BF16)
+    for tile in range(tiles):
         at = tile * LANES
-        stream = hidden[:, at : at + LANES].astype(F32)
-        normed = (stream * inv_rms[...]) * gain[tile : tile + 1, :]
-        normed = jnp.where(hist[tile : tile + 1, :] > 0.5, normed, 0.0).astype(BF16)
-        x_out[:, at : at + LANES] = normed
-        grads[at : at + LANES, :] = dot(normed, cot[...], (0, 0))
-    grads[D_OLD:, :] = jnp.zeros((cap, LANES), F32)
+        result = dot(normed_tile(tile, hidden, inv_rms, gain, hist), columns, (0, 0))
+        own_grads[at : at + LANES, :] = result[:, :LANES]
+        if staged:
+            other_grads[at : at + LANES, :] = result[:, LANES:]
+    own_grads[D_OLD:, :] = jnp.zeros((cap, LANES), F32)
+    other_grads[D_OLD:, :] = jnp.zeros((cap, LANES), F32)
     dp_count = len(rels[0])
     half = dp_count // len(owns)
+    part = cap // rep_count
     for at in range(dp_count):
-        first = ob[holder_at(rels, rep, me, at)]
-        owns[at // half][at % half] = grads[pl.ds(first + rep * part, part), :]
-        for away in range(1, rep_count):
-            mate = (rep + away) % rep_count
-            first = ob[holder_at(rels, mate, me, at)] if len(rels) > 1 else first
-            others[at // half][away - 1, at % half] = grads[pl.ds(first + mate * part, part), :].astype(BF16)
+        if staged:
+            first = ob[holder_at(rels, rep, me, at)]
+            owns[at // half][at % half] = packed_rows(own_grads, first, part)
+            first = ob[holder_at(rels, 1 - rep, me, at)]
+            others[at // half][0, at % half] = packed_rows(other_grads, first, part).astype(BF16)
+        else:
+            first = ob[at]
+            owns[0][at] = own_grads[pl.ds(first + rep * part, part), :]
+            for away in range(1, rep_count):
+                mate = (rep + away) % rep_count
+                others[0][away - 1, at] = own_grads[pl.ds(first + mate * part, part), :].astype(BF16)
+
+
+def packed_rows(grads, first, part):
+    return jnp.where(lower_half(part), grads[pl.ds(first, part), :], grads[pl.ds(first + part, part), :])
 
 
 def holder_at(rels, rep, me, at):
-    if len(rels) == 1:
-        return rels[0][at]
     return me ^ jnp.where(rep == 0, rels[0][at], rels[1][at])
 
 
-def project_kernel(dp_count, orders, cap, ob, x, *rest):
-    *pieces, out, dense, blocks, sems = rest
+def fill_normed(x, hidden, inv_rms, gain, hist):
+    for tile in range(D_OLD // LANES):
+        x[:, tile * LANES : (tile + 1) * LANES] = normed_tile(tile, hidden, inv_rms[...], gain, hist)
+
+
+def project_kernel(dp_count, orders, cap, ob, hidden, inv_rms, gain, hist, *rest):
+    *pieces, out, dense, x, blocks, sems = rest
     me = lax.axis_index("dp")
     rep = lax.axis_index("rep")
     part = cap // 2
@@ -93,6 +124,7 @@
         copies.append(pltpu.make_async_copy(piece, place, sems.at[at]))
     for copy in copies:
         copy.start()
+    fill_normed(x, hidden, inv_rms, gain, hist)
     for copy in copies:
         copy.wait()
     for p in range(dp_count):
@@ -103,7 +135,8 @@
     out[...] = dot(x[...], dense[0:D_OLD, :].astype(BF16), (1, 0)).astype(BF16)
 
 
-def project_gathered_kernel(dp_count, cap, ob, x, weights, out, dense):
+def project_gathered_kernel(dp_count, cap, ob, hidden, inv_rms, gain, hist, weights, out, dense, x):
+    fill_normed(x, hidden, inv_rms, gain, hist)
     for p in range(dp_count):
         dense[pl.ds(ob[p], cap), :] = weights[p * cap : (p + 1) * cap, :].astype(F32)
     out[...] = dot(x[...], dense[0:D_OLD, :].astype(BF16), (1, 0)).astype(BF16)
@@ -161,15 +194,24 @@
         places[:, first : first + step] = holder * (table_rows * LANES) + dest * slots + rank
 
 
-def pack_kernel(dp_count, slots, table_rows, chosen, keep, own_gain, mine, *rest):
-    *mate, weight, first, second, out = rest
+def pack_kernel(dp_count, slots, table_rows, staged, chosen, keep, own_gain, reduced, weight_in, first_in, second_in, out):
     pairs = dp_count * slots
-    grad = mine[...]
-    if mate:
-        grad, other = mine[0], mate[0][0]
-        own_first = lax.axis_index("rep") == 0
-        grad = jnp.concatenate([jnp.where(own_first, grad, other), jnp.where(own_first, other, grad)], axis=0)
-    high, low = split(weight[...].astype(F32) * grad)
+    rows = weight_in.shape[0]
+    weight, first, second = weight_in[...].astype(F32), first_in[...], second_in[...]
+    if staged:
+        turn = LANES // 2
+        lower = lower_half(rows)
+        grad = reduced[0]
+        grad = jnp.concatenate([grad, pltpu.roll(grad, turn, 1)], axis=0)
+        left = lax.axis_index("rep") == 0
+        weight, first, second = [
+            jnp.where(left, value, pltpu.roll(value, turn, 1)) for value in (weight, first, second)
+        ]
+        product = jnp.where(lower, weight * grad, 0.0)
+    else:
+        grad = reduced[...]
+        product = weight * grad
+    high, low = split(product)
     ones = jnp.ones((8, LANES), BF16)
     column = (dot(ones, high, (1, 1)) + dot(ones, low, (1, 1))) * own_gain[...]
     high, low = split(column)
@@ -177,40 +219,58 @@
     for part in (high, low):
         part = dot(part, chosen[...], (1, 1))[0:1] * keep[...]
         table += [part[:, r * LANES : (r + 1) * LANES] for r in range(table_rows)]
-    spare = out.shape[1] - 2 * slots - 2 * table_rows
+    updated = [0.9 * first + 0.1 * grad, 0.95 * second + 0.05 * grad * grad]
+    if staged:
+        updated = [jnp.where(lower, updated[0], pltpu.roll(updated[1], turn, 1))]
+    filled = len(updated) * slots
+    spare = out.shape[1] - filled - 2 * table_rows
     table = jnp.concatenate(table + [jnp.zeros((spare, LANES), F32)], axis=0).astype(BF16)
     picked = chosen[0:pairs]
-    updated = (0.9 * first[...] + 0.1 * grad, 0.95 * second[...] + 0.05 * grad * grad)
     for at, value in enumerate(updated):
         moved = dot(picked, value.astype(BF16), (1, 0)).astype(BF16).reshape(dp_count, slots, LANES)
         out[:, at * slots : (at + 1) * slots, :] = moved
     for q in range(dp_count):
-        out[q, 2 * slots :, :] = table
-
-
-def finish_kernel(
-    dp_count, slots, table_rows, ob, nb, src, places, moved, gain_grad, first, second, adam, ones, twos, table
-):
+        out[q, filled:, :] = table
+
+
+def finish_kernel(dp_count, slots, table_rows, staged, ob, nb, src, places, *rest):
+    arrived, rest = (rest[:2], rest[2:]) if staged else (rest[:1], rest[1:])
+    gain_grad, first, second, adam, ones, twos, table = rest
     me = lax.axis_index("dp")
     offset = offset_of(src, ob, nb, me, dp_count)
+    groups = 1 if staged else 2
+    pages = [(moved, 0) for moved in arrived] if staged else [(arrived[0], 0), (arrived[0], slots)]
     for i in range(dp_count):
         p = (i + offset) & (dp_count - 1)
         strided = pl.ds(i, slots, stride=dp_count)
-        ones[strided, :] = moved[p, 0:slots, :].astype(F32)
-        twos[strided, :] = moved[p, slots : 2 * slots, :].astype(F32)
+        for (moved, at), rows in zip(pages, (ones, twos)):
+            rows[strided, :] = moved[p, at : at + slots, :].astype(F32)
     cap = first.shape[0]
     live = lax.broadcasted_iota(jnp.int32, (cap, LANES), 0) < nb[me + 1] - nb[me]
-    first_next = jnp.where(live, ones[0:cap, :], 0.0)
-    second_next = jnp.where(live, twos[0:cap, :], 0.0)
+    one, two = ones[0:cap, :], twos[0:cap, :]
+    if staged:
+        left = lax.axis_index("rep") == 0
+        lower = lower_half(cap)
+        one, two = jnp.where(left, one, two), jnp.where(left, two, one)
+        turn = LANES // 2
+        one, two = (
+            jnp.where(lower, one, pltpu.roll(two, turn, 1)),
+            jnp.where(lower, pltpu.roll(one, turn, 1), two),
+        )
+    first_next = jnp.where(live, one, 0.0)
+    second_next = jnp.where(live, two, 0.0)
     first[...] = first_next
     second[...] = second_next
     adam[...] = first_next / (jnp.sqrt(second_next) + 1e-08)
-    at = 2 * slots
+    at = groups * slots
     for p in range(dp_count):
         here = p * table_rows
-        table[here : here + table_rows, 0:LANES] = moved[p, at : at + table_rows, :].astype(F32)
-        table[here : here + table_rows, LANES:] = moved[p, at + table_rows : at + 2 * table_rows, :].astype(F32)
-    values = table[...].astype(BF16)
+        terms = [
+            moved[p, at + r : at + r + table_rows, :].astype(F32) for moved in arrived for r in (0, table_rows)
+        ]
+        table[here : here + table_rows, :] = sum(terms[1:], terms[0])
+    high, low = split(table[...])
+    values = jnp.concatenate([high, low], axis=1)
     step = 1024
     for start in range(0, D_NEW, step):
         slot = places[:, start : start + step]
@@ -280,90 +340,96 @@
         return lax.ppermute(value, ("dp", "rep"), pairs)
 
     swap = [(0, 1), (1, 0)]
+    any_spec = pl.BlockSpec(memory_space=pl.ANY)
     if staged:
         gathered = lax.dynamic_slice_in_dim(weight_old, lax.axis_index("rep") * part, part)[None]
+        sent = across(gathered, doubling, 0)
     else:
         weights = lax.all_gather(weight_old, "dp", axis=0, tiled=True)
 
     tiles = D_OLD // LANES
-    hist, inv_rms = call(
-        statistics_kernel,
-        4,
-        (shape((tiles, LANES), F32), shape((tokens, LANES), F32)),
-        [VMEM_SPEC] * 2,
-        [],
-        units,
-        hidden_old,
-    )
-    if staged:
-        hist, sent = lax.optimization_barrier((hist, across(gathered, doubling, 0)))
-        gathered = jnp.concatenate([gathered, sent])
-        sent = across(gathered, doubling, 1)
-    normed, *blocks = call(
+    hist, inv_rms, *blocks = call(
         lambda *refs: token_kernel(rels, rep_count, cap, *refs),
-        5,
+        8,
         (
-            shape((tokens, D_OLD), BF16),
+            shape((tiles, LANES), F32),
+            shape((tokens, LANES), F32),
             *[shape((dp_count // parts, part, LANES), F32)] * parts,
             *[shape((rep_count - 1, dp_count // parts, part, LANES), BF16)] * parts,
         ),
-        [SMEM_SPEC] + [VMEM_SPEC] * 5,
-        [pltpu.VMEM((D_OLD + cap, LANES), F32)],
+        [SMEM_SPEC] + [VMEM_SPEC] * 2 + [any_spec] + [VMEM_SPEC],
+        [
+            pltpu.VMEM((tokens, D_OLD), BF16),
+            pltpu.VMEM((D_OLD + cap, LANES), F32),
+            pltpu.VMEM((D_OLD + cap, LANES), F32),
+            pltpu.SemaphoreType.DMA(()),
+        ],
         old_bounds,
-        hist,
-        inv_rms,
+        units,
         gain,
         hidden_old,
         cotangent,
     )
     owns, others = blocks[:parts], blocks[parts:]
-    chosen, keep, own_gain, places = call(
-        lambda *refs: index_kernel(dp_count, cap, slots, table_rows, *refs),
-        5,
-        (
-            shape((table_rows * LANES, cap), BF16),
-            shape((1, table_rows * LANES), F32),
-            shape((1, cap), F32),
-            shape((1, D_NEW), jnp.int32),
-        ),
-        [SMEM_SPEC] * 3 + [VMEM_SPEC] * 2,
-        [pltpu.VMEM((table_rows * LANES, LANES), jnp.int32), pltpu.VMEM((D_OLD // LANES + 8, LANES), F32)],
-        old_bounds,
-        new_bounds,
-        source_map,
-        gain,
-        units,
-    )
+    def indices(units):
+        return call(
+            lambda *refs: index_kernel(dp_count, cap, slots, table_rows, *refs),
+            5,
+            (
+                shape((table_rows * LANES, cap), BF16),
+                shape((1, table_rows * LANES), F32),
+                shape((1, cap), F32),
+                shape((1, D_NEW), jnp.int32),
+            ),
+            [SMEM_SPEC] * 3 + [VMEM_SPEC] * 2,
+            [pltpu.VMEM((table_rows * LANES, LANES), jnp.int32), pltpu.VMEM((D_OLD // LANES + 8, LANES), F32)],
+            old_bounds,
+            new_bounds,
+            source_map,
+            gain,
+            units,
+        )
+
     project_shape = shape((tokens, LANES), BF16)
-    dense = [pltpu.VMEM((D_OLD + cap, LANES), F32)]
+    dense = [pltpu.VMEM((D_OLD + cap, LANES), F32), pltpu.VMEM((tokens, D_OLD), BF16)]
     if staged:
         half = dp_count // 2
-        high = owns[1] + lax.ppermute(others[1][0], "rep", swap).astype(F32)
+        send, sent = lax.optimization_barrier((others[1][0], sent))
+        gathered = jnp.concatenate([gathered, sent])
+        sent = across(gathered, doubling, 1)
+        high = (owns[1] + lax.ppermute(send, "rep", swap).astype(F32)).astype(BF16)
         low = owns[0] + lax.ppermute(others[0][0], "rep", swap).astype(F32)
-        high, sent = lax.optimization_barrier((high.astype(BF16), sent))
+        high, sent = lax.optimization_barrier((high, sent))
         for stage in range(bits - 1):
             came = across(high, halving, stage)
             if stage < bits - 2:
                 gathered = jnp.concatenate([gathered, sent])
                 sent = across(gathered, doubling, stage + 2)
-                came, sent, chosen = lax.optimization_barrier((came, sent, chosen))
+                came, sent = lax.optimization_barrier((came, sent))
+            if stage == 1:
+                came, chosen = lax.optimization_barrier((came, chosen))
             came = came.astype(F32)
             half = half // 2
-            low, high = low[:half] + came[:half], low[half:] + came[half:]
-            if stage < 1:
-                high = high.astype(BF16)
-        grad_part = low + across(high, halving, bits - 1).astype(F32)
-        grads = [grad_part, lax.ppermute(grad_part, "rep", swap)]
+            low, high = low[:half] + came[:half], (low[half:] + came[half:]).astype(BF16)
+            if stage == 0:
+                high, late_units = lax.optimization_barrier((high, units))
+                chosen, keep, own_gain, places = indices(late_units)
+        came = across(high, halving, bits - 1)
         pieces = [gathered, sent]
         pieces += [lax.ppermute(piece, "rep", swap) for piece in pieces]
+        came, *pieces = lax.optimization_barrier((came, *pieces))
+        grad_own = low + came.astype(F32)
         projected = call(
             lambda *refs: project_kernel(dp_count, doubling, cap, *refs),
-            5,
+            6,
             project_shape,
-            [SMEM_SPEC, VMEM_SPEC] + [pl.BlockSpec(memory_space=pl.ANY)] * 4,
+            [SMEM_SPEC] + [VMEM_SPEC] * 4 + [any_spec] * 4,
             dense + [pltpu.VMEM((2, dp_count, part, LANES), BF16), pltpu.SemaphoreType.DMA((4,))],
             old_bounds,
-            normed,
+            hidden_old,
+            inv_rms,
+            gain,
+            hist,
             *pieces,
         )
     else:
@@ -373,47 +439,55 @@
             chip = chip + lax.ppermute(others[0][away - 1], "rep", ring).astype(F32)
         blocks = lax.all_to_all(chip.astype(BF16), "dp", split_axis=0, concat_axis=0)
         grad_part = jnp.sum(blocks.astype(F32), axis=0)
-        grads = [lax.all_gather(grad_part, "rep", axis=0, tiled=True)]
+        grad_own = lax.all_gather(grad_part, "rep", axis=0, tiled=True)
+        chosen, keep, own_gain, places = indices(units)
         projected = call(
             lambda *refs: project_gathered_kernel(dp_count, cap, *refs),
-            5,
+            6,
             project_shape,
-            [SMEM_SPEC] + [VMEM_SPEC] * 2,
+            [SMEM_SPEC] + [VMEM_SPEC] * 5,
             dense,
             old_bounds,
-            normed,
+            hidden_old,
+            inv_rms,
+            gain,
+            hist,
             weights,
         )
-    message = 2 * slots + 2 * table_rows
+
+    message = (1 if staged else 2) * slots + 2 * table_rows
     message = (message + 7) // 8 * 8
     packed = call(
-        lambda *refs: pack_kernel(dp_count, slots, table_rows, *refs),
+        lambda *refs: pack_kernel(dp_count, slots, table_rows, staged, *refs),
         3,
         shape((dp_count, message, LANES), BF16),
-        [VMEM_SPEC] * (6 + len(grads)),
+        [VMEM_SPEC] * 7,
         [],
         chosen,
         keep,
         own_gain,
-        *grads,
+        grad_own,
         weight_old,
         moment_first,
         moment_second,
     )
-    moved = lax.all_to_all(packed, "dp", split_axis=0, concat_axis=0)
+    moved = [lax.all_to_all(packed, "dp", split_axis=0, concat_axis=0)]
+    if staged:
+        arrived, projected = lax.optimization_barrier((moved[0], projected))
+        moved = [arrived, lax.ppermute(arrived, "rep", swap)]
     rows = shape((new_cap, LANES), F32)
     gain_grad, first_next, second_next, adam_step = call(
-        lambda *refs: finish_kernel(dp_count, slots, table_rows, *refs),
+        lambda *refs: finish_kernel(dp_count, slots, table_rows, staged, *refs),
         4,
         (shape((1, D_NEW), F32), rows, rows, rows),
-        [SMEM_SPEC] * 3 + [VMEM_SPEC] * 2,
+        [SMEM_SPEC] * 3 + [VMEM_SPEC] * (1 + len(moved)),
         [pltpu.VMEM((dp_count * slots, LANES), F32)] * 2
-        + [pltpu.VMEM((dp_count * table_rows, 2 * LANES), F32)],
+        + [pltpu.VMEM((dp_count * table_rows, LANES), F32)],
         old_bounds,
         new_bounds,
         source_map,
         places,
-        moved,
+        *moved,
     )
     return (projected, gain_grad.reshape(D_NEW), first_next, second_next, adam_step)
 

time: 88.1 us -> 71.5 us (0.81)
  waiting for transfers between devices: 31.8 us -> 22.7 us
  Pallas kernels: 27.7 us -> 24 us
  starting transfers between devices: 22.3 us -> 19.1 us
  local copies, waits for them, and re-layouts: 3.07 us -> 1.56 us
    ppermute x8, waiting for transfers between devices: 24.2 us -> 18.3 us  [across(): return lax.ppermute(value, ('dp', 'rep'), pairs)]
    pallas_call x6 -> x5, Pallas kernels: 27.7 us -> 24 us  [call(): pl.pallas_call(kernel, out_shape=out_shape, in_specs=specs, out_specs=jax...]
    ppermute x2, waiting for transfers between devices: 2.15 us -> 0.01 us  [on_device(): pieces += [lax.ppermute(piece, 'rep', swap) for piece in pieces]]
    ppermute x8, starting transfers between devices: 15.4 us -> 13.6 us  [across(): return lax.ppermute(value, ('dp', 'rep'), pairs)]
    unnamed x16 -> x14, local copies, waits for them, and re-layouts: 2.22 us -> 0.72 us
    all_to_all x1, waiting for transfers between devices: 4.03 us -> 2.89 us  [on_device(): moved = [lax.all_to_all(packed, 'dp', split_axis=0, concat_axis=0)]]
  transfers between devices with their start and end apart: 14 -> 14, of which waited for: 10 -> 9; matrix products, arithmetic and copies ran while one was open for 2% -> 2% of each run, Pallas kernels for 16% -> 24%
where the time goes in v4:
time: 71.5 us; the launch traced here: 70.9 us
  Pallas kernels  24 us (34%)
  waiting for transfers between devices  22.7 us (32%)
  starting transfers between devices  19.1 us (27%)
  other arithmetic  2.6 us (4%)
  local copies, waits for them, and re-layouts  1.56 us (2%)
  between operations  0.81 us (1%)
    pallas_call x5, Pallas kernels, call(): pl.pallas_call(kernel, out_shape=out_shape, in_specs=specs, out_specs=jax...  24 us
    ppermute x8, waiting for transfers between devices, across(): return lax.ppermute(value, ('dp', 'rep'), pairs)  18.3 us
    ppermute x8, starting transfers between devices, across(): return lax.ppermute(value, ('dp', 'rep'), pairs)  13.6 us
    all_to_all x1, starting transfers between devices, on_device(): moved = [lax.all_to_all(packed, 'dp', split_axis=0, concat_axis=0)]  4.88 us
    all_to_all x1, waiting for transfers between devices, on_device(): moved = [lax.all_to_all(packed, 'dp', split_axis=0, concat_axis=0)]  2.89 us
    ppermute x1, waiting for transfers between devices, on_device(): moved = [arrived, lax.ppermute(arrived, 'rep', swap)]  1.49 us
  transfers between devices with their start and end apart: 14, of which 9 were waited for; matrix products, arithmetic and copies ran while one was open for 2% of the time, Pallas kernels for 24%

profile of v4, /device:TPU:0, one launch (start us, length us, event | category | flops | bytes accessed | tf_op | source)
XLA Modules:
  0.0 70.9 jit_solution(15173375230946415112)
XLA Ops:
  0.6 0.8 %dynamic-slice_bitcast_fusion = bf16[1,256,128]{2,1,0:T(8,128)(2,1)S(1)} fusion(bf16[512,128]{1,0:T(8,128)(2,1)} %refs_4_.3, s32[]{:T(128)S(6)} %select_n.3), kind=kLoop, calls=%fused_computation.15 | loop fusion | bytes 131076 | tf_op jit(solution)/shard_map/broadcast_in_dim | solution.py:345
  1.5 4.0 %collective-permute-start.1 = (bf16[1,256,128]{2,1,0:T(8,128)(2,1)S(1)}, bf16[1,256,128]{2,1,0:T(8,128)(2,1)S(1)}, u32[]{:S(2)}, u32[]{:S(2)}) collective-permute-start(bf16[1,256,128]{2,1,0:T(8,128)(2,1)S(1)} %dynamic-slice_bitcast_fusion), channel_id=1, source_target_pairs={{0,16},{1,17},{2,18},{3,19},{4,20},{5,21},{6,22},{7,23},{8,24},{9,... | collective-permute-start | bytes 196616 | tf_op jit(solution)/shard_map/ppermute | solution.py:340
  5.5 7.2 %shard_map.128 = (f32[48,128]{1,0:T(8,128)}, f32[256,128]{1,0:T(8,128)}, f32[8,256,128]{2,1,0:T(8,128)}, f32[8,256,128]{2,1,0:T(8,128)}, bf16[1,8,256,128]{3,2,1...) custom-call(s32[17]{0:T(128)} %refs_0_.7, s32[1,8192]{1,0:T(1,128)} %bitcast.7, f32[48,128]{1,0:T(8,128)} %bitcast.9, ...), custom_call_target="tpu_custom_call" | custom-call | bytes 24000000 | tf_op jit(solution)/shard_map/pallas_call | solution.py:284
  12.8 0.5 collective-permute-start
  13.3 1.6 %collective-permute-start.3 = (bf16[2,256,128]{2,1,0:T(8,128)(2,1)S(1)}, bf16[2,256,128]{2,1,0:T(8,128)(2,1)S(1)}, u32[]{:S(2)}, u32[]{:S(2)}) collective-permute-start(bf16[2,256,128]{2,1,0:T(8,128)(2,1)S(1)} %pad_maximum_fusion.2), channel_id=1, source_target_pairs={{0,2},{1,9},{2,0},{3,11},{4,6},{5,13},{6,4},{7,15},{8,10},{9,1},{1... | collective-permute-start | bytes 393224 | tf_op jit(solution)/shard_map/ppermute | solution.py:340
  14.9 1.3 %add_convert_fusion = bf16[8,256,128]{2,1,0:T(8,128)(2,1)S(1)} fusion(f32[8,256,128]{2,1,0:T(8,128)} %get-tuple-element.40, bf16[8,256,128]{2,1,0:T(8,128)(2,1)S(1)} %collective-permute-done.2), kind=kLoop, calls=%fused_computation | loop fusion | flops 786432 | bytes 2097152 | tf_op jit(solution)/shard_map/convert_element_type | solution.py:400
  16.2 2.1 %collective-permute-done.3 = bf16[2,256,128]{2,1,0:T(8,128)(2,1)S(1)} collective-permute-done((bf16[2,256,128]{2,1,0:T(8,128)(2,1)S(1)}, bf16[2,256,128]{2,1,0:T(8,128)(2,1)S(1)}, u32[]{:S(2)}, u32[]{:S(2)}) %collective-permute-start.3) | collective-permute-done | bytes 131104 | tf_op jit(solution)/shard_map/ppermute | solution.py:340
  18.3 1.5 %collective-permute-start.4 = (bf16[8,256,128]{2,1,0:T(8,128)(2,1)S(1)}, bf16[8,256,128]{2,1,0:T(8,128)(2,1)S(1)}, u32[]{:S(2)}, u32[]{:S(2)}) collective-permute-start(bf16[8,256,128]{2,1,0:T(8,128)(2,1)S(1)} %add_convert_fusion), channel_id=1, source_target_pairs={{0,2},{1,9},{2,0},{3,11},{4,6},{5,13},{6,4},{7,15},{8,10},{9,1},{1... | collective-permute-start | bytes 1572872 | tf_op jit(solution)/shard_map/ppermute | solution.py:340
  19.9 1.6 %collective-permute-start.5 = (bf16[4,256,128]{2,1,0:T(8,128)(2,1)S(1)}, bf16[4,256,128]{2,1,0:T(8,128)(2,1)S(1)}, u32[]{:S(2)}, u32[]{:S(2)}) collective-permute-start(bf16[4,256,128]{2,1,0:T(8,128)(2,1)S(1)} %pad_maximum_fusion.1), channel_id=1, source_target_pairs={{0,4},{1,5},{2,6},{3,7},{4,0},{5,1},{6,2},{7,3},{8,12},{9,13},{10,... | collective-permute-start | bytes 786440 | tf_op jit(solution)/shard_map/ppermute | solution.py:340
  21.4 0.1 convert_add_fusion
  21.5 5.6 %collective-permute-done.5 = bf16[4,256,128]{2,1,0:T(8,128)(2,1)S(1)} collective-permute-done((bf16[4,256,128]{2,1,0:T(8,128)(2,1)S(1)}, bf16[4,256,128]{2,1,0:T(8,128)(2,1)S(1)}, u32[]{:S(2)}, u32[]{:S(2)}) %collective-permute-start.5) | collective-permute-done | bytes 262176 | tf_op jit(solution)/shard_map/ppermute | solution.py:340
  27.2 0.4 collective-permute-done.4
  27.7 1.6 %collective-permute-start.7 = (bf16[8,256,128]{2,1,0:T(8,128)(2,1)S(1)}, bf16[8,256,128]{2,1,0:T(8,128)(2,1)S(1)}, u32[]{:S(2)}, u32[]{:S(2)}) collective-permute-start(bf16[8,256,128]{2,1,0:T(8,128)(2,1)S(1)} %pad_maximum_fusion.refs_5_), channel_id=1, source_target_pairs={{0,8},{1,3},{2,10},{3,1},{4,12},{5,7},{6,14},{7,5},{8,0},{9,11},{1... | collective-permute-start | bytes 1572872 | tf_op jit(solution)/shard_map/ppermute | solution.py:340
  29.3 0.1 slice_add_fusion
  29.4 1.6 %collective-permute-start.6 = (bf16[4,256,128]{2,1,0:T(8,128)(2,1)S(1)}, bf16[4,256,128]{2,1,0:T(8,128)(2,1)S(1)}, u32[]{:S(2)}, u32[]{:S(2)}) collective-permute-start(bf16[4,256,128]{2,1,0:T(8,128)(2,1)S(1)} %get-tuple-element.47), channel_id=1, source_target_pairs={{0,4},{1,5},{2,6},{3,7},{4,0},{5,1},{6,2},{7,3},{8,12},{9,13},{10,... | collective-permute-start | bytes 786440 | tf_op jit(solution)/shard_map/ppermute | solution.py:340
  31.0 4.6 %shard_map.129 = (bf16[640,512]{1,0:T(8,128)(2,1)}, f32[1,640]{1,0:T(1,128)}, f32[1,512]{1,0:T(1,128)}, s32[1,8192]{1,0:T(1,128)}) custom-call(s32[17]{0:T(128)} %refs_0_.7, s32[17]{0:T(128)} %refs_1_.5, s32[8192]{0:T(1024)} %refs_2_.3, f32[48,128]{1,0:T(8,128)} %bitcast.10, s32[1,8192]{1,0:T(1,128)} %bitcast.8), custom_call_target="tpu_custom_call" | custom-call | bytes 15000000 | tf_op jit(solution)/shard_map/pallas_call | solution.py:284
  35.6 0.5 collective-permute-done.6
  36.1 0.8 %collective-permute-done.7.refs_6_ = bf16[8,256,128]{2,1,0:T(8,128)(2,1)S(1)} collective-permute-done((bf16[8,256,128]{2,1,0:T(8,128)(2,1)S(1)}, bf16[8,256,128]{2,1,0:T(8,128)(2,1)S(1)}, u32[]{:S(2)}, u32[]{:S(2)}) %collective-permute-start.7) | collective-permute-done | bytes 524320 | tf_op jit(solution)/shard_map/ppermute | solution.py:340
  36.9 0.1 collective-permute-start.11
  37.0 0.1 slice_add_fusion.3
  37.1 1.6 %collective-permute-start.8 = (bf16[2,256,128]{2,1,0:T(8,128)(2,1)S(1)}, bf16[2,256,128]{2,1,0:T(8,128)(2,1)S(1)}, u32[]{:S(2)}, u32[]{:S(2)}) collective-permute-start(bf16[2,256,128]{2,1,0:T(8,128)(2,1)S(1)} %get-tuple-element.74), channel_id=1, source_target_pairs={{0,8},{1,3},{2,10},{3,1},{4,12},{5,7},{6,14},{7,5},{8,0},{9,11},{1... | collective-permute-start | bytes 393224 | tf_op jit(solution)/shard_map/ppermute | solution.py:340
  38.8 3.4 %collective-permute-done.8 = bf16[2,256,128]{2,1,0:T(8,128)(2,1)S(1)} collective-permute-done((bf16[2,256,128]{2,1,0:T(8,128)(2,1)S(1)}, bf16[2,256,128]{2,1,0:T(8,128)(2,1)S(1)}, u32[]{:S(2)}, u32[]{:S(2)}) %collective-permute-start.8) | collective-permute-done | bytes 131104 | tf_op jit(solution)/shard_map/ppermute | solution.py:340
  42.2 0.1 collective-permute-start.9
  42.3 5.5 %collective-permute-done.9 = bf16[1,256,128]{2,1,0:T(8,128)(2,1)S(1)} collective-permute-done((bf16[1,256,128]{2,1,0:T(8,128)(2,1)S(1)}, bf16[1,256,128]{2,1,0:T(8,128)(2,1)S(1)}, u32[]{:S(2)}, u32[]{:S(2)}) %collective-permute-start.9) | collective-permute-done | bytes 65568 | tf_op jit(solution)/shard_map/ppermute | solution.py:340
  47.8 0.7 %fusion.3.refs_3_ = f32[1,256,128]{2,1,0:T(8,128)} fusion(f32[2,256,128]{2,1,0:T(8,128)S(1)} %convert_element_type.37, f32[2,256,128]{2,1,0:T(8,128)S(1)} %get-tuple-element.73, bf16[1,256,128]{2,1,0:T(8,128)(2,1)S(1)} %collective-permute-done.9), kind=kLoop, calls=%fused_computation.13 | loop fusion | flops 98304 | bytes 458752 | tf_op jit(solution)/shard_map/add | solution.py:421
  48.6 2.9 %shard_map.130 = bf16[16,56,128]{2,1,0:T(8,128)(2,1)} custom-call(bf16[640,512]{1,0:T(8,128)(2,1)} %get-tuple-element.52.refs_0_, f32[1,640]{1,0:T(1,128)} %get-tuple-element.53.refs_1_, f32[1,512]{1,0:T(1,128)} %get-tuple-element.54.refs_2_, f32[1,256,128]{2,1,0:T(8,128)} %fusion.3.refs_3_, bf16[512,128]{1,0:T(8,128)(2,1)} %refs_4_.3, f32[512,128]{1,0:T(8,128)} %refs_5_.1, ...), custom_call_target="tpu_custom_call" | custom-call | bytes 9000000 | tf_op jit(solution)/shard_map/pallas_call | solution.py:284
  51.5 4.9 %all-to-all-start = ((bf16[16,56,128]{2,1,0:T(8,128)(2,1)}), bf16[16,56,128]{2,1,0:T(8,128)(2,1)S(1)}, u32[]{:S(2)}, u32[]{:S(2)}) async-start(bf16[16,56,128]{2,1,0:T(8,128)(2,1)} %shard_map.130), calls=%async_computation | async-start | bytes 458752 | tf_op jit(solution)/shard_map/all_to_all | solution.py:474
  56.4 5.4 %shard_map.131 = bf16[256,128]{1,0:T(8,128)(2,1)} custom-call(s32[17]{0:T(128)} %refs_0_.7, bf16[256,6144]{1,0:T(8,128)(2,1)} %refs_1_.4, f32[256,128]{1,0:T(8,128)} %get-tuple-element.58.refs_2_, f32[48,128]{1,0:T(8,128)} %bitcast.11, f32[48,128]{1,0:T(8,128)} %get-tuple-element.59.refs_4_, bf16[8,256,128]{2,1,0:T(8,128)(2,1)} %copy-done, ...), custom_call_target="tpu_custom_call" | custom-call | bytes 18000000 | tf_op jit(solution)/shard_map/pallas_call | solution.py:284
  61.8 2.9 %all-to-all-done.refs_4_ = bf16[16,56,128]{2,1,0:T(8,128)(2,1)S(1)} async-done(((bf16[16,56,128]{2,1,0:T(8,128)(2,1)}), bf16[16,56,128]{2,1,0:T(8,128)(2,1)S(1)}, u32[]{:S(2)}, u32[]{:S(2)}) %all-to-all-start) | async-done | bytes 229408 | tf_op jit(solution)/shard_map/all_to_all | solution.py:474
  64.7 1.5 %collective-permute-done.12.refs_5_ = bf16[16,56,128]{2,1,0:T(8,128)(2,1)S(1)} collective-permute-done((bf16[16,56,128]{2,1,0:T(8,128)(2,1)S(1)}, bf16[16,56,128]{2,1,0:T(8,128)(2,1)S(1)}, u32[]{:S(2)}, u32[]{:S(2)}) %collective-permute-start.12) | collective-permute-done | bytes 229408 | tf_op jit(solution)/shard_map/ppermute | solution.py:477
  66.2 0.7 copy-done.6
  66.9 4.0 %shard_map.132 = (f32[1,8192]{1,0:T(1,128)}, f32[640,128]{1,0:T(8,128)}, f32[640,128]{1,0:T(8,128)}, f32[640,128]{1,0:T(8,128)}) custom-call(s32[17]{0:T(128)} %refs_0_.7, s32[17]{0:T(128)} %refs_1_.5, s32[8192]{0:T(1024)} %refs_2_.3, s32[1,8192]{1,0:T(1,128)} %get-tuple-element.65.refs_3_, bf16[16,56,128]{2,1,0:T(8,128)(2,1)} %copy-done.2, ...), custom_call_target="tpu_custom_call" | custom-call | bytes 12000000 | tf_op jit(solution)/shard_map/pallas_call | solution.py:284
  (28 shorter events, 0.4 us)
Async XLA Ops:
  1.5 11.2 %collective-permute-start.1 = (bf16[1,256,128]{2,1,0:T(8,128)(2,1)S(1)}, bf16[1,256,128]{2,1,0:T(8,128)(2,1)S(1)}, u32[]{:S(2)}, u32[]{:S(2)}) collective-permute-start(bf16[1,256,128]{2,1,0:T(8,128)(2,1)S(1)} %dynamic-slice_bitcast_fusion), channel_id=1, source_target_pairs={{0,16},{1,17},{2,18},{3,19},{4,20},{5,21},{6,22},{7,23},{8,24},{9,... | collective-permute-start | bytes 196616 | tf_op jit(solution)/shard_map/ppermute | solution.py:340
  12.7 8.8 %copy-start.1 = (f32[8,256,128]{2,1,0:T(8,128)S(1)}, f32[8,256,128]{2,1,0:T(8,128)}, u32[]{:S(2)}) copy-start(f32[8,256,128]{2,1,0:T(8,128)} %get-tuple-element.38) | copy-start | bytes 3145732
  12.7 2.2 %collective-permute-start.2 = (bf16[8,256,128]{2,1,0:T(8,128)(2,1)}, bf16[8,256,128]{2,1,0:T(8,128)(2,1)S(1)}, u32[]{:S(2)}, u32[]{:S(2)}) collective-permute-start(bf16[8,256,128]{2,1,0:T(8,128)(2,1)} %bitcast.13), channel_id=1, source_target_pairs={{0,1},{1,0},{2,3},{3,2},{4,5},{5,4},{6,7},{7,6},{8,9},{9,8},{10,11... | collective-permute-start | bytes 1572872 | tf_op jit(solution)/shard_map/ppermute | solution.py:400
  12.8 8.7 %collective-permute-start = (bf16[8,256,128]{2,1,0:T(8,128)(2,1)}, bf16[8,256,128]{2,1,0:T(8,128)(2,1)S(1)}, u32[]{:S(2)}, u32[]{:S(2)}) collective-permute-start(bf16[8,256,128]{2,1,0:T(8,128)(2,1)} %bitcast.12), channel_id=1, source_target_pairs={{0,1},{1,0},{2,3},{3,2},{4,5},{5,4},{6,7},{7,6},{8,9},{9,8},{10,11... | collective-permute-start | bytes 1572872 | tf_op jit(solution)/shard_map/ppermute | solution.py:401
  13.3 5.0 %collective-permute-start.3 = (bf16[2,256,128]{2,1,0:T(8,128)(2,1)S(1)}, bf16[2,256,128]{2,1,0:T(8,128)(2,1)S(1)}, u32[]{:S(2)}, u32[]{:S(2)}) collective-permute-start(bf16[2,256,128]{2,1,0:T(8,128)(2,1)S(1)} %pad_maximum_fusion.2), channel_id=1, source_target_pairs={{0,2},{1,9},{2,0},{3,11},{4,6},{5,13},{6,4},{7,15},{8,10},{9,1},{1... | collective-permute-start | bytes 393224 | tf_op jit(solution)/shard_map/ppermute | solution.py:340
  18.3 9.2 %collective-permute-start.4 = (bf16[8,256,128]{2,1,0:T(8,128)(2,1)S(1)}, bf16[8,256,128]{2,1,0:T(8,128)(2,1)S(1)}, u32[]{:S(2)}, u32[]{:S(2)}) collective-permute-start(bf16[8,256,128]{2,1,0:T(8,128)(2,1)S(1)} %add_convert_fusion), channel_id=1, source_target_pairs={{0,2},{1,9},{2,0},{3,11},{4,6},{5,13},{6,4},{7,15},{8,10},{9,1},{1... | collective-permute-start | bytes 1572872 | tf_op jit(solution)/shard_map/ppermute | solution.py:340
  19.9 7.3 %collective-permute-start.5 = (bf16[4,256,128]{2,1,0:T(8,128)(2,1)S(1)}, bf16[4,256,128]{2,1,0:T(8,128)(2,1)S(1)}, u32[]{:S(2)}, u32[]{:S(2)}) collective-permute-start(bf16[4,256,128]{2,1,0:T(8,128)(2,1)S(1)} %pad_maximum_fusion.1), channel_id=1, source_target_pairs={{0,4},{1,5},{2,6},{3,7},{4,0},{5,1},{6,2},{7,3},{8,12},{9,13},{10,... | collective-permute-start | bytes 786440 | tf_op jit(solution)/shard_map/ppermute | solution.py:340
  27.6 20.9 %copy-start = (bf16[8,256,128]{2,1,0:T(8,128)(2,1)}, bf16[8,256,128]{2,1,0:T(8,128)(2,1)S(1)}, u32[]{:S(2)}) copy-start(bf16[8,256,128]{2,1,0:T(8,128)(2,1)S(1)} %pad_maximum_fusion.refs_5_) | copy-start | bytes 1572868
  27.7 9.2 %collective-permute-start.7 = (bf16[8,256,128]{2,1,0:T(8,128)(2,1)S(1)}, bf16[8,256,128]{2,1,0:T(8,128)(2,1)S(1)}, u32[]{:S(2)}, u32[]{:S(2)}) collective-permute-start(bf16[8,256,128]{2,1,0:T(8,128)(2,1)S(1)} %pad_maximum_fusion.refs_5_), channel_id=1, source_target_pairs={{0,8},{1,3},{2,10},{3,1},{4,12},{5,7},{6,14},{7,5},{8,0},{9,11},{1... | collective-permute-start | bytes 1572872 | tf_op jit(solution)/shard_map/ppermute | solution.py:340
  29.4 6.7 %collective-permute-start.6 = (bf16[4,256,128]{2,1,0:T(8,128)(2,1)S(1)}, bf16[4,256,128]{2,1,0:T(8,128)(2,1)S(1)}, u32[]{:S(2)}, u32[]{:S(2)}) collective-permute-start(bf16[4,256,128]{2,1,0:T(8,128)(2,1)S(1)} %get-tuple-element.47), channel_id=1, source_target_pairs={{0,4},{1,5},{2,6},{3,7},{4,0},{5,1},{6,2},{7,3},{8,12},{9,13},{10,... | collective-permute-start | bytes 786440 | tf_op jit(solution)/shard_map/ppermute | solution.py:340
  31.0 11.3 %collective-permute-start.10 = (bf16[8,256,128]{2,1,0:T(8,128)(2,1)S(1)}, bf16[8,256,128]{2,1,0:T(8,128)(2,1)S(1)}, u32[]{:S(2)}, u32[]{:S(2)}) collective-permute-start(bf16[8,256,128]{2,1,0:T(8,128)(2,1)S(1)} %pad_maximum_fusion.refs_5_), channel_id=1, source_target_pairs={{0,1},{1,0},{2,3},{3,2},{4,5},{5,4},{6,7},{7,6},{8,9},{9,8},{10,11... | collective-permute-start | bytes 1572872 | tf_op jit(solution)/shard_map/ppermute | solution.py:419
  36.9 19.5 %copy-start.3 = (bf16[8,256,128]{2,1,0:T(8,128)(2,1)}, bf16[8,256,128]{2,1,0:T(8,128)(2,1)S(1)}, u32[]{:S(2)}) copy-start(bf16[8,256,128]{2,1,0:T(8,128)(2,1)S(1)} %collective-permute-done.7.refs_6_) | copy-start | bytes 1572868
  36.9 10.9 %collective-permute-start.11 = (bf16[8,256,128]{2,1,0:T(8,128)(2,1)S(1)}, bf16[8,256,128]{2,1,0:T(8,128)(2,1)S(1)}, u32[]{:S(2)}, u32[]{:S(2)}) collective-permute-start(bf16[8,256,128]{2,1,0:T(8,128)(2,1)S(1)} %collective-permute-done.7.refs_6_), channel_id=1, source_target_pairs={{0,1},{1,0},{2,3},{3,2},{4,5},{5,4},{6,7},{7,6},{8,9},{9,8},{10,11... | collective-permute-start | bytes 1572872 | tf_op jit(solution)/shard_map/ppermute | solution.py:419
  37.1 5.0 %collective-permute-start.8 = (bf16[2,256,128]{2,1,0:T(8,128)(2,1)S(1)}, bf16[2,256,128]{2,1,0:T(8,128)(2,1)S(1)}, u32[]{:S(2)}, u32[]{:S(2)}) collective-permute-start(bf16[2,256,128]{2,1,0:T(8,128)(2,1)S(1)} %get-tuple-element.74), channel_id=1, source_target_pairs={{0,8},{1,3},{2,10},{3,1},{4,12},{5,7},{6,14},{7,5},{8,0},{9,11},{1... | collective-permute-start | bytes 393224 | tf_op jit(solution)/shard_map/ppermute | solution.py:340
  42.2 5.6 %collective-permute-start.9 = (bf16[1,256,128]{2,1,0:T(8,128)(2,1)S(1)}, bf16[1,256,128]{2,1,0:T(8,128)(2,1)S(1)}, u32[]{:S(2)}, u32[]{:S(2)}) collective-permute-start(bf16[1,256,128]{2,1,0:T(8,128)(2,1)S(1)} %fusion.2), channel_id=1, source_target_pairs={{0,16},{1,17},{2,18},{3,19},{4,20},{5,21},{6,22},{7,23},{8,24},{9,... | collective-permute-start | bytes 196616 | tf_op jit(solution)/shard_map/ppermute | solution.py:340
  42.3 14.1 %copy-start.4 = (bf16[8,256,128]{2,1,0:T(8,128)(2,1)}, bf16[8,256,128]{2,1,0:T(8,128)(2,1)S(1)}, u32[]{:S(2)}) copy-start(bf16[8,256,128]{2,1,0:T(8,128)(2,1)S(1)} %collective-permute-done.10.refs_7_) | copy-start | bytes 1572868
  47.8 8.6 %copy-start.5 = (bf16[8,256,128]{2,1,0:T(8,128)(2,1)}, bf16[8,256,128]{2,1,0:T(8,128)(2,1)S(1)}, u32[]{:S(2)}) copy-start(bf16[8,256,128]{2,1,0:T(8,128)(2,1)S(1)} %collective-permute-done.11.refs_8_) | copy-start | bytes 1572868
  51.5 13.2 %all-to-all-start = ((bf16[16,56,128]{2,1,0:T(8,128)(2,1)}), bf16[16,56,128]{2,1,0:T(8,128)(2,1)S(1)}, u32[]{:S(2)}, u32[]{:S(2)}) async-start(bf16[16,56,128]{2,1,0:T(8,128)(2,1)} %shard_map.130), calls=%async_computation | async-start | bytes 458752 | tf_op jit(solution)/shard_map/all_to_all | solution.py:474
  64.7 1.5 %copy-start.2 = (bf16[16,56,128]{2,1,0:T(8,128)(2,1)}, bf16[16,56,128]{2,1,0:T(8,128)(2,1)S(1)}, u32[]{:S(2)}) copy-start(bf16[16,56,128]{2,1,0:T(8,128)(2,1)S(1)} %all-to-all-done.refs_4_) | copy-start | bytes 688132
  64.7 1.5 %collective-permute-start.12 = (bf16[16,56,128]{2,1,0:T(8,128)(2,1)S(1)}, bf16[16,56,128]{2,1,0:T(8,128)(2,1)S(1)}, u32[]{:S(2)}, u32[]{:S(2)}) collective-permute-start(bf16[16,56,128]{2,1,0:T(8,128)(2,1)S(1)} %all-to-all-done.refs_4_), channel_id=1, source_target_pairs={{0,1},{1,0},{2,3},{3,2},{4,5},{5,4},{6,7},{7,6},{8,9},{9,8},{10,11... | collective-permute-start | bytes 688136 | tf_op jit(solution)/shard_map/ppermute | solution.py:477
  66.2 0.7 copy-start.6

commit v5 on v4

--- a/solution.py
+++ b/solution.py
@@ -150,10 +150,11 @@
     return holder
 
 
-def index_kernel(dp_count, cap, slots, table_rows, ob, nb, src, gain, units, chosen, keep, own_gain, places, rows, gains):
+def index_kernel(dp_count, cap, slots, table_rows, ob, nb, src, gain, units, chosen, keep, own_gain, places, offset, rows, gains):
     me = lax.axis_index("dp")
     mine = ob[me]
     groups = cap // LANES
+    offset[0] = offset_of(src, ob, nb, me, dp_count)
     rows[...] = jnp.full(rows.shape, -1, jnp.int32)
     for q in range(dp_count):
         start = nb[q] + ((me - offset_of(src, ob, nb, q, dp_count)) & (dp_count - 1))
@@ -194,14 +195,15 @@
         places[:, first : first + step] = holder * (table_rows * LANES) + dest * slots + rank
 
 
-def pack_kernel(dp_count, slots, table_rows, staged, chosen, keep, own_gain, reduced, weight_in, first_in, second_in, out):
+def pack_kernel(dp_count, slots, table_rows, staged, chosen, keep, own_gain, *rest):
+    *reduced, weight_in, first_in, second_in, out = rest
     pairs = dp_count * slots
     rows = weight_in.shape[0]
     weight, first, second = weight_in[...].astype(F32), first_in[...], second_in[...]
     if staged:
         turn = LANES // 2
         lower = lower_half(rows)
-        grad = reduced[0]
+        grad = reduced[0][0] + reduced[1][0].astype(F32)
         grad = jnp.concatenate([grad, pltpu.roll(grad, turn, 1)], axis=0)
         left = lax.axis_index("rep") == 0
         weight, first, second = [
@@ -209,15 +211,15 @@
         ]
         product = jnp.where(lower, weight * grad, 0.0)
     else:
-        grad = reduced[...]
+        grad = reduced[0][...]
         product = weight * grad
     high, low = split(product)
     ones = jnp.ones((8, LANES), BF16)
     column = (dot(ones, high, (1, 1)) + dot(ones, low, (1, 1))) * own_gain[...]
-    high, low = split(column)
+    picked = dot(jnp.concatenate(split(column), axis=0), chosen[...], (1, 1))
     table = []
-    for part in (high, low):
-        part = dot(part, chosen[...], (1, 1))[0:1] * keep[...]
+    for part in (picked[0:1], picked[8:9]):
+        part = part * keep[...]
         table += [part[:, r * LANES : (r + 1) * LANES] for r in range(table_rows)]
     updated = [0.9 * first + 0.1 * grad, 0.95 * second + 0.05 * grad * grad]
     if staged:
@@ -233,11 +235,11 @@
         out[q, filled:, :] = table
 
 
-def finish_kernel(dp_count, slots, table_rows, staged, ob, nb, src, places, *rest):
+def finish_kernel(dp_count, slots, table_rows, staged, nb, offset_in, places, *rest):
     arrived, rest = (rest[:2], rest[2:]) if staged else (rest[:1], rest[1:])
     gain_grad, first, second, adam, ones, twos, table = rest
     me = lax.axis_index("dp")
-    offset = offset_of(src, ob, nb, me, dp_count)
+    offset = offset_in[0]
     groups = 1 if staged else 2
     pages = [(moved, 0) for moved in arrived] if staged else [(arrived[0], 0), (arrived[0], slots)]
     for i in range(dp_count):
@@ -270,22 +272,28 @@
         ]
         table[here : here + table_rows, :] = sum(terms[1:], terms[0])
     high, low = split(table[...])
-    values = jnp.concatenate([high, low], axis=1)
+    values = jnp.concatenate([high.astype(F32).T, low.astype(F32).T], axis=0).astype(BF16)
     step = 1024
     for start in range(0, D_NEW, step):
         slot = places[:, start : start + step]
-        spread = dot(values, one_hot(values.shape[0], slot >> 7), (0, 0))
+        spread = dot(values, one_hot(values.shape[1], slot >> 7), (1, 0))
         mask = lax.broadcasted_iota(jnp.int32, (LANES, step), 0) == (slot & 127)
         value = jnp.where(mask, spread[:LANES] + spread[LANES:], 0.0)
         gain_grad[:, start : start + step] = jnp.sum(value, axis=0, keepdims=True)
 
 
+def resident(value):
+    return pltpu.with_memory_space_constraint(value, pltpu.VMEM)
+
+
 def call(kernel, micros, out_shape, specs, scratch, *args):
+    scalars = jax.ShapeDtypeStruct((1,), jnp.int32)
+    out_specs = jax.tree.map(lambda out: SMEM_SPEC if out == scalars else VMEM_SPEC, out_shape)
     return pl.pallas_call(
         kernel,
         out_shape=out_shape,
         in_specs=specs,
-        out_specs=jax.tree.map(lambda _: VMEM_SPEC, out_shape),
+        out_specs=out_specs,
         scratch_shapes=scratch,
         cost_estimate=pl.CostEstimate(flops=0, transcendentals=0, bytes_accessed=micros * BYTES_PER_US),
         compiler_params=pltpu.CompilerParams(vmem_limit_bytes=VMEM_LIMIT),
@@ -354,8 +362,8 @@
         (
             shape((tiles, LANES), F32),
             shape((tokens, LANES), F32),
-            *[shape((dp_count // parts, part, LANES), F32)] * parts,
-            *[shape((rep_count - 1, dp_count // parts, part, LANES), BF16)] * parts,
+            *[pltpu.VMEM((dp_count // parts, part, LANES), F32)] * parts,
+            *[pltpu.VMEM((rep_count - 1, dp_count // parts, part, LANES), BF16)] * parts,
         ),
         [SMEM_SPEC] + [VMEM_SPEC] * 2 + [any_spec] + [VMEM_SPEC],
         [
@@ -376,10 +384,11 @@
             lambda *refs: index_kernel(dp_count, cap, slots, table_rows, *refs),
             5,
             (
-                shape((table_rows * LANES, cap), BF16),
-                shape((1, table_rows * LANES), F32),
-                shape((1, cap), F32),
-                shape((1, D_NEW), jnp.int32),
+                pltpu.VMEM((table_rows * LANES, cap), BF16),
+                pltpu.VMEM((1, table_rows * LANES), F32),
+                pltpu.VMEM((1, cap), F32),
+                pltpu.VMEM((1, D_NEW), jnp.int32),
+                shape((1,), jnp.int32),
             ),
             [SMEM_SPEC] * 3 + [VMEM_SPEC] * 2,
             [pltpu.VMEM((table_rows * LANES, LANES), jnp.int32), pltpu.VMEM((D_OLD // LANES + 8, LANES), F32)],
@@ -413,12 +422,12 @@
             low, high = low[:half] + came[:half], (low[half:] + came[half:]).astype(BF16)
             if stage == 0:
                 high, late_units = lax.optimization_barrier((high, units))
-                chosen, keep, own_gain, places = indices(late_units)
+                chosen, keep, own_gain, places, offset = indices(late_units)
         came = across(high, halving, bits - 1)
         pieces = [gathered, sent]
         pieces += [lax.ppermute(piece, "rep", swap) for piece in pieces]
         came, *pieces = lax.optimization_barrier((came, *pieces))
-        grad_own = low + came.astype(F32)
+        reduced = [resident(low), resident(came)]
         projected = call(
             lambda *refs: project_kernel(dp_count, doubling, cap, *refs),
             6,
@@ -439,8 +448,8 @@
             chip = chip + lax.ppermute(others[0][away - 1], "rep", ring).astype(F32)
         blocks = lax.all_to_all(chip.astype(BF16), "dp", split_axis=0, concat_axis=0)
         grad_part = jnp.sum(blocks.astype(F32), axis=0)
-        grad_own = lax.all_gather(grad_part, "rep", axis=0, tiled=True)
-        chosen, keep, own_gain, places = indices(units)
+        reduced = [lax.all_gather(grad_part, "rep", axis=0, tiled=True)]
+        chosen, keep, own_gain, places, offset = indices(units)
         projected = call(
             lambda *refs: project_gathered_kernel(dp_count, cap, *refs),
             6,
@@ -460,33 +469,29 @@
     packed = call(
         lambda *refs: pack_kernel(dp_count, slots, table_rows, staged, *refs),
         3,
-        shape((dp_count, message, LANES), BF16),
-        [VMEM_SPEC] * 7,
+        pltpu.VMEM((dp_count, message, LANES), BF16),
+        [VMEM_SPEC] * (6 + len(reduced)),
         [],
-        chosen,
-        keep,
-        own_gain,
-        grad_own,
-        weight_old,
-        moment_first,
-        moment_second,
+        *[resident(value) for value in (chosen, keep, own_gain)],
+        *reduced,
+        *[resident(value) for value in (weight_old, moment_first, moment_second)],
     )
     moved = [lax.all_to_all(packed, "dp", split_axis=0, concat_axis=0)]
     if staged:
         arrived, projected = lax.optimization_barrier((moved[0], projected))
         moved = [arrived, lax.ppermute(arrived, "rep", swap)]
+        moved = [resident(value) for value in moved]
     rows = shape((new_cap, LANES), F32)
     gain_grad, first_next, second_next, adam_step = call(
         lambda *refs: finish_kernel(dp_count, slots, table_rows, staged, *refs),
         4,
         (shape((1, D_NEW), F32), rows, rows, rows),
-        [SMEM_SPEC] * 3 + [VMEM_SPEC] * (1 + len(moved)),
+        [SMEM_SPEC] * 2 + [VMEM_SPEC] * (1 + len(moved)),
         [pltpu.VMEM((dp_count * slots, LANES), F32)] * 2
         + [pltpu.VMEM((dp_count * table_rows, LANES), F32)],
-        old_bounds,
         new_bounds,
-        source_map,
-        places,
+        offset,
+        resident(places),
         *moved,
     )
     return (projected, gain_grad.reshape(D_NEW), first_next, second_next, adam_step)

time: 71.5 us -> 67.7 us (0.947)
  Pallas kernels: 24 us -> 21.6 us
  other arithmetic: 2.6 us -> 0.62 us
  waiting for transfers between devices: 22.7 us -> 24.1 us
    pallas_call x5, Pallas kernels: 24 us -> 21.6 us  [call(): pl.pallas_call(kernel, out_shape=out_shape, in_specs=specs, out_specs=out...]
    ppermute x8, waiting for transfers between devices: 18.3 us -> 19.7 us  [across(): return lax.ppermute(value, ('dp', 'rep'), pairs)]
    convert_element_type x1, other arithmetic: 1.33 us -> 0.11 us  [on_device(): high = (owns[1] + lax.ppermute(send, 'rep', swap).astype(F32)).astype(BF16)]
    add x1 -> x0, other arithmetic: 0.73 us -> none  [on_device(): grad_own = low + came.astype(F32)]
  transfers between devices with their start and end apart: 14 -> 14, of which waited for: 9 -> 9; matrix products, arithmetic and copies ran while one was open for 2% -> 1% of each run, Pallas kernels for 24% -> 24%
where the time goes in v5:
time: 67.7 us; the launch traced here: 67.2 us
  waiting for transfers between devices  24.1 us (36%)
  Pallas kernels  21.6 us (32%)
  starting transfers between devices  19.1 us (28%)
  local copies, waits for them, and re-layouts  0.88 us (1%)
  between operations  0.86 us (1%)
    pallas_call x5, Pallas kernels, call(): pl.pallas_call(kernel, out_shape=out_shape, in_specs=specs, out_specs=out...  21.6 us
    ppermute x8, waiting for transfers between devices, across(): return lax.ppermute(value, ('dp', 'rep'), pairs)  19.7 us
    ppermute x8, starting transfers between devices, across(): return lax.ppermute(value, ('dp', 'rep'), pairs)  13.6 us
    all_to_all x1, starting transfers between devices, on_device(): moved = [lax.all_to_all(packed, 'dp', split_axis=0, concat_axis=0)]  4.89 us
    all_to_all x1, waiting for transfers between devices, on_device(): moved = [lax.all_to_all(packed, 'dp', split_axis=0, concat_axis=0)]  2.89 us
    ppermute x1, waiting for transfers between devices, on_device(): moved = [arrived, lax.ppermute(arrived, 'rep', swap)]  1.49 us
  transfers between devices with their start and end apart: 14, of which 9 were waited for; matrix products, arithmetic and copies ran while one was open for 1% of the time, Pallas kernels for 24%

profile of v5, /device:TPU:0, one launch (start us, length us, event | category | flops | bytes accessed | tf_op | source)
XLA Modules:
  0.0 67.2 jit_solution(7907264773745207692)
XLA Ops:
  0.6 0.8 %dynamic-slice_bitcast_fusion = bf16[1,256,128]{2,1,0:T(8,128)(2,1)S(1)} fusion(bf16[512,128]{1,0:T(8,128)(2,1)} %refs_5_.1, s32[]{:T(128)S(6)} %select_n.3), kind=kLoop, calls=%fused_computation.14 | loop fusion | bytes 131076 | tf_op jit(solution)/shard_map/broadcast_in_dim | solution.py:353
  1.5 4.0 %collective-permute-start.1 = (bf16[1,256,128]{2,1,0:T(8,128)(2,1)S(1)}, bf16[1,256,128]{2,1,0:T(8,128)(2,1)S(1)}, u32[]{:S(2)}, u32[]{:S(2)}) collective-permute-start(bf16[1,256,128]{2,1,0:T(8,128)(2,1)S(1)} %dynamic-slice_bitcast_fusion), channel_id=1, source_target_pairs={{0,16},{1,17},{2,18},{3,19},{4,20},{5,21},{6,22},{7,23},{8,24},{9,... | collective-permute-start | bytes 196616 | tf_op jit(solution)/shard_map/ppermute | solution.py:348
  5.5 6.5 %shard_map.128 = (f32[48,128]{1,0:T(8,128)}, f32[256,128]{1,0:T(8,128)}, f32[8,256,128]{2,1,0:T(8,128)S(1)}, f32[8,256,128]{2,1,0:T(8,128)S(1)}, bf16[1,8,256,12...) custom-call(s32[17]{0:T(128)} %refs_0_.6, s32[1,8192]{1,0:T(1,128)} %bitcast.9, f32[48,128]{1,0:T(8,128)} %bitcast.11, ...), custom_call_target="tpu_custom_call" | custom-call | bytes 24000000 | tf_op jit(solution)/shard_map/pallas_call | solution.py:292
  12.0 0.1 collective-permute-start.2
  12.1 0.5 collective-permute-start
  12.6 1.6 %collective-permute-start.3 = (bf16[2,256,128]{2,1,0:T(8,128)(2,1)S(1)}, bf16[2,256,128]{2,1,0:T(8,128)(2,1)S(1)}, u32[]{:S(2)}, u32[]{:S(2)}) collective-permute-start(bf16[2,256,128]{2,1,0:T(8,128)(2,1)S(1)} %pad_maximum_fusion.2), channel_id=1, source_target_pairs={{0,2},{1,9},{2,0},{3,11},{4,6},{5,13},{6,4},{7,15},{8,10},{9,1},{1... | collective-permute-start | bytes 393224 | tf_op jit(solution)/shard_map/ppermute | solution.py:348
  14.2 0.1 add_convert_fusion
  14.3 3.4 %collective-permute-done.3 = bf16[2,256,128]{2,1,0:T(8,128)(2,1)S(1)} collective-permute-done((bf16[2,256,128]{2,1,0:T(8,128)(2,1)S(1)}, bf16[2,256,128]{2,1,0:T(8,128)(2,1)S(1)}, u32[]{:S(2)}, u32[]{:S(2)}) %collective-permute-start.3) | collective-permute-done | bytes 131104 | tf_op jit(solution)/shard_map/ppermute | solution.py:348
  17.6 1.5 %collective-permute-start.4 = (bf16[8,256,128]{2,1,0:T(8,128)(2,1)S(1)}, bf16[8,256,128]{2,1,0:T(8,128)(2,1)S(1)}, u32[]{:S(2)}, u32[]{:S(2)}) collective-permute-start(bf16[8,256,128]{2,1,0:T(8,128)(2,1)S(1)} %add_convert_fusion), channel_id=1, source_target_pairs={{0,2},{1,9},{2,0},{3,11},{4,6},{5,13},{6,4},{7,15},{8,10},{9,1},{1... | collective-permute-start | bytes 1572872 | tf_op jit(solution)/shard_map/ppermute | solution.py:348
  19.2 1.6 %collective-permute-start.5 = (bf16[4,256,128]{2,1,0:T(8,128)(2,1)S(1)}, bf16[4,256,128]{2,1,0:T(8,128)(2,1)S(1)}, u32[]{:S(2)}, u32[]{:S(2)}) collective-permute-start(bf16[4,256,128]{2,1,0:T(8,128)(2,1)S(1)} %pad_maximum_fusion.1), channel_id=1, source_target_pairs={{0,4},{1,5},{2,6},{3,7},{4,0},{5,1},{6,2},{7,3},{8,12},{9,13},{10,... | collective-permute-start | bytes 786440 | tf_op jit(solution)/shard_map/ppermute | solution.py:348
  20.8 0.1 convert_add_fusion
  20.8 5.6 %collective-permute-done.5 = bf16[4,256,128]{2,1,0:T(8,128)(2,1)S(1)} collective-permute-done((bf16[4,256,128]{2,1,0:T(8,128)(2,1)S(1)}, bf16[4,256,128]{2,1,0:T(8,128)(2,1)S(1)}, u32[]{:S(2)}, u32[]{:S(2)}) %collective-permute-start.5) | collective-permute-done | bytes 262176 | tf_op jit(solution)/shard_map/ppermute | solution.py:348
  26.5 0.4 collective-permute-done.4
  26.8 0.1 convert_element_type.30
  27.0 1.6 %collective-permute-start.7 = (bf16[8,256,128]{2,1,0:T(8,128)(2,1)S(1)}, bf16[8,256,128]{2,1,0:T(8,128)(2,1)S(1)}, u32[]{:S(2)}, u32[]{:S(2)}) collective-permute-start(bf16[8,256,128]{2,1,0:T(8,128)(2,1)S(1)} %pad_maximum_fusion.refs_5_), channel_id=1, source_target_pairs={{0,8},{1,3},{2,10},{3,1},{4,12},{5,7},{6,14},{7,5},{8,0},{9,11},{1... | collective-permute-start | bytes 1572872 | tf_op jit(solution)/shard_map/ppermute | solution.py:348
  28.7 0.1 slice_add_fusion
  28.8 1.6 %collective-permute-start.6 = (bf16[4,256,128]{2,1,0:T(8,128)(2,1)S(1)}, bf16[4,256,128]{2,1,0:T(8,128)(2,1)S(1)}, u32[]{:S(2)}, u32[]{:S(2)}) collective-permute-start(bf16[4,256,128]{2,1,0:T(8,128)(2,1)S(1)} %get-tuple-element.48), channel_id=1, source_target_pairs={{0,4},{1,5},{2,6},{3,7},{4,0},{5,1},{6,2},{7,3},{8,12},{9,13},{10,... | collective-permute-start | bytes 786440 | tf_op jit(solution)/shard_map/ppermute | solution.py:348
  30.4 4.4 %shard_map.129 = (bf16[640,512]{1,0:T(8,128)(2,1)S(1)}, f32[1,640]{1,0:T(1,128)S(1)}, f32[1,512]{1,0:T(1,128)S(1)}, s32[1,8192]{1,0:T(1,128)S(1)}, s32[1]{0:T(128)}) custom-call(s32[17]{0:T(128)} %refs_0_.6, s32[17]{0:T(128)} %refs_0_.7, s32[8192]{0:T(1024)} %refs_2_.1, f32[48,128]{1,0:T(8,128)} %bitcast.12, s32[1,8192]{1,0:T(1,128)} %bitcast.10), custom_call_target="tpu_custom_call" | custom-call | bytes 15000000 | tf_op jit(solution)/shard_map/pallas_call | solution.py:292
  34.8 0.7 collective-permute-done.6
  35.5 0.8 %collective-permute-done.7.refs_6_ = bf16[8,256,128]{2,1,0:T(8,128)(2,1)S(1)} collective-permute-done((bf16[8,256,128]{2,1,0:T(8,128)(2,1)S(1)}, bf16[8,256,128]{2,1,0:T(8,128)(2,1)S(1)}, u32[]{:S(2)}, u32[]{:S(2)}) %collective-permute-start.7) | collective-permute-done | bytes 524320 | tf_op jit(solution)/shard_map/ppermute | solution.py:348
  36.3 0.1 collective-permute-start.11
  36.4 0.1 slice_add_fusion.3
  36.4 1.6 %collective-permute-start.8 = (bf16[2,256,128]{2,1,0:T(8,128)(2,1)S(1)}, bf16[2,256,128]{2,1,0:T(8,128)(2,1)S(1)}, u32[]{:S(2)}, u32[]{:S(2)}) collective-permute-start(bf16[2,256,128]{2,1,0:T(8,128)(2,1)S(1)} %get-tuple-element.76), channel_id=1, source_target_pairs={{0,8},{1,3},{2,10},{3,1},{4,12},{5,7},{6,14},{7,5},{8,0},{9,11},{1... | collective-permute-start | bytes 393224 | tf_op jit(solution)/shard_map/ppermute | solution.py:348
  38.1 3.4 %collective-permute-done.8 = bf16[2,256,128]{2,1,0:T(8,128)(2,1)S(1)} collective-permute-done((bf16[2,256,128]{2,1,0:T(8,128)(2,1)S(1)}, bf16[2,256,128]{2,1,0:T(8,128)(2,1)S(1)}, u32[]{:S(2)}, u32[]{:S(2)}) %collective-permute-start.8) | collective-permute-done | bytes 131104 | tf_op jit(solution)/shard_map/ppermute | solution.py:348
  41.5 0.1 collective-permute-start.9
  41.6 5.5 %collective-permute-done.9.refs_4_ = bf16[1,256,128]{2,1,0:T(8,128)(2,1)S(1)} collective-permute-done((bf16[1,256,128]{2,1,0:T(8,128)(2,1)S(1)}, bf16[1,256,128]{2,1,0:T(8,128)(2,1)S(1)}, u32[]{:S(2)}, u32[]{:S(2)}) %collective-permute-start.9) | collective-permute-done | bytes 65568 | tf_op jit(solution)/shard_map/ppermute | solution.py:348
  47.2 1.4 %shard_map.130 = bf16[16,56,128]{2,1,0:T(8,128)(2,1)} custom-call(bf16[640,512]{1,0:T(8,128)(2,1)S(1)} %get-tuple-element.53.refs_0_, f32[1,640]{1,0:T(1,128)S(1)} %get-tuple-element.54.refs_1_, f32[1,512]{1,0:T(1,128)S(1)} %get-tuple-element.55.refs_2_, f32[1,256,128]{2,1,0:T(8,128)S(1)} %get-tuple-element.78.refs_3_, ...), custom_call_target="tpu_custom_call" | custom-call | bytes 9000000 | tf_op jit(solution)/shard_map/pallas_call | solution.py:292
  48.6 4.9 %all-to-all-start = ((bf16[16,56,128]{2,1,0:T(8,128)(2,1)}), bf16[16,56,128]{2,1,0:T(8,128)(2,1)S(1)}, u32[]{:S(2)}, u32[]{:S(2)}) async-start(bf16[16,56,128]{2,1,0:T(8,128)(2,1)} %shard_map.130), calls=%async_computation | async-start | bytes 458752 | tf_op jit(solution)/shard_map/all_to_all | solution.py:479
  53.5 5.4 %shard_map.131 = bf16[256,128]{1,0:T(8,128)(2,1)} custom-call(s32[17]{0:T(128)} %refs_0_.6, bf16[256,6144]{1,0:T(8,128)(2,1)} %refs_1_.3, f32[256,128]{1,0:T(8,128)} %get-tuple-element.59.refs_2_, f32[48,128]{1,0:T(8,128)} %bitcast.13, f32[48,128]{1,0:T(8,128)} %get-tuple-element.60.refs_4_, bf16[8,256,128]{2,1,0:T(8,128)(2,1)} %copy-done.3, ...), custom_call_target="tpu_custom_call" | custom-call | bytes 18000000 | tf_op jit(solution)/shard_map/pallas_call | solution.py:292
  58.9 2.9 %all-to-all-done.refs_3_ = bf16[16,56,128]{2,1,0:T(8,128)(2,1)S(1)} async-done(((bf16[16,56,128]{2,1,0:T(8,128)(2,1)}), bf16[16,56,128]{2,1,0:T(8,128)(2,1)S(1)}, u32[]{:S(2)}, u32[]{:S(2)}) %all-to-all-start) | async-done | bytes 229408 | tf_op jit(solution)/shard_map/all_to_all | solution.py:479
  61.8 1.5 %collective-permute-done.12.refs_4_ = bf16[16,56,128]{2,1,0:T(8,128)(2,1)S(1)} collective-permute-done((bf16[16,56,128]{2,1,0:T(8,128)(2,1)S(1)}, bf16[16,56,128]{2,1,0:T(8,128)(2,1)S(1)}, u32[]{:S(2)}, u32[]{:S(2)}) %collective-permute-start.12) | collective-permute-done | bytes 229408 | tf_op jit(solution)/shard_map/ppermute | solution.py:482
  63.3 3.9 %shard_map.132 = (f32[1,8192]{1,0:T(1,128)}, f32[640,128]{1,0:T(8,128)}, f32[640,128]{1,0:T(8,128)}, f32[640,128]{1,0:T(8,128)}) custom-call(s32[17]{0:T(128)} %refs_0_.7, s32[1]{0:T(128)} %get-tuple-element.66.refs_1_, s32[1,8192]{1,0:T(1,128)S(1)} %get-tuple-element.67.refs_2_, bf16[16,56,128]{2,1,0:T(8,128)(2,1)S(1)} %all-to-all-done.refs_3_, ...), custom_call_target="tpu_custom_call" | custom-call | bytes 12000000 | tf_op jit(solution)/shard_map/pallas_call | solution.py:292
  (27 shorter events, 0.2 us)
Async XLA Ops:
  1.5 10.5 %collective-permute-start.1 = (bf16[1,256,128]{2,1,0:T(8,128)(2,1)S(1)}, bf16[1,256,128]{2,1,0:T(8,128)(2,1)S(1)}, u32[]{:S(2)}, u32[]{:S(2)}) collective-permute-start(bf16[1,256,128]{2,1,0:T(8,128)(2,1)S(1)} %dynamic-slice_bitcast_fusion), channel_id=1, source_target_pairs={{0,16},{1,17},{2,18},{3,19},{4,20},{5,21},{6,22},{7,23},{8,24},{9,... | collective-permute-start | bytes 196616 | tf_op jit(solution)/shard_map/ppermute | solution.py:348
  12.0 2.2 %collective-permute-start.2 = (bf16[8,256,128]{2,1,0:T(8,128)(2,1)S(1)}, bf16[8,256,128]{2,1,0:T(8,128)(2,1)S(1)}, u32[]{:S(2)}, u32[]{:S(2)}) collective-permute-start(bf16[8,256,128]{2,1,0:T(8,128)(2,1)S(1)} %bitcast.8), channel_id=1, source_target_pairs={{0,1},{1,0},{2,3},{3,2},{4,5},{5,4},{6,7},{7,6},{8,9},{9,8},{10,11... | collective-permute-start | bytes 1572872 | tf_op jit(solution)/shard_map/ppermute | solution.py:409
  12.1 8.7 %collective-permute-start = (bf16[8,256,128]{2,1,0:T(8,128)(2,1)S(1)}, bf16[8,256,128]{2,1,0:T(8,128)(2,1)S(1)}, u32[]{:S(2)}, u32[]{:S(2)}) collective-permute-start(bf16[8,256,128]{2,1,0:T(8,128)(2,1)S(1)} %bitcast.7), channel_id=1, source_target_pairs={{0,1},{1,0},{2,3},{3,2},{4,5},{5,4},{6,7},{7,6},{8,9},{9,8},{10,11... | collective-permute-start | bytes 1572872 | tf_op jit(solution)/shard_map/ppermute | solution.py:410
  12.6 5.0 %collective-permute-start.3 = (bf16[2,256,128]{2,1,0:T(8,128)(2,1)S(1)}, bf16[2,256,128]{2,1,0:T(8,128)(2,1)S(1)}, u32[]{:S(2)}, u32[]{:S(2)}) collective-permute-start(bf16[2,256,128]{2,1,0:T(8,128)(2,1)S(1)} %pad_maximum_fusion.2), channel_id=1, source_target_pairs={{0,2},{1,9},{2,0},{3,11},{4,6},{5,13},{6,4},{7,15},{8,10},{9,1},{1... | collective-permute-start | bytes 393224 | tf_op jit(solution)/shard_map/ppermute | solution.py:348
  17.6 9.2 %collective-permute-start.4 = (bf16[8,256,128]{2,1,0:T(8,128)(2,1)S(1)}, bf16[8,256,128]{2,1,0:T(8,128)(2,1)S(1)}, u32[]{:S(2)}, u32[]{:S(2)}) collective-permute-start(bf16[8,256,128]{2,1,0:T(8,128)(2,1)S(1)} %add_convert_fusion), channel_id=1, source_target_pairs={{0,2},{1,9},{2,0},{3,11},{4,6},{5,13},{6,4},{7,15},{8,10},{9,1},{1... | collective-permute-start | bytes 1572872 | tf_op jit(solution)/shard_map/ppermute | solution.py:348
  19.2 7.3 %collective-permute-start.5 = (bf16[4,256,128]{2,1,0:T(8,128)(2,1)S(1)}, bf16[4,256,128]{2,1,0:T(8,128)(2,1)S(1)}, u32[]{:S(2)}, u32[]{:S(2)}) collective-permute-start(bf16[4,256,128]{2,1,0:T(8,128)(2,1)S(1)} %pad_maximum_fusion.1), channel_id=1, source_target_pairs={{0,4},{1,5},{2,6},{3,7},{4,0},{5,1},{6,2},{7,3},{8,12},{9,13},{10,... | collective-permute-start | bytes 786440 | tf_op jit(solution)/shard_map/ppermute | solution.py:348
  27.0 14.6 %copy-start.3 = (bf16[8,256,128]{2,1,0:T(8,128)(2,1)}, bf16[8,256,128]{2,1,0:T(8,128)(2,1)S(1)}, u32[]{:S(2)}) copy-start(bf16[8,256,128]{2,1,0:T(8,128)(2,1)S(1)} %pad_maximum_fusion.refs_5_) | copy-start | bytes 1572868
  27.0 20.2 %copy-start = (bf16[512,128]{1,0:T(8,128)(2,1)S(1)}, bf16[512,128]{1,0:T(8,128)(2,1)}, u32[]{:S(2)}) copy-start(bf16[512,128]{1,0:T(8,128)(2,1)} %refs_5_.1) | copy-start | bytes 393220
  27.0 20.2 %copy-start.1 = (f32[512,128]{1,0:T(8,128)S(1)}, f32[512,128]{1,0:T(8,128)}, u32[]{:S(2)}) copy-start(f32[512,128]{1,0:T(8,128)} %refs_6_.1) | copy-start | bytes 786436
  27.0 20.2 %copy-start.2 = (f32[512,128]{1,0:T(8,128)S(1)}, f32[512,128]{1,0:T(8,128)}, u32[]{:S(2)}) copy-start(f32[512,128]{1,0:T(8,128)} %refs_7_.1) | copy-start | bytes 786436
  27.0 9.2 %collective-permute-start.7 = (bf16[8,256,128]{2,1,0:T(8,128)(2,1)S(1)}, bf16[8,256,128]{2,1,0:T(8,128)(2,1)S(1)}, u32[]{:S(2)}, u32[]{:S(2)}) collective-permute-start(bf16[8,256,128]{2,1,0:T(8,128)(2,1)S(1)} %pad_maximum_fusion.refs_5_), channel_id=1, source_target_pairs={{0,8},{1,3},{2,10},{3,1},{4,12},{5,7},{6,14},{7,5},{8,0},{9,11},{1... | collective-permute-start | bytes 1572872 | tf_op jit(solution)/shard_map/ppermute | solution.py:348
  28.8 6.7 %collective-permute-start.6 = (bf16[4,256,128]{2,1,0:T(8,128)(2,1)S(1)}, bf16[4,256,128]{2,1,0:T(8,128)(2,1)S(1)}, u32[]{:S(2)}, u32[]{:S(2)}) collective-permute-start(bf16[4,256,128]{2,1,0:T(8,128)(2,1)S(1)} %get-tuple-element.48), channel_id=1, source_target_pairs={{0,4},{1,5},{2,6},{3,7},{4,0},{5,1},{6,2},{7,3},{8,12},{9,13},{10,... | collective-permute-start | bytes 786440 | tf_op jit(solution)/shard_map/ppermute | solution.py:348
  30.4 11.3 %collective-permute-start.10 = (bf16[8,256,128]{2,1,0:T(8,128)(2,1)S(1)}, bf16[8,256,128]{2,1,0:T(8,128)(2,1)S(1)}, u32[]{:S(2)}, u32[]{:S(2)}) collective-permute-start(bf16[8,256,128]{2,1,0:T(8,128)(2,1)S(1)} %pad_maximum_fusion.refs_5_), channel_id=1, source_target_pairs={{0,1},{1,0},{2,3},{3,2},{4,5},{5,4},{6,7},{7,6},{8,9},{9,8},{10,11... | collective-permute-start | bytes 1572872 | tf_op jit(solution)/shard_map/ppermute | solution.py:428
  36.3 17.2 %copy-start.4 = (bf16[8,256,128]{2,1,0:T(8,128)(2,1)}, bf16[8,256,128]{2,1,0:T(8,128)(2,1)S(1)}, u32[]{:S(2)}) copy-start(bf16[8,256,128]{2,1,0:T(8,128)(2,1)S(1)} %collective-permute-done.7.refs_6_) | copy-start | bytes 1572868
  36.3 10.9 %collective-permute-start.11 = (bf16[8,256,128]{2,1,0:T(8,128)(2,1)S(1)}, bf16[8,256,128]{2,1,0:T(8,128)(2,1)S(1)}, u32[]{:S(2)}, u32[]{:S(2)}) collective-permute-start(bf16[8,256,128]{2,1,0:T(8,128)(2,1)S(1)} %collective-permute-done.7.refs_6_), channel_id=1, source_target_pairs={{0,1},{1,0},{2,3},{3,2},{4,5},{5,4},{6,7},{7,6},{8,9},{9,8},{10,11... | collective-permute-start | bytes 1572872 | tf_op jit(solution)/shard_map/ppermute | solution.py:428
  36.4 5.0 %collective-permute-start.8 = (bf16[2,256,128]{2,1,0:T(8,128)(2,1)S(1)}, bf16[2,256,128]{2,1,0:T(8,128)(2,1)S(1)}, u32[]{:S(2)}, u32[]{:S(2)}) collective-permute-start(bf16[2,256,128]{2,1,0:T(8,128)(2,1)S(1)} %get-tuple-element.76), channel_id=1, source_target_pairs={{0,8},{1,3},{2,10},{3,1},{4,12},{5,7},{6,14},{7,5},{8,0},{9,11},{1... | collective-permute-start | bytes 393224 | tf_op jit(solution)/shard_map/ppermute | solution.py:348
  41.5 5.6 %collective-permute-start.9 = (bf16[1,256,128]{2,1,0:T(8,128)(2,1)S(1)}, bf16[1,256,128]{2,1,0:T(8,128)(2,1)S(1)}, u32[]{:S(2)}, u32[]{:S(2)}) collective-permute-start(bf16[1,256,128]{2,1,0:T(8,128)(2,1)S(1)} %get-tuple-element.77), channel_id=1, source_target_pairs={{0,16},{1,17},{2,18},{3,19},{4,20},{5,21},{6,22},{7,23},{8,24},{9,... | collective-permute-start | bytes 196616 | tf_op jit(solution)/shard_map/ppermute | solution.py:348
  41.6 11.9 %copy-start.5 = (bf16[8,256,128]{2,1,0:T(8,128)(2,1)}, bf16[8,256,128]{2,1,0:T(8,128)(2,1)S(1)}, u32[]{:S(2)}) copy-start(bf16[8,256,128]{2,1,0:T(8,128)(2,1)S(1)} %collective-permute-done.10.refs_7_) | copy-start | bytes 1572868
  47.2 6.3 %copy-start.6 = (bf16[8,256,128]{2,1,0:T(8,128)(2,1)}, bf16[8,256,128]{2,1,0:T(8,128)(2,1)S(1)}, u32[]{:S(2)}) copy-start(bf16[8,256,128]{2,1,0:T(8,128)(2,1)S(1)} %collective-permute-done.11.refs_8_) | copy-start | bytes 1572868
  48.6 13.2 %all-to-all-start = ((bf16[16,56,128]{2,1,0:T(8,128)(2,1)}), bf16[16,56,128]{2,1,0:T(8,128)(2,1)S(1)}, u32[]{:S(2)}, u32[]{:S(2)}) async-start(bf16[16,56,128]{2,1,0:T(8,128)(2,1)} %shard_map.130), calls=%async_computation | async-start | bytes 458752 | tf_op jit(solution)/shard_map/all_to_all | solution.py:479
  61.8 1.5 %collective-permute-start.12 = (bf16[16,56,128]{2,1,0:T(8,128)(2,1)S(1)}, bf16[16,56,128]{2,1,0:T(8,128)(2,1)S(1)}, u32[]{:S(2)}, u32[]{:S(2)}) collective-permute-start(bf16[16,56,128]{2,1,0:T(8,128)(2,1)S(1)} %all-to-all-done.refs_3_), channel_id=1, source_target_pairs={{0,1},{1,0},{2,3},{3,2},{4,5},{5,4},{6,7},{7,6},{8,9},{9,8},{10,11... | collective-permute-start | bytes 688136 | tf_op jit(solution)/shard_map/ppermute | solution.py:482

commit v6 on v5

--- a/solution.py
+++ b/solution.py
@@ -23,8 +23,8 @@
 
 def one_hot(rows, values):
     lanes = values.shape[1]
-    match = lax.broadcasted_iota(jnp.int32, (rows, lanes), 0) == values
-    return jnp.where(match, 1.0, 0.0).astype(BF16)
+    match = lax.broadcasted_iota(jnp.int32, (rows, lanes), 0).astype(BF16) == values.astype(BF16)
+    return jnp.where(match, jnp.ones((), BF16), jnp.zeros((), BF16))
 
 
 def split(value):
@@ -32,18 +32,17 @@
     return high, (value - high.astype(F32)).astype(BF16)
 
 
-def normed_tile(tile, hidden, inv_rms, gain, hist):
+def normed_tile(tile, hidden, inv_rms, gain):
     stream = hidden[:, tile * LANES : (tile + 1) * LANES].astype(F32)
-    normed = (stream * inv_rms) * gain[tile : tile + 1, :]
-    return jnp.where(hist[tile : tile + 1, :] > 0.5, normed, 0.0).astype(BF16)
+    return ((stream * inv_rms) * gain[tile : tile + 1, :]).astype(BF16)
 
 
 def lower_half(rows):
     return lax.broadcasted_iota(jnp.int32, (rows, LANES), 1) < LANES // 2
 
 
-def token_kernel(rels, rep_count, cap, ob, src, gain, hidden_hbm, cot, hist, inv_out, *rest):
-    *blocks, hidden, own_grads, other_grads, sem = rest
+def token_kernel(rels, rep_count, cap, ob, src, gain, hidden_hbm, cot, live_gain, inv_out, *rest):
+    *blocks, hist, hidden, own_grads, other_grads, sem = rest
     owns, others = blocks[: len(blocks) // 2], blocks[len(blocks) // 2 :]
     copy = pltpu.make_async_copy(hidden_hbm, hidden, sem)
     copy.start()
@@ -57,6 +56,7 @@
         units = src[:, at : at + step]
         total = total + dot(one_hot(tiles, units >> 7), one_hot(LANES, units & 127), (1, 1))
     hist[...] = total
+    live_gain[...] = jnp.where(total > 0.5, gain[...], 0.0)
     copy.wait()
     squares = jnp.zeros((tokens, LANES), F32)
     for tile in range(tiles):
@@ -75,7 +75,7 @@
         columns = jnp.concatenate(sides, axis=1).astype(BF16)
     for tile in range(tiles):
         at = tile * LANES
-        result = dot(normed_tile(tile, hidden, inv_rms, gain, hist), columns, (0, 0))
+        result = dot(normed_tile(tile, hidden, inv_rms, live_gain), columns, (0, 0))
         own_grads[at : at + LANES, :] = result[:, :LANES]
         if staged:
             other_grads[at : at + LANES, :] = result[:, LANES:]
@@ -106,12 +106,12 @@
     return me ^ jnp.where(rep == 0, rels[0][at], rels[1][at])
 
 
-def fill_normed(x, hidden, inv_rms, gain, hist):
+def fill_normed(x, hidden, inv_rms, gain):
     for tile in range(D_OLD // LANES):
-        x[:, tile * LANES : (tile + 1) * LANES] = normed_tile(tile, hidden, inv_rms[...], gain, hist)
-
-
-def project_kernel(dp_count, orders, cap, ob, hidden, inv_rms, gain, hist, *rest):
+        x[:, tile * LANES : (tile + 1) * LANES] = normed_tile(tile, hidden, inv_rms[...], gain)
+
+
+def project_kernel(dp_count, orders, cap, ob, hidden, inv_rms, gain, *rest):
     *pieces, out, dense, x, blocks, sems = rest
     me = lax.axis_index("dp")
     rep = lax.axis_index("rep")
@@ -124,7 +124,7 @@
         copies.append(pltpu.make_async_copy(piece, place, sems.at[at]))
     for copy in copies:
         copy.start()
-    fill_normed(x, hidden, inv_rms, gain, hist)
+    fill_normed(x, hidden, inv_rms, gain)
     for copy in copies:
         copy.wait()
     for p in range(dp_count):
@@ -135,8 +135,8 @@
     out[...] = dot(x[...], dense[0:D_OLD, :].astype(BF16), (1, 0)).astype(BF16)
 
 
-def project_gathered_kernel(dp_count, cap, ob, hidden, inv_rms, gain, hist, weights, out, dense, x):
-    fill_normed(x, hidden, inv_rms, gain, hist)
+def project_gathered_kernel(dp_count, cap, ob, hidden, inv_rms, gain, weights, out, dense, x):
+    fill_normed(x, hidden, inv_rms, gain)
     for p in range(dp_count):
         dense[pl.ds(ob[p], cap), :] = weights[p * cap : (p + 1) * cap, :].astype(F32)
     out[...] = dot(x[...], dense[0:D_OLD, :].astype(BF16), (1, 0)).astype(BF16)
@@ -150,7 +150,7 @@
     return holder
 
 
-def index_kernel(dp_count, cap, slots, table_rows, ob, nb, src, gain, units, chosen, keep, own_gain, places, offset, rows, gains):
+def index_kernel(dp_count, cap, slots, table_rows, ob, nb, src, gain, units, chosen, keep, own_gain, places, tables, offset, rows, gains):
     me = lax.axis_index("dp")
     mine = ob[me]
     groups = cap // LANES
@@ -192,7 +192,10 @@
             dest = jnp.where(past, p, dest)
             begin = jnp.where(past, nb[p], begin)
         rank = (position - begin) >> (dp_count.bit_length() - 1)
-        places[:, first : first + step] = holder * (table_rows * LANES) + dest * slots + rank
+        place = holder * (table_rows * LANES) + dest * slots + rank
+        places[:, first : first + step] = place & 127
+        spread = one_hot(dp_count * table_rows, place >> 7)
+        tables[:, first : first + step] = jnp.concatenate([spread, spread], axis=0)
 
 
 def pack_kernel(dp_count, slots, table_rows, staged, chosen, keep, own_gain, *rest):
@@ -235,7 +238,7 @@
         out[q, filled:, :] = table
 
 
-def finish_kernel(dp_count, slots, table_rows, staged, nb, offset_in, places, *rest):
+def finish_kernel(dp_count, slots, table_rows, staged, nb, offset_in, places, tables, *rest):
     arrived, rest = (rest[:2], rest[2:]) if staged else (rest[:1], rest[1:])
     gain_grad, first, second, adam, ones, twos, table = rest
     me = lax.axis_index("dp")
@@ -272,13 +275,12 @@
         ]
         table[here : here + table_rows, :] = sum(terms[1:], terms[0])
     high, low = split(table[...])
-    values = jnp.concatenate([high.astype(F32).T, low.astype(F32).T], axis=0).astype(BF16)
+    values = jnp.concatenate([high.astype(F32), low.astype(F32)], axis=0).T.astype(BF16)
     step = 1024
     for start in range(0, D_NEW, step):
-        slot = places[:, start : start + step]
-        spread = dot(values, one_hot(values.shape[1], slot >> 7), (1, 0))
-        mask = lax.broadcasted_iota(jnp.int32, (LANES, step), 0) == (slot & 127)
-        value = jnp.where(mask, spread[:LANES] + spread[LANES:], 0.0)
+        spread = dot(values, tables[:, start : start + step], (1, 0))
+        mask = lax.broadcasted_iota(jnp.int32, (LANES, step), 0) == places[:, start : start + step]
+        value = jnp.where(mask, spread, 0.0)
         gain_grad[:, start : start + step] = jnp.sum(value, axis=0, keepdims=True)
 
 
@@ -356,7 +358,7 @@
         weights = lax.all_gather(weight_old, "dp", axis=0, tiled=True)
 
     tiles = D_OLD // LANES
-    hist, inv_rms, *blocks = call(
+    live_gain, inv_rms, *blocks = call(
         lambda *refs: token_kernel(rels, rep_count, cap, *refs),
         8,
         (
@@ -367,6 +369,7 @@
         ),
         [SMEM_SPEC] + [VMEM_SPEC] * 2 + [any_spec] + [VMEM_SPEC],
         [
+            pltpu.VMEM((tiles, LANES), F32),
             pltpu.VMEM((tokens, D_OLD), BF16),
             pltpu.VMEM((D_OLD + cap, LANES), F32),
             pltpu.VMEM((D_OLD + cap, LANES), F32),
@@ -388,6 +391,7 @@
                 pltpu.VMEM((1, table_rows * LANES), F32),
                 pltpu.VMEM((1, cap), F32),
                 pltpu.VMEM((1, D_NEW), jnp.int32),
+                pltpu.VMEM((2 * dp_count * table_rows, D_NEW), BF16),
                 shape((1,), jnp.int32),
             ),
             [SMEM_SPEC] * 3 + [VMEM_SPEC] * 2,
@@ -406,9 +410,9 @@
         send, sent = lax.optimization_barrier((others[1][0], sent))
         gathered = jnp.concatenate([gathered, sent])
         sent = across(gathered, doubling, 1)
-        high = (owns[1] + lax.ppermute(send, "rep", swap).astype(F32)).astype(BF16)
+        pair, gathered = lax.optimization_barrier((lax.ppermute(send, "rep", swap), gathered))
+        high = (owns[1] + pair.astype(F32)).astype(BF16)
         low = owns[0] + lax.ppermute(others[0][0], "rep", swap).astype(F32)
-        high, sent = lax.optimization_barrier((high, sent))
         for stage in range(bits - 1):
             came = across(high, halving, stage)
             if stage < bits - 2:
@@ -422,7 +426,7 @@
             low, high = low[:half] + came[:half], (low[half:] + came[half:]).astype(BF16)
             if stage == 0:
                 high, late_units = lax.optimization_barrier((high, units))
-                chosen, keep, own_gain, places, offset = indices(late_units)
+                chosen, keep, own_gain, places, tables, offset = indices(late_units)
         came = across(high, halving, bits - 1)
         pieces = [gathered, sent]
         pieces += [lax.ppermute(piece, "rep", swap) for piece in pieces]
@@ -432,13 +436,12 @@
             lambda *refs: project_kernel(dp_count, doubling, cap, *refs),
             6,
             project_shape,
-            [SMEM_SPEC] + [VMEM_SPEC] * 4 + [any_spec] * 4,
+            [SMEM_SPEC] + [VMEM_SPEC] * 3 + [any_spec] * 4,
             dense + [pltpu.VMEM((2, dp_count, part, LANES), BF16), pltpu.SemaphoreType.DMA((4,))],
             old_bounds,
             hidden_old,
             inv_rms,
-            gain,
-            hist,
+            live_gain,
             *pieces,
         )
     else:
@@ -449,18 +452,17 @@
         blocks = lax.all_to_all(chip.astype(BF16), "dp", split_axis=0, concat_axis=0)
         grad_part = jnp.sum(blocks.astype(F32), axis=0)
         reduced = [lax.all_gather(grad_part, "rep", axis=0, tiled=True)]
-        chosen, keep, own_gain, places, offset = indices(units)
+        chosen, keep, own_gain, places, tables, offset = indices(units)
         projected = call(
             lambda *refs: project_gathered_kernel(dp_count, cap, *refs),
             6,
             project_shape,
-            [SMEM_SPEC] + [VMEM_SPEC] * 5,
+            [SMEM_SPEC] + [VMEM_SPEC] * 4,
             dense,
             old_bounds,
             hidden_old,
             inv_rms,
-            gain,
-            hist,
+            live_gain,
             weights,
         )
 
@@ -486,12 +488,13 @@
         lambda *refs: finish_kernel(dp_count, slots, table_rows, staged, *refs),
         4,
         (shape((1, D_NEW), F32), rows, rows, rows),
-        [SMEM_SPEC] * 2 + [VMEM_SPEC] * (1 + len(moved)),
+        [SMEM_SPEC] * 2 + [VMEM_SPEC] * (2 + len(moved)),
         [pltpu.VMEM((dp_count * slots, LANES), F32)] * 2
         + [pltpu.VMEM((dp_count * table_rows, LANES), F32)],
         new_bounds,
         offset,
         resident(places),
+        resident(tables),
         *moved,
     )
     return (projected, gain_grad.reshape(D_NEW), first_next, second_next, adam_step)

time: 67.7 us -> 66.6 us (0.984)
  waiting for transfers between devices: 24.1 us -> 22.2 us
  local copies, waits for them, and re-layouts: 0.88 us -> 1.73 us
    ppermute x8, waiting for transfers between devices: 19.7 us -> 17.8 us  [across(): return lax.ppermute(value, ('dp', 'rep'), pairs)]
    unnamed x14 -> x16, local copies, waits for them, and re-layouts: 0.03 us -> 0.84 us
  transfers between devices with their start and end apart: 14 -> 14, of which waited for: 9 -> 8; matrix products, arithmetic and copies ran while one was open for 1% -> 1% of each run, Pallas kernels for 24% -> 25%
where the time goes in v6:
time: 66.6 us; the launch traced here: 66.1 us
  waiting for transfers between devices  22.2 us (33%)
  Pallas kernels  21.6 us (32%)
  starting transfers between devices  19.2 us (29%)
  local copies, waits for them, and re-layouts  1.73 us (3%)
  between operations  0.83 us (1%)
    pallas_call x5, Pallas kernels, call(): pl.pallas_call(kernel, out_shape=out_shape, in_specs=specs, out_specs=out...  21.6 us
    ppermute x8, waiting for transfers between devices, across(): return lax.ppermute(value, ('dp', 'rep'), pairs)  17.8 us
    ppermute x8, starting transfers between devices, across(): return lax.ppermute(value, ('dp', 'rep'), pairs)  13.7 us
    all_to_all x1, starting transfers between devices, on_device(): moved = [lax.all_to_all(packed, 'dp', split_axis=0, concat_axis=0)]  4.89 us
    all_to_all x1, waiting for transfers between devices, on_device(): moved = [lax.all_to_all(packed, 'dp', split_axis=0, concat_axis=0)]  2.92 us
    ppermute x1, waiting for transfers between devices, on_device(): moved = [arrived, lax.ppermute(arrived, 'rep', swap)]  1.49 us
  transfers between devices with their start and end apart: 14, of which 8 were waited for; matrix products, arithmetic and copies ran while one was open for 1% of the time, Pallas kernels for 25%

profile of v6, /device:TPU:0, one launch (start us, length us, event | category | flops | bytes accessed | tf_op | source)
XLA Modules:
  0.0 66.1 jit_solution(17540995942610354834)
XLA Ops:
  0.6 0.8 %dynamic-slice_bitcast_fusion = bf16[1,256,128]{2,1,0:T(8,128)(2,1)S(1)} fusion(bf16[512,128]{1,0:T(8,128)(2,1)} %refs_5_.1, s32[]{:T(128)S(6)} %select_n.3), kind=kLoop, calls=%fused_computation.13 | loop fusion | bytes 131076 | tf_op jit(solution)/shard_map/broadcast_in_dim | solution.py:355
  1.5 4.0 %collective-permute-start.1 = (bf16[1,256,128]{2,1,0:T(8,128)(2,1)S(1)}, bf16[1,256,128]{2,1,0:T(8,128)(2,1)S(1)}, u32[]{:S(2)}, u32[]{:S(2)}) collective-permute-start(bf16[1,256,128]{2,1,0:T(8,128)(2,1)S(1)} %dynamic-slice_bitcast_fusion), channel_id=1, source_target_pairs={{0,16},{1,17},{2,18},{3,19},{4,20},{5,21},{6,22},{7,23},{8,24},{9,... | collective-permute-start | bytes 196616 | tf_op jit(solution)/shard_map/ppermute | solution.py:350
  5.5 6.6 %shard_map.128 = (f32[48,128]{1,0:T(8,128)}, f32[256,128]{1,0:T(8,128)}, f32[8,256,128]{2,1,0:T(8,128)S(1)}, f32[8,256,128]{2,1,0:T(8,128)S(1)}, bf16[1,8,256,12...) custom-call(s32[17]{0:T(128)} %refs_0_.6, s32[1,8192]{1,0:T(1,128)} %bitcast.9, f32[48,128]{1,0:T(8,128)} %bitcast.11, ...), custom_call_target="tpu_custom_call" | custom-call | bytes 24000000 | tf_op jit(solution)/shard_map/pallas_call | solution.py:294
  12.1 0.1 collective-permute-start.2
  12.2 0.5 collective-permute-start
  12.7 1.6 %collective-permute-start.4 = (bf16[2,256,128]{2,1,0:T(8,128)(2,1)S(1)}, bf16[2,256,128]{2,1,0:T(8,128)(2,1)S(1)}, u32[]{:S(2)}, u32[]{:S(2)}) collective-permute-start(bf16[2,256,128]{2,1,0:T(8,128)(2,1)S(1)} %pad_maximum_fusion.1), channel_id=1, source_target_pairs={{0,2},{1,9},{2,0},{3,11},{4,6},{5,13},{6,4},{7,15},{8,10},{9,1},{1... | collective-permute-start | bytes 393224 | tf_op jit(solution)/shard_map/ppermute | solution.py:350
  14.3 0.1 add_convert_fusion
  14.4 1.4 %collective-permute-start.3 = (bf16[8,256,128]{2,1,0:T(8,128)(2,1)S(1)}, bf16[8,256,128]{2,1,0:T(8,128)(2,1)S(1)}, u32[]{:S(2)}, u32[]{:S(2)}) collective-permute-start(bf16[8,256,128]{2,1,0:T(8,128)(2,1)S(1)} %add_convert_fusion), channel_id=1, source_target_pairs={{0,2},{1,9},{2,0},{3,11},{4,6},{5,13},{6,4},{7,15},{8,10},{9,1},{1... | collective-permute-start | bytes 1572872 | tf_op jit(solution)/shard_map/ppermute | solution.py:350
  15.8 2.0 %collective-permute-done.4 = bf16[2,256,128]{2,1,0:T(8,128)(2,1)S(1)} collective-permute-done((bf16[2,256,128]{2,1,0:T(8,128)(2,1)S(1)}, bf16[2,256,128]{2,1,0:T(8,128)(2,1)S(1)}, u32[]{:S(2)}, u32[]{:S(2)}) %collective-permute-start.4) | collective-permute-done | bytes 131104 | tf_op jit(solution)/shard_map/ppermute | solution.py:350
  17.8 1.6 %collective-permute-start.5 = (bf16[4,256,128]{2,1,0:T(8,128)(2,1)S(1)}, bf16[4,256,128]{2,1,0:T(8,128)(2,1)S(1)}, u32[]{:S(2)}, u32[]{:S(2)}) collective-permute-start(bf16[4,256,128]{2,1,0:T(8,128)(2,1)S(1)} %pad_maximum_fusion), channel_id=1, source_target_pairs={{0,4},{1,5},{2,6},{3,7},{4,0},{5,1},{6,2},{7,3},{8,12},{9,13},{10,... | collective-permute-start | bytes 786440 | tf_op jit(solution)/shard_map/ppermute | solution.py:350
  19.4 0.1 convert_add_fusion
  19.5 5.8 %collective-permute-done.5 = bf16[4,256,128]{2,1,0:T(8,128)(2,1)S(1)} collective-permute-done((bf16[4,256,128]{2,1,0:T(8,128)(2,1)S(1)}, bf16[4,256,128]{2,1,0:T(8,128)(2,1)S(1)}, u32[]{:S(2)}, u32[]{:S(2)}) %collective-permute-start.5) | collective-permute-done | bytes 262176 | tf_op jit(solution)/shard_map/ppermute | solution.py:350
  25.3 0.1 convert_element_type.30
  25.5 1.6 %collective-permute-start.7 = (bf16[8,256,128]{2,1,0:T(8,128)(2,1)S(1)}, bf16[8,256,128]{2,1,0:T(8,128)(2,1)S(1)}, u32[]{:S(2)}, u32[]{:S(2)}) collective-permute-start(bf16[8,256,128]{2,1,0:T(8,128)(2,1)S(1)} %constant_dynamic-update-slice_fusion.refs_4_), channel_id=1, source_target_pairs={{0,8},{1,3},{2,10},{3,1},{4,12},{5,7},{6,14},{7,5},{8,0},{9,11},{1... | collective-permute-start | bytes 1572872 | tf_op jit(solution)/shard_map/ppermute | solution.py:350
  27.1 0.1 slice_add_fusion
  27.2 1.6 %collective-permute-start.6 = (bf16[4,256,128]{2,1,0:T(8,128)(2,1)S(1)}, bf16[4,256,128]{2,1,0:T(8,128)(2,1)S(1)}, u32[]{:S(2)}, u32[]{:S(2)}) collective-permute-start(bf16[4,256,128]{2,1,0:T(8,128)(2,1)S(1)} %get-tuple-element.49), channel_id=1, source_target_pairs={{0,4},{1,5},{2,6},{3,7},{4,0},{5,1},{6,2},{7,3},{8,12},{9,13},{10,... | collective-permute-start | bytes 786440 | tf_op jit(solution)/shard_map/ppermute | solution.py:350
  28.8 4.6 %shard_map.129 = (bf16[640,512]{1,0:T(8,128)(2,1)S(1)}, f32[1,640]{1,0:T(1,128)S(1)}, f32[1,512]{1,0:T(1,128)S(1)}, s32[1,8192]{1,0:T(1,128)S(1)}, bf16[160,8192]{1,0:T(8,128)(2,1)S(1)}, /*index=5*/s32[1]{0:T(128)}) custom-call(s32[17]{0:T(128)} %refs_0_.6, s32[17]{0:T(128)} %refs_0_.7, s32[8192]{0:T(1024)} %refs_2_.1, f32[48,128]{1,0:T(8,128)} %bitcast.12, ...), custom_call_target="tpu_custom_call" | custom-call | bytes 15000000 | tf_op jit(solution)/shard_map/pallas_call | solution.py:294
  33.4 0.2 collective-permute-done.6
  33.6 1.1 %collective-permute-done.7.refs_5_ = bf16[8,256,128]{2,1,0:T(8,128)(2,1)S(1)} collective-permute-done((bf16[8,256,128]{2,1,0:T(8,128)(2,1)S(1)}, bf16[8,256,128]{2,1,0:T(8,128)(2,1)S(1)}, u32[]{:S(2)}, u32[]{:S(2)}) %collective-permute-start.7) | collective-permute-done | bytes 524320 | tf_op jit(solution)/shard_map/ppermute | solution.py:350
  34.7 0.1 collective-permute-start.11
  34.8 0.1 slice_add_fusion.3
  34.9 1.6 %collective-permute-start.8 = (bf16[2,256,128]{2,1,0:T(8,128)(2,1)S(1)}, bf16[2,256,128]{2,1,0:T(8,128)(2,1)S(1)}, u32[]{:S(2)}, u32[]{:S(2)}) collective-permute-start(bf16[2,256,128]{2,1,0:T(8,128)(2,1)S(1)} %get-tuple-element.78), channel_id=1, source_target_pairs={{0,8},{1,3},{2,10},{3,1},{4,12},{5,7},{6,14},{7,5},{8,0},{9,11},{1... | collective-permute-start | bytes 393224 | tf_op jit(solution)/shard_map/ppermute | solution.py:350
  36.5 3.4 %collective-permute-done.8 = bf16[2,256,128]{2,1,0:T(8,128)(2,1)S(1)} collective-permute-done((bf16[2,256,128]{2,1,0:T(8,128)(2,1)S(1)}, bf16[2,256,128]{2,1,0:T(8,128)(2,1)S(1)}, u32[]{:S(2)}, u32[]{:S(2)}) %collective-permute-start.8) | collective-permute-done | bytes 131104 | tf_op jit(solution)/shard_map/ppermute | solution.py:350
  40.0 0.2 collective-permute-start.9
  40.2 5.4 %collective-permute-done.9.refs_4_ = bf16[1,256,128]{2,1,0:T(8,128)(2,1)S(1)} collective-permute-done((bf16[1,256,128]{2,1,0:T(8,128)(2,1)S(1)}, bf16[1,256,128]{2,1,0:T(8,128)(2,1)S(1)}, u32[]{:S(2)}, u32[]{:S(2)}) %collective-permute-start.9) | collective-permute-done | bytes 65568 | tf_op jit(solution)/shard_map/ppermute | solution.py:350
  45.6 0.8 %copy-done.6 = bf16[8,256,128]{2,1,0:T(8,128)(2,1)} copy-done((bf16[8,256,128]{2,1,0:T(8,128)(2,1)}, bf16[8,256,128]{2,1,0:T(8,128)(2,1)S(1)}, u32[]{:S(2)}) %copy-start.6) | copy-done | bytes 524312
  46.4 1.4 %shard_map.130 = bf16[16,56,128]{2,1,0:T(8,128)(2,1)} custom-call(bf16[640,512]{1,0:T(8,128)(2,1)S(1)} %get-tuple-element.54.refs_0_, f32[1,640]{1,0:T(1,128)S(1)} %get-tuple-element.55.refs_1_, f32[1,512]{1,0:T(1,128)S(1)} %get-tuple-element.56.refs_2_, f32[1,256,128]{2,1,0:T(8,128)S(1)} %get-tuple-element.80.refs_3_, ...), custom_call_target="tpu_custom_call" | custom-call | bytes 9000000 | tf_op jit(solution)/shard_map/pallas_call | solution.py:294
  47.8 4.9 %all-to-all-start = ((bf16[16,56,128]{2,1,0:T(8,128)(2,1)}), bf16[16,56,128]{2,1,0:T(8,128)(2,1)S(1)}, u32[]{:S(2)}, u32[]{:S(2)}) async-start(bf16[16,56,128]{2,1,0:T(8,128)(2,1)} %shard_map.130), calls=%async_computation | async-start | bytes 458752 | tf_op jit(solution)/shard_map/all_to_all | solution.py:481
  52.7 5.4 %shard_map.131 = bf16[256,128]{1,0:T(8,128)(2,1)} custom-call(s32[17]{0:T(128)} %refs_0_.6, bf16[256,6144]{1,0:T(8,128)(2,1)} %refs_1_.3, f32[256,128]{1,0:T(8,128)} %get-tuple-element.60.refs_2_, f32[48,128]{1,0:T(8,128)} %get-tuple-element.61.refs_3_, bf16[8,256,128]{2,1,0:T(8,128)(2,1)} %copy-done.3, bf16[8,256,128]{2,1,0:T(8,128)(2,1)} %copy-done.4, ...), custom_call_target="tpu_custom_call" | custom-call | bytes 18000000 | tf_op jit(solution)/shard_map/pallas_call | solution.py:294
  58.1 2.9 %all-to-all-done.refs_4_ = bf16[16,56,128]{2,1,0:T(8,128)(2,1)S(1)} async-done(((bf16[16,56,128]{2,1,0:T(8,128)(2,1)}), bf16[16,56,128]{2,1,0:T(8,128)(2,1)S(1)}, u32[]{:S(2)}, u32[]{:S(2)}) %all-to-all-start) | async-done | bytes 229408 | tf_op jit(solution)/shard_map/all_to_all | solution.py:481
  61.1 1.5 %collective-permute-done.12.refs_5_ = bf16[16,56,128]{2,1,0:T(8,128)(2,1)S(1)} collective-permute-done((bf16[16,56,128]{2,1,0:T(8,128)(2,1)S(1)}, bf16[16,56,128]{2,1,0:T(8,128)(2,1)S(1)}, u32[]{:S(2)}, u32[]{:S(2)}) %collective-permute-start.12) | collective-permute-done | bytes 229408 | tf_op jit(solution)/shard_map/ppermute | solution.py:484
  62.5 3.6 %shard_map.132 = (f32[1,8192]{1,0:T(1,128)}, f32[640,128]{1,0:T(8,128)}, f32[640,128]{1,0:T(8,128)}, f32[640,128]{1,0:T(8,128)}) custom-call(s32[17]{0:T(128)} %refs_0_.7, s32[1]{0:T(128)} %get-tuple-element.67.refs_1_, s32[1,8192]{1,0:T(1,128)S(1)} %get-tuple-element.68.refs_2_, bf16[160,8192]{1,0:T(8,128)(2,1)S(1)} %get-tuple-element.69.refs_3_, ...), custom_call_target="tpu_custom_call" | custom-call | bytes 12000000 | tf_op jit(solution)/shard_map/pallas_call | solution.py:294
  (29 shorter events, 0.2 us)
Async XLA Ops:
  1.5 10.6 %collective-permute-start.1 = (bf16[1,256,128]{2,1,0:T(8,128)(2,1)S(1)}, bf16[1,256,128]{2,1,0:T(8,128)(2,1)S(1)}, u32[]{:S(2)}, u32[]{:S(2)}) collective-permute-start(bf16[1,256,128]{2,1,0:T(8,128)(2,1)S(1)} %dynamic-slice_bitcast_fusion), channel_id=1, source_target_pairs={{0,16},{1,17},{2,18},{3,19},{4,20},{5,21},{6,22},{7,23},{8,24},{9,... | collective-permute-start | bytes 196616 | tf_op jit(solution)/shard_map/ppermute | solution.py:350
  12.1 2.2 %collective-permute-start.2 = (bf16[8,256,128]{2,1,0:T(8,128)(2,1)S(1)}, bf16[8,256,128]{2,1,0:T(8,128)(2,1)S(1)}, u32[]{:S(2)}, u32[]{:S(2)}) collective-permute-start(bf16[8,256,128]{2,1,0:T(8,128)(2,1)S(1)} %bitcast.8), channel_id=1, source_target_pairs={{0,1},{1,0},{2,3},{3,2},{4,5},{5,4},{6,7},{7,6},{8,9},{9,8},{10,11... | collective-permute-start | bytes 1572872 | tf_op jit(solution)/shard_map/ppermute | solution.py:413
  12.2 7.2 %collective-permute-start = (bf16[8,256,128]{2,1,0:T(8,128)(2,1)S(1)}, bf16[8,256,128]{2,1,0:T(8,128)(2,1)S(1)}, u32[]{:S(2)}, u32[]{:S(2)}) collective-permute-start(bf16[8,256,128]{2,1,0:T(8,128)(2,1)S(1)} %bitcast.7), channel_id=1, source_target_pairs={{0,1},{1,0},{2,3},{3,2},{4,5},{5,4},{6,7},{7,6},{8,9},{9,8},{10,11... | collective-permute-start | bytes 1572872 | tf_op jit(solution)/shard_map/ppermute | solution.py:415
  12.7 5.0 %collective-permute-start.4 = (bf16[2,256,128]{2,1,0:T(8,128)(2,1)S(1)}, bf16[2,256,128]{2,1,0:T(8,128)(2,1)S(1)}, u32[]{:S(2)}, u32[]{:S(2)}) collective-permute-start(bf16[2,256,128]{2,1,0:T(8,128)(2,1)S(1)} %pad_maximum_fusion.1), channel_id=1, source_target_pairs={{0,2},{1,9},{2,0},{3,11},{4,6},{5,13},{6,4},{7,15},{8,10},{9,1},{1... | collective-permute-start | bytes 393224 | tf_op jit(solution)/shard_map/ppermute | solution.py:350
  14.4 10.9 %collective-permute-start.3 = (bf16[8,256,128]{2,1,0:T(8,128)(2,1)S(1)}, bf16[8,256,128]{2,1,0:T(8,128)(2,1)S(1)}, u32[]{:S(2)}, u32[]{:S(2)}) collective-permute-start(bf16[8,256,128]{2,1,0:T(8,128)(2,1)S(1)} %add_convert_fusion), channel_id=1, source_target_pairs={{0,2},{1,9},{2,0},{3,11},{4,6},{5,13},{6,4},{7,15},{8,10},{9,1},{1... | collective-permute-start | bytes 1572872 | tf_op jit(solution)/shard_map/ppermute | solution.py:350
  17.8 7.5 %collective-permute-start.5 = (bf16[4,256,128]{2,1,0:T(8,128)(2,1)S(1)}, bf16[4,256,128]{2,1,0:T(8,128)(2,1)S(1)}, u32[]{:S(2)}, u32[]{:S(2)}) collective-permute-start(bf16[4,256,128]{2,1,0:T(8,128)(2,1)S(1)} %pad_maximum_fusion), channel_id=1, source_target_pairs={{0,4},{1,5},{2,6},{3,7},{4,0},{5,1},{6,2},{7,3},{8,12},{9,13},{10,... | collective-permute-start | bytes 786440 | tf_op jit(solution)/shard_map/ppermute | solution.py:350
  25.4 14.6 %copy-start.3 = (bf16[8,256,128]{2,1,0:T(8,128)(2,1)}, bf16[8,256,128]{2,1,0:T(8,128)(2,1)S(1)}, u32[]{:S(2)}) copy-start(bf16[8,256,128]{2,1,0:T(8,128)(2,1)S(1)} %constant_dynamic-update-slice_fusion.refs_4_) | copy-start | bytes 1572868
  25.4 21.0 %copy-start = (bf16[512,128]{1,0:T(8,128)(2,1)S(1)}, bf16[512,128]{1,0:T(8,128)(2,1)}, u32[]{:S(2)}) copy-start(bf16[512,128]{1,0:T(8,128)(2,1)} %refs_5_.1) | copy-start | bytes 393220
  25.4 21.0 %copy-start.1 = (f32[512,128]{1,0:T(8,128)S(1)}, f32[512,128]{1,0:T(8,128)}, u32[]{:S(2)}) copy-start(f32[512,128]{1,0:T(8,128)} %refs_6_.1) | copy-start | bytes 786436
  25.4 21.0 %copy-start.2 = (f32[512,128]{1,0:T(8,128)S(1)}, f32[512,128]{1,0:T(8,128)}, u32[]{:S(2)}) copy-start(f32[512,128]{1,0:T(8,128)} %refs_7_.1) | copy-start | bytes 786436
  25.5 9.2 %collective-permute-start.7 = (bf16[8,256,128]{2,1,0:T(8,128)(2,1)S(1)}, bf16[8,256,128]{2,1,0:T(8,128)(2,1)S(1)}, u32[]{:S(2)}, u32[]{:S(2)}) collective-permute-start(bf16[8,256,128]{2,1,0:T(8,128)(2,1)S(1)} %constant_dynamic-update-slice_fusion.refs_4_), channel_id=1, source_target_pairs={{0,8},{1,3},{2,10},{3,1},{4,12},{5,7},{6,14},{7,5},{8,0},{9,11},{1... | collective-permute-start | bytes 1572872 | tf_op jit(solution)/shard_map/ppermute | solution.py:350
  27.2 6.4 %collective-permute-start.6 = (bf16[4,256,128]{2,1,0:T(8,128)(2,1)S(1)}, bf16[4,256,128]{2,1,0:T(8,128)(2,1)S(1)}, u32[]{:S(2)}, u32[]{:S(2)}) collective-permute-start(bf16[4,256,128]{2,1,0:T(8,128)(2,1)S(1)} %get-tuple-element.49), channel_id=1, source_target_pairs={{0,4},{1,5},{2,6},{3,7},{4,0},{5,1},{6,2},{7,3},{8,12},{9,13},{10,... | collective-permute-start | bytes 786440 | tf_op jit(solution)/shard_map/ppermute | solution.py:350
  28.8 11.4 %collective-permute-start.10 = (bf16[8,256,128]{2,1,0:T(8,128)(2,1)S(1)}, bf16[8,256,128]{2,1,0:T(8,128)(2,1)S(1)}, u32[]{:S(2)}, u32[]{:S(2)}) collective-permute-start(bf16[8,256,128]{2,1,0:T(8,128)(2,1)S(1)} %constant_dynamic-update-slice_fusion.refs_4_), channel_id=1, source_target_pairs={{0,1},{1,0},{2,3},{3,2},{4,5},{5,4},{6,7},{7,6},{8,9},{9,8},{10,11... | collective-permute-start | bytes 1572872 | tf_op jit(solution)/shard_map/ppermute | solution.py:432
  34.7 10.9 %copy-start.4 = (bf16[8,256,128]{2,1,0:T(8,128)(2,1)}, bf16[8,256,128]{2,1,0:T(8,128)(2,1)S(1)}, u32[]{:S(2)}) copy-start(bf16[8,256,128]{2,1,0:T(8,128)(2,1)S(1)} %collective-permute-done.7.refs_5_) | copy-start | bytes 1572868
  34.7 10.9 %collective-permute-start.11 = (bf16[8,256,128]{2,1,0:T(8,128)(2,1)S(1)}, bf16[8,256,128]{2,1,0:T(8,128)(2,1)S(1)}, u32[]{:S(2)}, u32[]{:S(2)}) collective-permute-start(bf16[8,256,128]{2,1,0:T(8,128)(2,1)S(1)} %collective-permute-done.7.refs_5_), channel_id=1, source_target_pairs={{0,1},{1,0},{2,3},{3,2},{4,5},{5,4},{6,7},{7,6},{8,9},{9,8},{10,11... | collective-permute-start | bytes 1572872 | tf_op jit(solution)/shard_map/ppermute | solution.py:432
  34.9 5.0 %collective-permute-start.8 = (bf16[2,256,128]{2,1,0:T(8,128)(2,1)S(1)}, bf16[2,256,128]{2,1,0:T(8,128)(2,1)S(1)}, u32[]{:S(2)}, u32[]{:S(2)}) collective-permute-start(bf16[2,256,128]{2,1,0:T(8,128)(2,1)S(1)} %get-tuple-element.78), channel_id=1, source_target_pairs={{0,8},{1,3},{2,10},{3,1},{4,12},{5,7},{6,14},{7,5},{8,0},{9,11},{1... | collective-permute-start | bytes 393224 | tf_op jit(solution)/shard_map/ppermute | solution.py:350
  40.0 5.6 %collective-permute-start.9 = (bf16[1,256,128]{2,1,0:T(8,128)(2,1)S(1)}, bf16[1,256,128]{2,1,0:T(8,128)(2,1)S(1)}, u32[]{:S(2)}, u32[]{:S(2)}) collective-permute-start(bf16[1,256,128]{2,1,0:T(8,128)(2,1)S(1)} %get-tuple-element.79), channel_id=1, source_target_pairs={{0,16},{1,17},{2,18},{3,19},{4,20},{5,21},{6,22},{7,23},{8,24},{9,... | collective-permute-start | bytes 196616 | tf_op jit(solution)/shard_map/ppermute | solution.py:350
  40.2 5.4 %copy-start.5 = (bf16[8,256,128]{2,1,0:T(8,128)(2,1)}, bf16[8,256,128]{2,1,0:T(8,128)(2,1)S(1)}, u32[]{:S(2)}) copy-start(bf16[8,256,128]{2,1,0:T(8,128)(2,1)S(1)} %collective-permute-done.10.refs_6_) | copy-start | bytes 1572868
  45.6 0.8 %copy-start.6 = (bf16[8,256,128]{2,1,0:T(8,128)(2,1)}, bf16[8,256,128]{2,1,0:T(8,128)(2,1)S(1)}, u32[]{:S(2)}) copy-start(bf16[8,256,128]{2,1,0:T(8,128)(2,1)S(1)} %collective-permute-done.11.refs_7_) | copy-start | bytes 1572868
  47.8 13.2 %all-to-all-start = ((bf16[16,56,128]{2,1,0:T(8,128)(2,1)}), bf16[16,56,128]{2,1,0:T(8,128)(2,1)S(1)}, u32[]{:S(2)}, u32[]{:S(2)}) async-start(bf16[16,56,128]{2,1,0:T(8,128)(2,1)} %shard_map.130), calls=%async_computation | async-start | bytes 458752 | tf_op jit(solution)/shard_map/all_to_all | solution.py:481
  61.1 1.5 %collective-permute-start.12 = (bf16[16,56,128]{2,1,0:T(8,128)(2,1)S(1)}, bf16[16,56,128]{2,1,0:T(8,128)(2,1)S(1)}, u32[]{:S(2)}, u32[]{:S(2)}) collective-permute-start(bf16[16,56,128]{2,1,0:T(8,128)(2,1)S(1)} %all-to-all-done.refs_4_), channel_id=1, source_target_pairs={{0,1},{1,0},{2,3},{3,2},{4,5},{5,4},{6,7},{7,6},{8,9},{9,8},{10,11... | collective-permute-start | bytes 688136 | tf_op jit(solution)/shard_map/ppermute | solution.py:484

commit v7 on v6

--- a/solution.py
+++ b/solution.py
@@ -150,7 +150,7 @@
     return holder
 
 
-def index_kernel(dp_count, cap, slots, table_rows, ob, nb, src, gain, units, chosen, keep, own_gain, places, tables, offset, rows, gains):
+def index_kernel(dp_count, cap, slots, table_rows, ob, nb, src, gain, chosen, keep, own_gain, offset, rows, gains):
     me = lax.axis_index("dp")
     mine = ob[me]
     groups = cap // LANES
@@ -179,6 +179,9 @@
     earlier = lax.broadcasted_iota(jnp.int32, same.shape, 0) < lax.broadcasted_iota(jnp.int32, same.shape, 1)
     repeated = jnp.max(jnp.where(earlier, same, 0.0), axis=0, keepdims=True)
     keep[...] = jnp.where(repeated < 0.5, 1.0, 0.0)
+
+
+def place_kernel(dp_count, slots, table_rows, ob, nb, units, places, tables):
     step = 1024
     for first in range(0, D_NEW, step):
         source = units[:, first : first + step]
@@ -329,7 +332,7 @@
     staged = rep_count == 2 and dp_count >= 4
     bits = dp_count.bit_length() - 1
     line = list(range(bits - 1))
-    halving = [line + [bits - 1], line[::-1] + [bits - 1]]
+    halving = [line + [bits - 1], line[-1:] + line[:-1] + [bits - 1]]
     doubling = [[bits - 1] + line, [bits - 1] + line[::-1]]
     if staged:
         rels = [
@@ -382,25 +385,22 @@
         cotangent,
     )
     owns, others = blocks[:parts], blocks[parts:]
-    def indices(units):
+    def indices(src):
         return call(
             lambda *refs: index_kernel(dp_count, cap, slots, table_rows, *refs),
-            5,
+            3,
             (
                 pltpu.VMEM((table_rows * LANES, cap), BF16),
                 pltpu.VMEM((1, table_rows * LANES), F32),
                 pltpu.VMEM((1, cap), F32),
-                pltpu.VMEM((1, D_NEW), jnp.int32),
-                pltpu.VMEM((2 * dp_count * table_rows, D_NEW), BF16),
                 shape((1,), jnp.int32),
             ),
-            [SMEM_SPEC] * 3 + [VMEM_SPEC] * 2,
+            [SMEM_SPEC] * 3 + [VMEM_SPEC],
             [pltpu.VMEM((table_rows * LANES, LANES), jnp.int32), pltpu.VMEM((D_OLD // LANES + 8, LANES), F32)],
             old_bounds,
             new_bounds,
-            source_map,
+            src,
             gain,
-            units,
         )
 
     project_shape = shape((tokens, LANES), BF16)
@@ -415,18 +415,19 @@
         low = owns[0] + lax.ppermute(others[0][0], "rep", swap).astype(F32)
         for stage in range(bits - 1):
             came = across(high, halving, stage)
+            came, sent = lax.optimization_barrier((came, sent))
+            if stage == 1:
+                came, chosen = lax.optimization_barrier((came, chosen))
             if stage < bits - 2:
                 gathered = jnp.concatenate([gathered, sent])
                 sent = across(gathered, doubling, stage + 2)
-                came, sent = lax.optimization_barrier((came, sent))
-            if stage == 1:
-                came, chosen = lax.optimization_barrier((came, chosen))
+                came, gathered = lax.optimization_barrier((came, gathered))
+            if stage == 0:
+                gathered, late_src = lax.optimization_barrier((gathered, source_map))
+                chosen, keep, own_gain, offset = indices(late_src)
             came = came.astype(F32)
             half = half // 2
             low, high = low[:half] + came[:half], (low[half:] + came[half:]).astype(BF16)
-            if stage == 0:
-                high, late_units = lax.optimization_barrier((high, units))
-                chosen, keep, own_gain, places, tables, offset = indices(late_units)
         came = across(high, halving, bits - 1)
         pieces = [gathered, sent]
         pieces += [lax.ppermute(piece, "rep", swap) for piece in pieces]
@@ -452,7 +453,7 @@
         blocks = lax.all_to_all(chip.astype(BF16), "dp", split_axis=0, concat_axis=0)
         grad_part = jnp.sum(blocks.astype(F32), axis=0)
         reduced = [lax.all_gather(grad_part, "rep", axis=0, tiled=True)]
-        chosen, keep, own_gain, places, tables, offset = indices(units)
+        chosen, keep, own_gain, offset = indices(source_map)
         projected = call(
             lambda *refs: project_gathered_kernel(dp_count, cap, *refs),
             6,
@@ -478,9 +479,20 @@
         *reduced,
         *[resident(value) for value in (weight_old, moment_first, moment_second)],
     )
+    packed, late_units = lax.optimization_barrier((packed, units))
+    places, tables = call(
+        lambda *refs: place_kernel(dp_count, slots, table_rows, *refs),
+        2,
+        (pltpu.VMEM((1, D_NEW), jnp.int32), pltpu.VMEM((2 * dp_count * table_rows, D_NEW), BF16)),
+        [SMEM_SPEC] * 2 + [VMEM_SPEC],
+        [],
+        old_bounds,
+        new_bounds,
+        late_units,
+    )
     moved = [lax.all_to_all(packed, "dp", split_axis=0, concat_axis=0)]
     if staged:
-        arrived, projected = lax.optimization_barrier((moved[0], projected))
+        arrived, projected, places = lax.optimization_barrier((moved[0], projected, places))
         moved = [arrived, lax.ppermute(arrived, "rep", swap)]
         moved = [resident(value) for value in moved]
     rows = shape((new_cap, LANES), F32)

time: 66.6 us -> 75.3 us (1.13)
  waiting for transfers between devices: 22.2 us -> 34.2 us
  starting transfers between devices: 19.2 us -> 15.1 us
  Pallas kernels: 21.6 us -> 22.4 us
    ppermute x8, waiting for transfers between devices: 17.8 us -> 28.9 us  [across(): return lax.ppermute(value, ('dp', 'rep'), pairs)]
    ppermute x8, starting transfers between devices: 13.7 us -> 10.8 us  [across(): return lax.ppermute(value, ('dp', 'rep'), pairs)]
    ppermute x1, waiting for transfers between devices: 0.01 us -> 1.38 us  [on_device(): lax.ppermute(send, 'rep', swap)]
    all_to_all x1, starting transfers between devices: 4.89 us -> 3.72 us  [on_device(): moved = [lax.all_to_all(packed, 'dp', split_axis=0, concat_axis=0)]]
    pallas_call x5 -> x6, Pallas kernels: 21.6 us -> 22.4 us  [call(): pl.pallas_call(kernel, out_shape=out_shape, in_specs=specs, out_specs=out...]
  transfers between devices with their start and end apart: 14 -> 14, of which waited for: 8 -> 8; matrix products, arithmetic and copies ran while one was open for 1% -> 1% of each run, Pallas kernels for 25% -> 23%
where the time goes in v7:
time: 75.3 us; the launch traced here: 74.8 us
  waiting for transfers between devices  34.2 us (45%)
  Pallas kernels  22.4 us (30%)
  starting transfers between devices  15.1 us (20%)
  local copies, waits for them, and re-layouts  1.74 us (2%)
  between operations  0.82 us (1%)
    ppermute x8, waiting for transfers between devices, across(): return lax.ppermute(value, ('dp', 'rep'), pairs)  28.9 us
    pallas_call x6, Pallas kernels, call(): pl.pallas_call(kernel, out_shape=out_shape, in_specs=specs, out_specs=out...  22.4 us
    ppermute x8, starting transfers between devices, across(): return lax.ppermute(value, ('dp', 'rep'), pairs)  10.8 us
    all_to_all x1, starting transfers between devices, on_device(): moved = [lax.all_to_all(packed, 'dp', split_axis=0, concat_axis=0)]  3.72 us
    all_to_all x1, waiting for transfers between devices, on_device(): moved = [lax.all_to_all(packed, 'dp', split_axis=0, concat_axis=0)]  2.42 us
  transfers between devices with their start and end apart: 14, of which 8 were waited for; matrix products, arithmetic and copies ran while one was open for 1% of the time, Pallas kernels for 23%

profile of v7, /device:TPU:0, one launch (start us, length us, event | category | flops | bytes accessed | tf_op | source)
XLA Modules:
  0.0 74.8 jit_solution(503480489711342041)
XLA Ops:
  0.6 0.8 %dynamic-slice_bitcast_fusion = bf16[1,256,128]{2,1,0:T(8,128)(2,1)S(1)} fusion(bf16[512,128]{1,0:T(8,128)(2,1)} %refs_5_.1, s32[]{:T(128)S(6)} %select_n.3), kind=kLoop, calls=%fused_computation.12 | loop fusion | bytes 131076 | tf_op jit(solution)/shard_map/broadcast_in_dim | solution.py:358
  1.5 4.0 %collective-permute-start.1 = (bf16[1,256,128]{2,1,0:T(8,128)(2,1)S(1)}, bf16[1,256,128]{2,1,0:T(8,128)(2,1)S(1)}, u32[]{:S(2)}, u32[]{:S(2)}) collective-permute-start(bf16[1,256,128]{2,1,0:T(8,128)(2,1)S(1)} %dynamic-slice_bitcast_fusion), channel_id=1, source_target_pairs={{0,16},{1,17},{2,18},{3,19},{4,20},{5,21},{6,22},{7,23},{8,24},{9,... | collective-permute-start | bytes 196616 | tf_op jit(solution)/shard_map/ppermute | solution.py:353
  5.5 6.6 %shard_map.128 = (f32[48,128]{1,0:T(8,128)}, f32[256,128]{1,0:T(8,128)}, f32[8,256,128]{2,1,0:T(8,128)S(1)}, f32[8,256,128]{2,1,0:T(8,128)S(1)}, bf16[1,8,256,12...) custom-call(s32[17]{0:T(128)} %refs_0_.8, s32[1,8192]{1,0:T(1,128)} %bitcast.9, f32[48,128]{1,0:T(8,128)} %bitcast.11, ...), custom_call_target="tpu_custom_call" | custom-call | bytes 24000000 | tf_op jit(solution)/shard_map/pallas_call | solution.py:297
  12.1 0.1 collective-permute-start.2
  12.2 0.5 collective-permute-start
  12.7 1.4 %collective-permute-done.2 = bf16[8,256,128]{2,1,0:T(8,128)(2,1)S(1)} collective-permute-done((bf16[8,256,128]{2,1,0:T(8,128)(2,1)S(1)}, bf16[8,256,128]{2,1,0:T(8,128)(2,1)S(1)}, u32[]{:S(2)}, u32[]{:S(2)}) %collective-permute-start.2) | collective-permute-done | bytes 524320 | tf_op jit(solution)/shard_map/ppermute | solution.py:413
  14.1 0.1 add_convert_fusion
  14.2 1.6 %collective-permute-start.3 = (bf16[8,256,128]{2,1,0:T(8,128)(2,1)S(1)}, bf16[8,256,128]{2,1,0:T(8,128)(2,1)S(1)}, u32[]{:S(2)}, u32[]{:S(2)}) collective-permute-start(bf16[8,256,128]{2,1,0:T(8,128)(2,1)S(1)} %add_convert_fusion), channel_id=1, source_target_pairs={{0,2},{1,9},{2,0},{3,11},{4,6},{5,13},{6,4},{7,15},{8,10},{9,1},{1... | collective-permute-start | bytes 1572872 | tf_op jit(solution)/shard_map/ppermute | solution.py:353
  15.8 0.5 collective-permute-start.4
  16.3 0.1 convert_add_fusion
  16.4 8.4 %collective-permute-done.4 = bf16[2,256,128]{2,1,0:T(8,128)(2,1)S(1)} collective-permute-done((bf16[2,256,128]{2,1,0:T(8,128)(2,1)S(1)}, bf16[2,256,128]{2,1,0:T(8,128)(2,1)S(1)}, u32[]{:S(2)}, u32[]{:S(2)}) %collective-permute-start.4) | collective-permute-done | bytes 131104 | tf_op jit(solution)/shard_map/ppermute | solution.py:353
  24.9 0.1 convert_element_type.30
  25.0 0.1 slice_add_fusion
  25.1 1.6 %collective-permute-start.5 = (bf16[4,256,128]{2,1,0:T(8,128)(2,1)S(1)}, bf16[4,256,128]{2,1,0:T(8,128)(2,1)S(1)}, u32[]{:S(2)}, u32[]{:S(2)}) collective-permute-start(bf16[4,256,128]{2,1,0:T(8,128)(2,1)S(1)} %get-tuple-element.94), channel_id=1, source_target_pairs={{0,4},{1,3},{2,6},{3,1},{4,0},{5,7},{6,2},{7,5},{8,12},{9,11},{10,... | collective-permute-start | bytes 786440 | tf_op jit(solution)/shard_map/ppermute | solution.py:353
  26.7 0.5 collective-permute-start.6
  27.2 6.7 %collective-permute-done.5 = bf16[4,256,128]{2,1,0:T(8,128)(2,1)S(1)} collective-permute-done((bf16[4,256,128]{2,1,0:T(8,128)(2,1)S(1)}, bf16[4,256,128]{2,1,0:T(8,128)(2,1)S(1)}, u32[]{:S(2)}, u32[]{:S(2)}) %collective-permute-start.5) | collective-permute-done | bytes 262176 | tf_op jit(solution)/shard_map/ppermute | solution.py:353
  33.9 2.8 %collective-permute-done.6 = bf16[4,256,128]{2,1,0:T(8,128)(2,1)S(1)} collective-permute-done((bf16[4,256,128]{2,1,0:T(8,128)(2,1)S(1)}, bf16[4,256,128]{2,1,0:T(8,128)(2,1)S(1)}, u32[]{:S(2)}, u32[]{:S(2)}) %collective-permute-start.6) | collective-permute-done | bytes 262176 | tf_op jit(solution)/shard_map/ppermute | solution.py:353
  36.8 1.6 %collective-permute-start.8 = (bf16[8,256,128]{2,1,0:T(8,128)(2,1)S(1)}, bf16[8,256,128]{2,1,0:T(8,128)(2,1)S(1)}, u32[]{:S(2)}, u32[]{:S(2)}) collective-permute-start(bf16[8,256,128]{2,1,0:T(8,128)(2,1)S(1)} %constant_dynamic-update-slice_fusion.2.refs_4_), channel_id=1, source_target_pairs={{0,8},{1,3},{2,10},{3,1},{4,12},{5,7},{6,14},{7,5},{8,0},{9,11},{1... | collective-permute-start | bytes 1572872 | tf_op jit(solution)/shard_map/ppermute | solution.py:353
  38.4 3.9 %shard_map.129 = (bf16[640,512]{1,0:T(8,128)(2,1)S(1)}, f32[1,640]{1,0:T(1,128)S(1)}, f32[1,512]{1,0:T(1,128)S(1)}, s32[1]{0:T(128)}) custom-call(s32[17]{0:T(128)} %refs_0_.8, s32[17]{0:T(128)} %refs_0_.9, s32[8192]{0:T(1024)} %refs_2_, f32[48,128]{1,0:T(8,128)} %bitcast.12), custom_call_target="tpu_custom_call" | custom-call | bytes 9000000 | tf_op jit(solution)/shard_map/pallas_call | solution.py:297
  42.4 0.1 slice_add_fusion.3
  42.4 0.5 collective-permute-start.7
  43.0 4.5 %collective-permute-done.7 = bf16[2,256,128]{2,1,0:T(8,128)(2,1)S(1)} collective-permute-done((bf16[2,256,128]{2,1,0:T(8,128)(2,1)S(1)}, bf16[2,256,128]{2,1,0:T(8,128)(2,1)S(1)}, u32[]{:S(2)}, u32[]{:S(2)}) %collective-permute-start.7) | collective-permute-done | bytes 131104 | tf_op jit(solution)/shard_map/ppermute | solution.py:353
  47.6 0.4 collective-permute-start.9
  48.0 6.5 %collective-permute-done.9.refs_4_ = bf16[1,256,128]{2,1,0:T(8,128)(2,1)S(1)} collective-permute-done((bf16[1,256,128]{2,1,0:T(8,128)(2,1)S(1)}, bf16[1,256,128]{2,1,0:T(8,128)(2,1)S(1)}, u32[]{:S(2)}, u32[]{:S(2)}) %collective-permute-start.9) | collective-permute-done | bytes 65568 | tf_op jit(solution)/shard_map/ppermute | solution.py:353
  54.4 0.8 %copy-done.6 = bf16[8,256,128]{2,1,0:T(8,128)(2,1)} copy-done((bf16[8,256,128]{2,1,0:T(8,128)(2,1)}, bf16[8,256,128]{2,1,0:T(8,128)(2,1)S(1)}, u32[]{:S(2)}) %copy-start.6) | copy-done | bytes 524312
  55.2 1.4 %shard_map.130 = bf16[16,56,128]{2,1,0:T(8,128)(2,1)} custom-call(bf16[640,512]{1,0:T(8,128)(2,1)S(1)} %get-tuple-element.64.refs_0_, f32[1,640]{1,0:T(1,128)S(1)} %get-tuple-element.65.refs_1_, f32[1,512]{1,0:T(1,128)S(1)} %get-tuple-element.66.refs_2_, f32[1,256,128]{2,1,0:T(8,128)S(1)} %get-tuple-element.98.refs_3_, ...), custom_call_target="tpu_custom_call" | custom-call | bytes 9000000 | tf_op jit(solution)/shard_map/pallas_call | solution.py:297
  56.6 3.7 %all-to-all-start = ((bf16[16,56,128]{2,1,0:T(8,128)(2,1)}), bf16[16,56,128]{2,1,0:T(8,128)(2,1)S(1)}, u32[]{:S(2)}, u32[]{:S(2)}) async-start(bf16[16,56,128]{2,1,0:T(8,128)(2,1)} %shard_map.130), calls=%async_computation | async-start | bytes 458752 | tf_op jit(solution)/shard_map/all_to_all | solution.py:493
  60.4 1.5 %shard_map.132 = (s32[1,8192]{1,0:T(1,128)S(1)}, bf16[160,8192]{1,0:T(8,128)(2,1)S(1)}) custom-call(s32[17]{0:T(128)} %refs_0_.8, s32[17]{0:T(128)} %refs_0_.9, s32[1,8192]{1,0:T(1,128)} %bitcast.10), custom_call_target="tpu_custom_call" | custom-call | bytes 6000000 | tf_op jit(solution)/shard_map/pallas_call | solution.py:297
  61.9 5.4 %shard_map.131 = bf16[256,128]{1,0:T(8,128)(2,1)} custom-call(s32[17]{0:T(128)} %refs_0_.8, bf16[256,6144]{1,0:T(8,128)(2,1)} %refs_1_.4, f32[256,128]{1,0:T(8,128)} %get-tuple-element.76.refs_2_, f32[48,128]{1,0:T(8,128)} %get-tuple-element.77.refs_3_, bf16[8,256,128]{2,1,0:T(8,128)(2,1)} %copy-done.3, bf16[8,256,128]{2,1,0:T(8,128)(2,1)} %copy-done.4, ...), custom_call_target="tpu_custom_call" | custom-call | bytes 18000000 | tf_op jit(solution)/shard_map/pallas_call | solution.py:297
  67.3 2.4 %all-to-all-done.refs_4_ = bf16[16,56,128]{2,1,0:T(8,128)(2,1)S(1)} async-done(((bf16[16,56,128]{2,1,0:T(8,128)(2,1)}), bf16[16,56,128]{2,1,0:T(8,128)(2,1)S(1)}, u32[]{:S(2)}, u32[]{:S(2)}) %all-to-all-start) | async-done | bytes 229408 | tf_op jit(solution)/shard_map/all_to_all | solution.py:493
  69.7 1.5 %collective-permute-done.12.refs_5_ = bf16[16,56,128]{2,1,0:T(8,128)(2,1)S(1)} collective-permute-done((bf16[16,56,128]{2,1,0:T(8,128)(2,1)S(1)}, bf16[16,56,128]{2,1,0:T(8,128)(2,1)S(1)}, u32[]{:S(2)}, u32[]{:S(2)}) %collective-permute-start.12) | collective-permute-done | bytes 229408 | tf_op jit(solution)/shard_map/ppermute | solution.py:496
  71.2 3.6 %shard_map.133 = (f32[1,8192]{1,0:T(1,128)}, f32[640,128]{1,0:T(8,128)}, f32[640,128]{1,0:T(8,128)}, f32[640,128]{1,0:T(8,128)}) custom-call(s32[17]{0:T(128)} %refs_0_.9, s32[1]{0:T(128)} %get-tuple-element.85.refs_1_, s32[1,8192]{1,0:T(1,128)S(1)} %get-tuple-element.86.refs_2_, bf16[160,8192]{1,0:T(8,128)(2,1)S(1)} %get-tuple-element.87.refs_3_, ...), custom_call_target="tpu_custom_call" | custom-call | bytes 12000000 | tf_op jit(solution)/shard_map/pallas_call | solution.py:297
  (30 shorter events, 0.2 us)
Async XLA Ops:
  1.5 10.6 %collective-permute-start.1 = (bf16[1,256,128]{2,1,0:T(8,128)(2,1)S(1)}, bf16[1,256,128]{2,1,0:T(8,128)(2,1)S(1)}, u32[]{:S(2)}, u32[]{:S(2)}) collective-permute-start(bf16[1,256,128]{2,1,0:T(8,128)(2,1)S(1)} %dynamic-slice_bitcast_fusion), channel_id=1, source_target_pairs={{0,16},{1,17},{2,18},{3,19},{4,20},{5,21},{6,22},{7,23},{8,24},{9,... | collective-permute-start | bytes 196616 | tf_op jit(solution)/shard_map/ppermute | solution.py:353
  12.1 2.0 %collective-permute-start.2 = (bf16[8,256,128]{2,1,0:T(8,128)(2,1)S(1)}, bf16[8,256,128]{2,1,0:T(8,128)(2,1)S(1)}, u32[]{:S(2)}, u32[]{:S(2)}) collective-permute-start(bf16[8,256,128]{2,1,0:T(8,128)(2,1)S(1)} %bitcast.8), channel_id=1, source_target_pairs={{0,1},{1,0},{2,3},{3,2},{4,5},{5,4},{6,7},{7,6},{8,9},{9,8},{10,11... | collective-permute-start | bytes 1572872 | tf_op jit(solution)/shard_map/ppermute | solution.py:413
  12.2 4.1 %collective-permute-start = (bf16[8,256,128]{2,1,0:T(8,128)(2,1)S(1)}, bf16[8,256,128]{2,1,0:T(8,128)(2,1)S(1)}, u32[]{:S(2)}, u32[]{:S(2)}) collective-permute-start(bf16[8,256,128]{2,1,0:T(8,128)(2,1)S(1)} %bitcast.7), channel_id=1, source_target_pairs={{0,1},{1,0},{2,3},{3,2},{4,5},{5,4},{6,7},{7,6},{8,9},{9,8},{10,11... | collective-permute-start | bytes 1572872 | tf_op jit(solution)/shard_map/ppermute | solution.py:415
  14.2 10.7 %collective-permute-start.3 = (bf16[8,256,128]{2,1,0:T(8,128)(2,1)S(1)}, bf16[8,256,128]{2,1,0:T(8,128)(2,1)S(1)}, u32[]{:S(2)}, u32[]{:S(2)}) collective-permute-start(bf16[8,256,128]{2,1,0:T(8,128)(2,1)S(1)} %add_convert_fusion), channel_id=1, source_target_pairs={{0,2},{1,9},{2,0},{3,11},{4,6},{5,13},{6,4},{7,15},{8,10},{9,1},{1... | collective-permute-start | bytes 1572872 | tf_op jit(solution)/shard_map/ppermute | solution.py:353
  15.8 9.1 %collective-permute-start.4 = (bf16[2,256,128]{2,1,0:T(8,128)(2,1)S(1)}, bf16[2,256,128]{2,1,0:T(8,128)(2,1)S(1)}, u32[]{:S(2)}, u32[]{:S(2)}) collective-permute-start(bf16[2,256,128]{2,1,0:T(8,128)(2,1)S(1)} %pad_maximum_fusion), channel_id=1, source_target_pairs={{0,2},{1,9},{2,0},{3,11},{4,6},{5,13},{6,4},{7,15},{8,10},{9,1},{1... | collective-permute-start | bytes 393224 | tf_op jit(solution)/shard_map/ppermute | solution.py:353
  25.0 30.3 %copy-start = (bf16[512,128]{1,0:T(8,128)(2,1)S(1)}, bf16[512,128]{1,0:T(8,128)(2,1)}, u32[]{:S(2)}) copy-start(bf16[512,128]{1,0:T(8,128)(2,1)} %refs_5_.1) | copy-start | bytes 393220
  25.0 30.2 %copy-start.1 = (f32[512,128]{1,0:T(8,128)S(1)}, f32[512,128]{1,0:T(8,128)}, u32[]{:S(2)}) copy-start(f32[512,128]{1,0:T(8,128)} %refs_6_.1) | copy-start | bytes 786436
  25.0 30.2 %copy-start.2 = (f32[512,128]{1,0:T(8,128)S(1)}, f32[512,128]{1,0:T(8,128)}, u32[]{:S(2)}) copy-start(f32[512,128]{1,0:T(8,128)} %refs_7_.1) | copy-start | bytes 786436
  25.1 8.8 %collective-permute-start.5 = (bf16[4,256,128]{2,1,0:T(8,128)(2,1)S(1)}, bf16[4,256,128]{2,1,0:T(8,128)(2,1)S(1)}, u32[]{:S(2)}, u32[]{:S(2)}) collective-permute-start(bf16[4,256,128]{2,1,0:T(8,128)(2,1)S(1)} %get-tuple-element.94), channel_id=1, source_target_pairs={{0,4},{1,3},{2,6},{3,1},{4,0},{5,7},{6,2},{7,5},{8,12},{9,11},{10,... | collective-permute-start | bytes 786440 | tf_op jit(solution)/shard_map/ppermute | solution.py:353
  26.7 10.0 %collective-permute-start.6 = (bf16[4,256,128]{2,1,0:T(8,128)(2,1)S(1)}, bf16[4,256,128]{2,1,0:T(8,128)(2,1)S(1)}, u32[]{:S(2)}, u32[]{:S(2)}) collective-permute-start(bf16[4,256,128]{2,1,0:T(8,128)(2,1)S(1)} %constant_dynamic-update-slice_fusion), channel_id=1, source_target_pairs={{0,4},{1,5},{2,6},{3,7},{4,0},{5,1},{6,2},{7,3},{8,12},{9,13},{10,... | collective-permute-start | bytes 786440 | tf_op jit(solution)/shard_map/ppermute | solution.py:353
  36.7 25.1 %copy-start.3 = (bf16[8,256,128]{2,1,0:T(8,128)(2,1)}, bf16[8,256,128]{2,1,0:T(8,128)(2,1)S(1)}, u32[]{:S(2)}) copy-start(bf16[8,256,128]{2,1,0:T(8,128)(2,1)S(1)} %constant_dynamic-update-slice_fusion.2.refs_4_) | copy-start | bytes 1572868
  36.8 10.7 %collective-permute-start.8 = (bf16[8,256,128]{2,1,0:T(8,128)(2,1)S(1)}, bf16[8,256,128]{2,1,0:T(8,128)(2,1)S(1)}, u32[]{:S(2)}, u32[]{:S(2)}) collective-permute-start(bf16[8,256,128]{2,1,0:T(8,128)(2,1)S(1)} %constant_dynamic-update-slice_fusion.2.refs_4_), channel_id=1, source_target_pairs={{0,8},{1,3},{2,10},{3,1},{4,12},{5,7},{6,14},{7,5},{8,0},{9,11},{1... | collective-permute-start | bytes 1572872 | tf_op jit(solution)/shard_map/ppermute | solution.py:353
  42.4 5.0 %collective-permute-start.7 = (bf16[2,256,128]{2,1,0:T(8,128)(2,1)S(1)}, bf16[2,256,128]{2,1,0:T(8,128)(2,1)S(1)}, u32[]{:S(2)}, u32[]{:S(2)}) collective-permute-start(bf16[2,256,128]{2,1,0:T(8,128)(2,1)S(1)} %get-tuple-element.96), channel_id=1, source_target_pairs={{0,8},{1,5},{2,10},{3,7},{4,12},{5,1},{6,14},{7,3},{8,0},{9,13},{1... | collective-permute-start | bytes 393224 | tf_op jit(solution)/shard_map/ppermute | solution.py:353
  43.0 5.0 %collective-permute-start.10 = (bf16[8,256,128]{2,1,0:T(8,128)(2,1)S(1)}, bf16[8,256,128]{2,1,0:T(8,128)(2,1)S(1)}, u32[]{:S(2)}, u32[]{:S(2)}) collective-permute-start(bf16[8,256,128]{2,1,0:T(8,128)(2,1)S(1)} %constant_dynamic-update-slice_fusion.2.refs_4_), channel_id=1, source_target_pairs={{0,1},{1,0},{2,3},{3,2},{4,5},{5,4},{6,7},{7,6},{8,9},{9,8},{10,11... | collective-permute-start | bytes 1572872 | tf_op jit(solution)/shard_map/ppermute | solution.py:433
  47.5 6.9 %copy-start.4 = (bf16[8,256,128]{2,1,0:T(8,128)(2,1)}, bf16[8,256,128]{2,1,0:T(8,128)(2,1)S(1)}, u32[]{:S(2)}) copy-start(bf16[8,256,128]{2,1,0:T(8,128)(2,1)S(1)} %collective-permute-done.8.refs_5_) | copy-start | bytes 1572868
  47.5 6.9 %collective-permute-start.11 = (bf16[8,256,128]{2,1,0:T(8,128)(2,1)S(1)}, bf16[8,256,128]{2,1,0:T(8,128)(2,1)S(1)}, u32[]{:S(2)}, u32[]{:S(2)}) collective-permute-start(bf16[8,256,128]{2,1,0:T(8,128)(2,1)S(1)} %collective-permute-done.8.refs_5_), channel_id=1, source_target_pairs={{0,1},{1,0},{2,3},{3,2},{4,5},{5,4},{6,7},{7,6},{8,9},{9,8},{10,11... | collective-permute-start | bytes 1572872 | tf_op jit(solution)/shard_map/ppermute | solution.py:433
  47.6 6.9 %collective-permute-start.9 = (bf16[1,256,128]{2,1,0:T(8,128)(2,1)S(1)}, bf16[1,256,128]{2,1,0:T(8,128)(2,1)S(1)}, u32[]{:S(2)}, u32[]{:S(2)}) collective-permute-start(bf16[1,256,128]{2,1,0:T(8,128)(2,1)S(1)} %get-tuple-element.97), channel_id=1, source_target_pairs={{0,16},{1,17},{2,18},{3,19},{4,20},{5,21},{6,22},{7,23},{8,24},{9,... | collective-permute-start | bytes 196616 | tf_op jit(solution)/shard_map/ppermute | solution.py:353
  48.0 6.5 %copy-start.5 = (bf16[8,256,128]{2,1,0:T(8,128)(2,1)}, bf16[8,256,128]{2,1,0:T(8,128)(2,1)S(1)}, u32[]{:S(2)}) copy-start(bf16[8,256,128]{2,1,0:T(8,128)(2,1)S(1)} %collective-permute-done.10.refs_6_) | copy-start | bytes 1572868
  54.4 0.8 %copy-start.6 = (bf16[8,256,128]{2,1,0:T(8,128)(2,1)}, bf16[8,256,128]{2,1,0:T(8,128)(2,1)S(1)}, u32[]{:S(2)}) copy-start(bf16[8,256,128]{2,1,0:T(8,128)(2,1)S(1)} %collective-permute-done.11.refs_7_) | copy-start | bytes 1572868
  56.6 13.1 %all-to-all-start = ((bf16[16,56,128]{2,1,0:T(8,128)(2,1)}), bf16[16,56,128]{2,1,0:T(8,128)(2,1)S(1)}, u32[]{:S(2)}, u32[]{:S(2)}) async-start(bf16[16,56,128]{2,1,0:T(8,128)(2,1)} %shard_map.130), calls=%async_computation | async-start | bytes 458752 | tf_op jit(solution)/shard_map/all_to_all | solution.py:493
  69.7 1.5 %collective-permute-start.12 = (bf16[16,56,128]{2,1,0:T(8,128)(2,1)S(1)}, bf16[16,56,128]{2,1,0:T(8,128)(2,1)S(1)}, u32[]{:S(2)}, u32[]{:S(2)}) collective-permute-start(bf16[16,56,128]{2,1,0:T(8,128)(2,1)S(1)} %all-to-all-done.refs_4_), channel_id=1, source_target_pairs={{0,1},{1,0},{2,3},{3,2},{4,5},{5,4},{6,7},{7,6},{8,9},{9,8},{10,11... | collective-permute-start | bytes 688136 | tf_op jit(solution)/shard_map/ppermute | solution.py:496

commit v8 on v7

--- a/solution.py
+++ b/solution.py
@@ -44,8 +44,14 @@
 def token_kernel(rels, rep_count, cap, ob, src, gain, hidden_hbm, cot, live_gain, inv_out, *rest):
     *blocks, hist, hidden, own_grads, other_grads, sem = rest
     owns, others = blocks[: len(blocks) // 2], blocks[len(blocks) // 2 :]
-    copy = pltpu.make_async_copy(hidden_hbm, hidden, sem)
-    copy.start()
+    pieces = sem.shape[0]
+    width = D_OLD // pieces
+    copies = []
+    for piece in range(pieces):
+        columns = pl.ds(piece * width, width)
+        copies.append(pltpu.make_async_copy(hidden_hbm.at[:, columns], hidden.at[:, columns], sem.at[piece]))
+    for copy in copies:
+        copy.start()
     me = lax.axis_index("dp")
     rep = lax.axis_index("rep")
     tiles = D_OLD // LANES
@@ -57,9 +63,10 @@
         total = total + dot(one_hot(tiles, units >> 7), one_hot(LANES, units & 127), (1, 1))
     hist[...] = total
     live_gain[...] = jnp.where(total > 0.5, gain[...], 0.0)
-    copy.wait()
     squares = jnp.zeros((tokens, LANES), F32)
     for tile in range(tiles):
+        if tile * LANES % width == 0:
+            copies[tile * LANES // width].wait()
         stream = hidden[:, tile * LANES : (tile + 1) * LANES].astype(F32)
         squares = squares + stream * stream * hist[tile : tile + 1, :]
     inv_rms = lax.rsqrt(jnp.sum(squares, axis=1, keepdims=True) / D_NEW + 1e-05)
@@ -332,7 +339,7 @@
     staged = rep_count == 2 and dp_count >= 4
     bits = dp_count.bit_length() - 1
     line = list(range(bits - 1))
-    halving = [line + [bits - 1], line[-1:] + line[:-1] + [bits - 1]]
+    halving = [line + [bits - 1], line[::-1] + [bits - 1]]
     doubling = [[bits - 1] + line, [bits - 1] + line[::-1]]
     if staged:
         rels = [
@@ -355,8 +362,7 @@
     swap = [(0, 1), (1, 0)]
     any_spec = pl.BlockSpec(memory_space=pl.ANY)
     if staged:
-        gathered = lax.dynamic_slice_in_dim(weight_old, lax.axis_index("rep") * part, part)[None]
-        sent = across(gathered, doubling, 0)
+        sent = across(weight_old, doubling, 0)
     else:
         weights = lax.all_gather(weight_old, "dp", axis=0, tiled=True)
 
@@ -376,7 +382,7 @@
             pltpu.VMEM((tokens, D_OLD), BF16),
             pltpu.VMEM((D_OLD + cap, LANES), F32),
             pltpu.VMEM((D_OLD + cap, LANES), F32),
-            pltpu.SemaphoreType.DMA(()),
+            pltpu.SemaphoreType.DMA((6,)),
         ],
         old_bounds,
         units,
@@ -408,26 +414,27 @@
     if staged:
         half = dp_count // 2
         send, sent = lax.optimization_barrier((others[1][0], sent))
-        gathered = jnp.concatenate([gathered, sent])
+        mine = lax.axis_index("rep") * part
+        gathered = [lax.dynamic_slice_in_dim(block, mine, part)[None] for block in (weight_old, sent)]
+        gathered = jnp.concatenate(gathered)
         sent = across(gathered, doubling, 1)
         pair, gathered = lax.optimization_barrier((lax.ppermute(send, "rep", swap), gathered))
         high = (owns[1] + pair.astype(F32)).astype(BF16)
         low = owns[0] + lax.ppermute(others[0][0], "rep", swap).astype(F32)
         for stage in range(bits - 1):
             came = across(high, halving, stage)
-            came, sent = lax.optimization_barrier((came, sent))
-            if stage == 1:
-                came, chosen = lax.optimization_barrier((came, chosen))
             if stage < bits - 2:
                 gathered = jnp.concatenate([gathered, sent])
                 sent = across(gathered, doubling, stage + 2)
-                came, gathered = lax.optimization_barrier((came, gathered))
-            if stage == 0:
-                gathered, late_src = lax.optimization_barrier((gathered, source_map))
-                chosen, keep, own_gain, offset = indices(late_src)
+                came, sent = lax.optimization_barrier((came, sent))
+            if stage == 1:
+                came, chosen = lax.optimization_barrier((came, chosen))
             came = came.astype(F32)
             half = half // 2
             low, high = low[:half] + came[:half], (low[half:] + came[half:]).astype(BF16)
+            if stage == 0:
+                high, late_src = lax.optimization_barrier((high, source_map))
+                chosen, keep, own_gain, offset = indices(late_src)
         came = across(high, halving, bits - 1)
         pieces = [gathered, sent]
         pieces += [lax.ppermute(piece, "rep", swap) for piece in pieces]

time: 75.3 us -> 67.5 us (0.90)
  waiting for transfers between devices: 34.2 us -> 18.7 us
  starting transfers between devices: 15.1 us -> 22 us
  other arithmetic: 0.57 us -> 2.67 us
  local copies, waits for them, and re-layouts: 1.74 us -> 0.9 us
    ppermute x8, waiting for transfers between devices: 28.9 us -> 15.8 us  [across(): return lax.ppermute(value, ('dp', 'rep'), pairs)]
    ppermute x8, starting transfers between devices: 10.8 us -> 15.3 us  [across(): return lax.ppermute(value, ('dp', 'rep'), pairs)]
    all_to_all x1, starting transfers between devices: 3.72 us -> 6.05 us  [on_device(): moved = [lax.all_to_all(packed, 'dp', split_axis=0, concat_axis=0)]]
    ppermute x1, waiting for transfers between devices: 1.38 us -> 0.01 us  [on_device(): lax.ppermute(send, 'rep', swap)]
    convert_element_type x1, other arithmetic: 0.11 us -> 1.15 us  [on_device(): high = (owns[1] + pair.astype(F32)).astype(BF16)]
    add x1, other arithmetic: 0.09 us -> 1.13 us  [on_device(): low = owns[0] + lax.ppermute(others[0][0], 'rep', swap).astype(F32)]
    all_to_all x1, waiting for transfers between devices: 2.42 us -> 1.43 us  [on_device(): moved = [lax.all_to_all(packed, 'dp', split_axis=0, concat_axis=0)]]
    broadcast_in_dim x1 -> x2, local copies, waits for them, and re-layouts: 0.85 us -> 0.02 us  [on_device(): lax.dynamic_slice_in_dim(block, mine, part)[None]]
  transfers between devices with their start and end apart: 14 -> 14, of which waited for: 8 -> 9; matrix products, arithmetic and copies ran while one was open for 1% -> 4% of each run, Pallas kernels for 23% -> 25%
where the time goes in v8:
time: 67.5 us; the launch traced here: 66.9 us
  starting transfers between devices  22 us (33%)
  Pallas kernels  21.9 us (32%)
  waiting for transfers between devices  18.7 us (28%)
  other arithmetic  2.67 us (4%)
  local copies, waits for them, and re-layouts  0.9 us (1%)
  between operations  0.82 us (1%)
    pallas_call x6, Pallas kernels, call(): pl.pallas_call(kernel, out_shape=out_shape, in_specs=specs, out_specs=out...  21.9 us
    ppermute x8, waiting for transfers between devices, across(): return lax.ppermute(value, ('dp', 'rep'), pairs)  15.8 us
    ppermute x8, starting transfers between devices, across(): return lax.ppermute(value, ('dp', 'rep'), pairs)  15.3 us
    all_to_all x1, starting transfers between devices, on_device(): moved = [lax.all_to_all(packed, 'dp', split_axis=0, concat_axis=0)]  6.05 us
    ppermute x1, waiting for transfers between devices, on_device(): moved = [arrived, lax.ppermute(arrived, 'rep', swap)]  1.49 us
    all_to_all x1, waiting for transfers between devices, on_device(): moved = [lax.all_to_all(packed, 'dp', split_axis=0, concat_axis=0)]  1.43 us
  transfers between devices with their start and end apart: 14, of which 9 were waited for; matrix products, arithmetic and copies ran while one was open for 4% of the time, Pallas kernels for 25%

profile of v8, /device:TPU:0, one launch (start us, length us, event | category | flops | bytes accessed | tf_op | source)
XLA Modules:
  0.0 66.9 jit_solution(15541965958785363750)
XLA Ops:
  0.6 4.1 %collective-permute-start.1 = (bf16[512,128]{1,0:T(8,128)(2,1)}, bf16[512,128]{1,0:T(8,128)(2,1)S(1)}, u32[]{:S(2)}, u32[]{:S(2)}) collective-permute-start(bf16[512,128]{1,0:T(8,128)(2,1)} %refs_5_.1), channel_id=1, source_target_pairs={{0,16},{1,17},{2,18},{3,19},{4,20},{5,21},{6,22},{7,23},{8,24},{9,... | collective-permute-start | bytes 393224 | tf_op jit(solution)/shard_map/ppermute | solution.py:360
  4.7 6.1 %shard_map.128 = (f32[48,128]{1,0:T(8,128)}, f32[256,128]{1,0:T(8,128)}, f32[8,256,128]{2,1,0:T(8,128)S(1)}, f32[8,256,128]{2,1,0:T(8,128)S(1)}, bf16[1,8,256,12...) custom-call(s32[17]{0:T(128)} %refs_0_.8, s32[1,8192]{1,0:T(1,128)} %bitcast.11, f32[48,128]{1,0:T(8,128)} %bitcast.13, ...), custom_call_target="tpu_custom_call" | custom-call | bytes 24000000 | tf_op jit(solution)/shard_map/pallas_call | solution.py:304
  10.8 0.4 collective-permute-done.1
  11.3 0.5 collective-permute-start
  11.8 1.6 %collective-permute-start.4 = (bf16[2,256,128]{2,1,0:T(8,128)(2,1)S(1)}, bf16[2,256,128]{2,1,0:T(8,128)(2,1)S(1)}, u32[]{:S(2)}, u32[]{:S(2)}) collective-permute-start(bf16[2,256,128]{2,1,0:T(8,128)(2,1)S(1)} %pad_maximum_fusion.1), channel_id=1, source_target_pairs={{0,2},{1,9},{2,0},{3,11},{4,6},{5,13},{6,4},{7,15},{8,10},{9,1},{1... | collective-permute-start | bytes 393224 | tf_op jit(solution)/shard_map/ppermute | solution.py:360
  13.4 1.1 %add_convert_fusion = bf16[8,256,128]{2,1,0:T(8,128)(2,1)S(1)} fusion(f32[8,256,128]{2,1,0:T(8,128)S(1)} %get-tuple-element.45, bf16[8,256,128]{2,1,0:T(8,128)(2,1)} %collective-permute-done.2), kind=kLoop, calls=%fused_computation | loop fusion | flops 786432 | bytes 2097152 | tf_op jit(solution)/shard_map/convert_element_type | solution.py:422
  14.6 1.5 %collective-permute-start.3 = (bf16[8,256,128]{2,1,0:T(8,128)(2,1)S(1)}, bf16[8,256,128]{2,1,0:T(8,128)(2,1)S(1)}, u32[]{:S(2)}, u32[]{:S(2)}) collective-permute-start(bf16[8,256,128]{2,1,0:T(8,128)(2,1)S(1)} %add_convert_fusion), channel_id=1, source_target_pairs={{0,2},{1,9},{2,0},{3,11},{4,6},{5,13},{6,4},{7,15},{8,10},{9,1},{1... | collective-permute-start | bytes 1572872 | tf_op jit(solution)/shard_map/ppermute | solution.py:360
  16.1 0.8 %collective-permute-done.4 = bf16[2,256,128]{2,1,0:T(8,128)(2,1)S(1)} collective-permute-done((bf16[2,256,128]{2,1,0:T(8,128)(2,1)S(1)}, bf16[2,256,128]{2,1,0:T(8,128)(2,1)S(1)}, u32[]{:S(2)}, u32[]{:S(2)}) %collective-permute-start.4) | collective-permute-done | bytes 131104 | tf_op jit(solution)/shard_map/ppermute | solution.py:360
  16.9 1.6 %collective-permute-start.5 = (bf16[4,256,128]{2,1,0:T(8,128)(2,1)S(1)}, bf16[4,256,128]{2,1,0:T(8,128)(2,1)S(1)}, u32[]{:S(2)}, u32[]{:S(2)}) collective-permute-start(bf16[4,256,128]{2,1,0:T(8,128)(2,1)S(1)} %pad_maximum_fusion), channel_id=1, source_target_pairs={{0,4},{1,5},{2,6},{3,7},{4,0},{5,1},{6,2},{7,3},{8,12},{9,13},{10,... | collective-permute-start | bytes 786440 | tf_op jit(solution)/shard_map/ppermute | solution.py:360
  18.5 1.1 %convert_add_fusion = f32[8,256,128]{2,1,0:T(8,128)S(1)} fusion(f32[8,256,128]{2,1,0:T(8,128)S(1)} %get-tuple-element.43, bf16[8,256,128]{2,1,0:T(8,128)(2,1)} %collective-permute-done), kind=kLoop, calls=%fused_computation.1 | loop fusion | flops 524288 | bytes 2621440 | tf_op jit(solution)/shard_map/add | solution.py:423
  19.7 4.6 %collective-permute-done.5 = bf16[4,256,128]{2,1,0:T(8,128)(2,1)S(1)} collective-permute-done((bf16[4,256,128]{2,1,0:T(8,128)(2,1)S(1)}, bf16[4,256,128]{2,1,0:T(8,128)(2,1)S(1)}, u32[]{:S(2)}, u32[]{:S(2)}) %collective-permute-start.5) | collective-permute-done | bytes 262176 | tf_op jit(solution)/shard_map/ppermute | solution.py:360
  24.3 0.1 convert_element_type.30
  24.5 1.4 %collective-permute-start.7 = (bf16[8,256,128]{2,1,0:T(8,128)(2,1)S(1)}, bf16[8,256,128]{2,1,0:T(8,128)(2,1)S(1)}, u32[]{:S(2)}, u32[]{:S(2)}) collective-permute-start(bf16[8,256,128]{2,1,0:T(8,128)(2,1)S(1)} %constant_dynamic-update-slice_fusion.refs_4_), channel_id=1, source_target_pairs={{0,8},{1,3},{2,10},{3,1},{4,12},{5,7},{6,14},{7,5},{8,0},{9,11},{1... | collective-permute-start | bytes 1572872 | tf_op jit(solution)/shard_map/ppermute | solution.py:360
  25.8 0.1 slice_add_fusion
  26.0 1.6 %collective-permute-start.6 = (bf16[4,256,128]{2,1,0:T(8,128)(2,1)S(1)}, bf16[4,256,128]{2,1,0:T(8,128)(2,1)S(1)}, u32[]{:S(2)}, u32[]{:S(2)}) collective-permute-start(bf16[4,256,128]{2,1,0:T(8,128)(2,1)S(1)} %get-tuple-element.52), channel_id=1, source_target_pairs={{0,4},{1,5},{2,6},{3,7},{4,0},{5,1},{6,2},{7,3},{8,12},{9,13},{10,... | collective-permute-start | bytes 786440 | tf_op jit(solution)/shard_map/ppermute | solution.py:360
  27.6 3.9 %shard_map.129 = (bf16[640,512]{1,0:T(8,128)(2,1)S(1)}, f32[1,640]{1,0:T(1,128)S(1)}, f32[1,512]{1,0:T(1,128)S(1)}, s32[1]{0:T(128)}) custom-call(s32[17]{0:T(128)} %refs_0_.8, s32[17]{0:T(128)} %refs_0_.9, s32[8192]{0:T(1024)} %refs_2_, f32[48,128]{1,0:T(8,128)} %bitcast.14), custom_call_target="tpu_custom_call" | custom-call | bytes 9000000 | tf_op jit(solution)/shard_map/pallas_call | solution.py:304
  31.5 1.4 %collective-permute-done.6 = bf16[4,256,128]{2,1,0:T(8,128)(2,1)S(1)} collective-permute-done((bf16[4,256,128]{2,1,0:T(8,128)(2,1)S(1)}, bf16[4,256,128]{2,1,0:T(8,128)(2,1)S(1)}, u32[]{:S(2)}, u32[]{:S(2)}) %collective-permute-start.6) | collective-permute-done | bytes 262176 | tf_op jit(solution)/shard_map/ppermute | solution.py:360
  32.9 0.8 %collective-permute-done.7.refs_5_ = bf16[8,256,128]{2,1,0:T(8,128)(2,1)S(1)} collective-permute-done((bf16[8,256,128]{2,1,0:T(8,128)(2,1)S(1)}, bf16[8,256,128]{2,1,0:T(8,128)(2,1)S(1)}, u32[]{:S(2)}, u32[]{:S(2)}) %collective-permute-start.7) | collective-permute-done | bytes 524320 | tf_op jit(solution)/shard_map/ppermute | solution.py:360
  33.8 0.1 collective-permute-start.11
  33.8 0.1 slice_add_fusion.3
  33.9 1.4 %collective-permute-start.8 = (bf16[2,256,128]{2,1,0:T(8,128)(2,1)S(1)}, bf16[2,256,128]{2,1,0:T(8,128)(2,1)S(1)}, u32[]{:S(2)}, u32[]{:S(2)}) collective-permute-start(bf16[2,256,128]{2,1,0:T(8,128)(2,1)S(1)} %get-tuple-element.84), channel_id=1, source_target_pairs={{0,8},{1,3},{2,10},{3,1},{4,12},{5,7},{6,14},{7,5},{8,0},{9,11},{1... | collective-permute-start | bytes 393224 | tf_op jit(solution)/shard_map/ppermute | solution.py:360
  35.3 3.7 %collective-permute-done.8 = bf16[2,256,128]{2,1,0:T(8,128)(2,1)S(1)} collective-permute-done((bf16[2,256,128]{2,1,0:T(8,128)(2,1)S(1)}, bf16[2,256,128]{2,1,0:T(8,128)(2,1)S(1)}, u32[]{:S(2)}, u32[]{:S(2)}) %collective-permute-start.8) | collective-permute-done | bytes 131104 | tf_op jit(solution)/shard_map/ppermute | solution.py:360
  39.0 2.2 %collective-permute-start.9 = (bf16[1,256,128]{2,1,0:T(8,128)(2,1)S(1)}, bf16[1,256,128]{2,1,0:T(8,128)(2,1)S(1)}, u32[]{:S(2)}, u32[]{:S(2)}) collective-permute-start(bf16[1,256,128]{2,1,0:T(8,128)(2,1)S(1)} %get-tuple-element.85), channel_id=1, source_target_pairs={{0,16},{1,17},{2,18},{3,19},{4,20},{5,21},{6,22},{7,23},{8,24},{9,... | collective-permute-start | bytes 196616 | tf_op jit(solution)/shard_map/ppermute | solution.py:360
  41.2 4.0 %collective-permute-done.9.refs_4_ = bf16[1,256,128]{2,1,0:T(8,128)(2,1)S(1)} collective-permute-done((bf16[1,256,128]{2,1,0:T(8,128)(2,1)S(1)}, bf16[1,256,128]{2,1,0:T(8,128)(2,1)S(1)}, u32[]{:S(2)}, u32[]{:S(2)}) %collective-permute-start.9) | collective-permute-done | bytes 65568 | tf_op jit(solution)/shard_map/ppermute | solution.py:360
  45.2 0.8 %copy-done.6 = bf16[8,256,128]{2,1,0:T(8,128)(2,1)} copy-done((bf16[8,256,128]{2,1,0:T(8,128)(2,1)}, bf16[8,256,128]{2,1,0:T(8,128)(2,1)S(1)}, u32[]{:S(2)}) %copy-start.6) | copy-done | bytes 524312
  46.0 1.4 %shard_map.130 = bf16[16,56,128]{2,1,0:T(8,128)(2,1)} custom-call(bf16[640,512]{1,0:T(8,128)(2,1)S(1)} %get-tuple-element.57.refs_0_, f32[1,640]{1,0:T(1,128)S(1)} %get-tuple-element.58.refs_1_, f32[1,512]{1,0:T(1,128)S(1)} %get-tuple-element.59.refs_2_, f32[1,256,128]{2,1,0:T(8,128)S(1)} %get-tuple-element.86.refs_3_, ...), custom_call_target="tpu_custom_call" | custom-call | bytes 9000000 | tf_op jit(solution)/shard_map/pallas_call | solution.py:304
  47.4 6.1 %all-to-all-start = ((bf16[16,56,128]{2,1,0:T(8,128)(2,1)}), bf16[16,56,128]{2,1,0:T(8,128)(2,1)S(1)}, u32[]{:S(2)}, u32[]{:S(2)}) async-start(bf16[16,56,128]{2,1,0:T(8,128)(2,1)} %shard_map.130), calls=%async_computation | async-start | bytes 458752 | tf_op jit(solution)/shard_map/all_to_all | solution.py:500
  53.5 1.5 %shard_map.132 = (s32[1,8192]{1,0:T(1,128)S(1)}, bf16[160,8192]{1,0:T(8,128)(2,1)S(1)}) custom-call(s32[17]{0:T(128)} %refs_0_.8, s32[17]{0:T(128)} %refs_0_.9, s32[1,8192]{1,0:T(1,128)} %bitcast.12), custom_call_target="tpu_custom_call" | custom-call | bytes 6000000 | tf_op jit(solution)/shard_map/pallas_call | solution.py:304
  55.0 5.4 %shard_map.131 = bf16[256,128]{1,0:T(8,128)(2,1)} custom-call(s32[17]{0:T(128)} %refs_0_.8, bf16[256,6144]{1,0:T(8,128)(2,1)} %refs_1_.4, f32[256,128]{1,0:T(8,128)} %get-tuple-element.64.refs_2_, f32[48,128]{1,0:T(8,128)} %get-tuple-element.65.refs_3_, bf16[8,256,128]{2,1,0:T(8,128)(2,1)} %copy-done.3, bf16[8,256,128]{2,1,0:T(8,128)(2,1)} %copy-done.4, ...), custom_call_target="tpu_custom_call" | custom-call | bytes 18000000 | tf_op jit(solution)/shard_map/pallas_call | solution.py:304
  60.4 1.4 %all-to-all-done.refs_4_ = bf16[16,56,128]{2,1,0:T(8,128)(2,1)S(1)} async-done(((bf16[16,56,128]{2,1,0:T(8,128)(2,1)}), bf16[16,56,128]{2,1,0:T(8,128)(2,1)S(1)}, u32[]{:S(2)}, u32[]{:S(2)}) %all-to-all-start) | async-done | bytes 229408 | tf_op jit(solution)/shard_map/all_to_all | solution.py:500
  61.8 1.5 %collective-permute-done.12.refs_5_ = bf16[16,56,128]{2,1,0:T(8,128)(2,1)S(1)} collective-permute-done((bf16[16,56,128]{2,1,0:T(8,128)(2,1)S(1)}, bf16[16,56,128]{2,1,0:T(8,128)(2,1)S(1)}, u32[]{:S(2)}, u32[]{:S(2)}) %collective-permute-start.12) | collective-permute-done | bytes 229408 | tf_op jit(solution)/shard_map/ppermute | solution.py:503
  63.3 3.6 %shard_map.133 = (f32[1,8192]{1,0:T(1,128)}, f32[640,128]{1,0:T(8,128)}, f32[640,128]{1,0:T(8,128)}, f32[640,128]{1,0:T(8,128)}) custom-call(s32[17]{0:T(128)} %refs_0_.9, s32[1]{0:T(128)} %get-tuple-element.73.refs_1_, s32[1,8192]{1,0:T(1,128)S(1)} %get-tuple-element.74.refs_2_, bf16[160,8192]{1,0:T(8,128)(2,1)S(1)} %get-tuple-element.75.refs_3_, ...), custom_call_target="tpu_custom_call" | custom-call | bytes 12000000 | tf_op jit(solution)/shard_map/pallas_call | solution.py:304
  (31 shorter events, 0.3 us)
Async XLA Ops:
  0.6 11.1 %copy-start = (bf16[512,128]{1,0:T(8,128)(2,1)S(1)}, bf16[512,128]{1,0:T(8,128)(2,1)}, u32[]{:S(2)}) copy-start(bf16[512,128]{1,0:T(8,128)(2,1)} %refs_5_.1) | copy-start | bytes 393220
  0.6 10.6 %collective-permute-start.1 = (bf16[512,128]{1,0:T(8,128)(2,1)}, bf16[512,128]{1,0:T(8,128)(2,1)S(1)}, u32[]{:S(2)}, u32[]{:S(2)}) collective-permute-start(bf16[512,128]{1,0:T(8,128)(2,1)} %refs_5_.1), channel_id=1, source_target_pairs={{0,16},{1,17},{2,18},{3,19},{4,20},{5,21},{6,22},{7,23},{8,24},{9,... | collective-permute-start | bytes 393224 | tf_op jit(solution)/shard_map/ppermute | solution.py:360
  11.3 2.2 %collective-permute-start.2 = (bf16[8,256,128]{2,1,0:T(8,128)(2,1)S(1)}, bf16[8,256,128]{2,1,0:T(8,128)(2,1)}, u32[]{:S(2)}, u32[]{:S(2)}) collective-permute-start(bf16[8,256,128]{2,1,0:T(8,128)(2,1)S(1)} %bitcast.10), channel_id=1, source_target_pairs={{0,1},{1,0},{2,3},{3,2},{4,5},{5,4},{6,7},{7,6},{8,9},{9,8},{10,11... | collective-permute-start | bytes 1572872 | tf_op jit(solution)/shard_map/ppermute | solution.py:421
  11.3 7.3 %collective-permute-start = (bf16[8,256,128]{2,1,0:T(8,128)(2,1)S(1)}, bf16[8,256,128]{2,1,0:T(8,128)(2,1)}, u32[]{:S(2)}, u32[]{:S(2)}) collective-permute-start(bf16[8,256,128]{2,1,0:T(8,128)(2,1)S(1)} %bitcast.9), channel_id=1, source_target_pairs={{0,1},{1,0},{2,3},{3,2},{4,5},{5,4},{6,7},{7,6},{8,9},{9,8},{10,11... | collective-permute-start | bytes 1572872 | tf_op jit(solution)/shard_map/ppermute | solution.py:423
  11.8 5.0 %collective-permute-start.4 = (bf16[2,256,128]{2,1,0:T(8,128)(2,1)S(1)}, bf16[2,256,128]{2,1,0:T(8,128)(2,1)S(1)}, u32[]{:S(2)}, u32[]{:S(2)}) collective-permute-start(bf16[2,256,128]{2,1,0:T(8,128)(2,1)S(1)} %pad_maximum_fusion.1), channel_id=1, source_target_pairs={{0,2},{1,9},{2,0},{3,11},{4,6},{5,13},{6,4},{7,15},{8,10},{9,1},{1... | collective-permute-start | bytes 393224 | tf_op jit(solution)/shard_map/ppermute | solution.py:360
  14.6 9.7 %collective-permute-start.3 = (bf16[8,256,128]{2,1,0:T(8,128)(2,1)S(1)}, bf16[8,256,128]{2,1,0:T(8,128)(2,1)S(1)}, u32[]{:S(2)}, u32[]{:S(2)}) collective-permute-start(bf16[8,256,128]{2,1,0:T(8,128)(2,1)S(1)} %add_convert_fusion), channel_id=1, source_target_pairs={{0,2},{1,9},{2,0},{3,11},{4,6},{5,13},{6,4},{7,15},{8,10},{9,1},{1... | collective-permute-start | bytes 1572872 | tf_op jit(solution)/shard_map/ppermute | solution.py:360
  16.9 7.4 %collective-permute-start.5 = (bf16[4,256,128]{2,1,0:T(8,128)(2,1)S(1)}, bf16[4,256,128]{2,1,0:T(8,128)(2,1)S(1)}, u32[]{:S(2)}, u32[]{:S(2)}) collective-permute-start(bf16[4,256,128]{2,1,0:T(8,128)(2,1)S(1)} %pad_maximum_fusion), channel_id=1, source_target_pairs={{0,4},{1,5},{2,6},{3,7},{4,0},{5,1},{6,2},{7,3},{8,12},{9,13},{10,... | collective-permute-start | bytes 786440 | tf_op jit(solution)/shard_map/ppermute | solution.py:360
  24.4 14.6 %copy-start.3 = (bf16[8,256,128]{2,1,0:T(8,128)(2,1)}, bf16[8,256,128]{2,1,0:T(8,128)(2,1)S(1)}, u32[]{:S(2)}) copy-start(bf16[8,256,128]{2,1,0:T(8,128)(2,1)S(1)} %constant_dynamic-update-slice_fusion.refs_4_) | copy-start | bytes 1572868
  24.4 21.6 %copy-start.1 = (f32[512,128]{1,0:T(8,128)S(1)}, f32[512,128]{1,0:T(8,128)}, u32[]{:S(2)}) copy-start(f32[512,128]{1,0:T(8,128)} %refs_6_.1) | copy-start | bytes 786436
  24.5 21.6 %copy-start.2 = (f32[512,128]{1,0:T(8,128)S(1)}, f32[512,128]{1,0:T(8,128)}, u32[]{:S(2)}) copy-start(f32[512,128]{1,0:T(8,128)} %refs_7_.1) | copy-start | bytes 786436
  24.5 9.2 %collective-permute-start.7 = (bf16[8,256,128]{2,1,0:T(8,128)(2,1)S(1)}, bf16[8,256,128]{2,1,0:T(8,128)(2,1)S(1)}, u32[]{:S(2)}, u32[]{:S(2)}) collective-permute-start(bf16[8,256,128]{2,1,0:T(8,128)(2,1)S(1)} %constant_dynamic-update-slice_fusion.refs_4_), channel_id=1, source_target_pairs={{0,8},{1,3},{2,10},{3,1},{4,12},{5,7},{6,14},{7,5},{8,0},{9,11},{1... | collective-permute-start | bytes 1572872 | tf_op jit(solution)/shard_map/ppermute | solution.py:360
  26.0 6.9 %collective-permute-start.6 = (bf16[4,256,128]{2,1,0:T(8,128)(2,1)S(1)}, bf16[4,256,128]{2,1,0:T(8,128)(2,1)S(1)}, u32[]{:S(2)}, u32[]{:S(2)}) collective-permute-start(bf16[4,256,128]{2,1,0:T(8,128)(2,1)S(1)} %get-tuple-element.52), channel_id=1, source_target_pairs={{0,4},{1,5},{2,6},{3,7},{4,0},{5,1},{6,2},{7,3},{8,12},{9,13},{10,... | collective-permute-start | bytes 786440 | tf_op jit(solution)/shard_map/ppermute | solution.py:360
  27.6 13.6 %collective-permute-start.10 = (bf16[8,256,128]{2,1,0:T(8,128)(2,1)S(1)}, bf16[8,256,128]{2,1,0:T(8,128)(2,1)S(1)}, u32[]{:S(2)}, u32[]{:S(2)}) collective-permute-start(bf16[8,256,128]{2,1,0:T(8,128)(2,1)S(1)} %constant_dynamic-update-slice_fusion.refs_4_), channel_id=1, source_target_pairs={{0,1},{1,0},{2,3},{3,2},{4,5},{5,4},{6,7},{7,6},{8,9},{9,8},{10,11... | collective-permute-start | bytes 1572872 | tf_op jit(solution)/shard_map/ppermute | solution.py:440
  33.7 13.7 %copy-start.4 = (bf16[8,256,128]{2,1,0:T(8,128)(2,1)}, bf16[8,256,128]{2,1,0:T(8,128)(2,1)S(1)}, u32[]{:S(2)}) copy-start(bf16[8,256,128]{2,1,0:T(8,128)(2,1)S(1)} %collective-permute-done.7.refs_5_) | copy-start | bytes 1572868
  33.8 11.5 %collective-permute-start.11 = (bf16[8,256,128]{2,1,0:T(8,128)(2,1)S(1)}, bf16[8,256,128]{2,1,0:T(8,128)(2,1)S(1)}, u32[]{:S(2)}, u32[]{:S(2)}) collective-permute-start(bf16[8,256,128]{2,1,0:T(8,128)(2,1)S(1)} %collective-permute-done.7.refs_5_), channel_id=1, source_target_pairs={{0,1},{1,0},{2,3},{3,2},{4,5},{5,4},{6,7},{7,6},{8,9},{9,8},{10,11... | collective-permute-start | bytes 1572872 | tf_op jit(solution)/shard_map/ppermute | solution.py:440
  33.9 5.0 %collective-permute-start.8 = (bf16[2,256,128]{2,1,0:T(8,128)(2,1)S(1)}, bf16[2,256,128]{2,1,0:T(8,128)(2,1)S(1)}, u32[]{:S(2)}, u32[]{:S(2)}) collective-permute-start(bf16[2,256,128]{2,1,0:T(8,128)(2,1)S(1)} %get-tuple-element.84), channel_id=1, source_target_pairs={{0,8},{1,3},{2,10},{3,1},{4,12},{5,7},{6,14},{7,5},{8,0},{9,11},{1... | collective-permute-start | bytes 393224 | tf_op jit(solution)/shard_map/ppermute | solution.py:360
  39.0 6.2 %collective-permute-start.9 = (bf16[1,256,128]{2,1,0:T(8,128)(2,1)S(1)}, bf16[1,256,128]{2,1,0:T(8,128)(2,1)S(1)}, u32[]{:S(2)}, u32[]{:S(2)}) collective-permute-start(bf16[1,256,128]{2,1,0:T(8,128)(2,1)S(1)} %get-tuple-element.85), channel_id=1, source_target_pairs={{0,16},{1,17},{2,18},{3,19},{4,20},{5,21},{6,22},{7,23},{8,24},{9,... | collective-permute-start | bytes 196616 | tf_op jit(solution)/shard_map/ppermute | solution.py:360
  41.2 4.1 %copy-start.5 = (bf16[8,256,128]{2,1,0:T(8,128)(2,1)}, bf16[8,256,128]{2,1,0:T(8,128)(2,1)S(1)}, u32[]{:S(2)}) copy-start(bf16[8,256,128]{2,1,0:T(8,128)(2,1)S(1)} %collective-permute-done.10.refs_6_) | copy-start | bytes 1572868
  45.2 0.8 %copy-start.6 = (bf16[8,256,128]{2,1,0:T(8,128)(2,1)}, bf16[8,256,128]{2,1,0:T(8,128)(2,1)S(1)}, u32[]{:S(2)}) copy-start(bf16[8,256,128]{2,1,0:T(8,128)(2,1)S(1)} %collective-permute-done.11.refs_7_) | copy-start | bytes 1572868
  47.4 14.4 %all-to-all-start = ((bf16[16,56,128]{2,1,0:T(8,128)(2,1)}), bf16[16,56,128]{2,1,0:T(8,128)(2,1)S(1)}, u32[]{:S(2)}, u32[]{:S(2)}) async-start(bf16[16,56,128]{2,1,0:T(8,128)(2,1)} %shard_map.130), calls=%async_computation | async-start | bytes 458752 | tf_op jit(solution)/shard_map/all_to_all | solution.py:500
  61.8 1.5 %collective-permute-start.12 = (bf16[16,56,128]{2,1,0:T(8,128)(2,1)S(1)}, bf16[16,56,128]{2,1,0:T(8,128)(2,1)S(1)}, u32[]{:S(2)}, u32[]{:S(2)}) collective-permute-start(bf16[16,56,128]{2,1,0:T(8,128)(2,1)S(1)} %all-to-all-done.refs_4_), channel_id=1, source_target_pairs={{0,1},{1,0},{2,3},{3,2},{4,5},{5,4},{6,7},{7,6},{8,9},{9,8},{10,11... | collective-permute-start | bytes 688136 | tf_op jit(solution)/shard_map/ppermute | solution.py:503

commit v9 on v8

--- a/solution.py
+++ b/solution.py
@@ -336,10 +336,11 @@
 
     units = source_map.reshape(1, D_NEW)
     gain = gain_old.reshape(D_OLD // LANES, LANES)
-    staged = rep_count == 2 and dp_count >= 4
+    staged = rep_count == 2 and dp_count >= 8
     bits = dp_count.bit_length() - 1
     line = list(range(bits - 1))
-    halving = [line + [bits - 1], line[::-1] + [bits - 1]]
+    ends = [line[:1] + line[-1:], line[-1:] + line[:1]]
+    halving = [pair + line[1:-1] + [bits - 1] for pair in ends]
     doubling = [[bits - 1] + line, [bits - 1] + line[::-1]]
     if staged:
         rels = [
@@ -374,7 +375,7 @@
             shape((tiles, LANES), F32),
             shape((tokens, LANES), F32),
             *[pltpu.VMEM((dp_count // parts, part, LANES), F32)] * parts,
-            *[pltpu.VMEM((rep_count - 1, dp_count // parts, part, LANES), BF16)] * parts,
+            *[shape((rep_count - 1, dp_count // parts, part, LANES), BF16)] * parts,
         ),
         [SMEM_SPEC] + [VMEM_SPEC] * 2 + [any_spec] + [VMEM_SPEC],
         [
@@ -394,7 +395,7 @@
     def indices(src):
         return call(
             lambda *refs: index_kernel(dp_count, cap, slots, table_rows, *refs),
-            3,
+            0,
             (
                 pltpu.VMEM((table_rows * LANES, cap), BF16),
                 pltpu.VMEM((1, table_rows * LANES), F32),
@@ -413,31 +414,36 @@
     dense = [pltpu.VMEM((D_OLD + cap, LANES), F32), pltpu.VMEM((tokens, D_OLD), BF16)]
     if staged:
         half = dp_count // 2
-        send, sent = lax.optimization_barrier((others[1][0], sent))
         mine = lax.axis_index("rep") * part
-        gathered = [lax.dynamic_slice_in_dim(block, mine, part)[None] for block in (weight_old, sent)]
-        gathered = jnp.concatenate(gathered)
-        sent = across(gathered, doubling, 1)
-        pair, gathered = lax.optimization_barrier((lax.ppermute(send, "rep", swap), gathered))
-        high = (owns[1] + pair.astype(F32)).astype(BF16)
-        low = owns[0] + lax.ppermute(others[0][0], "rep", swap).astype(F32)
+        with jax.named_scope("weights_1"):
+            send, sent = lax.optimization_barrier((others[1][0], sent))
+            gathered = [lax.dynamic_slice_in_dim(block, mine, part)[None] for block in (weight_old, sent)]
+            gathered = jnp.concatenate(gathered)
+            sent = across(gathered, doubling, 1)
+        with jax.named_scope("pair_exchange"):
+            pair, gathered = lax.optimization_barrier((lax.ppermute(send, "rep", swap), gathered))
+            high = (owns[1] + pair.astype(F32)).astype(BF16)
+            low = owns[0] + lax.ppermute(others[0][0], "rep", swap).astype(F32)
+        chosen, keep, own_gain, offset = indices(source_map)
         for stage in range(bits - 1):
-            came = across(high, halving, stage)
+            with jax.named_scope(f"gradient_{stage + 1}"):
+                came = across(high, halving, stage)
             if stage < bits - 2:
-                gathered = jnp.concatenate([gathered, sent])
-                sent = across(gathered, doubling, stage + 2)
+                with jax.named_scope(f"weights_{stage + 2}"):
+                    gathered = jnp.concatenate([gathered, sent])
+                    sent = across(gathered, doubling, stage + 2)
+            if stage != 1:
                 came, sent = lax.optimization_barrier((came, sent))
             if stage == 1:
                 came, chosen = lax.optimization_barrier((came, chosen))
             came = came.astype(F32)
             half = half // 2
             low, high = low[:half] + came[:half], (low[half:] + came[half:]).astype(BF16)
-            if stage == 0:
-                high, late_src = lax.optimization_barrier((high, source_map))
-                chosen, keep, own_gain, offset = indices(late_src)
-        came = across(high, halving, bits - 1)
-        pieces = [gathered, sent]
-        pieces += [lax.ppermute(piece, "rep", swap) for piece in pieces]
+        with jax.named_scope("gradient_last"):
+            came = across(high, halving, bits - 1)
+        with jax.named_scope("weights_pair"):
+            pieces = [gathered, sent]
+            pieces += [lax.ppermute(piece, "rep", swap) for piece in pieces]
         came, *pieces = lax.optimization_barrier((came, *pieces))
         reduced = [resident(low), resident(came)]
         projected = call(

time: 67.5 us -> 67.1 us (level)
  other arithmetic: 2.67 us -> 0.59 us
  waiting for transfers between devices: 18.7 us -> 20.5 us
    all_to_all x1, waiting for transfers between devices: 1.43 us -> 2.56 us  [on_device(): moved = [lax.all_to_all(packed, 'dp', split_axis=0, concat_axis=0)]]
    convert_element_type x1, other arithmetic: 1.15 us -> 0.11 us  [on_device(): high = (owns[1] + pair.astype(F32)).astype(BF16)]
    add x1, other arithmetic: 1.13 us -> 0.09 us  [on_device(): low = owns[0] + lax.ppermute(others[0][0], 'rep', swap).astype(F32)]
    ppermute x8, waiting for transfers between devices: 15.8 us -> 16.5 us  [across(): return lax.ppermute(value, ('dp', 'rep'), pairs)]
  transfers between devices with their start and end apart: 14 -> 14, of which waited for: 9 -> 9; matrix products, arithmetic and copies ran while one was open for 4% -> 1% of each run, Pallas kernels for 25% -> 26%
where the time goes in v9:
time: 67.1 us; the launch traced here: 66.6 us
  Pallas kernels  22.1 us (33%)
  starting transfers between devices  21.6 us (32%)
  waiting for transfers between devices  20.5 us (31%)
  local copies, waits for them, and re-layouts  0.9 us (1%)
  between operations  0.81 us (1%)
    pallas_call x6, Pallas kernels, call(): pl.pallas_call(kernel, out_shape=out_shape, in_specs=specs, out_specs=out...  22.1 us
    ppermute x8, waiting for transfers between devices, across(): return lax.ppermute(value, ('dp', 'rep'), pairs)  16.5 us
    ppermute x8, starting transfers between devices, across(): return lax.ppermute(value, ('dp', 'rep'), pairs)  14.8 us
    all_to_all x1, starting transfers between devices, on_device(): moved = [lax.all_to_all(packed, 'dp', split_axis=0, concat_axis=0)]  6.27 us
    all_to_all x1, waiting for transfers between devices, on_device(): moved = [lax.all_to_all(packed, 'dp', split_axis=0, concat_axis=0)]  2.56 us
    ppermute x1, waiting for transfers between devices, on_device(): moved = [arrived, lax.ppermute(arrived, 'rep', swap)]  1.49 us
  transfers between devices with their start and end apart: 14, of which 9 were waited for; matrix products, arithmetic and copies ran while one was open for 1% of the time, Pallas kernels for 26%

profile of v9, /device:TPU:0, one launch (start us, length us, event | category | flops | bytes accessed | tf_op | source)
XLA Modules:
  0.0 66.6 jit_solution(4740761605249829633)
XLA Ops:
  0.6 4.1 %collective-permute-start.1 = (bf16[512,128]{1,0:T(8,128)(2,1)}, bf16[512,128]{1,0:T(8,128)(2,1)S(1)}, u32[]{:S(2)}, u32[]{:S(2)}) collective-permute-start(bf16[512,128]{1,0:T(8,128)(2,1)} %refs_5_.1), channel_id=1, source_target_pairs={{0,16},{1,17},{2,18},{3,19},{4,20},{5,21},{6,22},{7,23},{8,24},{9,... | collective-permute-start | bytes 393224 | tf_op jit(solution)/shard_map/ppermute | solution.py:361
  4.7 6.3 %shard_map.128 = (f32[48,128]{1,0:T(8,128)}, f32[256,128]{1,0:T(8,128)}, f32[8,256,128]{2,1,0:T(8,128)S(1)}, f32[8,256,128]{2,1,0:T(8,128)S(1)}, bf16[1,8,256,12...) custom-call(s32[17]{0:T(128)} %refs_0_.8, s32[1,8192]{1,0:T(1,128)} %bitcast.9, f32[48,128]{1,0:T(8,128)} %bitcast.11, ...), custom_call_target="tpu_custom_call" | custom-call | bytes 24000000 | tf_op jit(solution)/shard_map/pallas_call | solution.py:304
  11.1 0.2 collective-permute-done.1
  11.3 0.5 collective-permute-start
  11.8 1.6 %collective-permute-start.4 = (bf16[2,256,128]{2,1,0:T(8,128)(2,1)S(1)}, bf16[2,256,128]{2,1,0:T(8,128)(2,1)S(1)}, u32[]{:S(2)}, u32[]{:S(2)}) collective-permute-start(bf16[2,256,128]{2,1,0:T(8,128)(2,1)S(1)} %pad_maximum_fusion.1), channel_id=1, source_target_pairs={{0,2},{1,9},{2,0},{3,11},{4,6},{5,13},{6,4},{7,15},{8,10},{9,1},{1... | collective-permute-start | bytes 393224 | tf_op jit(solution)/shard_map/weights_1/ppermute | solution.py:361
  13.4 0.1 add_convert_fusion
  13.5 1.5 %collective-permute-start.3 = (bf16[8,256,128]{2,1,0:T(8,128)(2,1)S(1)}, bf16[8,256,128]{2,1,0:T(8,128)(2,1)S(1)}, u32[]{:S(2)}, u32[]{:S(2)}) collective-permute-start(bf16[8,256,128]{2,1,0:T(8,128)(2,1)S(1)} %add_convert_fusion), channel_id=1, source_target_pairs={{0,2},{1,9},{2,0},{3,11},{4,6},{5,13},{6,4},{7,15},{8,10},{9,1},{1... | collective-permute-start | bytes 1572872 | tf_op jit(solution)/shard_map/gradient_1/ppermute | solution.py:361
  15.1 1.8 %collective-permute-done.4 = bf16[2,256,128]{2,1,0:T(8,128)(2,1)S(1)} collective-permute-done((bf16[2,256,128]{2,1,0:T(8,128)(2,1)S(1)}, bf16[2,256,128]{2,1,0:T(8,128)(2,1)S(1)}, u32[]{:S(2)}, u32[]{:S(2)}) %collective-permute-start.4) | collective-permute-done | bytes 131104 | tf_op jit(solution)/shard_map/weights_1/ppermute | solution.py:361
  16.9 1.6 %collective-permute-start.5 = (bf16[4,256,128]{2,1,0:T(8,128)(2,1)S(1)}, bf16[4,256,128]{2,1,0:T(8,128)(2,1)S(1)}, u32[]{:S(2)}, u32[]{:S(2)}) collective-permute-start(bf16[4,256,128]{2,1,0:T(8,128)(2,1)S(1)} %pad_maximum_fusion), channel_id=1, source_target_pairs={{0,4},{1,5},{2,6},{3,7},{4,0},{5,1},{6,2},{7,3},{8,12},{9,13},{10,... | collective-permute-start | bytes 786440 | tf_op jit(solution)/shard_map/weights_2/ppermute | solution.py:361
  18.5 0.1 convert_add_fusion
  18.7 5.6 %collective-permute-done.5 = bf16[4,256,128]{2,1,0:T(8,128)(2,1)S(1)} collective-permute-done((bf16[4,256,128]{2,1,0:T(8,128)(2,1)S(1)}, bf16[4,256,128]{2,1,0:T(8,128)(2,1)S(1)}, u32[]{:S(2)}, u32[]{:S(2)}) %collective-permute-start.5) | collective-permute-done | bytes 262176 | tf_op jit(solution)/shard_map/weights_2/ppermute | solution.py:361
  24.3 0.1 convert_element_type.30
  24.4 0.0 copy-start.2
  24.4 0.1 slice_add_fusion
  24.6 1.6 %collective-permute-start.6 = (bf16[4,256,128]{2,1,0:T(8,128)(2,1)S(1)}, bf16[4,256,128]{2,1,0:T(8,128)(2,1)S(1)}, u32[]{:S(2)}, u32[]{:S(2)}) collective-permute-start(bf16[4,256,128]{2,1,0:T(8,128)(2,1)S(1)} %get-tuple-element.78), channel_id=1, source_target_pairs={{0,8},{1,3},{2,10},{3,1},{4,12},{5,7},{6,14},{7,5},{8,0},{9,11},{1... | collective-permute-start | bytes 786440 | tf_op jit(solution)/shard_map/gradient_2/ppermute | solution.py:361
  26.2 0.5 collective-permute-start.8
  26.8 3.9 %shard_map.129 = (bf16[640,512]{1,0:T(8,128)(2,1)S(1)}, f32[1,640]{1,0:T(1,128)S(1)}, f32[1,512]{1,0:T(1,128)S(1)}, s32[1]{0:T(128)}) custom-call(s32[17]{0:T(128)} %refs_0_.8, s32[17]{0:T(128)} %refs_0_.9, s32[8192]{0:T(1024)} %refs_2_.1, f32[48,128]{1,0:T(8,128)} %bitcast.12), custom_call_target="tpu_custom_call" | custom-call | tf_op jit(solution)/shard_map/pallas_call | solution.py:304
  30.7 0.3 collective-permute-done.6
  31.0 0.1 slice_add_fusion.3
  31.1 1.6 %collective-permute-start.7 = (bf16[2,256,128]{2,1,0:T(8,128)(2,1)S(1)}, bf16[2,256,128]{2,1,0:T(8,128)(2,1)S(1)}, u32[]{:S(2)}, u32[]{:S(2)}) collective-permute-start(bf16[2,256,128]{2,1,0:T(8,128)(2,1)S(1)} %get-tuple-element.80), channel_id=1, source_target_pairs={{0,4},{1,5},{2,6},{3,7},{4,0},{5,1},{6,2},{7,3},{8,12},{9,13},{10,... | collective-permute-start | bytes 393224 | tf_op jit(solution)/shard_map/gradient_3/ppermute | solution.py:361
  32.7 3.4 %collective-permute-done.7 = bf16[2,256,128]{2,1,0:T(8,128)(2,1)S(1)} collective-permute-done((bf16[2,256,128]{2,1,0:T(8,128)(2,1)S(1)}, bf16[2,256,128]{2,1,0:T(8,128)(2,1)S(1)}, u32[]{:S(2)}, u32[]{:S(2)}) %collective-permute-start.7) | collective-permute-done | bytes 131104 | tf_op jit(solution)/shard_map/gradient_3/ppermute | solution.py:361
  36.1 0.5 collective-permute-done.8.refs_5_
  36.7 2.2 %collective-permute-start.9 = (bf16[1,256,128]{2,1,0:T(8,128)(2,1)S(1)}, bf16[1,256,128]{2,1,0:T(8,128)(2,1)S(1)}, u32[]{:S(2)}, u32[]{:S(2)}) collective-permute-start(bf16[1,256,128]{2,1,0:T(8,128)(2,1)S(1)} %get-tuple-element.81), channel_id=1, source_target_pairs={{0,16},{1,17},{2,18},{3,19},{4,20},{5,21},{6,22},{7,23},{8,24},{9,... | collective-permute-start | bytes 196616 | tf_op jit(solution)/shard_map/gradient_last/ppermute | solution.py:361
  38.8 4.7 %collective-permute-done.9.refs_4_ = bf16[1,256,128]{2,1,0:T(8,128)(2,1)S(1)} collective-permute-done((bf16[1,256,128]{2,1,0:T(8,128)(2,1)S(1)}, bf16[1,256,128]{2,1,0:T(8,128)(2,1)S(1)}, u32[]{:S(2)}, u32[]{:S(2)}) %collective-permute-start.9) | collective-permute-done | bytes 65568 | tf_op jit(solution)/shard_map/gradient_last/ppermute | solution.py:361
  43.6 0.8 %copy-done.6 = bf16[8,256,128]{2,1,0:T(8,128)(2,1)} copy-done((bf16[8,256,128]{2,1,0:T(8,128)(2,1)}, bf16[8,256,128]{2,1,0:T(8,128)(2,1)S(1)}, u32[]{:S(2)}) %copy-start.6) | copy-done | bytes 524312
  44.4 1.4 %shard_map.130 = bf16[16,56,128]{2,1,0:T(8,128)(2,1)} custom-call(bf16[640,512]{1,0:T(8,128)(2,1)S(1)} %get-tuple-element.51.refs_0_, f32[1,640]{1,0:T(1,128)S(1)} %get-tuple-element.52.refs_1_, f32[1,512]{1,0:T(1,128)S(1)} %get-tuple-element.53.refs_2_, f32[1,256,128]{2,1,0:T(8,128)S(1)} %get-tuple-element.82.refs_3_, ...), custom_call_target="tpu_custom_call" | custom-call | bytes 9000000 | tf_op jit(solution)/shard_map/pallas_call | solution.py:304
  45.8 6.3 %all-to-all-start = ((bf16[16,56,128]{2,1,0:T(8,128)(2,1)}), bf16[16,56,128]{2,1,0:T(8,128)(2,1)S(1)}, u32[]{:S(2)}, u32[]{:S(2)}) async-start(bf16[16,56,128]{2,1,0:T(8,128)(2,1)} %shard_map.130), calls=%async_computation | async-start | bytes 458752 | tf_op jit(solution)/shard_map/all_to_all | solution.py:506
  52.0 1.5 %shard_map.132 = (s32[1,8192]{1,0:T(1,128)S(1)}, bf16[160,8192]{1,0:T(8,128)(2,1)S(1)}) custom-call(s32[17]{0:T(128)} %refs_0_.8, s32[17]{0:T(128)} %refs_0_.9, s32[1,8192]{1,0:T(1,128)} %bitcast.10), custom_call_target="tpu_custom_call" | custom-call | bytes 6000000 | tf_op jit(solution)/shard_map/pallas_call | solution.py:304
  53.5 5.4 %shard_map.131 = bf16[256,128]{1,0:T(8,128)(2,1)} custom-call(s32[17]{0:T(128)} %refs_0_.8, bf16[256,6144]{1,0:T(8,128)(2,1)} %refs_1_.4, f32[256,128]{1,0:T(8,128)} %get-tuple-element.60.refs_2_, f32[48,128]{1,0:T(8,128)} %get-tuple-element.61.refs_3_, bf16[8,256,128]{2,1,0:T(8,128)(2,1)} %copy-done.3, bf16[8,256,128]{2,1,0:T(8,128)(2,1)} %copy-done.4, ...), custom_call_target="tpu_custom_call" | custom-call | bytes 18000000 | tf_op jit(solution)/shard_map/pallas_call | solution.py:304
  59.0 2.6 %all-to-all-done.refs_4_ = bf16[16,56,128]{2,1,0:T(8,128)(2,1)S(1)} async-done(((bf16[16,56,128]{2,1,0:T(8,128)(2,1)}), bf16[16,56,128]{2,1,0:T(8,128)(2,1)S(1)}, u32[]{:S(2)}, u32[]{:S(2)}) %all-to-all-start) | async-done | bytes 229408 | tf_op jit(solution)/shard_map/all_to_all | solution.py:506
  61.5 1.5 %collective-permute-done.12.refs_5_ = bf16[16,56,128]{2,1,0:T(8,128)(2,1)S(1)} collective-permute-done((bf16[16,56,128]{2,1,0:T(8,128)(2,1)S(1)}, bf16[16,56,128]{2,1,0:T(8,128)(2,1)S(1)}, u32[]{:S(2)}, u32[]{:S(2)}) %collective-permute-start.12) | collective-permute-done | bytes 229408 | tf_op jit(solution)/shard_map/ppermute | solution.py:509
  63.0 3.6 %shard_map.133 = (f32[1,8192]{1,0:T(1,128)}, f32[640,128]{1,0:T(8,128)}, f32[640,128]{1,0:T(8,128)}, f32[640,128]{1,0:T(8,128)}) custom-call(s32[17]{0:T(128)} %refs_0_.9, s32[1]{0:T(128)} %get-tuple-element.69.refs_1_, s32[1,8192]{1,0:T(1,128)S(1)} %get-tuple-element.70.refs_2_, bf16[160,8192]{1,0:T(8,128)(2,1)S(1)} %get-tuple-element.71.refs_3_, ...), custom_call_target="tpu_custom_call" | custom-call | bytes 12000000 | tf_op jit(solution)/shard_map/pallas_call | solution.py:304
  (31 shorter events, 0.3 us)
Async XLA Ops:
  0.6 11.1 %copy-start = (bf16[512,128]{1,0:T(8,128)(2,1)S(1)}, bf16[512,128]{1,0:T(8,128)(2,1)}, u32[]{:S(2)}) copy-start(bf16[512,128]{1,0:T(8,128)(2,1)} %refs_5_.1) | copy-start | bytes 393220
  0.6 10.6 %collective-permute-start.1 = (bf16[512,128]{1,0:T(8,128)(2,1)}, bf16[512,128]{1,0:T(8,128)(2,1)S(1)}, u32[]{:S(2)}, u32[]{:S(2)}) collective-permute-start(bf16[512,128]{1,0:T(8,128)(2,1)} %refs_5_.1), channel_id=1, source_target_pairs={{0,16},{1,17},{2,18},{3,19},{4,20},{5,21},{6,22},{7,23},{8,24},{9,... | collective-permute-start | bytes 393224 | tf_op jit(solution)/shard_map/ppermute | solution.py:361
  11.3 2.2 %collective-permute-start.2 = (bf16[8,256,128]{2,1,0:T(8,128)(2,1)}, bf16[8,256,128]{2,1,0:T(8,128)(2,1)S(1)}, u32[]{:S(2)}, u32[]{:S(2)}) collective-permute-start(bf16[8,256,128]{2,1,0:T(8,128)(2,1)} %bitcast.14), channel_id=1, source_target_pairs={{0,1},{1,0},{2,3},{3,2},{4,5},{5,4},{6,7},{7,6},{8,9},{9,8},{10,11... | collective-permute-start | bytes 1572872 | tf_op jit(solution)/shard_map/pair_exchange/ppermute | solution.py:424
  11.3 7.3 %collective-permute-start = (bf16[8,256,128]{2,1,0:T(8,128)(2,1)}, bf16[8,256,128]{2,1,0:T(8,128)(2,1)S(1)}, u32[]{:S(2)}, u32[]{:S(2)}) collective-permute-start(bf16[8,256,128]{2,1,0:T(8,128)(2,1)} %bitcast.13), channel_id=1, source_target_pairs={{0,1},{1,0},{2,3},{3,2},{4,5},{5,4},{6,7},{7,6},{8,9},{9,8},{10,11... | collective-permute-start | bytes 1572872 | tf_op jit(solution)/shard_map/pair_exchange/ppermute | solution.py:426
  11.8 5.0 %collective-permute-start.4 = (bf16[2,256,128]{2,1,0:T(8,128)(2,1)S(1)}, bf16[2,256,128]{2,1,0:T(8,128)(2,1)S(1)}, u32[]{:S(2)}, u32[]{:S(2)}) collective-permute-start(bf16[2,256,128]{2,1,0:T(8,128)(2,1)S(1)} %pad_maximum_fusion.1), channel_id=1, source_target_pairs={{0,2},{1,9},{2,0},{3,11},{4,6},{5,13},{6,4},{7,15},{8,10},{9,1},{1... | collective-permute-start | bytes 393224 | tf_op jit(solution)/shard_map/weights_1/ppermute | solution.py:361
  13.5 10.8 %collective-permute-start.3 = (bf16[8,256,128]{2,1,0:T(8,128)(2,1)S(1)}, bf16[8,256,128]{2,1,0:T(8,128)(2,1)S(1)}, u32[]{:S(2)}, u32[]{:S(2)}) collective-permute-start(bf16[8,256,128]{2,1,0:T(8,128)(2,1)S(1)} %add_convert_fusion), channel_id=1, source_target_pairs={{0,2},{1,9},{2,0},{3,11},{4,6},{5,13},{6,4},{7,15},{8,10},{9,1},{1... | collective-permute-start | bytes 1572872 | tf_op jit(solution)/shard_map/gradient_1/ppermute | solution.py:361
  16.9 7.4 %collective-permute-start.5 = (bf16[4,256,128]{2,1,0:T(8,128)(2,1)S(1)}, bf16[4,256,128]{2,1,0:T(8,128)(2,1)S(1)}, u32[]{:S(2)}, u32[]{:S(2)}) collective-permute-start(bf16[4,256,128]{2,1,0:T(8,128)(2,1)S(1)} %pad_maximum_fusion), channel_id=1, source_target_pairs={{0,4},{1,5},{2,6},{3,7},{4,0},{5,1},{6,2},{7,3},{8,12},{9,13},{10,... | collective-permute-start | bytes 786440 | tf_op jit(solution)/shard_map/weights_2/ppermute | solution.py:361
  24.4 20.0 %copy-start.1 = (f32[512,128]{1,0:T(8,128)S(1)}, f32[512,128]{1,0:T(8,128)}, u32[]{:S(2)}) copy-start(f32[512,128]{1,0:T(8,128)} %refs_6_.1) | copy-start | bytes 786436
  24.4 19.9 %copy-start.2 = (f32[512,128]{1,0:T(8,128)S(1)}, f32[512,128]{1,0:T(8,128)}, u32[]{:S(2)}) copy-start(f32[512,128]{1,0:T(8,128)} %refs_7_.1) | copy-start | bytes 786436
  24.6 6.4 %collective-permute-start.6 = (bf16[4,256,128]{2,1,0:T(8,128)(2,1)S(1)}, bf16[4,256,128]{2,1,0:T(8,128)(2,1)S(1)}, u32[]{:S(2)}, u32[]{:S(2)}) collective-permute-start(bf16[4,256,128]{2,1,0:T(8,128)(2,1)S(1)} %get-tuple-element.78), channel_id=1, source_target_pairs={{0,8},{1,3},{2,10},{3,1},{4,12},{5,7},{6,14},{7,5},{8,0},{9,11},{1... | collective-permute-start | bytes 786440 | tf_op jit(solution)/shard_map/gradient_2/ppermute | solution.py:361
  26.2 27.3 %copy-start.3 = (bf16[8,256,128]{2,1,0:T(8,128)(2,1)}, bf16[8,256,128]{2,1,0:T(8,128)(2,1)S(1)}, u32[]{:S(2)}) copy-start(bf16[8,256,128]{2,1,0:T(8,128)(2,1)S(1)} %constant_dynamic-update-slice_fusion.refs_4_) | copy-start | bytes 1572868
  26.2 10.4 %collective-permute-start.8 = (bf16[8,256,128]{2,1,0:T(8,128)(2,1)S(1)}, bf16[8,256,128]{2,1,0:T(8,128)(2,1)S(1)}, u32[]{:S(2)}, u32[]{:S(2)}) collective-permute-start(bf16[8,256,128]{2,1,0:T(8,128)(2,1)S(1)} %constant_dynamic-update-slice_fusion.refs_4_), channel_id=1, source_target_pairs={{0,8},{1,3},{2,10},{3,1},{4,12},{5,7},{6,14},{7,5},{8,0},{9,11},{1... | collective-permute-start | bytes 1572872 | tf_op jit(solution)/shard_map/weights_3/ppermute | solution.py:361
  31.1 5.0 %collective-permute-start.7 = (bf16[2,256,128]{2,1,0:T(8,128)(2,1)S(1)}, bf16[2,256,128]{2,1,0:T(8,128)(2,1)S(1)}, u32[]{:S(2)}, u32[]{:S(2)}) collective-permute-start(bf16[2,256,128]{2,1,0:T(8,128)(2,1)S(1)} %get-tuple-element.80), channel_id=1, source_target_pairs={{0,4},{1,5},{2,6},{3,7},{4,0},{5,1},{6,2},{7,3},{8,12},{9,13},{10,... | collective-permute-start | bytes 393224 | tf_op jit(solution)/shard_map/gradient_3/ppermute | solution.py:361
  32.7 6.1 %collective-permute-start.10 = (bf16[8,256,128]{2,1,0:T(8,128)(2,1)S(1)}, bf16[8,256,128]{2,1,0:T(8,128)(2,1)S(1)}, u32[]{:S(2)}, u32[]{:S(2)}) collective-permute-start(bf16[8,256,128]{2,1,0:T(8,128)(2,1)S(1)} %constant_dynamic-update-slice_fusion.refs_4_), channel_id=1, source_target_pairs={{0,1},{1,0},{2,3},{3,2},{4,5},{5,4},{6,7},{7,6},{8,9},{9,8},{10,11... | collective-permute-start | bytes 1572872 | tf_op jit(solution)/shard_map/weights_pair/ppermute | solution.py:446
  36.6 9.1 %copy-start.4 = (bf16[8,256,128]{2,1,0:T(8,128)(2,1)}, bf16[8,256,128]{2,1,0:T(8,128)(2,1)S(1)}, u32[]{:S(2)}) copy-start(bf16[8,256,128]{2,1,0:T(8,128)(2,1)S(1)} %collective-permute-done.8.refs_5_) | copy-start | bytes 1572868
  36.6 6.9 %collective-permute-start.11 = (bf16[8,256,128]{2,1,0:T(8,128)(2,1)S(1)}, bf16[8,256,128]{2,1,0:T(8,128)(2,1)S(1)}, u32[]{:S(2)}, u32[]{:S(2)}) collective-permute-start(bf16[8,256,128]{2,1,0:T(8,128)(2,1)S(1)} %collective-permute-done.8.refs_5_), channel_id=1, source_target_pairs={{0,1},{1,0},{2,3},{3,2},{4,5},{5,4},{6,7},{7,6},{8,9},{9,8},{10,11... | collective-permute-start | bytes 1572872 | tf_op jit(solution)/shard_map/weights_pair/ppermute | solution.py:446
  36.7 6.9 %collective-permute-start.9 = (bf16[1,256,128]{2,1,0:T(8,128)(2,1)S(1)}, bf16[1,256,128]{2,1,0:T(8,128)(2,1)S(1)}, u32[]{:S(2)}, u32[]{:S(2)}) collective-permute-start(bf16[1,256,128]{2,1,0:T(8,128)(2,1)S(1)} %get-tuple-element.81), channel_id=1, source_target_pairs={{0,16},{1,17},{2,18},{3,19},{4,20},{5,21},{6,22},{7,23},{8,24},{9,... | collective-permute-start | bytes 196616 | tf_op jit(solution)/shard_map/gradient_last/ppermute | solution.py:361
  38.8 4.7 %copy-start.5 = (bf16[8,256,128]{2,1,0:T(8,128)(2,1)}, bf16[8,256,128]{2,1,0:T(8,128)(2,1)S(1)}, u32[]{:S(2)}) copy-start(bf16[8,256,128]{2,1,0:T(8,128)(2,1)S(1)} %collective-permute-done.10.refs_6_) | copy-start | bytes 1572868
  43.6 0.8 %copy-start.6 = (bf16[8,256,128]{2,1,0:T(8,128)(2,1)}, bf16[8,256,128]{2,1,0:T(8,128)(2,1)S(1)}, u32[]{:S(2)}) copy-start(bf16[8,256,128]{2,1,0:T(8,128)(2,1)S(1)} %collective-permute-done.11.refs_7_) | copy-start | bytes 1572868
  45.8 15.8 %all-to-all-start = ((bf16[16,56,128]{2,1,0:T(8,128)(2,1)}), bf16[16,56,128]{2,1,0:T(8,128)(2,1)S(1)}, u32[]{:S(2)}, u32[]{:S(2)}) async-start(bf16[16,56,128]{2,1,0:T(8,128)(2,1)} %shard_map.130), calls=%async_computation | async-start | bytes 458752 | tf_op jit(solution)/shard_map/all_to_all | solution.py:506
  61.5 1.5 %collective-permute-start.12 = (bf16[16,56,128]{2,1,0:T(8,128)(2,1)S(1)}, bf16[16,56,128]{2,1,0:T(8,128)(2,1)S(1)}, u32[]{:S(2)}, u32[]{:S(2)}) collective-permute-start(bf16[16,56,128]{2,1,0:T(8,128)(2,1)S(1)} %all-to-all-done.refs_4_), channel_id=1, source_target_pairs={{0,1},{1,0},{2,3},{3,2},{4,5},{5,4},{6,7},{7,6},{8,9},{9,8},{10,11... | collective-permute-start | bytes 688136 | tf_op jit(solution)/shard_map/ppermute | solution.py:509

commit v10 on v9

--- a/solution.py
+++ b/solution.py
@@ -250,7 +250,7 @@
 
 def finish_kernel(dp_count, slots, table_rows, staged, nb, offset_in, places, tables, *rest):
     arrived, rest = (rest[:2], rest[2:]) if staged else (rest[:1], rest[1:])
-    gain_grad, first, second, adam, ones, twos, table = rest
+    gain_grad, first, second, adam, ones, twos, steps, table, sems = rest
     me = lax.axis_index("dp")
     offset = offset_in[0]
     groups = 1 if staged else 2
@@ -274,9 +274,15 @@
         )
     first_next = jnp.where(live, one, 0.0)
     second_next = jnp.where(live, two, 0.0)
-    first[...] = first_next
-    second[...] = second_next
-    adam[...] = first_next / (jnp.sqrt(second_next) + 1e-08)
+    ones[0:cap, :] = first_next
+    twos[0:cap, :] = second_next
+    steps[0:cap, :] = first_next / (jnp.sqrt(second_next) + 1e-08)
+    copies = [
+        pltpu.make_async_copy(rows.at[pl.ds(0, cap), :], out, sems.at[at])
+        for at, (rows, out) in enumerate(((ones, first), (twos, second), (steps, adam)))
+    ]
+    for copy in copies:
+        copy.start()
     at = groups * slots
     for p in range(dp_count):
         here = p * table_rows
@@ -292,15 +298,19 @@
         mask = lax.broadcasted_iota(jnp.int32, (LANES, step), 0) == places[:, start : start + step]
         value = jnp.where(mask, spread, 0.0)
         gain_grad[:, start : start + step] = jnp.sum(value, axis=0, keepdims=True)
+    for copy in copies:
+        copy.wait()
 
 
 def resident(value):
     return pltpu.with_memory_space_constraint(value, pltpu.VMEM)
 
 
-def call(kernel, micros, out_shape, specs, scratch, *args):
+def call(kernel, micros, out_shape, specs, scratch, *args, direct=None):
     scalars = jax.ShapeDtypeStruct((1,), jnp.int32)
-    out_specs = jax.tree.map(lambda out: SMEM_SPEC if out == scalars else VMEM_SPEC, out_shape)
+    any_spec = pl.BlockSpec(memory_space=pl.ANY)
+    spec_of = lambda out: SMEM_SPEC if out == scalars else any_spec if out == direct else VMEM_SPEC
+    out_specs = jax.tree.map(spec_of, out_shape)
     return pl.pallas_call(
         kernel,
         out_shape=out_shape,
@@ -444,7 +454,7 @@
         with jax.named_scope("weights_pair"):
             pieces = [gathered, sent]
             pieces += [lax.ppermute(piece, "rep", swap) for piece in pieces]
-        came, *pieces = lax.optimization_barrier((came, *pieces))
+        came, *pieces[:3] = lax.optimization_barrier((came, *pieces[:3]))
         reduced = [resident(low), resident(came)]
         projected = call(
             lambda *refs: project_kernel(dp_count, doubling, cap, *refs),
@@ -514,13 +524,14 @@
         4,
         (shape((1, D_NEW), F32), rows, rows, rows),
         [SMEM_SPEC] * 2 + [VMEM_SPEC] * (2 + len(moved)),
-        [pltpu.VMEM((dp_count * slots, LANES), F32)] * 2
-        + [pltpu.VMEM((dp_count * table_rows, LANES), F32)],
+        [pltpu.VMEM((dp_count * slots, LANES), F32)] * 3
+        + [pltpu.VMEM((dp_count * table_rows, LANES), F32), pltpu.SemaphoreType.DMA((3,))],
         new_bounds,
         offset,
         resident(places),
         resident(tables),
         *moved,
+        direct=rows,
     )
     return (projected, gain_grad.reshape(D_NEW), first_next, second_next, adam_step)
 

time: 67.1 us -> 67.4 us (level)
  local copies, waits for them, and re-layouts: 0.9 us -> 0.11 us
    unnamed x16 -> x12, local copies, waits for them, and re-layouts: 0.85 us -> 0.06 us
  transfers between devices with their start and end apart: 14 -> 14, of which waited for: 9 -> 8; matrix products, arithmetic and copies ran while one was open for 1% -> 1% of each run, Pallas kernels for 26% -> 28%
where the time goes in v10:
time: 67.4 us; the launch traced here: 66.9 us
  Pallas kernels  22.7 us (34%)
  starting transfers between devices  21.8 us (32%)
  waiting for transfers between devices  20.7 us (31%)
  between operations  0.99 us (1%)
    pallas_call x6, Pallas kernels, call(): pl.pallas_call(kernel, out_shape=out_shape, in_specs=specs, out_specs=out...  22.7 us
    ppermute x8, waiting for transfers between devices, across(): return lax.ppermute(value, ('dp', 'rep'), pairs)  16.6 us
    ppermute x8, starting transfers between devices, across(): return lax.ppermute(value, ('dp', 'rep'), pairs)  14.9 us
    all_to_all x1, starting transfers between devices, on_device(): moved = [lax.all_to_all(packed, 'dp', split_axis=0, concat_axis=0)]  6.28 us
    all_to_all x1, waiting for transfers between devices, on_device(): moved = [lax.all_to_all(packed, 'dp', split_axis=0, concat_axis=0)]  2.55 us
    ppermute x1, waiting for transfers between devices, on_device(): moved = [arrived, lax.ppermute(arrived, 'rep', swap)]  1.49 us
  transfers between devices with their start and end apart: 14, of which 8 were waited for; matrix products, arithmetic and copies ran while one was open for 1% of the time, Pallas kernels for 28%

profile of v10, /device:TPU:0, one launch (start us, length us, event | category | flops | bytes accessed | tf_op | source)
XLA Modules:
  0.0 66.9 jit_solution(3552075836527171623)
XLA Ops:
  0.6 4.1 %collective-permute-start.1 = (bf16[512,128]{1,0:T(8,128)(2,1)}, bf16[512,128]{1,0:T(8,128)(2,1)S(1)}, u32[]{:S(2)}, u32[]{:S(2)}) collective-permute-start(bf16[512,128]{1,0:T(8,128)(2,1)} %refs_5_.1), channel_id=1, source_target_pairs={{0,16},{1,17},{2,18},{3,19},{4,20},{5,21},{6,22},{7,23},{8,24},{9,... | collective-permute-start | bytes 393224 | tf_op jit(solution)/shard_map/ppermute | solution.py:371
  4.7 6.3 %shard_map.128 = (f32[48,128]{1,0:T(8,128)}, f32[256,128]{1,0:T(8,128)}, f32[8,256,128]{2,1,0:T(8,128)S(1)}, f32[8,256,128]{2,1,0:T(8,128)S(1)}, bf16[1,8,256,12...) custom-call(s32[17]{0:T(128)} %refs_0_.8, s32[1,8192]{1,0:T(1,128)} %bitcast.9, f32[48,128]{1,0:T(8,128)} %bitcast.11, ...), custom_call_target="tpu_custom_call" | custom-call | bytes 24000000 | tf_op jit(solution)/shard_map/pallas_call | solution.py:314
  11.1 0.2 collective-permute-done.1
  11.3 0.5 collective-permute-start
  11.8 1.6 %collective-permute-start.4 = (bf16[2,256,128]{2,1,0:T(8,128)(2,1)S(1)}, bf16[2,256,128]{2,1,0:T(8,128)(2,1)S(1)}, u32[]{:S(2)}, u32[]{:S(2)}) collective-permute-start(bf16[2,256,128]{2,1,0:T(8,128)(2,1)S(1)} %pad_maximum_fusion.1), channel_id=1, source_target_pairs={{0,2},{1,9},{2,0},{3,11},{4,6},{5,13},{6,4},{7,15},{8,10},{9,1},{1... | collective-permute-start | bytes 393224 | tf_op jit(solution)/shard_map/weights_1/ppermute | solution.py:371
  13.4 0.1 add_convert_fusion
  13.5 1.5 %collective-permute-start.3 = (bf16[8,256,128]{2,1,0:T(8,128)(2,1)S(1)}, bf16[8,256,128]{2,1,0:T(8,128)(2,1)S(1)}, u32[]{:S(2)}, u32[]{:S(2)}) collective-permute-start(bf16[8,256,128]{2,1,0:T(8,128)(2,1)S(1)} %add_convert_fusion), channel_id=1, source_target_pairs={{0,2},{1,9},{2,0},{3,11},{4,6},{5,13},{6,4},{7,15},{8,10},{9,1},{1... | collective-permute-start | bytes 1572872 | tf_op jit(solution)/shard_map/gradient_1/ppermute | solution.py:371
  15.1 1.8 %collective-permute-done.4 = bf16[2,256,128]{2,1,0:T(8,128)(2,1)S(1)} collective-permute-done((bf16[2,256,128]{2,1,0:T(8,128)(2,1)S(1)}, bf16[2,256,128]{2,1,0:T(8,128)(2,1)S(1)}, u32[]{:S(2)}, u32[]{:S(2)}) %collective-permute-start.4) | collective-permute-done | bytes 131104 | tf_op jit(solution)/shard_map/weights_1/ppermute | solution.py:371
  16.9 1.6 %collective-permute-start.5 = (bf16[4,256,128]{2,1,0:T(8,128)(2,1)S(1)}, bf16[4,256,128]{2,1,0:T(8,128)(2,1)S(1)}, u32[]{:S(2)}, u32[]{:S(2)}) collective-permute-start(bf16[4,256,128]{2,1,0:T(8,128)(2,1)S(1)} %pad_maximum_fusion), channel_id=1, source_target_pairs={{0,4},{1,5},{2,6},{3,7},{4,0},{5,1},{6,2},{7,3},{8,12},{9,13},{10,... | collective-permute-start | bytes 786440 | tf_op jit(solution)/shard_map/weights_2/ppermute | solution.py:371
  18.5 0.1 convert_add_fusion
  18.7 5.6 %collective-permute-done.5 = bf16[4,256,128]{2,1,0:T(8,128)(2,1)S(1)} collective-permute-done((bf16[4,256,128]{2,1,0:T(8,128)(2,1)S(1)}, bf16[4,256,128]{2,1,0:T(8,128)(2,1)S(1)}, u32[]{:S(2)}, u32[]{:S(2)}) %collective-permute-start.5) | collective-permute-done | bytes 262176 | tf_op jit(solution)/shard_map/weights_2/ppermute | solution.py:371
  24.3 0.1 convert_element_type.30
  24.4 0.0 copy-start.1
  24.4 0.1 slice_add_fusion
  24.6 1.6 %collective-permute-start.6 = (bf16[4,256,128]{2,1,0:T(8,128)(2,1)S(1)}, bf16[4,256,128]{2,1,0:T(8,128)(2,1)S(1)}, u32[]{:S(2)}, u32[]{:S(2)}) collective-permute-start(bf16[4,256,128]{2,1,0:T(8,128)(2,1)S(1)} %get-tuple-element.76), channel_id=1, source_target_pairs={{0,8},{1,3},{2,10},{3,1},{4,12},{5,7},{6,14},{7,5},{8,0},{9,11},{1... | collective-permute-start | bytes 786440 | tf_op jit(solution)/shard_map/gradient_2/ppermute | solution.py:371
  26.2 0.6 collective-permute-start.8
  26.8 3.9 %shard_map.129 = (bf16[640,512]{1,0:T(8,128)(2,1)S(1)}, f32[1,640]{1,0:T(1,128)S(1)}, f32[1,512]{1,0:T(1,128)S(1)}, s32[1]{0:T(128)}) custom-call(s32[17]{0:T(128)} %refs_0_.8, s32[17]{0:T(128)} %refs_0_.9, s32[8192]{0:T(1024)} %refs_2_.1, f32[48,128]{1,0:T(8,128)} %bitcast.12), custom_call_target="tpu_custom_call" | custom-call | tf_op jit(solution)/shard_map/pallas_call | solution.py:314
  30.7 0.1 collective-permute-start.10
  30.8 0.2 collective-permute-done.6
  31.0 0.1 slice_add_fusion.3
  31.1 1.6 %collective-permute-start.7 = (bf16[2,256,128]{2,1,0:T(8,128)(2,1)S(1)}, bf16[2,256,128]{2,1,0:T(8,128)(2,1)S(1)}, u32[]{:S(2)}, u32[]{:S(2)}) collective-permute-start(bf16[2,256,128]{2,1,0:T(8,128)(2,1)S(1)} %get-tuple-element.78), channel_id=1, source_target_pairs={{0,4},{1,5},{2,6},{3,7},{4,0},{5,1},{6,2},{7,3},{8,12},{9,13},{10,... | collective-permute-start | bytes 393224 | tf_op jit(solution)/shard_map/gradient_3/ppermute | solution.py:371
  32.7 4.1 %collective-permute-done.7 = bf16[2,256,128]{2,1,0:T(8,128)(2,1)S(1)} collective-permute-done((bf16[2,256,128]{2,1,0:T(8,128)(2,1)S(1)}, bf16[2,256,128]{2,1,0:T(8,128)(2,1)S(1)}, u32[]{:S(2)}, u32[]{:S(2)}) %collective-permute-start.7) | collective-permute-done | bytes 131104 | tf_op jit(solution)/shard_map/gradient_3/ppermute | solution.py:371
  36.9 0.1 collective-permute-start.11
  37.0 2.2 %collective-permute-start.9 = (bf16[1,256,128]{2,1,0:T(8,128)(2,1)S(1)}, bf16[1,256,128]{2,1,0:T(8,128)(2,1)S(1)}, u32[]{:S(2)}, u32[]{:S(2)}) collective-permute-start(bf16[1,256,128]{2,1,0:T(8,128)(2,1)S(1)} %get-tuple-element.79), channel_id=1, source_target_pairs={{0,16},{1,17},{2,18},{3,19},{4,20},{5,21},{6,22},{7,23},{8,24},{9,... | collective-permute-start | bytes 196616 | tf_op jit(solution)/shard_map/gradient_last/ppermute | solution.py:371
  39.1 4.7 %collective-permute-done.9.refs_4_ = bf16[1,256,128]{2,1,0:T(8,128)(2,1)S(1)} collective-permute-done((bf16[1,256,128]{2,1,0:T(8,128)(2,1)S(1)}, bf16[1,256,128]{2,1,0:T(8,128)(2,1)S(1)}, u32[]{:S(2)}, u32[]{:S(2)}) %collective-permute-start.9) | collective-permute-done | bytes 65568 | tf_op jit(solution)/shard_map/gradient_last/ppermute | solution.py:371
  43.8 1.4 %shard_map.130 = bf16[16,56,128]{2,1,0:T(8,128)(2,1)} custom-call(bf16[640,512]{1,0:T(8,128)(2,1)S(1)} %get-tuple-element.50.refs_0_, f32[1,640]{1,0:T(1,128)S(1)} %get-tuple-element.51.refs_1_, f32[1,512]{1,0:T(1,128)S(1)} %get-tuple-element.52.refs_2_, f32[1,256,128]{2,1,0:T(8,128)S(1)} %get-tuple-element.80.refs_3_, ...), custom_call_target="tpu_custom_call" | custom-call | bytes 9000000 | tf_op jit(solution)/shard_map/pallas_call | solution.py:314
  45.2 6.3 %all-to-all-start = ((bf16[16,56,128]{2,1,0:T(8,128)(2,1)}), bf16[16,56,128]{2,1,0:T(8,128)(2,1)S(1)}, u32[]{:S(2)}, u32[]{:S(2)}) async-start(bf16[16,56,128]{2,1,0:T(8,128)(2,1)} %shard_map.130), calls=%async_computation | async-start | bytes 458752 | tf_op jit(solution)/shard_map/all_to_all | solution.py:516
  51.5 1.5 %shard_map.132 = (s32[1,8192]{1,0:T(1,128)S(1)}, bf16[160,8192]{1,0:T(8,128)(2,1)S(1)}) custom-call(s32[17]{0:T(128)} %refs_0_.8, s32[17]{0:T(128)} %refs_0_.9, s32[1,8192]{1,0:T(1,128)} %bitcast.10), custom_call_target="tpu_custom_call" | custom-call | bytes 6000000 | tf_op jit(solution)/shard_map/pallas_call | solution.py:314
  53.0 5.4 %shard_map.131 = bf16[256,128]{1,0:T(8,128)(2,1)} custom-call(s32[17]{0:T(128)} %refs_0_.8, bf16[256,6144]{1,0:T(8,128)(2,1)} %refs_1_.4, f32[256,128]{1,0:T(8,128)} %get-tuple-element.59.refs_2_, f32[48,128]{1,0:T(8,128)} %get-tuple-element.60.refs_3_, bf16[8,256,128]{2,1,0:T(8,128)(2,1)} %copy-done.3, bf16[8,256,128]{2,1,0:T(8,128)(2,1)} %collective-permute-done.8.refs_5_, ...), custom_call_target="tpu_custom_call" | custom-call | bytes 18000000 | tf_op jit(solution)/shard_map/pallas_call | solution.py:314
  58.5 2.5 %all-to-all-done.refs_4_ = bf16[16,56,128]{2,1,0:T(8,128)(2,1)S(1)} async-done(((bf16[16,56,128]{2,1,0:T(8,128)(2,1)}), bf16[16,56,128]{2,1,0:T(8,128)(2,1)S(1)}, u32[]{:S(2)}, u32[]{:S(2)}) %all-to-all-start) | async-done | bytes 229408 | tf_op jit(solution)/shard_map/all_to_all | solution.py:516
  61.0 1.5 %collective-permute-done.12.refs_5_ = bf16[16,56,128]{2,1,0:T(8,128)(2,1)S(1)} collective-permute-done((bf16[16,56,128]{2,1,0:T(8,128)(2,1)S(1)}, bf16[16,56,128]{2,1,0:T(8,128)(2,1)S(1)}, u32[]{:S(2)}, u32[]{:S(2)}) %collective-permute-start.12) | collective-permute-done | bytes 229408 | tf_op jit(solution)/shard_map/ppermute | solution.py:519
  62.5 4.2 %shard_map.133 = (f32[1,8192]{1,0:T(1,128)}, f32[640,128]{1,0:T(8,128)}, f32[640,128]{1,0:T(8,128)}, f32[640,128]{1,0:T(8,128)}) custom-call(s32[17]{0:T(128)} %refs_0_.9, s32[1]{0:T(128)} %get-tuple-element.67.refs_1_, s32[1,8192]{1,0:T(1,128)S(1)} %get-tuple-element.68.refs_2_, bf16[160,8192]{1,0:T(8,128)(2,1)S(1)} %get-tuple-element.69.refs_3_, ...), custom_call_target="tpu_custom_call" | custom-call | bytes 12000000 | tf_op jit(solution)/shard_map/pallas_call | solution.py:314
  (27 shorter events, 0.3 us)
Async XLA Ops:
  0.6 11.1 %copy-start = (bf16[512,128]{1,0:T(8,128)(2,1)S(1)}, bf16[512,128]{1,0:T(8,128)(2,1)}, u32[]{:S(2)}) copy-start(bf16[512,128]{1,0:T(8,128)(2,1)} %refs_5_.1) | copy-start | bytes 393220
  0.6 10.6 %collective-permute-start.1 = (bf16[512,128]{1,0:T(8,128)(2,1)}, bf16[512,128]{1,0:T(8,128)(2,1)S(1)}, u32[]{:S(2)}, u32[]{:S(2)}) collective-permute-start(bf16[512,128]{1,0:T(8,128)(2,1)} %refs_5_.1), channel_id=1, source_target_pairs={{0,16},{1,17},{2,18},{3,19},{4,20},{5,21},{6,22},{7,23},{8,24},{9,... | collective-permute-start | bytes 393224 | tf_op jit(solution)/shard_map/ppermute | solution.py:371
  11.3 2.2 %collective-permute-start.2 = (bf16[8,256,128]{2,1,0:T(8,128)(2,1)}, bf16[8,256,128]{2,1,0:T(8,128)(2,1)S(1)}, u32[]{:S(2)}, u32[]{:S(2)}) collective-permute-start(bf16[8,256,128]{2,1,0:T(8,128)(2,1)} %bitcast.14), channel_id=1, source_target_pairs={{0,1},{1,0},{2,3},{3,2},{4,5},{5,4},{6,7},{7,6},{8,9},{9,8},{10,11... | collective-permute-start | bytes 1572872 | tf_op jit(solution)/shard_map/pair_exchange/ppermute | solution.py:434
  11.3 7.3 %collective-permute-start = (bf16[8,256,128]{2,1,0:T(8,128)(2,1)}, bf16[8,256,128]{2,1,0:T(8,128)(2,1)S(1)}, u32[]{:S(2)}, u32[]{:S(2)}) collective-permute-start(bf16[8,256,128]{2,1,0:T(8,128)(2,1)} %bitcast.13), channel_id=1, source_target_pairs={{0,1},{1,0},{2,3},{3,2},{4,5},{5,4},{6,7},{7,6},{8,9},{9,8},{10,11... | collective-permute-start | bytes 1572872 | tf_op jit(solution)/shard_map/pair_exchange/ppermute | solution.py:436
  11.8 5.0 %collective-permute-start.4 = (bf16[2,256,128]{2,1,0:T(8,128)(2,1)S(1)}, bf16[2,256,128]{2,1,0:T(8,128)(2,1)S(1)}, u32[]{:S(2)}, u32[]{:S(2)}) collective-permute-start(bf16[2,256,128]{2,1,0:T(8,128)(2,1)S(1)} %pad_maximum_fusion.1), channel_id=1, source_target_pairs={{0,2},{1,9},{2,0},{3,11},{4,6},{5,13},{6,4},{7,15},{8,10},{9,1},{1... | collective-permute-start | bytes 393224 | tf_op jit(solution)/shard_map/weights_1/ppermute | solution.py:371
  13.5 10.8 %collective-permute-start.3 = (bf16[8,256,128]{2,1,0:T(8,128)(2,1)S(1)}, bf16[8,256,128]{2,1,0:T(8,128)(2,1)S(1)}, u32[]{:S(2)}, u32[]{:S(2)}) collective-permute-start(bf16[8,256,128]{2,1,0:T(8,128)(2,1)S(1)} %add_convert_fusion), channel_id=1, source_target_pairs={{0,2},{1,9},{2,0},{3,11},{4,6},{5,13},{6,4},{7,15},{8,10},{9,1},{1... | collective-permute-start | bytes 1572872 | tf_op jit(solution)/shard_map/gradient_1/ppermute | solution.py:371
  16.9 7.4 %collective-permute-start.5 = (bf16[4,256,128]{2,1,0:T(8,128)(2,1)S(1)}, bf16[4,256,128]{2,1,0:T(8,128)(2,1)S(1)}, u32[]{:S(2)}, u32[]{:S(2)}) collective-permute-start(bf16[4,256,128]{2,1,0:T(8,128)(2,1)S(1)} %pad_maximum_fusion), channel_id=1, source_target_pairs={{0,4},{1,5},{2,6},{3,7},{4,0},{5,1},{6,2},{7,3},{8,12},{9,13},{10,... | collective-permute-start | bytes 786440 | tf_op jit(solution)/shard_map/weights_2/ppermute | solution.py:371
  24.4 19.4 %copy-start.1 = (f32[512,128]{1,0:T(8,128)S(1)}, f32[512,128]{1,0:T(8,128)}, u32[]{:S(2)}) copy-start(f32[512,128]{1,0:T(8,128)} %refs_6_.1) | copy-start | bytes 786436
  24.4 19.4 %copy-start.2 = (f32[512,128]{1,0:T(8,128)S(1)}, f32[512,128]{1,0:T(8,128)}, u32[]{:S(2)}) copy-start(f32[512,128]{1,0:T(8,128)} %refs_7_.1) | copy-start | bytes 786436
  24.6 6.4 %collective-permute-start.6 = (bf16[4,256,128]{2,1,0:T(8,128)(2,1)S(1)}, bf16[4,256,128]{2,1,0:T(8,128)(2,1)S(1)}, u32[]{:S(2)}, u32[]{:S(2)}) collective-permute-start(bf16[4,256,128]{2,1,0:T(8,128)(2,1)S(1)} %get-tuple-element.76), channel_id=1, source_target_pairs={{0,8},{1,3},{2,10},{3,1},{4,12},{5,7},{6,14},{7,5},{8,0},{9,11},{1... | collective-permute-start | bytes 786440 | tf_op jit(solution)/shard_map/gradient_2/ppermute | solution.py:371
  26.2 26.8 %copy-start.3 = (bf16[8,256,128]{2,1,0:T(8,128)(2,1)}, bf16[8,256,128]{2,1,0:T(8,128)(2,1)S(1)}, u32[]{:S(2)}) copy-start(bf16[8,256,128]{2,1,0:T(8,128)(2,1)S(1)} %constant_dynamic-update-slice_fusion.refs_4_) | copy-start | bytes 1572868
  26.2 10.6 %collective-permute-start.8 = (bf16[8,256,128]{2,1,0:T(8,128)(2,1)S(1)}, bf16[8,256,128]{2,1,0:T(8,128)(2,1)}, u32[]{:S(2)}, u32[]{:S(2)}) collective-permute-start(bf16[8,256,128]{2,1,0:T(8,128)(2,1)S(1)} %constant_dynamic-update-slice_fusion.refs_4_), channel_id=1, source_target_pairs={{0,8},{1,3},{2,10},{3,1},{4,12},{5,7},{6,14},{7,5},{8,0},{9,11},{1... | collective-permute-start | bytes 1572872 | tf_op jit(solution)/shard_map/weights_3/ppermute | solution.py:371
  30.7 8.5 %collective-permute-start.10 = (bf16[8,256,128]{2,1,0:T(8,128)(2,1)S(1)}, bf16[8,256,128]{2,1,0:T(8,128)(2,1)S(1)}, u32[]{:S(2)}, u32[]{:S(2)}) collective-permute-start(bf16[8,256,128]{2,1,0:T(8,128)(2,1)S(1)} %constant_dynamic-update-slice_fusion.refs_4_), channel_id=1, source_target_pairs={{0,1},{1,0},{2,3},{3,2},{4,5},{5,4},{6,7},{7,6},{8,9},{9,8},{10,11... | collective-permute-start | bytes 1572872 | tf_op jit(solution)/shard_map/weights_pair/ppermute | solution.py:456
  31.1 5.7 %collective-permute-start.7 = (bf16[2,256,128]{2,1,0:T(8,128)(2,1)S(1)}, bf16[2,256,128]{2,1,0:T(8,128)(2,1)S(1)}, u32[]{:S(2)}, u32[]{:S(2)}) collective-permute-start(bf16[2,256,128]{2,1,0:T(8,128)(2,1)S(1)} %get-tuple-element.78), channel_id=1, source_target_pairs={{0,4},{1,5},{2,6},{3,7},{4,0},{5,1},{6,2},{7,3},{8,12},{9,13},{10,... | collective-permute-start | bytes 393224 | tf_op jit(solution)/shard_map/gradient_3/ppermute | solution.py:371
  36.9 16.2 %collective-permute-start.11 = (bf16[8,256,128]{2,1,0:T(8,128)(2,1)}, bf16[8,256,128]{2,1,0:T(8,128)(2,1)}, u32[]{:S(2)}, u32[]{:S(2)}) collective-permute-start(bf16[8,256,128]{2,1,0:T(8,128)(2,1)} %collective-permute-done.8.refs_5_), channel_id=1, source_target_pairs={{0,1},{1,0},{2,3},{3,2},{4,5},{5,4},{6,7},{7,6},{8,9},{9,8},{10,11... | collective-permute-start | bytes 1572872 | tf_op jit(solution)/shard_map/weights_pair/ppermute | solution.py:456
  37.0 6.9 %collective-permute-start.9 = (bf16[1,256,128]{2,1,0:T(8,128)(2,1)S(1)}, bf16[1,256,128]{2,1,0:T(8,128)(2,1)S(1)}, u32[]{:S(2)}, u32[]{:S(2)}) collective-permute-start(bf16[1,256,128]{2,1,0:T(8,128)(2,1)S(1)} %get-tuple-element.79), channel_id=1, source_target_pairs={{0,16},{1,17},{2,18},{3,19},{4,20},{5,21},{6,22},{7,23},{8,24},{9,... | collective-permute-start | bytes 196616 | tf_op jit(solution)/shard_map/gradient_last/ppermute | solution.py:371
  39.1 6.1 %copy-start.4 = (bf16[8,256,128]{2,1,0:T(8,128)(2,1)}, bf16[8,256,128]{2,1,0:T(8,128)(2,1)S(1)}, u32[]{:S(2)}) copy-start(bf16[8,256,128]{2,1,0:T(8,128)(2,1)S(1)} %collective-permute-done.10.refs_6_) | copy-start | bytes 1572868
  45.2 15.8 %all-to-all-start = ((bf16[16,56,128]{2,1,0:T(8,128)(2,1)}), bf16[16,56,128]{2,1,0:T(8,128)(2,1)S(1)}, u32[]{:S(2)}, u32[]{:S(2)}) async-start(bf16[16,56,128]{2,1,0:T(8,128)(2,1)} %shard_map.130), calls=%async_computation | async-start | bytes 458752 | tf_op jit(solution)/shard_map/all_to_all | solution.py:516
  61.0 1.5 %collective-permute-start.12 = (bf16[16,56,128]{2,1,0:T(8,128)(2,1)S(1)}, bf16[16,56,128]{2,1,0:T(8,128)(2,1)S(1)}, u32[]{:S(2)}, u32[]{:S(2)}) collective-permute-start(bf16[16,56,128]{2,1,0:T(8,128)(2,1)S(1)} %all-to-all-done.refs_4_), channel_id=1, source_target_pairs={{0,1},{1,0},{2,3},{3,2},{4,5},{5,4},{6,7},{7,6},{8,9},{9,8},{10,11... | collective-permute-start | bytes 688136 | tf_op jit(solution)/shard_map/ppermute | solution.py:519

commit v11 on v9

--- a/solution.py
+++ b/solution.py
@@ -424,7 +424,6 @@
             pair, gathered = lax.optimization_barrier((lax.ppermute(send, "rep", swap), gathered))
             high = (owns[1] + pair.astype(F32)).astype(BF16)
             low = owns[0] + lax.ppermute(others[0][0], "rep", swap).astype(F32)
-        chosen, keep, own_gain, offset = indices(source_map)
         for stage in range(bits - 1):
             with jax.named_scope(f"gradient_{stage + 1}"):
                 came = across(high, halving, stage)
@@ -432,9 +431,12 @@
                 with jax.named_scope(f"weights_{stage + 2}"):
                     gathered = jnp.concatenate([gathered, sent])
                     sent = across(gathered, doubling, stage + 2)
+            if stage == 0:
+                gathered, late_src = lax.optimization_barrier((gathered, source_map))
+                chosen, keep, own_gain, offset = indices(late_src)
             if stage != 1:
                 came, sent = lax.optimization_barrier((came, sent))
-            if stage == 1:
+            if stage == 0:
                 came, chosen = lax.optimization_barrier((came, chosen))
             came = came.astype(F32)
             half = half // 2
@@ -444,7 +446,7 @@
         with jax.named_scope("weights_pair"):
             pieces = [gathered, sent]
             pieces += [lax.ppermute(piece, "rep", swap) for piece in pieces]
-        came, *pieces = lax.optimization_barrier((came, *pieces))
+        came, *pieces[:3] = lax.optimization_barrier((came, *pieces[:3]))
         reduced = [resident(low), resident(came)]
         projected = call(
             lambda *refs: project_kernel(dp_count, doubling, cap, *refs),

time: 67.1 us -> 66.5 us (level)
  local copies, waits for them, and re-layouts: 0.9 us -> 0.13 us
    unnamed x16 -> x12, local copies, waits for them, and re-layouts: 0.85 us -> 0.05 us
  transfers between devices with their start and end apart: 14 -> 14, of which waited for: 9 -> 9; matrix products, arithmetic and copies ran while one was open for 1% -> 1% of each run, Pallas kernels for 26% -> 28%
where the time goes in v11:
time: 66.5 us; the launch traced here: 66 us
  Pallas kernels  22.1 us (33%)
  starting transfers between devices  21.7 us (33%)
  waiting for transfers between devices  20.6 us (31%)
  between operations  0.81 us (1%)
    pallas_call x6, Pallas kernels, call(): pl.pallas_call(kernel, out_shape=out_shape, in_specs=specs, out_specs=out...  22.1 us
    ppermute x8, waiting for transfers between devices, across(): return lax.ppermute(value, ('dp', 'rep'), pairs)  16.6 us
    ppermute x8, starting transfers between devices, across(): return lax.ppermute(value, ('dp', 'rep'), pairs)  14.8 us
    all_to_all x1, starting transfers between devices, on_device(): moved = [lax.all_to_all(packed, 'dp', split_axis=0, concat_axis=0)]  6.27 us
    all_to_all x1, waiting for transfers between devices, on_device(): moved = [lax.all_to_all(packed, 'dp', split_axis=0, concat_axis=0)]  2.55 us
    ppermute x1, waiting for transfers between devices, on_device(): moved = [arrived, lax.ppermute(arrived, 'rep', swap)]  1.49 us
  transfers between devices with their start and end apart: 14, of which 9 were waited for; matrix products, arithmetic and copies ran while one was open for 1% of the time, Pallas kernels for 28%

profile of v11, /device:TPU:0, one launch (start us, length us, event | category | flops | bytes accessed | tf_op | source)
XLA Modules:
  0.0 66.0 jit_solution(7829364288406289962)
XLA Ops:
  0.6 4.1 %collective-permute-start = (bf16[512,128]{1,0:T(8,128)(2,1)}, bf16[512,128]{1,0:T(8,128)(2,1)S(1)}, u32[]{:S(2)}, u32[]{:S(2)}) collective-permute-start(bf16[512,128]{1,0:T(8,128)(2,1)} %refs_5_.1), channel_id=1, source_target_pairs={{0,16},{1,17},{2,18},{3,19},{4,20},{5,21},{6,22},{7,23},{8,24},{9,... | collective-permute-start | bytes 393224 | tf_op jit(solution)/shard_map/ppermute | solution.py:361
  4.7 6.3 %shard_map.128 = (f32[48,128]{1,0:T(8,128)}, f32[256,128]{1,0:T(8,128)}, f32[8,256,128]{2,1,0:T(8,128)S(1)}, f32[8,256,128]{2,1,0:T(8,128)S(1)}, bf16[1,8,256,12...) custom-call(s32[17]{0:T(128)} %refs_0_.8, s32[1,8192]{1,0:T(1,128)} %bitcast.9, f32[48,128]{1,0:T(8,128)} %bitcast.11, ...), custom_call_target="tpu_custom_call" | custom-call | bytes 24000000 | tf_op jit(solution)/shard_map/pallas_call | solution.py:304
  11.1 0.2 collective-permute-done
  11.3 0.5 collective-permute-start.5
  11.8 1.6 %collective-permute-start.3 = (bf16[2,256,128]{2,1,0:T(8,128)(2,1)S(1)}, bf16[2,256,128]{2,1,0:T(8,128)(2,1)S(1)}, u32[]{:S(2)}, u32[]{:S(2)}) collective-permute-start(bf16[2,256,128]{2,1,0:T(8,128)(2,1)S(1)} %pad_maximum_fusion), channel_id=1, source_target_pairs={{0,2},{1,9},{2,0},{3,11},{4,6},{5,13},{6,4},{7,15},{8,10},{9,1},{1... | collective-permute-start | bytes 393224 | tf_op jit(solution)/shard_map/weights_1/ppermute | solution.py:361
  13.4 0.1 add_convert_fusion
  13.5 1.5 %collective-permute-start.2 = (bf16[8,256,128]{2,1,0:T(8,128)(2,1)S(1)}, bf16[8,256,128]{2,1,0:T(8,128)(2,1)S(1)}, u32[]{:S(2)}, u32[]{:S(2)}) collective-permute-start(bf16[8,256,128]{2,1,0:T(8,128)(2,1)S(1)} %add_convert_fusion), channel_id=1, source_target_pairs={{0,2},{1,9},{2,0},{3,11},{4,6},{5,13},{6,4},{7,15},{8,10},{9,1},{1... | collective-permute-start | bytes 1572872 | tf_op jit(solution)/shard_map/gradient_1/ppermute | solution.py:361
  15.1 1.7 %collective-permute-done.3 = bf16[2,256,128]{2,1,0:T(8,128)(2,1)S(1)} collective-permute-done((bf16[2,256,128]{2,1,0:T(8,128)(2,1)S(1)}, bf16[2,256,128]{2,1,0:T(8,128)(2,1)S(1)}, u32[]{:S(2)}, u32[]{:S(2)}) %collective-permute-start.3) | collective-permute-done | bytes 131104 | tf_op jit(solution)/shard_map/weights_1/ppermute | solution.py:361
  16.9 1.6 %collective-permute-start.4 = (bf16[4,256,128]{2,1,0:T(8,128)(2,1)S(1)}, bf16[4,256,128]{2,1,0:T(8,128)(2,1)S(1)}, u32[]{:S(2)}, u32[]{:S(2)}) collective-permute-start(bf16[4,256,128]{2,1,0:T(8,128)(2,1)S(1)} %constant_dynamic-update-slice_fusion), channel_id=1, source_target_pairs={{0,4},{1,5},{2,6},{3,7},{4,0},{5,1},{6,2},{7,3},{8,12},{9,13},{10,... | collective-permute-start | bytes 786440 | tf_op jit(solution)/shard_map/weights_2/ppermute | solution.py:361
  18.5 0.1 convert_add_fusion
  18.6 3.9 %shard_map.129 = (bf16[640,512]{1,0:T(8,128)(2,1)S(1)}, f32[1,640]{1,0:T(1,128)S(1)}, f32[1,512]{1,0:T(1,128)S(1)}, s32[1]{0:T(128)}) custom-call(s32[17]{0:T(128)} %refs_0_.8, s32[17]{0:T(128)} %refs_0_.9, s32[8192]{0:T(1024)} %refs_2_, f32[48,128]{1,0:T(8,128)} %bitcast.12), custom_call_target="tpu_custom_call" | custom-call | tf_op jit(solution)/shard_map/pallas_call | solution.py:304
  22.6 1.7 %collective-permute-done.4 = bf16[4,256,128]{2,1,0:T(8,128)(2,1)S(1)} collective-permute-done((bf16[4,256,128]{2,1,0:T(8,128)(2,1)S(1)}, bf16[4,256,128]{2,1,0:T(8,128)(2,1)S(1)}, u32[]{:S(2)}, u32[]{:S(2)}) %collective-permute-start.4) | collective-permute-done | bytes 262176 | tf_op jit(solution)/shard_map/weights_2/ppermute | solution.py:361
  24.3 0.1 convert_element_type.30
  24.4 0.0 copy-start.1
  24.4 0.1 slice_add_fusion.1
  24.5 1.6 %collective-permute-start.6 = (bf16[4,256,128]{2,1,0:T(8,128)(2,1)S(1)}, bf16[4,256,128]{2,1,0:T(8,128)(2,1)S(1)}, u32[]{:S(2)}, u32[]{:S(2)}) collective-permute-start(bf16[4,256,128]{2,1,0:T(8,128)(2,1)S(1)} %get-tuple-element.80), channel_id=1, source_target_pairs={{0,8},{1,3},{2,10},{3,1},{4,12},{5,7},{6,14},{7,5},{8,0},{9,11},{1... | collective-permute-start | bytes 786440 | tf_op jit(solution)/shard_map/gradient_2/ppermute | solution.py:361
  26.2 0.6 collective-permute-start.8
  26.8 4.2 %collective-permute-done.6 = bf16[4,256,128]{2,1,0:T(8,128)(2,1)S(1)} collective-permute-done((bf16[4,256,128]{2,1,0:T(8,128)(2,1)S(1)}, bf16[4,256,128]{2,1,0:T(8,128)(2,1)S(1)}, u32[]{:S(2)}, u32[]{:S(2)}) %collective-permute-start.6) | collective-permute-done | bytes 262176 | tf_op jit(solution)/shard_map/gradient_2/ppermute | solution.py:361
  31.0 0.1 slice_add_fusion.3
  31.1 1.6 %collective-permute-start.7 = (bf16[2,256,128]{2,1,0:T(8,128)(2,1)S(1)}, bf16[2,256,128]{2,1,0:T(8,128)(2,1)S(1)}, u32[]{:S(2)}, u32[]{:S(2)}) collective-permute-start(bf16[2,256,128]{2,1,0:T(8,128)(2,1)S(1)} %get-tuple-element.82), channel_id=1, source_target_pairs={{0,4},{1,5},{2,6},{3,7},{4,0},{5,1},{6,2},{7,3},{8,12},{9,13},{10,... | collective-permute-start | bytes 393224 | tf_op jit(solution)/shard_map/gradient_3/ppermute | solution.py:361
  32.7 3.4 %collective-permute-done.7 = bf16[2,256,128]{2,1,0:T(8,128)(2,1)S(1)} collective-permute-done((bf16[2,256,128]{2,1,0:T(8,128)(2,1)S(1)}, bf16[2,256,128]{2,1,0:T(8,128)(2,1)S(1)}, u32[]{:S(2)}, u32[]{:S(2)}) %collective-permute-start.7) | collective-permute-done | bytes 131104 | tf_op jit(solution)/shard_map/gradient_3/ppermute | solution.py:361
  36.1 0.6 collective-permute-done.8.refs_5_
  36.7 0.1 collective-permute-start.11
  36.9 2.2 %collective-permute-start.9 = (bf16[1,256,128]{2,1,0:T(8,128)(2,1)S(1)}, bf16[1,256,128]{2,1,0:T(8,128)(2,1)S(1)}, u32[]{:S(2)}, u32[]{:S(2)}) collective-permute-start(bf16[1,256,128]{2,1,0:T(8,128)(2,1)S(1)} %get-tuple-element.83), channel_id=1, source_target_pairs={{0,16},{1,17},{2,18},{3,19},{4,20},{5,21},{6,22},{7,23},{8,24},{9,... | collective-permute-start | bytes 196616 | tf_op jit(solution)/shard_map/gradient_last/ppermute | solution.py:361
  39.0 4.7 %collective-permute-done.9.refs_4_ = bf16[1,256,128]{2,1,0:T(8,128)(2,1)S(1)} collective-permute-done((bf16[1,256,128]{2,1,0:T(8,128)(2,1)S(1)}, bf16[1,256,128]{2,1,0:T(8,128)(2,1)S(1)}, u32[]{:S(2)}, u32[]{:S(2)}) %collective-permute-start.9) | collective-permute-done | bytes 65568 | tf_op jit(solution)/shard_map/gradient_last/ppermute | solution.py:361
  43.7 1.4 %shard_map.130 = bf16[16,56,128]{2,1,0:T(8,128)(2,1)} custom-call(bf16[640,512]{1,0:T(8,128)(2,1)S(1)} %get-tuple-element.51.refs_0_, f32[1,640]{1,0:T(1,128)S(1)} %get-tuple-element.52.refs_1_, f32[1,512]{1,0:T(1,128)S(1)} %get-tuple-element.53.refs_2_, f32[1,256,128]{2,1,0:T(8,128)S(1)} %get-tuple-element.84.refs_3_, ...), custom_call_target="tpu_custom_call" | custom-call | bytes 9000000 | tf_op jit(solution)/shard_map/pallas_call | solution.py:304
  45.1 6.3 %all-to-all-start = ((bf16[16,56,128]{2,1,0:T(8,128)(2,1)}), bf16[16,56,128]{2,1,0:T(8,128)(2,1)S(1)}, u32[]{:S(2)}, u32[]{:S(2)}) async-start(bf16[16,56,128]{2,1,0:T(8,128)(2,1)} %shard_map.130), calls=%async_computation | async-start | bytes 458752 | tf_op jit(solution)/shard_map/all_to_all | solution.py:508
  51.4 1.5 %shard_map.132 = (s32[1,8192]{1,0:T(1,128)S(1)}, bf16[160,8192]{1,0:T(8,128)(2,1)S(1)}) custom-call(s32[17]{0:T(128)} %refs_0_.8, s32[17]{0:T(128)} %refs_0_.9, s32[1,8192]{1,0:T(1,128)} %bitcast.10), custom_call_target="tpu_custom_call" | custom-call | bytes 6000000 | tf_op jit(solution)/shard_map/pallas_call | solution.py:304
  52.9 5.4 %shard_map.131 = bf16[256,128]{1,0:T(8,128)(2,1)} custom-call(s32[17]{0:T(128)} %refs_0_.8, bf16[256,6144]{1,0:T(8,128)(2,1)} %refs_1_.4, f32[256,128]{1,0:T(8,128)} %get-tuple-element.63.refs_2_, f32[48,128]{1,0:T(8,128)} %get-tuple-element.64.refs_3_, bf16[8,256,128]{2,1,0:T(8,128)(2,1)} %copy-done.3, bf16[8,256,128]{2,1,0:T(8,128)(2,1)} %collective-permute-done.8.refs_5_, ...), custom_call_target="tpu_custom_call" | custom-call | bytes 18000000 | tf_op jit(solution)/shard_map/pallas_call | solution.py:304
  58.3 2.5 %all-to-all-done.refs_4_ = bf16[16,56,128]{2,1,0:T(8,128)(2,1)S(1)} async-done(((bf16[16,56,128]{2,1,0:T(8,128)(2,1)}), bf16[16,56,128]{2,1,0:T(8,128)(2,1)S(1)}, u32[]{:S(2)}, u32[]{:S(2)}) %all-to-all-start) | async-done | bytes 229408 | tf_op jit(solution)/shard_map/all_to_all | solution.py:508
  60.9 1.5 %collective-permute-done.12.refs_5_ = bf16[16,56,128]{2,1,0:T(8,128)(2,1)S(1)} collective-permute-done((bf16[16,56,128]{2,1,0:T(8,128)(2,1)S(1)}, bf16[16,56,128]{2,1,0:T(8,128)(2,1)S(1)}, u32[]{:S(2)}, u32[]{:S(2)}) %collective-permute-start.12) | collective-permute-done | bytes 229408 | tf_op jit(solution)/shard_map/ppermute | solution.py:511
  62.4 3.6 %shard_map.133 = (f32[1,8192]{1,0:T(1,128)}, f32[640,128]{1,0:T(8,128)}, f32[640,128]{1,0:T(8,128)}, f32[640,128]{1,0:T(8,128)}) custom-call(s32[17]{0:T(128)} %refs_0_.9, s32[1]{0:T(128)} %get-tuple-element.71.refs_1_, s32[1,8192]{1,0:T(1,128)S(1)} %get-tuple-element.72.refs_2_, bf16[160,8192]{1,0:T(8,128)(2,1)S(1)} %get-tuple-element.73.refs_3_, ...), custom_call_target="tpu_custom_call" | custom-call | bytes 12000000 | tf_op jit(solution)/shard_map/pallas_call | solution.py:304
  (27 shorter events, 0.2 us)
Async XLA Ops:
  0.6 11.1 %copy-start = (bf16[512,128]{1,0:T(8,128)(2,1)S(1)}, bf16[512,128]{1,0:T(8,128)(2,1)}, u32[]{:S(2)}) copy-start(bf16[512,128]{1,0:T(8,128)(2,1)} %refs_5_.1) | copy-start | bytes 393220
  0.6 10.6 %collective-permute-start = (bf16[512,128]{1,0:T(8,128)(2,1)}, bf16[512,128]{1,0:T(8,128)(2,1)S(1)}, u32[]{:S(2)}, u32[]{:S(2)}) collective-permute-start(bf16[512,128]{1,0:T(8,128)(2,1)} %refs_5_.1), channel_id=1, source_target_pairs={{0,16},{1,17},{2,18},{3,19},{4,20},{5,21},{6,22},{7,23},{8,24},{9,... | collective-permute-start | bytes 393224 | tf_op jit(solution)/shard_map/ppermute | solution.py:361
  11.3 2.2 %collective-permute-start.1 = (bf16[8,256,128]{2,1,0:T(8,128)(2,1)}, bf16[8,256,128]{2,1,0:T(8,128)(2,1)S(1)}, u32[]{:S(2)}, u32[]{:S(2)}) collective-permute-start(bf16[8,256,128]{2,1,0:T(8,128)(2,1)} %bitcast.14), channel_id=1, source_target_pairs={{0,1},{1,0},{2,3},{3,2},{4,5},{5,4},{6,7},{7,6},{8,9},{9,8},{10,11... | collective-permute-start | bytes 1572872 | tf_op jit(solution)/shard_map/pair_exchange/ppermute | solution.py:424
  11.3 7.3 %collective-permute-start.5 = (bf16[8,256,128]{2,1,0:T(8,128)(2,1)}, bf16[8,256,128]{2,1,0:T(8,128)(2,1)S(1)}, u32[]{:S(2)}, u32[]{:S(2)}) collective-permute-start(bf16[8,256,128]{2,1,0:T(8,128)(2,1)} %bitcast.13), channel_id=1, source_target_pairs={{0,1},{1,0},{2,3},{3,2},{4,5},{5,4},{6,7},{7,6},{8,9},{9,8},{10,11... | collective-permute-start | bytes 1572872 | tf_op jit(solution)/shard_map/pair_exchange/ppermute | solution.py:426
  11.8 5.0 %collective-permute-start.3 = (bf16[2,256,128]{2,1,0:T(8,128)(2,1)S(1)}, bf16[2,256,128]{2,1,0:T(8,128)(2,1)S(1)}, u32[]{:S(2)}, u32[]{:S(2)}) collective-permute-start(bf16[2,256,128]{2,1,0:T(8,128)(2,1)S(1)} %pad_maximum_fusion), channel_id=1, source_target_pairs={{0,2},{1,9},{2,0},{3,11},{4,6},{5,13},{6,4},{7,15},{8,10},{9,1},{1... | collective-permute-start | bytes 393224 | tf_op jit(solution)/shard_map/weights_1/ppermute | solution.py:361
  13.5 10.8 %collective-permute-start.2 = (bf16[8,256,128]{2,1,0:T(8,128)(2,1)S(1)}, bf16[8,256,128]{2,1,0:T(8,128)(2,1)S(1)}, u32[]{:S(2)}, u32[]{:S(2)}) collective-permute-start(bf16[8,256,128]{2,1,0:T(8,128)(2,1)S(1)} %add_convert_fusion), channel_id=1, source_target_pairs={{0,2},{1,9},{2,0},{3,11},{4,6},{5,13},{6,4},{7,15},{8,10},{9,1},{1... | collective-permute-start | bytes 1572872 | tf_op jit(solution)/shard_map/gradient_1/ppermute | solution.py:361
  16.9 7.4 %collective-permute-start.4 = (bf16[4,256,128]{2,1,0:T(8,128)(2,1)S(1)}, bf16[4,256,128]{2,1,0:T(8,128)(2,1)S(1)}, u32[]{:S(2)}, u32[]{:S(2)}) collective-permute-start(bf16[4,256,128]{2,1,0:T(8,128)(2,1)S(1)} %constant_dynamic-update-slice_fusion), channel_id=1, source_target_pairs={{0,4},{1,5},{2,6},{3,7},{4,0},{5,1},{6,2},{7,3},{8,12},{9,13},{10,... | collective-permute-start | bytes 786440 | tf_op jit(solution)/shard_map/weights_2/ppermute | solution.py:361
  24.4 19.3 %copy-start.1 = (f32[512,128]{1,0:T(8,128)S(1)}, f32[512,128]{1,0:T(8,128)}, u32[]{:S(2)}) copy-start(f32[512,128]{1,0:T(8,128)} %refs_6_.1) | copy-start | bytes 786436
  24.4 19.3 %copy-start.2 = (f32[512,128]{1,0:T(8,128)S(1)}, f32[512,128]{1,0:T(8,128)}, u32[]{:S(2)}) copy-start(f32[512,128]{1,0:T(8,128)} %refs_7_.1) | copy-start | bytes 786436
  24.5 6.4 %collective-permute-start.6 = (bf16[4,256,128]{2,1,0:T(8,128)(2,1)S(1)}, bf16[4,256,128]{2,1,0:T(8,128)(2,1)S(1)}, u32[]{:S(2)}, u32[]{:S(2)}) collective-permute-start(bf16[4,256,128]{2,1,0:T(8,128)(2,1)S(1)} %get-tuple-element.80), channel_id=1, source_target_pairs={{0,8},{1,3},{2,10},{3,1},{4,12},{5,7},{6,14},{7,5},{8,0},{9,11},{1... | collective-permute-start | bytes 786440 | tf_op jit(solution)/shard_map/gradient_2/ppermute | solution.py:361
  26.2 26.7 %copy-start.3 = (bf16[8,256,128]{2,1,0:T(8,128)(2,1)}, bf16[8,256,128]{2,1,0:T(8,128)(2,1)S(1)}, u32[]{:S(2)}) copy-start(bf16[8,256,128]{2,1,0:T(8,128)(2,1)S(1)} %constant_dynamic-update-slice_fusion.2.refs_4_) | copy-start | bytes 1572868
  26.2 10.5 %collective-permute-start.8 = (bf16[8,256,128]{2,1,0:T(8,128)(2,1)S(1)}, bf16[8,256,128]{2,1,0:T(8,128)(2,1)}, u32[]{:S(2)}, u32[]{:S(2)}) collective-permute-start(bf16[8,256,128]{2,1,0:T(8,128)(2,1)S(1)} %constant_dynamic-update-slice_fusion.2.refs_4_), channel_id=1, source_target_pairs={{0,8},{1,3},{2,10},{3,1},{4,12},{5,7},{6,14},{7,5},{8,0},{9,11},{1... | collective-permute-start | bytes 1572872 | tf_op jit(solution)/shard_map/weights_3/ppermute | solution.py:361
  26.8 12.3 %collective-permute-start.10 = (bf16[8,256,128]{2,1,0:T(8,128)(2,1)S(1)}, bf16[8,256,128]{2,1,0:T(8,128)(2,1)S(1)}, u32[]{:S(2)}, u32[]{:S(2)}) collective-permute-start(bf16[8,256,128]{2,1,0:T(8,128)(2,1)S(1)} %constant_dynamic-update-slice_fusion.2.refs_4_), channel_id=1, source_target_pairs={{0,1},{1,0},{2,3},{3,2},{4,5},{5,4},{6,7},{7,6},{8,9},{9,8},{10,11... | collective-permute-start | bytes 1572872 | tf_op jit(solution)/shard_map/weights_pair/ppermute | solution.py:448
  31.1 5.0 %collective-permute-start.7 = (bf16[2,256,128]{2,1,0:T(8,128)(2,1)S(1)}, bf16[2,256,128]{2,1,0:T(8,128)(2,1)S(1)}, u32[]{:S(2)}, u32[]{:S(2)}) collective-permute-start(bf16[2,256,128]{2,1,0:T(8,128)(2,1)S(1)} %get-tuple-element.82), channel_id=1, source_target_pairs={{0,4},{1,5},{2,6},{3,7},{4,0},{5,1},{6,2},{7,3},{8,12},{9,13},{10,... | collective-permute-start | bytes 393224 | tf_op jit(solution)/shard_map/gradient_3/ppermute | solution.py:361
  36.7 16.2 %collective-permute-start.11 = (bf16[8,256,128]{2,1,0:T(8,128)(2,1)}, bf16[8,256,128]{2,1,0:T(8,128)(2,1)}, u32[]{:S(2)}, u32[]{:S(2)}) collective-permute-start(bf16[8,256,128]{2,1,0:T(8,128)(2,1)} %collective-permute-done.8.refs_5_), channel_id=1, source_target_pairs={{0,1},{1,0},{2,3},{3,2},{4,5},{5,4},{6,7},{7,6},{8,9},{9,8},{10,11... | collective-permute-start | bytes 1572872 | tf_op jit(solution)/shard_map/weights_pair/ppermute | solution.py:448
  36.9 6.9 %collective-permute-start.9 = (bf16[1,256,128]{2,1,0:T(8,128)(2,1)S(1)}, bf16[1,256,128]{2,1,0:T(8,128)(2,1)S(1)}, u32[]{:S(2)}, u32[]{:S(2)}) collective-permute-start(bf16[1,256,128]{2,1,0:T(8,128)(2,1)S(1)} %get-tuple-element.83), channel_id=1, source_target_pairs={{0,16},{1,17},{2,18},{3,19},{4,20},{5,21},{6,22},{7,23},{8,24},{9,... | collective-permute-start | bytes 196616 | tf_op jit(solution)/shard_map/gradient_last/ppermute | solution.py:361
  39.0 4.7 %copy-start.4 = (bf16[8,256,128]{2,1,0:T(8,128)(2,1)}, bf16[8,256,128]{2,1,0:T(8,128)(2,1)S(1)}, u32[]{:S(2)}) copy-start(bf16[8,256,128]{2,1,0:T(8,128)(2,1)S(1)} %collective-permute-done.10.refs_6_) | copy-start | bytes 1572868
  45.1 15.8 %all-to-all-start = ((bf16[16,56,128]{2,1,0:T(8,128)(2,1)}), bf16[16,56,128]{2,1,0:T(8,128)(2,1)S(1)}, u32[]{:S(2)}, u32[]{:S(2)}) async-start(bf16[16,56,128]{2,1,0:T(8,128)(2,1)} %shard_map.130), calls=%async_computation | async-start | bytes 458752 | tf_op jit(solution)/shard_map/all_to_all | solution.py:508
  60.9 1.5 %collective-permute-start.12 = (bf16[16,56,128]{2,1,0:T(8,128)(2,1)S(1)}, bf16[16,56,128]{2,1,0:T(8,128)(2,1)S(1)}, u32[]{:S(2)}, u32[]{:S(2)}) collective-permute-start(bf16[16,56,128]{2,1,0:T(8,128)(2,1)S(1)} %all-to-all-done.refs_4_), channel_id=1, source_target_pairs={{0,1},{1,0},{2,3},{3,2},{4,5},{5,4},{6,7},{7,6},{8,9},{9,8},{10,11... | collective-permute-start | bytes 688136 | tf_op jit(solution)/shard_map/ppermute | solution.py:511

commit v12 on v11

--- a/solution.py
+++ b/solution.py
@@ -434,7 +434,7 @@
             if stage == 0:
                 gathered, late_src = lax.optimization_barrier((gathered, source_map))
                 chosen, keep, own_gain, offset = indices(late_src)
-            if stage != 1:
+            if stage == 0:
                 came, sent = lax.optimization_barrier((came, sent))
             if stage == 0:
                 came, chosen = lax.optimization_barrier((came, chosen))
@@ -444,22 +444,9 @@
         with jax.named_scope("gradient_last"):
             came = across(high, halving, bits - 1)
         with jax.named_scope("weights_pair"):
-            pieces = [gathered, sent]
-            pieces += [lax.ppermute(piece, "rep", swap) for piece in pieces]
-        came, *pieces[:3] = lax.optimization_barrier((came, *pieces[:3]))
+            from_mate = lax.ppermute(gathered, "rep", swap)
+        came, gathered, from_mate = lax.optimization_barrier((came, gathered, from_mate))
         reduced = [resident(low), resident(came)]
-        projected = call(
-            lambda *refs: project_kernel(dp_count, doubling, cap, *refs),
-            6,
-            project_shape,
-            [SMEM_SPEC] + [VMEM_SPEC] * 3 + [any_spec] * 4,
-            dense + [pltpu.VMEM((2, dp_count, part, LANES), BF16), pltpu.SemaphoreType.DMA((4,))],
-            old_bounds,
-            hidden_old,
-            inv_rms,
-            live_gain,
-            *pieces,
-        )
     else:
         chip = owns[0]
         for away in range(1, rep_count):
@@ -494,6 +481,23 @@
         *reduced,
         *[resident(value) for value in (weight_old, moment_first, moment_second)],
     )
+    if staged:
+        packed, late = lax.optimization_barrier((packed, sent))
+        projected = call(
+            lambda *refs: project_kernel(dp_count, doubling, cap, *refs),
+            6,
+            project_shape,
+            [SMEM_SPEC] + [VMEM_SPEC] * 3 + [any_spec] * 4,
+            dense + [pltpu.VMEM((2, dp_count, part, LANES), BF16), pltpu.SemaphoreType.DMA((4,))],
+            old_bounds,
+            hidden_old,
+            inv_rms,
+            live_gain,
+            gathered,
+            late,
+            from_mate,
+            lax.ppermute(late, "rep", swap),
+        )
     packed, late_units = lax.optimization_barrier((packed, units))
     places, tables = call(
         lambda *refs: place_kernel(dp_count, slots, table_rows, *refs),

time: 66.5 us -> 65.3 us (0.982)
  waiting for transfers between devices: 20.6 us -> 18.8 us
  starting transfers between devices: 21.7 us -> 22.4 us
    ppermute x8, waiting for transfers between devices: 16.6 us -> 14.3 us  [across(): return lax.ppermute(value, ('dp', 'rep'), pairs)]
    all_to_all x1, starting transfers between devices: 6.27 us -> 6.98 us  [on_device(): moved = [lax.all_to_all(packed, 'dp', split_axis=0, concat_axis=0)]]
  transfers between devices with their start and end apart: 14 -> 14, of which waited for: 9 -> 8; matrix products, arithmetic and copies ran while one was open for 1% -> 1% of each run, Pallas kernels for 28% -> 29%
where the time goes in v12:
time: 65.3 us; the launch traced here: 64.8 us
  starting transfers between devices  22.4 us (34%)
  Pallas kernels  22.1 us (34%)
  waiting for transfers between devices  18.8 us (29%)
  between operations  0.82 us (1%)
    pallas_call x6, Pallas kernels, call(): pl.pallas_call(kernel, out_shape=out_shape, in_specs=specs, out_specs=out...  22.1 us
    ppermute x8, starting transfers between devices, across(): return lax.ppermute(value, ('dp', 'rep'), pairs)  14.8 us
    ppermute x8, waiting for transfers between devices, across(): return lax.ppermute(value, ('dp', 'rep'), pairs)  14.3 us
    all_to_all x1, starting transfers between devices, on_device(): moved = [lax.all_to_all(packed, 'dp', split_axis=0, concat_axis=0)]  6.98 us
    all_to_all x1, waiting for transfers between devices, on_device(): moved = [lax.all_to_all(packed, 'dp', split_axis=0, concat_axis=0)]  2.97 us
    ppermute x1, waiting for transfers between devices, on_device(): moved = [arrived, lax.ppermute(arrived, 'rep', swap)]  1.49 us
  transfers between devices with their start and end apart: 14, of which 8 were waited for; matrix products, arithmetic and copies ran while one was open for 1% of the time, Pallas kernels for 29%

profile of v12, /device:TPU:0, one launch (start us, length us, event | category | flops | bytes accessed | tf_op | source)
XLA Modules:
  0.0 64.8 jit_solution(448997491981498319)
XLA Ops:
  0.6 4.1 %collective-permute-start = (bf16[512,128]{1,0:T(8,128)(2,1)}, bf16[512,128]{1,0:T(8,128)(2,1)S(1)}, u32[]{:S(2)}, u32[]{:S(2)}) collective-permute-start(bf16[512,128]{1,0:T(8,128)(2,1)} %refs_5_.1), channel_id=1, source_target_pairs={{0,16},{1,17},{2,18},{3,19},{4,20},{5,21},{6,22},{7,23},{8,24},{9,... | collective-permute-start | bytes 393224 | tf_op jit(solution)/shard_map/ppermute | solution.py:361
  4.7 6.3 %shard_map.128 = (f32[48,128]{1,0:T(8,128)}, f32[256,128]{1,0:T(8,128)}, f32[8,256,128]{2,1,0:T(8,128)S(1)}, f32[8,256,128]{2,1,0:T(8,128)S(1)}, bf16[1,8,256,12...) custom-call(s32[17]{0:T(128)} %refs_0_.8, s32[1,8192]{1,0:T(1,128)} %bitcast.9, f32[48,128]{1,0:T(8,128)} %bitcast.11, ...), custom_call_target="tpu_custom_call" | custom-call | bytes 24000000 | tf_op jit(solution)/shard_map/pallas_call | solution.py:304
  11.1 0.2 collective-permute-done
  11.3 0.5 collective-permute-start.5
  11.8 1.6 %collective-permute-start.3 = (bf16[2,256,128]{2,1,0:T(8,128)(2,1)S(1)}, bf16[2,256,128]{2,1,0:T(8,128)(2,1)S(1)}, u32[]{:S(2)}, u32[]{:S(2)}) collective-permute-start(bf16[2,256,128]{2,1,0:T(8,128)(2,1)S(1)} %pad_maximum_fusion), channel_id=1, source_target_pairs={{0,2},{1,9},{2,0},{3,11},{4,6},{5,13},{6,4},{7,15},{8,10},{9,1},{1... | collective-permute-start | bytes 393224 | tf_op jit(solution)/shard_map/weights_1/ppermute | solution.py:361
  13.4 0.1 add_convert_fusion
  13.5 1.5 %collective-permute-start.2 = (bf16[8,256,128]{2,1,0:T(8,128)(2,1)S(1)}, bf16[8,256,128]{2,1,0:T(8,128)(2,1)S(1)}, u32[]{:S(2)}, u32[]{:S(2)}) collective-permute-start(bf16[8,256,128]{2,1,0:T(8,128)(2,1)S(1)} %add_convert_fusion), channel_id=1, source_target_pairs={{0,2},{1,9},{2,0},{3,11},{4,6},{5,13},{6,4},{7,15},{8,10},{9,1},{1... | collective-permute-start | bytes 1572872 | tf_op jit(solution)/shard_map/gradient_1/ppermute | solution.py:361
  15.1 1.7 %collective-permute-done.3 = bf16[2,256,128]{2,1,0:T(8,128)(2,1)S(1)} collective-permute-done((bf16[2,256,128]{2,1,0:T(8,128)(2,1)S(1)}, bf16[2,256,128]{2,1,0:T(8,128)(2,1)S(1)}, u32[]{:S(2)}, u32[]{:S(2)}) %collective-permute-start.3) | collective-permute-done | bytes 131104 | tf_op jit(solution)/shard_map/weights_1/ppermute | solution.py:361
  16.9 1.6 %collective-permute-start.4 = (bf16[4,256,128]{2,1,0:T(8,128)(2,1)S(1)}, bf16[4,256,128]{2,1,0:T(8,128)(2,1)S(1)}, u32[]{:S(2)}, u32[]{:S(2)}) collective-permute-start(bf16[4,256,128]{2,1,0:T(8,128)(2,1)S(1)} %constant_dynamic-update-slice_fusion), channel_id=1, source_target_pairs={{0,4},{1,5},{2,6},{3,7},{4,0},{5,1},{6,2},{7,3},{8,12},{9,13},{10,... | collective-permute-start | bytes 786440 | tf_op jit(solution)/shard_map/weights_2/ppermute | solution.py:361
  18.5 0.1 convert_add_fusion
  18.6 3.9 %shard_map.129 = (bf16[640,512]{1,0:T(8,128)(2,1)S(1)}, f32[1,640]{1,0:T(1,128)S(1)}, f32[1,512]{1,0:T(1,128)S(1)}, s32[1]{0:T(128)}) custom-call(s32[17]{0:T(128)} %refs_0_.8, s32[17]{0:T(128)} %refs_0_.9, s32[8192]{0:T(1024)} %refs_2_, f32[48,128]{1,0:T(8,128)} %bitcast.12), custom_call_target="tpu_custom_call" | custom-call | tf_op jit(solution)/shard_map/pallas_call | solution.py:304
  22.5 1.8 %collective-permute-done.4 = bf16[4,256,128]{2,1,0:T(8,128)(2,1)S(1)} collective-permute-done((bf16[4,256,128]{2,1,0:T(8,128)(2,1)S(1)}, bf16[4,256,128]{2,1,0:T(8,128)(2,1)S(1)}, u32[]{:S(2)}, u32[]{:S(2)}) %collective-permute-start.4) | collective-permute-done | bytes 262176 | tf_op jit(solution)/shard_map/weights_2/ppermute | solution.py:361
  24.3 0.1 convert_element_type.30
  24.4 0.0 copy-start.1
  24.4 0.0 copy-start.2
  24.4 0.1 slice_add_fusion.1
  24.5 1.6 %collective-permute-start.6 = (bf16[4,256,128]{2,1,0:T(8,128)(2,1)S(1)}, bf16[4,256,128]{2,1,0:T(8,128)(2,1)S(1)}, u32[]{:S(2)}, u32[]{:S(2)}) collective-permute-start(bf16[4,256,128]{2,1,0:T(8,128)(2,1)S(1)} %get-tuple-element.78), channel_id=1, source_target_pairs={{0,8},{1,3},{2,10},{3,1},{4,12},{5,7},{6,14},{7,5},{8,0},{9,11},{1... | collective-permute-start | bytes 786440 | tf_op jit(solution)/shard_map/gradient_2/ppermute | solution.py:361
  26.2 0.1 collective-permute-start.9
  26.3 0.5 collective-permute-start.10
  26.9 4.1 %collective-permute-done.6 = bf16[4,256,128]{2,1,0:T(8,128)(2,1)S(1)} collective-permute-done((bf16[4,256,128]{2,1,0:T(8,128)(2,1)S(1)}, bf16[4,256,128]{2,1,0:T(8,128)(2,1)S(1)}, u32[]{:S(2)}, u32[]{:S(2)}) %collective-permute-start.6) | collective-permute-done | bytes 262176 | tf_op jit(solution)/shard_map/gradient_2/ppermute | solution.py:361
  31.0 0.1 slice_add_fusion.3
  31.1 1.6 %collective-permute-start.7 = (bf16[2,256,128]{2,1,0:T(8,128)(2,1)S(1)}, bf16[2,256,128]{2,1,0:T(8,128)(2,1)S(1)}, u32[]{:S(2)}, u32[]{:S(2)}) collective-permute-start(bf16[2,256,128]{2,1,0:T(8,128)(2,1)S(1)} %get-tuple-element.80), channel_id=1, source_target_pairs={{0,4},{1,5},{2,6},{3,7},{4,0},{5,1},{6,2},{7,3},{8,12},{9,13},{10,... | collective-permute-start | bytes 393224 | tf_op jit(solution)/shard_map/gradient_3/ppermute | solution.py:361
  32.7 3.4 %collective-permute-done.7 = bf16[2,256,128]{2,1,0:T(8,128)(2,1)S(1)} collective-permute-done((bf16[2,256,128]{2,1,0:T(8,128)(2,1)S(1)}, bf16[2,256,128]{2,1,0:T(8,128)(2,1)S(1)}, u32[]{:S(2)}, u32[]{:S(2)}) %collective-permute-start.7) | collective-permute-done | bytes 131104 | tf_op jit(solution)/shard_map/gradient_3/ppermute | solution.py:361
  36.2 2.2 %collective-permute-start.8 = (bf16[1,256,128]{2,1,0:T(8,128)(2,1)S(1)}, bf16[1,256,128]{2,1,0:T(8,128)(2,1)S(1)}, u32[]{:S(2)}, u32[]{:S(2)}) collective-permute-start(bf16[1,256,128]{2,1,0:T(8,128)(2,1)S(1)} %get-tuple-element.81), channel_id=1, source_target_pairs={{0,16},{1,17},{2,18},{3,19},{4,20},{5,21},{6,22},{7,23},{8,24},{9,... | collective-permute-start | bytes 196616 | tf_op jit(solution)/shard_map/gradient_last/ppermute | solution.py:361
  38.3 3.1 %collective-permute-done.8.refs_4_ = bf16[1,256,128]{2,1,0:T(8,128)(2,1)S(1)} collective-permute-done((bf16[1,256,128]{2,1,0:T(8,128)(2,1)S(1)}, bf16[1,256,128]{2,1,0:T(8,128)(2,1)S(1)}, u32[]{:S(2)}, u32[]{:S(2)}) %collective-permute-start.8) | collective-permute-done | bytes 65568 | tf_op jit(solution)/shard_map/gradient_last/ppermute | solution.py:361
  41.4 1.4 %shard_map.130 = bf16[16,56,128]{2,1,0:T(8,128)(2,1)} custom-call(bf16[640,512]{1,0:T(8,128)(2,1)S(1)} %get-tuple-element.50.refs_0_, f32[1,640]{1,0:T(1,128)S(1)} %get-tuple-element.51.refs_1_, f32[1,512]{1,0:T(1,128)S(1)} %get-tuple-element.52.refs_2_, f32[1,256,128]{2,1,0:T(8,128)S(1)} %get-tuple-element.82.refs_3_, ...), custom_call_target="tpu_custom_call" | custom-call | bytes 9000000 | tf_op jit(solution)/shard_map/pallas_call | solution.py:304
  42.8 7.0 %all-to-all-start = ((bf16[16,56,128]{2,1,0:T(8,128)(2,1)}), bf16[16,56,128]{2,1,0:T(8,128)(2,1)S(1)}, u32[]{:S(2)}, u32[]{:S(2)}) async-start(bf16[16,56,128]{2,1,0:T(8,128)(2,1)} %shard_map.130), calls=%async_computation | async-start | bytes 458752 | tf_op jit(solution)/shard_map/all_to_all | solution.py:512
  49.8 1.5 %shard_map.132 = (s32[1,8192]{1,0:T(1,128)S(1)}, bf16[160,8192]{1,0:T(8,128)(2,1)S(1)}) custom-call(s32[17]{0:T(128)} %refs_0_.8, s32[17]{0:T(128)} %refs_0_.9, s32[1,8192]{1,0:T(1,128)} %bitcast.10), custom_call_target="tpu_custom_call" | custom-call | bytes 6000000 | tf_op jit(solution)/shard_map/pallas_call | solution.py:304
  51.4 5.4 %shard_map.131 = bf16[256,128]{1,0:T(8,128)(2,1)} custom-call(s32[17]{0:T(128)} %refs_0_.8, bf16[256,6144]{1,0:T(8,128)(2,1)} %refs_1_.4, f32[256,128]{1,0:T(8,128)} %get-tuple-element.61.refs_2_, f32[48,128]{1,0:T(8,128)} %get-tuple-element.62.refs_3_, bf16[8,256,128]{2,1,0:T(8,128)(2,1)} %copy-done.3, ...), custom_call_target="tpu_custom_call" | custom-call | bytes 18000000 | tf_op jit(solution)/shard_map/pallas_call | solution.py:304
  56.8 3.0 %all-to-all-done.refs_4_ = bf16[16,56,128]{2,1,0:T(8,128)(2,1)S(1)} async-done(((bf16[16,56,128]{2,1,0:T(8,128)(2,1)}), bf16[16,56,128]{2,1,0:T(8,128)(2,1)S(1)}, u32[]{:S(2)}, u32[]{:S(2)}) %all-to-all-start) | async-done | bytes 229408 | tf_op jit(solution)/shard_map/all_to_all | solution.py:512
  59.7 1.5 %collective-permute-done.12.refs_5_ = bf16[16,56,128]{2,1,0:T(8,128)(2,1)S(1)} collective-permute-done((bf16[16,56,128]{2,1,0:T(8,128)(2,1)S(1)}, bf16[16,56,128]{2,1,0:T(8,128)(2,1)S(1)}, u32[]{:S(2)}, u32[]{:S(2)}) %collective-permute-start.12) | collective-permute-done | bytes 229408 | tf_op jit(solution)/shard_map/ppermute | solution.py:515
  61.2 3.6 %shard_map.133 = (f32[1,8192]{1,0:T(1,128)}, f32[640,128]{1,0:T(8,128)}, f32[640,128]{1,0:T(8,128)}, f32[640,128]{1,0:T(8,128)}) custom-call(s32[17]{0:T(128)} %refs_0_.9, s32[1]{0:T(128)} %get-tuple-element.69.refs_1_, s32[1,8192]{1,0:T(1,128)S(1)} %get-tuple-element.70.refs_2_, bf16[160,8192]{1,0:T(8,128)(2,1)S(1)} %get-tuple-element.71.refs_3_, ...), custom_call_target="tpu_custom_call" | custom-call | bytes 12000000 | tf_op jit(solution)/shard_map/pallas_call | solution.py:304
  (27 shorter events, 0.2 us)
Async XLA Ops:
  0.6 11.1 %copy-start = (bf16[512,128]{1,0:T(8,128)(2,1)S(1)}, bf16[512,128]{1,0:T(8,128)(2,1)}, u32[]{:S(2)}) copy-start(bf16[512,128]{1,0:T(8,128)(2,1)} %refs_5_.1) | copy-start | bytes 393220
  0.6 10.6 %collective-permute-start = (bf16[512,128]{1,0:T(8,128)(2,1)}, bf16[512,128]{1,0:T(8,128)(2,1)S(1)}, u32[]{:S(2)}, u32[]{:S(2)}) collective-permute-start(bf16[512,128]{1,0:T(8,128)(2,1)} %refs_5_.1), channel_id=1, source_target_pairs={{0,16},{1,17},{2,18},{3,19},{4,20},{5,21},{6,22},{7,23},{8,24},{9,... | collective-permute-start | bytes 393224 | tf_op jit(solution)/shard_map/ppermute | solution.py:361
  11.3 2.2 %collective-permute-start.1 = (bf16[8,256,128]{2,1,0:T(8,128)(2,1)}, bf16[8,256,128]{2,1,0:T(8,128)(2,1)S(1)}, u32[]{:S(2)}, u32[]{:S(2)}) collective-permute-start(bf16[8,256,128]{2,1,0:T(8,128)(2,1)} %bitcast.14), channel_id=1, source_target_pairs={{0,1},{1,0},{2,3},{3,2},{4,5},{5,4},{6,7},{7,6},{8,9},{9,8},{10,11... | collective-permute-start | bytes 1572872 | tf_op jit(solution)/shard_map/pair_exchange/ppermute | solution.py:424
  11.3 7.3 %collective-permute-start.5 = (bf16[8,256,128]{2,1,0:T(8,128)(2,1)}, bf16[8,256,128]{2,1,0:T(8,128)(2,1)S(1)}, u32[]{:S(2)}, u32[]{:S(2)}) collective-permute-start(bf16[8,256,128]{2,1,0:T(8,128)(2,1)} %bitcast.13), channel_id=1, source_target_pairs={{0,1},{1,0},{2,3},{3,2},{4,5},{5,4},{6,7},{7,6},{8,9},{9,8},{10,11... | collective-permute-start | bytes 1572872 | tf_op jit(solution)/shard_map/pair_exchange/ppermute | solution.py:426
  11.8 5.0 %collective-permute-start.3 = (bf16[2,256,128]{2,1,0:T(8,128)(2,1)S(1)}, bf16[2,256,128]{2,1,0:T(8,128)(2,1)S(1)}, u32[]{:S(2)}, u32[]{:S(2)}) collective-permute-start(bf16[2,256,128]{2,1,0:T(8,128)(2,1)S(1)} %pad_maximum_fusion), channel_id=1, source_target_pairs={{0,2},{1,9},{2,0},{3,11},{4,6},{5,13},{6,4},{7,15},{8,10},{9,1},{1... | collective-permute-start | bytes 393224 | tf_op jit(solution)/shard_map/weights_1/ppermute | solution.py:361
  13.5 10.8 %collective-permute-start.2 = (bf16[8,256,128]{2,1,0:T(8,128)(2,1)S(1)}, bf16[8,256,128]{2,1,0:T(8,128)(2,1)S(1)}, u32[]{:S(2)}, u32[]{:S(2)}) collective-permute-start(bf16[8,256,128]{2,1,0:T(8,128)(2,1)S(1)} %add_convert_fusion), channel_id=1, source_target_pairs={{0,2},{1,9},{2,0},{3,11},{4,6},{5,13},{6,4},{7,15},{8,10},{9,1},{1... | collective-permute-start | bytes 1572872 | tf_op jit(solution)/shard_map/gradient_1/ppermute | solution.py:361
  16.9 7.4 %collective-permute-start.4 = (bf16[4,256,128]{2,1,0:T(8,128)(2,1)S(1)}, bf16[4,256,128]{2,1,0:T(8,128)(2,1)S(1)}, u32[]{:S(2)}, u32[]{:S(2)}) collective-permute-start(bf16[4,256,128]{2,1,0:T(8,128)(2,1)S(1)} %constant_dynamic-update-slice_fusion), channel_id=1, source_target_pairs={{0,4},{1,5},{2,6},{3,7},{4,0},{5,1},{6,2},{7,3},{8,12},{9,13},{10,... | collective-permute-start | bytes 786440 | tf_op jit(solution)/shard_map/weights_2/ppermute | solution.py:361
  24.4 17.0 %copy-start.1 = (f32[512,128]{1,0:T(8,128)S(1)}, f32[512,128]{1,0:T(8,128)}, u32[]{:S(2)}) copy-start(f32[512,128]{1,0:T(8,128)} %refs_6_.1) | copy-start | bytes 786436
  24.4 17.0 %copy-start.2 = (f32[512,128]{1,0:T(8,128)S(1)}, f32[512,128]{1,0:T(8,128)}, u32[]{:S(2)}) copy-start(f32[512,128]{1,0:T(8,128)} %refs_7_.1) | copy-start | bytes 786436
  24.5 6.4 %collective-permute-start.6 = (bf16[4,256,128]{2,1,0:T(8,128)(2,1)S(1)}, bf16[4,256,128]{2,1,0:T(8,128)(2,1)S(1)}, u32[]{:S(2)}, u32[]{:S(2)}) collective-permute-start(bf16[4,256,128]{2,1,0:T(8,128)(2,1)S(1)} %get-tuple-element.78), channel_id=1, source_target_pairs={{0,8},{1,3},{2,10},{3,1},{4,12},{5,7},{6,14},{7,5},{8,0},{9,11},{1... | collective-permute-start | bytes 786440 | tf_op jit(solution)/shard_map/gradient_2/ppermute | solution.py:361
  26.2 25.1 %copy-start.3 = (bf16[8,256,128]{2,1,0:T(8,128)(2,1)}, bf16[8,256,128]{2,1,0:T(8,128)(2,1)S(1)}, u32[]{:S(2)}) copy-start(bf16[8,256,128]{2,1,0:T(8,128)(2,1)S(1)} %constant_dynamic-update-slice_fusion.2.refs_4_) | copy-start | bytes 1572868
  26.2 15.2 %collective-permute-start.9 = (bf16[8,256,128]{2,1,0:T(8,128)(2,1)S(1)}, bf16[8,256,128]{2,1,0:T(8,128)(2,1)S(1)}, u32[]{:S(2)}, u32[]{:S(2)}) collective-permute-start(bf16[8,256,128]{2,1,0:T(8,128)(2,1)S(1)} %constant_dynamic-update-slice_fusion.2.refs_4_), channel_id=1, source_target_pairs={{0,1},{1,0},{2,3},{3,2},{4,5},{5,4},{6,7},{7,6},{8,9},{9,8},{10,11... | collective-permute-start | bytes 1572872 | tf_op jit(solution)/shard_map/weights_pair/ppermute | solution.py:447
  26.3 16.5 %collective-permute-start.10 = (bf16[8,256,128]{2,1,0:T(8,128)(2,1)S(1)}, bf16[8,256,128]{2,1,0:T(8,128)(2,1)}, u32[]{:S(2)}, u32[]{:S(2)}) collective-permute-start(bf16[8,256,128]{2,1,0:T(8,128)(2,1)S(1)} %constant_dynamic-update-slice_fusion.2.refs_4_), channel_id=1, source_target_pairs={{0,8},{1,3},{2,10},{3,1},{4,12},{5,7},{6,14},{7,5},{8,0},{9,11},{1... | collective-permute-start | bytes 1572872 | tf_op jit(solution)/shard_map/weights_3/ppermute | solution.py:361
  31.1 5.0 %collective-permute-start.7 = (bf16[2,256,128]{2,1,0:T(8,128)(2,1)S(1)}, bf16[2,256,128]{2,1,0:T(8,128)(2,1)S(1)}, u32[]{:S(2)}, u32[]{:S(2)}) collective-permute-start(bf16[2,256,128]{2,1,0:T(8,128)(2,1)S(1)} %get-tuple-element.80), channel_id=1, source_target_pairs={{0,4},{1,5},{2,6},{3,7},{4,0},{5,1},{6,2},{7,3},{8,12},{9,13},{10,... | collective-permute-start | bytes 393224 | tf_op jit(solution)/shard_map/gradient_3/ppermute | solution.py:361
  36.2 5.2 %collective-permute-start.8 = (bf16[1,256,128]{2,1,0:T(8,128)(2,1)S(1)}, bf16[1,256,128]{2,1,0:T(8,128)(2,1)S(1)}, u32[]{:S(2)}, u32[]{:S(2)}) collective-permute-start(bf16[1,256,128]{2,1,0:T(8,128)(2,1)S(1)} %get-tuple-element.81), channel_id=1, source_target_pairs={{0,16},{1,17},{2,18},{3,19},{4,20},{5,21},{6,22},{7,23},{8,24},{9,... | collective-permute-start | bytes 196616 | tf_op jit(solution)/shard_map/gradient_last/ppermute | solution.py:361
  41.4 1.4 %copy-start.4 = (bf16[8,256,128]{2,1,0:T(8,128)(2,1)}, bf16[8,256,128]{2,1,0:T(8,128)(2,1)S(1)}, u32[]{:S(2)}) copy-start(bf16[8,256,128]{2,1,0:T(8,128)(2,1)S(1)} %collective-permute-done.9.refs_6_) | copy-start | bytes 1572868
  42.8 8.5 %collective-permute-start.11 = (bf16[8,256,128]{2,1,0:T(8,128)(2,1)}, bf16[8,256,128]{2,1,0:T(8,128)(2,1)}, u32[]{:S(2)}, u32[]{:S(2)}) collective-permute-start(bf16[8,256,128]{2,1,0:T(8,128)(2,1)} %collective-permute-done.10.refs_5_), channel_id=1, source_target_pairs={{0,1},{1,0},{2,3},{3,2},{4,5},{5,4},{6,7},{7,6},{8,9},{9,8},{10,11... | collective-permute-start | bytes 1572872 | tf_op jit(solution)/shard_map/ppermute | solution.py:499
  42.8 16.9 %all-to-all-start = ((bf16[16,56,128]{2,1,0:T(8,128)(2,1)}), bf16[16,56,128]{2,1,0:T(8,128)(2,1)S(1)}, u32[]{:S(2)}, u32[]{:S(2)}) async-start(bf16[16,56,128]{2,1,0:T(8,128)(2,1)} %shard_map.130), calls=%async_computation | async-start | bytes 458752 | tf_op jit(solution)/shard_map/all_to_all | solution.py:512
  59.7 1.5 %collective-permute-start.12 = (bf16[16,56,128]{2,1,0:T(8,128)(2,1)S(1)}, bf16[16,56,128]{2,1,0:T(8,128)(2,1)S(1)}, u32[]{:S(2)}, u32[]{:S(2)}) collective-permute-start(bf16[16,56,128]{2,1,0:T(8,128)(2,1)S(1)} %all-to-all-done.refs_4_), channel_id=1, source_target_pairs={{0,1},{1,0},{2,3},{3,2},{4,5},{5,4},{6,7},{7,6},{8,9},{9,8},{10,11... | collective-permute-start | bytes 688136 | tf_op jit(solution)/shard_map/ppermute | solution.py:515
